TPU v7x, 32 devices: a whole 2x2x4 slice. The times are simulated.
32 devices in a mesh: groups: 2 (over x), seq: 16 (over z, y, core).
Axes of the slice: x: 2, y: 2, z: 4, core: 2. Of those that a mesh axis runs over, the one named last changes fastest.
Arguments:
- span_keys: bfloat16 [32768, 512], P(('groups', 'seq')), parts along dimension 0, may hold values from -6 to 6
- span_values: bfloat16 [32768, 512], P(('groups', 'seq')), parts along dimension 0, may hold values from -6 to 6
- block_device: int32 [4096, 1], P(('groups', 'seq')), parts along dimension 0, may hold values from 0 to 15; in each aligned block of 128 rows (0 to 127, 128 to 255, ...) at most 16 rows name the same one
- block_row: int32 [4096], P(('groups', 'seq')), parts along dimension 0, may hold values from 0 to 7
- cache_len: int32 [256], P(('groups', 'seq')), parts along dimension 0, may hold values from 1 to 512, 16384 in all
- cache_keys: bfloat16 [256, 512, 512], P(('groups', 'seq')), parts along dimension 0, may hold values from -6 to 6
- cache_values: bfloat16 [256, 512, 512], P(('groups', 'seq')), parts along dimension 0, may hold values from -6 to 6
- queries: bfloat16 [256, 4, 8192], P(('groups', 'seq')), parts along dimension 0, may hold values from -250 to 250, as said below
- step_keys: bfloat16 [256, 4, 512], P(('groups', 'seq')), parts along dimension 0, may hold values from -6 to 6
- step_values: bfloat16 [256, 4, 512], P(('groups', 'seq')), parts along dimension 0, may hold values from -6 to 6
Outputs:
- attended: bfloat16 [256, 4, 8192], P(('groups', 'seq')), parts along dimension 0
There are 2 independent parts, one for each index of `groups`. A program takes and returns all parts, laid end to end along the dimension named above; each array names one. Nothing has to cross between parts.
Inputs may be any that keep to these rules, and one draw needn't show every extreme that they name: Float queries of order one; a few heads may be much larger. `cache_len`: the lengths of each part along groups sum to 16384.
All inputs are finite; a program needn't handle non-finite values.
Results may differ from a plain program's by a relative error of at most 0.012.
The roundings to bfloat16 on the way count: a program that leaves them out, or rounds other values in their place, can miss the bound.
Values may be sent and summed in bfloat16 or wider, within the bound.
No kernel may reach another device: no remote copies, remote signals or barrier semaphores. Data moves between devices by JAX's collectives and lax.ppermute only.
A program may use at most 128 MiB of HBM per device.

v0:
```python
import functools

import jax
import jax.numpy as jnp
from jax import lax
from jax.experimental import pallas as pl
from jax.experimental.pallas import tpu as pltpu
from jax.sharding import PartitionSpec as P


KVH = 4
QH = 64
HD = 128
BLK = 8
PLANES = 4
CHUNK = 256
SPAN = 128
UNROLL = 4
NEG = -1e30


def frequencies(half_width):
    freq_index = jnp.arange(half_width, dtype=jnp.float32)
    base_freq = 1.0 / 500000.0 ** (freq_index / half_width)
    wavelen = 2.0 * jnp.pi / base_freq
    smooth = (8192.0 / wavelen - 1.0) / 3.0
    blended = (1.0 - smooth) * base_freq / 8.0 + smooth * base_freq
    scaled = jnp.where(wavelen > 8192.0, base_freq / 8.0, blended)
    return jnp.where(wavelen < 2048.0, base_freq, scaled)


def turn_tables(positions):
    freq = frequencies(HD // 2)
    angles = positions.astype(jnp.float32)[..., None] * jnp.concatenate([freq, freq])
    sign = jnp.where(jnp.arange(HD) < HD // 2, -1.0, 1.0).astype(jnp.float32)
    return jnp.cos(angles), jnp.sin(angles) * sign


def pack_kernel(n, cap, target, rows, rel, keys, values, *refs):
    meta = refs[0]
    outs = refs[1 : 1 + n]
    slots, fill, sems = refs[1 + n :]
    blocks = keys.shape[0]

    def clear(i, _):
        fill[i] = 0
        for k in range(cap):
            meta[i * cap + k] = -1
        return 0

    lax.fori_loop(0, n, clear, 0)

    def put(b, _):
        dest = target[b]
        slot = fill[dest]
        fill[dest] = slot + 1
        meta[dest * cap + slot] = rows[b]
        message = rel[dest]
        slots[message, 0, slot] = keys[b]
        slots[message, 1, slot] = values[b]
        return 0

    lax.fori_loop(0, blocks, put, 0, unroll=2)
    copies = [pltpu.make_async_copy(slots.at[i], outs[i], sems.at[i]) for i in range(n)]
    for copy in copies:
        copy.start()
    for copy in copies:
        copy.wait()


def pack(n, cap, target, rows, rel, keys, values):
    width = keys.shape[-1]
    message = jax.ShapeDtypeStruct((2, cap, BLK, width), jnp.bfloat16)
    smem = pl.BlockSpec(memory_space=pltpu.SMEM)
    vmem = pl.BlockSpec(memory_space=pltpu.VMEM)
    return pl.pallas_call(
        functools.partial(pack_kernel, n, cap),
        out_shape=(jax.ShapeDtypeStruct((n * cap,), jnp.int32),) + (message,) * n,
        in_specs=[smem, smem, smem, vmem, vmem],
        out_specs=(smem,) + (pl.BlockSpec(memory_space=pl.ANY),) * n,
        scratch_shapes=[
            pltpu.VMEM((n, 2, cap, BLK, width), jnp.bfloat16),
            pltpu.SMEM((n,), jnp.int32),
            pltpu.SemaphoreType.DMA((n,)),
        ],
        name="pack",
    )(target, rows, rel, keys, values)


def absorb(row, q_ref, pieces, state, fresh):
    acc, top, total = state
    scale = HD ** (-0.5)
    heads = range(KVH)
    queries = [q_ref[row, head] for head in heads]
    keys = [[piece[0](head) for piece in pieces] for head in heads]
    values = [[piece[1](head) for piece in pieces] for head in heads]
    if not fresh:
        old_acc = [acc[row, head] for head in heads]
        old_top = [top[row, head] for head in heads]
        old_total = [total[row, head] for head in heads]
    scores = [
        [
            jnp.where(
                piece[2],
                lax.dot_general(
                    queries[head], key, (((1,), (1,)), ((), ())), preferred_element_type=jnp.float32
                )
                * scale,
                NEG,
            )
            for piece, key in zip(pieces, keys[head])
        ]
        for head in heads
    ]
    new = []
    for head in heads:
        peak = functools.reduce(
            jnp.maximum, [jnp.max(one, axis=-1, keepdims=True) for one in scores[head]]
        )
        new_top = jnp.broadcast_to(peak, (peak.shape[0], HD)) if fresh else jnp.maximum(
            old_top[head], peak
        )
        raw = [jnp.exp(one - new_top[:, :1]) for one in scores[head]]
        added = sum(jnp.sum(one, axis=-1, keepdims=True) for one in raw)
        mixed = sum(
            jnp.dot(one.astype(jnp.bfloat16), value, preferred_element_type=jnp.float32)
            for one, value in zip(raw, values[head])
        )
        if fresh:
            new.append((mixed, new_top, jnp.broadcast_to(added, new_top.shape)))
        else:
            factor = jnp.exp(old_top[head] - new_top)
            new.append(
                (old_acc[head] * factor + mixed, new_top, old_total[head] * factor + added)
            )
    for head in heads:
        acc[row, head], top[row, head], total[row, head] = new[head]


def resident_kernel(
    lens, q_ref, step_k, step_v, keys, values, acc, top, total, kbuf, vbuf, sems
):
    rows, slot_count = kbuf.shape[0], kbuf.shape[1]
    piece = min(CHUNK, slot_count)
    pieces = slot_count // piece
    steps = step_k.shape[1]
    width = q_ref.shape[2]
    group = width // steps

    def copies(r, i):
        part = pl.ds(i * piece, piece)
        return (
            pltpu.make_async_copy(keys.at[r, part], kbuf.at[r, part], sems.at[0, r, i]),
            pltpu.make_async_copy(values.at[r, part], vbuf.at[r, part], sems.at[1, r, i]),
        )

    def fetch(r, _):
        for i in range(pieces):

            @pl.when((i == 0) | (i * piece < lens[r]))
            def _():
                for copy in copies(r, i):
                    copy.start()

        return 0

    lax.fori_loop(0, rows, fetch, 0)
    lane = lax.broadcasted_iota(jnp.int32, (width, piece), 1)
    causal = (
        lax.broadcasted_iota(jnp.int32, (width, steps), 1)
        <= lax.broadcasted_iota(jnp.int32, (width, steps), 0) // group
    )

    def one_row(r, _):
        def part(i):
            span = pl.ds(i * piece, piece)
            return (
                lambda head: kbuf[r, span, head * HD : (head + 1) * HD],
                lambda head: vbuf[r, span, head * HD : (head + 1) * HD],
                lane + i * piece < lens[r],
            )

        own = (
            lambda head: step_k[r, :, head * HD : (head + 1) * HD],
            lambda head: step_v[r, :, head * HD : (head + 1) * HD],
            causal,
        )
        for copy in copies(r, 0):
            copy.wait()
        absorb(r, q_ref, [own, part(0)], (acc, top, total), True)
        for i in range(1, pieces):

            @pl.when(i * piece < lens[r])
            def _():
                for copy in copies(r, i):
                    copy.wait()
                absorb(r, q_ref, [part(i)], (acc, top, total), False)

        return 0

    lax.fori_loop(0, rows, one_row, 0)


def state_shapes(rows, width):
    shape = jax.ShapeDtypeStruct((rows, KVH, width, HD), jnp.float32)
    return (shape,) * 3


def resident(lens, grouped, step_k, step_v, keys, values):
    rows, slot_count, feature = keys.shape
    pieces = slot_count // min(CHUNK, slot_count)
    vmem = pl.BlockSpec(memory_space=pltpu.VMEM)
    hbm = pl.BlockSpec(memory_space=pl.ANY)
    return pl.pallas_call(
        resident_kernel,
        out_shape=state_shapes(rows, grouped.shape[2]),
        in_specs=[pl.BlockSpec(memory_space=pltpu.SMEM), vmem, vmem, vmem, hbm, hbm],
        out_specs=(vmem,) * 3,
        scratch_shapes=[
            pltpu.VMEM((rows, slot_count, feature), jnp.bfloat16),
            pltpu.VMEM((rows, slot_count, feature), jnp.bfloat16),
            pltpu.SemaphoreType.DMA((2, rows, pieces)),
        ],
        cost_estimate=pl.CostEstimate(
            flops=2 * 10**9, bytes_accessed=16 * 2**20, transcendentals=10**6
        ),
        name="resident",
    )(lens, grouped, step_k, step_v, keys, values)


def span_kernel(
    kind, count, cap, base, used, slot_of, row_of, rank_of, start, tokens_of,
    q_ref, ca, sa, cb, sb, *refs,
):
    messages = refs[:count]
    refs = refs[count:]
    if kind == "partial":
        out, stats, acc, top, total, got, kbuf, vbuf, sems = refs
        loads = []
    elif kind == "state":
        *before, acc, top, total, got, kbuf, vbuf, sems = refs
        loads = list(zip(before, (acc, top, total)))
    else:
        *before, part, stats, out, acc, top, total, scr, got, kbuf, vbuf, sems = refs
        loads = list(zip(before, (acc, top, total)))
    state = (acc, top, total)
    rows = q_ref.shape[0]
    width = q_ref.shape[2]
    feature = kbuf.shape[1]
    fetches = [pltpu.make_async_copy(messages[j], got.at[j], sems.at[j]) for j in range(count)]
    for fetch in fetches:
        fetch.start()
    loads = [
        pltpu.make_async_copy(a, b, sems.at[count + i]) for i, (a, b) in enumerate(loads)
    ]
    for load in loads:
        load.start()
    last = start[rows - 1] * BLK + tokens_of[rows - 1]
    tail = pl.ds(pl.multiple_of(last, BLK), SPAN)
    vbuf[tail, :] = jnp.zeros((SPAN, feature), jnp.float32)
    unroll = min(UNROLL, cap)
    for j in range(count):
        first = base[j]
        fetches[j].wait()

        def place(step, _):
            ready = []
            for u in range(unroll):
                k = step * unroll + u
                slot = slot_of[first + k]
                r = row_of[first + k]
                rank = rank_of[first + k]
                c_a, s_a = ca[r], sa[r]
                c_b, s_b = cb[pl.ds(rank, 1), :], sb[pl.ds(rank, 1), :]
                cosine = c_a * c_b - s_a * s_b
                sine = s_a * c_b + c_a * s_b
                where = pl.ds(pl.multiple_of(slot * BLK, BLK), BLK)
                value = got[j, 1, k].astype(jnp.float32)
                key = got[j, 0, k].astype(jnp.float32)
                turned = []
                for head in range(KVH):
                    piece = key[:, head * HD : (head + 1) * HD]
                    turned.append(piece * cosine + pltpu.roll(piece, HD // 2, 1) * sine)
                ready.append((where, turned, value))
            for where, turned, value in ready:
                vbuf[where, :] = value
                for head in range(KVH):
                    kbuf[where, head * HD : (head + 1) * HD] = turned[head]
            return 0

        lax.fori_loop(0, (used[j] + unroll - 1) // unroll, place, 0)
    for load in loads:
        load.wait()
    lane = lax.broadcasted_iota(jnp.int32, (width, SPAN), 1)
    eye = lax.broadcasted_iota(jnp.int32, (width, width), 0) == lax.broadcasted_iota(
        jnp.int32, (width, width), 1
    )

    def one_row(r, _):
        tokens = tokens_of[r]
        origin = start[r] * BLK
        if kind == "partial":
            acc[r] = jnp.zeros_like(acc[r])
            top[r] = jnp.full_like(top[r], NEG)
            total[r] = jnp.zeros_like(total[r])

        def piece(i, _):
            where = pl.ds(pl.multiple_of(origin + i * SPAN, BLK), SPAN)
            block = (
                lambda head: kbuf[where, head * HD : (head + 1) * HD].astype(jnp.bfloat16),
                lambda head: vbuf[where, head * HD : (head + 1) * HD].astype(jnp.bfloat16),
                lane + i * SPAN < tokens,
            )
            absorb(r, q_ref, [block], state, False)
            return 0

        lax.fori_loop(0, (tokens + SPAN - 1) // SPAN, piece, 0)
        if kind == "partial":
            done = []
            for head in range(KVH):
                held = total[r, head]
                safe = jnp.where(held > 0.0, held, 1.0)
                lines = [
                    jnp.sum(jnp.where(eye, one[:, :width], 0.0), axis=0, keepdims=True)
                    for one in (top[r, head], held)
                ]
                done.append(((acc[r, head] / safe).astype(jnp.bfloat16), lines))
            for head in range(KVH):
                out[r, head] = done[head][0]
                for i in range(2):
                    stats[r, head, pl.ds(i, 1), :] = done[head][1][i]
        if kind == "final":
            steps = out.shape[1]
            group = width // steps
            done = []
            for head in range(KVH):
                lines = []
                for i in range(2):
                    line = jnp.broadcast_to(stats[r, head, pl.ds(i, 1), :], (width, width))
                    lines.append(jnp.sum(jnp.where(eye, line, 0.0), axis=1, keepdims=True))
                other_top, other_total = lines
                other_top = jnp.where(other_total > 0.0, other_top, NEG)
                old_top = top[r, head]
                new_top = jnp.maximum(old_top, other_top)
                mine = jnp.exp(old_top - new_top)
                theirs = jnp.exp(other_top - new_top) * other_total
                whole = total[r, head] * mine + theirs
                merged = acc[r, head] * mine + part[r, head].astype(jnp.float32) * theirs
                done.append(merged / whole)
            for head in range(KVH):
                scr[head] = done[head]
            for head in range(KVH):
                for g in range(group):
                    column = (head * group + g) * HD
                    out[r, :, column : column + HD] = scr[
                        head, pl.ds(g, steps, stride=group), :
                    ].astype(jnp.bfloat16)
        return 0

    lax.fori_loop(0, rows, one_row, 0)


def span(kind, cap, scalars, grouped, tables, messages, state, extra, steps):
    rows, _, width, _ = grouped.shape
    feature = messages[0].shape[-1]
    count = len(messages)
    room = (count * cap + 1) * BLK + SPAN
    smem = pl.BlockSpec(memory_space=pltpu.SMEM)
    vmem = pl.BlockSpec(memory_space=pltpu.VMEM)
    hbm = pl.BlockSpec(memory_space=pl.ANY)
    hold = [pltpu.VMEM((rows, KVH, width, HD), jnp.float32)] * 3
    scratch = []
    if kind == "partial":
        out_shape = (
            jax.ShapeDtypeStruct((rows, KVH, width, HD), jnp.bfloat16),
            jax.ShapeDtypeStruct((rows, KVH, 2, width), jnp.float32),
        )
        scratch += hold
    elif kind == "state":
        out_shape = state_shapes(rows, width)
    else:
        out_shape = jax.ShapeDtypeStruct((rows, steps, QH * HD), jnp.bfloat16)
        scratch += hold + [pltpu.VMEM((KVH, width, HD), jnp.float32)]
    scratch += [
        pltpu.VMEM((count, 2, cap, BLK, feature), jnp.bfloat16),
        pltpu.VMEM((room, feature), jnp.float32),
        pltpu.VMEM((room, feature), jnp.float32),
        pltpu.SemaphoreType.DMA((count + 3,)),
    ]
    return pl.pallas_call(
        functools.partial(span_kernel, kind, count, cap),
        out_shape=out_shape,
        in_specs=[smem] * 7 + [vmem] * 5 + [hbm] * (count + len(state)) + [vmem] * len(extra),
        out_specs=jax.tree.map(lambda _: vmem, out_shape),
        scratch_shapes=scratch,
        cost_estimate=pl.CostEstimate(
            flops=10**9, bytes_accessed=12 * 2**20, transcendentals=10**6
        ),
    )(*scalars, grouped, *tables, *messages, *state, *extra)


PHASES = {"d": (2, 2, 2, 2), "f": (0, 3, 3, 0), "g": (3, 0, 0, 3), "b": (1, 1, 1, 1)}


def site_plane(plane, flip):
    dest = plane ^ flip
    half = PLANES // 2
    if (plane < half) != (dest < half) and dest in (half - 1, half):
        return PLANES - 1 - dest
    return dest


def came_from(phase, plane):
    flips = PHASES[phase]
    return next(s for s in range(PLANES) if site_plane(s, flips[s]) == plane)


def for_mirror(phase, plane):
    source = came_from(phase, plane)
    return int(source ^ PHASES[phase][source] != plane)


def route(n, phase, offset):
    in_plane = n // PLANES
    return [
        (
            plane * in_plane + place,
            site_plane(plane, flip) * in_plane + (place + offset) % in_plane,
        )
        for plane, flip in enumerate(PHASES[phase])
        for place in range(in_plane)
    ]


def by_plane(table, plane):
    table = jnp.array(table, jnp.int32)
    chosen = jnp.arange(PLANES, dtype=jnp.int32) == plane
    return jnp.sum(jnp.where(chosen.reshape((-1,) + (1,) * (table.ndim - 1)), table, 0), axis=0)


def body(
    span_keys,
    span_values,
    block_device,
    block_row,
    cache_len,
    cache_keys,
    cache_values,
    queries,
    step_keys,
    step_values,
):
    n = lax.axis_size("seq")
    in_plane = n // PLANES
    me = lax.axis_index("seq").astype(jnp.int32)
    plane, place = me // in_plane, me % in_plane
    rows = cache_len.shape[0]
    feature = span_keys.shape[1]
    blocks = span_keys.shape[0] // BLK
    cap = max(2, (2 * blocks + n - 1) // n)
    steps = queries.shape[1]
    group = QH // KVH
    seq = jnp.arange(n, dtype=jnp.int32)
    names = list(PHASES)

    phase_of_flip = [
        [next(i for i, p in enumerate(names) if PHASES[p][z] == z ^ d) for d in range(PLANES)]
        for z in range(PLANES)
    ]
    rel = (
        jnp.repeat(by_plane(phase_of_flip, plane), in_plane) * in_plane
        + (seq % in_plane - place) % in_plane
    )
    grouped = (
        queries.reshape(rows, steps, KVH, group, HD)
        .transpose(0, 2, 1, 3, 4)
        .reshape(rows, KVH, steps * group, HD)
    )
    half = PLANES // 2
    swap = [
        (a * in_plane + i, b * in_plane + i)
        for a, b in ((half - 1, half), (half, half - 1))
        for i in range(in_plane)
    ]
    mirrored = lax.ppermute(grouped, "seq", swap)

    meta, *messages = pack(
        n,
        cap,
        block_device[:, 0],
        block_row,
        rel,
        span_keys.reshape(blocks, BLK, feature),
        span_values.reshape(blocks, BLK, feature),
    )
    packed = {p: messages[i * in_plane : (i + 1) * in_plane] for i, p in enumerate(names)}

    def send(phase, after=None):
        out = []
        for offset in range(in_plane):
            value = packed[phase][offset]
            if after is not None:
                value, after[offset] = lax.optimization_barrier((value, after[offset]))
            pairs = route(n, phase, offset)
            if any(a != b for a, b in pairs):
                value = lax.ppermute(value, "seq", pairs)
            out.append(value)
        return out

    got = {}
    got["d"] = send("d")
    got["f"] = send("f")
    got["g"] = send("g", got["d"])
    got["b"] = send("b", got["g"])

    table = meta.reshape(PLANES, in_plane, cap)
    mirror_plane = [p if p in (0, PLANES - 1) else PLANES - 1 - p for p in range(PLANES)]
    table_mirror = jnp.concatenate([table[p][None] for p in mirror_plane])
    notes = jnp.concatenate(
        [
            table.reshape(n, cap),
            table_mirror.reshape(n, cap),
            jnp.broadcast_to(cache_len[None], (n, rows)),
        ],
        axis=1,
    )
    notes = lax.all_to_all(notes, "seq", split_axis=0, concat_axis=0, tiled=True)
    mirror_me = by_plane(mirror_plane, plane) * in_plane + place
    mirror_len = jnp.sum(jnp.where((seq == mirror_me)[:, None], notes[:, 2 * cap :], 0), axis=0)
    rows_of = jnp.stack([notes[:, :cap], notes[:, cap : 2 * cap]])

    came = by_plane([[came_from(p, z) for p in names] for z in range(PLANES)], plane)
    other = by_plane([[for_mirror(p, z) for p in names] for z in range(PLANES)], plane)
    offsets = jnp.arange(in_plane, dtype=jnp.int32)
    source = came[:, None] * in_plane + (place - offsets[None]) % in_plane
    entry = (other[:, None] * n + source).reshape(-1)
    kernel_of_phase = {"d": 1, "f": 1, "g": 2, "b": 3}
    stage = jnp.array([[kernel_of_phase[p]] for p in names], jnp.int32)
    stage = jnp.where(other[:, None] == 1, 0, stage)
    stage = jnp.broadcast_to(stage, (len(names), in_plane)).reshape(-1)
    same = entry[:, None] == jnp.arange(2 * n, dtype=jnp.int32)[None]
    stage_of = jnp.max(jnp.where(same, stage[:, None], -1), axis=0).reshape(2, n)

    row_ids = jnp.arange(rows, dtype=jnp.int32)
    hits = rows_of[..., None] == row_ids
    kinds = [(0, None), (1, None), (1, 0), (0, 1), (0, 2), (0, 3)]
    columns = [
        hits[s] if k is None else hits[s] & (stage_of[s] == k)[:, None, None] for s, k in kinds
    ]
    columns = jnp.concatenate([c.reshape(n * cap, rows) for c in columns], axis=1)
    order = jnp.arange(n * cap, dtype=jnp.int32)
    earlier = jnp.dot(
        (order[:, None] > order[None, :]).astype(jnp.bfloat16),
        columns.astype(jnp.bfloat16),
        preferred_element_type=jnp.float32,
    ).astype(jnp.int32)
    number = jnp.sum(columns.astype(jnp.int32), axis=0).reshape(len(kinds), rows)
    below = row_ids[:, None] > row_ids[None, :]
    begin = jnp.sum(jnp.where(below[None], number[:, None, :], 0), axis=2)
    begin_flat = jnp.where(
        jnp.arange(len(kinds))[:, None] < 2, 0, begin
    ).reshape(-1)
    where = jnp.where(columns, earlier + begin_flat[None], 0)
    where = jnp.sum(where.reshape(n * cap, len(kinds), rows), axis=2)
    member = jnp.any(columns.reshape(n * cap, len(kinds), rows), axis=2)
    rank_of = jnp.concatenate([where[:, 0], where[:, 1]])
    spare = SPAN // BLK
    trash = {0: 2 * in_plane * cap + spare, 1: 2 * in_plane * cap + spare, 2: in_plane * cap + spare}
    own_slot = jnp.where(
        member[:, 3], where[:, 3], jnp.where(member[:, 4], where[:, 4], where[:, 5])
    )
    own_trash = jnp.where(stage_of[0] == 1, trash[1], trash[2])
    own_slot = jnp.where(
        rows_of[0].reshape(-1) < 0, jnp.repeat(own_trash, cap), own_slot
    )
    mirror_slot = jnp.where(rows_of[1].reshape(-1) < 0, trash[0], where[:, 2])
    slot_of = jnp.concatenate([own_slot, mirror_slot])
    row_of = jnp.maximum(rows_of.reshape(-1), 0)
    filled = jnp.sum((rows_of >= 0).astype(jnp.int32), axis=2).reshape(-1)
    used = jnp.sum(jnp.where(same, filled[None], 0), axis=1)
    base = entry * cap

    own_tables = turn_tables(cache_len[:, None] + jnp.arange(BLK, dtype=jnp.int32)[None])
    mirror_tables = turn_tables(mirror_len[:, None] + jnp.arange(BLK, dtype=jnp.int32)[None])
    rank_tables = turn_tables(order * BLK)

    def scalars(phases, kernel):
        def part(value):
            return jnp.concatenate(
                [
                    value[names.index(p) * in_plane : (names.index(p) + 1) * in_plane]
                    for p in phases
                ]
            )

        column = kernel + 2
        return (
            part(base),
            jnp.where(part(stage) == kernel, part(used), 0),
            slot_of,
            row_of,
            rank_of,
            begin[column],
            number[column] * BLK,
        )

    state = resident(cache_len, grouped, step_keys, step_values, cache_keys, cache_values)
    partial, stats = span(
        "partial", cap, scalars("df", 0), mirrored,
        mirror_tables + rank_tables, got["d"] + got["f"], (), (), steps,
    )
    partial = lax.ppermute(partial, "seq", swap)
    stats = lax.ppermute(stats, "seq", swap)
    state = span(
        "state", cap, scalars("df", 1), grouped,
        own_tables + rank_tables, got["d"] + got["f"], tuple(state), (), steps,
    )
    state = span(
        "state", cap, scalars("g", 2), grouped,
        own_tables + rank_tables, got["g"], tuple(state), (), steps,
    )
    return span(
        "final", cap, scalars("b", 3), grouped,
        own_tables + rank_tables, got["b"], tuple(state), (partial, stats), steps,
    )


def solution(mesh):
    placed = (
        P(("groups", "seq"), None),
        P(("groups", "seq"), None),
        P(("groups", "seq"), None),
        P(("groups", "seq")),
        P(("groups", "seq")),
        P(("groups", "seq"), None, None),
        P(("groups", "seq"), None, None),
        P(("groups", "seq"), None, None),
        P(("groups", "seq"), None, None),
        P(("groups", "seq"), None, None),
    )

    return jax.shard_map(
        body,
        mesh=mesh,
        in_specs=placed,
        out_specs=P(("groups", "seq"), None, None),
        check_vma=False,
    )
```

profile of v0, /device:TPU:26, one launch (start us, length us, event | category | flops | bytes accessed | tf_op | source)
XLA Modules:
  0.0 140.5 jit_solution(17186491295463860261)
XLA Ops:
  0.0 0.8 select_reduce_fusion.3
  2.2 5.5 %pack.1 = (s32[256]{0:T(256)}, bf16[2,16,8,512]{3,2,1,0:T(8,128)(2,1)}, bf16[2,16,8,512]{3,2,1,0:T(8,128)(2,1)}, bf16[2,16,8,512]{3,2,1,0:T(8,128)(2,1)}, bf16[2...) custom-call(s32[128]{0:T(128)} %bitcast.68, ...), custom_call_target="tpu_custom_call" | custom-call | tf_op jit(solution)/shard_map/pack/pallas_call | solution.py:76
  7.8 0.9 fusion.14
  8.6 0.7 reshape_reshape.3
  9.7 0.7 pad.11.clone
  10.5 0.7 add_add_fusion
  11.1 6.1 %all-to-all-start = ((s32[16,1,40]{2,1,0:T(1,128)}), s32[16,1,40]{2,1,0:T(1,128)S(1)}, u32[]{:S(2)}, u32[]{:S(2)}) async-start(s32[16,1,40]{2,1,0:T(1,128)} %bitcast.5), calls=%async_computation | async-start | bytes 16384 | tf_op jit(solution)/shard_map/all_to_all | solution.py:527
  17.8 2.4 %collective-permute-start.6 = (bf16[2,16,8,512]{3,2,1,0:T(8,128)(2,1)}, bf16[2,16,8,512]{3,2,1,0:T(8,128)(2,1)S(1)}, u32[]{:S(2)}, u32[]{:S(2)}) collective-permute-start(bf16[2,16,8,512]{3,2,1,0:T(8,128)(2,1)} %get-tuple-element.62), channel_id=1, source_target_pairs={{0,6},{1,7},{2,4},{3,5},{4,14},{5,15},{6,12},{7,13},{8,2},{9,3},{1... | collective-permute-start | bytes 786440 | tf_op jit(solution)/shard_map/ppermute | solution.py:506
  20.1 3.3 %collective-permute-start.9 = (bf16[2,16,8,512]{3,2,1,0:T(8,128)(2,1)}, bf16[2,16,8,512]{3,2,1,0:T(8,128)(2,1)S(1)}, u32[]{:S(2)}, u32[]{:S(2)}) collective-permute-start(bf16[2,16,8,512]{3,2,1,0:T(8,128)(2,1)} %get-tuple-element.67), channel_id=1, source_target_pairs={{0,7},{1,4},{2,5},{3,6},{4,15},{5,12},{6,13},{7,14},{8,3},{9,0},{1... | collective-permute-start | bytes 786440 | tf_op jit(solution)/shard_map/ppermute | solution.py:506
  23.4 1.6 %reshape.464 = bf16[8,4,4,16,128]{4,3,2,1,0:T(8,128)(2,1)S(1)} reshape(bf16[8,4,8192]{2,1,0:T(4,128)(2,1)} %param.22) | data formatting | bytes 1048576 | tf_op jit(solution)/shard_map/reshape | solution.py:475
  25.1 1.5 %collective-permute-start.15 = (bf16[8,4,64,128]{3,2,1,0:T(8,128)(2,1)S(1)}, bf16[8,4,64,128]{3,2,1,0:T(8,128)(2,1)}, u32[]{:S(2)}, u32[]{:S(2)}) collective-permute-start(bf16[8,4,64,128]{3,2,1,0:T(8,128)(2,1)S(1)} %bitcast.51), channel_id=1, source_target_pairs={{4,8},{5,9},{6,10},{7,11},{8,4},{9,5},{10,6},{11,7},{20,24},{21,25... | collective-permute-start | bytes 1572872 | tf_op jit(solution)/shard_map/ppermute | solution.py:485
  27.5 0.7 fusion.15
  29.5 1.3 fusion.4
  33.0 0.7 slice_multiply_fusion
  35.2 0.9 fusion.6
  36.7 1.2 compare_select_fusion.4
  38.6 1.0 collective-permute-done.6.refs_2_
  40.2 2.4 %collective-permute-done.9.refs_3_ = bf16[2,16,8,512]{3,2,1,0:T(8,128)(2,1)S(1)} collective-permute-done((bf16[2,16,8,512]{3,2,1,0:T(8,128)(2,1)}, bf16[2,16,8,512]{3,2,1,0:T(8,128)(2,1)S(1)}, u32[]{:S(2)}, u32[]{:S(2)}) %collective-permute-start.9) | collective-permute-done | bytes 262176 | tf_op jit(solution)/shard_map/ppermute | solution.py:506
  42.6 2.7 %collective-permute-start.1 = (bf16[2,16,8,512]{3,2,1,0:T(8,128)(2,1)}, bf16[2,16,8,512]{3,2,1,0:T(8,128)(2,1)S(1)}, u32[]{:S(2)}, u32[]{:S(2)}) collective-permute-start(bf16[2,16,8,512]{3,2,1,0:T(8,128)(2,1)} %get-tuple-element.53), channel_id=1, source_target_pairs={{0,12},{1,13},{2,14},{3,15},{4,4},{5,5},{6,6},{7,7},{8,8},{9,9},{1... | collective-permute-start | bytes 786440 | tf_op jit(solution)/shard_map/ppermute | solution.py:506
  47.2 1.3 collective-permute-done.12.refs_5_
  48.5 3.5 %collective-permute-start.4 = (bf16[2,16,8,512]{3,2,1,0:T(8,128)(2,1)}, bf16[2,16,8,512]{3,2,1,0:T(8,128)(2,1)S(1)}, u32[]{:S(2)}, u32[]{:S(2)}) collective-permute-start(bf16[2,16,8,512]{3,2,1,0:T(8,128)(2,1)} %get-tuple-element.58), channel_id=1, source_target_pairs={{0,13},{1,14},{2,15},{3,12},{4,5},{5,6},{6,7},{7,4},{8,9},{9,10},{... | collective-permute-start | bytes 786440 | tf_op jit(solution)/shard_map/ppermute | solution.py:506
  52.6 5.6 %collective-permute-start.10 = (bf16[2,16,8,512]{3,2,1,0:T(8,128)(2,1)}, bf16[2,16,8,512]{3,2,1,0:T(8,128)(2,1)}, u32[]{:S(2)}, u32[]{:S(2)}) collective-permute-start(bf16[2,16,8,512]{3,2,1,0:T(8,128)(2,1)} %get-tuple-element.68), channel_id=1, source_target_pairs={{0,15},{1,12},{2,13},{3,14},{4,7},{5,4},{6,5},{7,6},{8,11},{9,8},{... | collective-permute-start | bytes 786440 | tf_op jit(solution)/shard_map/ppermute | solution.py:506
  58.3 4.3 %shard_map.147 = (bf16[8,4,64,128]{3,2,1,0:T(8,128)(2,1)}, f32[8,4,2,64]{3,2,1,0:T(2,128)}) custom-call(s32[8]{0:T(128)} %bitcast.62, s32[8]{0:T(128)} %get-tuple-element.123.used, s32[512]{0:T(512)} %pad_add_fusion.2.slot_of, s32[512]{0:T(512)} %max.7.row_of, s32[512]{0:T(512)} %pad_add_fusion.3.rank_of, s32[8]{0:T(128)} %get-tuple-element.115.start, ...), custom_call_target="tpu_custom_call" | custom-call | flops 1000000000 | bytes 12582912 | tf_op jit(solution)/shard_map/pallas_call | solution.py:390
  62.6 0.7 collective-permute-start.16
  63.4 0.8 collective-permute-start.17
  64.2 8.3 %resident.1 = (f32[8,4,64,128]{3,2,1,0:T(8,128)}, f32[8,4,64,128]{3,2,1,0:T(8,128)}, f32[8,4,64,128]{3,2,1,0:T(8,128)}) custom-call(s32[8]{0:T(128)} %lens.1, bf16[8,4,64,128]{3,2,1,0:T(8,128)(2,1)} %bitcast.52, bf16[8,4,512]{2,1,0:T(4,128)(2,1)} %step_k.1, bf16[8,4,512]{2,1,0:T(4,128)(2,1)} %step_v.1, bf16[8,512,512]{2,1,0:T(8,128)(2,1)} %keys.1, ...), custom_call_target="tpu_custom_call" | custom-call | flops 2000000000 | bytes 16777216 | tf_op jit(solution)/shard_map/resident/pallas_call | solution.py:214
  73.9 29.5 %collective-permute-start.2 = (bf16[2,16,8,512]{3,2,1,0:T(8,128)(2,1)S(1)}, bf16[2,16,8,512]{3,2,1,0:T(8,128)(2,1)S(1)}, u32[]{:S(2)}, u32[]{:S(2)}) collective-permute-start(bf16[2,16,8,512]{3,2,1,0:T(8,128)(2,1)S(1)} %copy-done.21), channel_id=1, source_target_pairs={{0,4},{1,5},{2,6},{3,7},{4,0},{5,1},{6,2},{7,3},{8,12},{9,13},{10,... | collective-permute-start | bytes 786440 | tf_op jit(solution)/shard_map/ppermute | solution.py:506
  103.4 1.4 %collective-permute-start.8 = (bf16[2,16,8,512]{3,2,1,0:T(8,128)(2,1)S(1)}, bf16[2,16,8,512]{3,2,1,0:T(8,128)(2,1)S(1)}, u32[]{:S(2)}, u32[]{:S(2)}) collective-permute-start(bf16[2,16,8,512]{3,2,1,0:T(8,128)(2,1)S(1)} %copy-done.19), channel_id=1, source_target_pairs={{0,6},{1,7},{2,4},{3,5},{4,2},{5,3},{6,0},{7,1},{8,14},{9,15},{10,... | collective-permute-start | bytes 786440 | tf_op jit(solution)/shard_map/ppermute | solution.py:506
  104.8 2.3 %collective-permute-start.11 = (bf16[2,16,8,512]{3,2,1,0:T(8,128)(2,1)S(1)}, bf16[2,16,8,512]{3,2,1,0:T(8,128)(2,1)S(1)}, u32[]{:S(2)}, u32[]{:S(2)}) collective-permute-start(bf16[2,16,8,512]{3,2,1,0:T(8,128)(2,1)S(1)} %copy-done.18), channel_id=1, source_target_pairs={{0,7},{1,4},{2,5},{3,6},{4,3},{5,0},{6,1},{7,2},{8,15},{9,12},{10,... | collective-permute-start | bytes 786440 | tf_op jit(solution)/shard_map/ppermute | solution.py:506
  107.7 12.2 %shard_map.145 = (f32[8,4,64,128]{3,2,1,0:T(8,128)}, f32[8,4,64,128]{3,2,1,0:T(8,128)}, f32[8,4,64,128]{3,2,1,0:T(8,128)}) custom-call(s32[8]{0:T(128)} %bitcast.63, s32[8]{0:T(128)} %get-tuple-element.124.used, s32[512]{0:T(512)} %pad_add_fusion.2.slot_of, s32[512]{0:T(512)} %max.7.row_of, s32[512]{0:T(512)} %pad_add_fusion.3.rank_of, ...), custom_call_target="tpu_custom_call" | custom-call | flops 1000000000 | bytes 12582912 | tf_op jit(solution)/shard_map/pallas_call | solution.py:390
  120.0 9.1 %shard_map.146 = (f32[8,4,64,128]{3,2,1,0:T(8,128)}, f32[8,4,64,128]{3,2,1,0:T(8,128)}, f32[8,4,64,128]{3,2,1,0:T(8,128)}) custom-call(s32[4]{0:T(128)} %get-tuple-element.139.base, s32[4]{0:T(128)} %get-tuple-element.137.used, s32[512]{0:T(512)} %pad_add_fusion.2.slot_of, s32[512]{0:T(512)} %max.7.row_of, s32[512]{0:T(512)} %pad_add_fusion.3.rank_of, ...), custom_call_target="tpu_custom_call" | custom-call | flops 1000000000 | bytes 12582912 | tf_op jit(solution)/shard_map/pallas_call | solution.py:390
  130.3 10.2 %shard_map.148 = bf16[8,4,8192]{2,1,0:T(4,128)(2,1)} custom-call(s32[4]{0:T(128)} %get-tuple-element.140.base, s32[4]{0:T(128)} %get-tuple-element.138.used, s32[512]{0:T(512)} %pad_add_fusion.2.slot_of, s32[512]{0:T(512)} %max.7.row_of, s32[512]{0:T(512)} %pad_add_fusion.3.rank_of, s32[8]{0:T(128)} %get-tuple-element.118.start, ...), custom_call_target="tpu_custom_call" | custom-call | flops 1000000000 | bytes 12582912 | tf_op jit(solution)/shard_map/pallas_call | solution.py:390
  (150 shorter events, 13.7 us)
Async XLA Ops:
  0.0 28.2 %copy-start.22 = (s32[4]{0:T(128)S(1)}, s32[4]{0:T(128)}, u32[]{:S(2)}) copy-start(s32[4]{0:T(128)} %constant.126.clone) | copy-start | bytes 52
  0.0 26.6 %copy-start.17 = (s32[8]{0:T(128)S(1)}, s32[8]{0:T(128)}, u32[]{:S(2)}) copy-start(s32[8]{0:T(128)} %lens.1) | copy-start | bytes 100
  11.1 19.8 %all-to-all-start = ((s32[16,1,40]{2,1,0:T(1,128)}), s32[16,1,40]{2,1,0:T(1,128)S(1)}, u32[]{:S(2)}, u32[]{:S(2)}) async-start(s32[16,1,40]{2,1,0:T(1,128)} %bitcast.5), calls=%async_computation | async-start | bytes 16384 | tf_op jit(solution)/shard_map/all_to_all | solution.py:527
  17.2 20.7 %collective-permute-start = (bf16[2,16,8,512]{3,2,1,0:T(8,128)(2,1)}, bf16[2,16,8,512]{3,2,1,0:T(8,128)(2,1)S(1)}, u32[]{:S(2)}, u32[]{:S(2)}) collective-permute-start(bf16[2,16,8,512]{3,2,1,0:T(8,128)(2,1)} %get-tuple-element.52), channel_id=1, source_target_pairs={{0,4},{1,5},{2,6},{3,7},{4,12},{5,13},{6,14},{7,15},{8,0},{9,1},{1... | collective-permute-start | bytes 786440 | tf_op jit(solution)/shard_map/ppermute | solution.py:506
  17.8 20.2 %collective-permute-start.3 = (bf16[2,16,8,512]{3,2,1,0:T(8,128)(2,1)}, bf16[2,16,8,512]{3,2,1,0:T(8,128)(2,1)S(1)}, u32[]{:S(2)}, u32[]{:S(2)}) collective-permute-start(bf16[2,16,8,512]{3,2,1,0:T(8,128)(2,1)} %get-tuple-element.57), channel_id=1, source_target_pairs={{0,5},{1,6},{2,7},{3,4},{4,13},{5,14},{6,15},{7,12},{8,1},{9,2},{1... | collective-permute-start | bytes 786440 | tf_op jit(solution)/shard_map/ppermute | solution.py:506
  17.8 21.9 %collective-permute-start.6 = (bf16[2,16,8,512]{3,2,1,0:T(8,128)(2,1)}, bf16[2,16,8,512]{3,2,1,0:T(8,128)(2,1)S(1)}, u32[]{:S(2)}, u32[]{:S(2)}) collective-permute-start(bf16[2,16,8,512]{3,2,1,0:T(8,128)(2,1)} %get-tuple-element.62), channel_id=1, source_target_pairs={{0,6},{1,7},{2,4},{3,5},{4,14},{5,15},{6,12},{7,13},{8,2},{9,3},{1... | collective-permute-start | bytes 786440 | tf_op jit(solution)/shard_map/ppermute | solution.py:506
  20.1 22.5 %collective-permute-start.9 = (bf16[2,16,8,512]{3,2,1,0:T(8,128)(2,1)}, bf16[2,16,8,512]{3,2,1,0:T(8,128)(2,1)S(1)}, u32[]{:S(2)}, u32[]{:S(2)}) collective-permute-start(bf16[2,16,8,512]{3,2,1,0:T(8,128)(2,1)} %get-tuple-element.67), channel_id=1, source_target_pairs={{0,7},{1,4},{2,5},{3,6},{4,15},{5,12},{6,13},{7,14},{8,3},{9,0},{1... | collective-permute-start | bytes 786440 | tf_op jit(solution)/shard_map/ppermute | solution.py:506
  25.0 39.1 %copy-start = (bf16[8,4,4,16,128]{4,3,1,2,0:T(8,128)(2,1)}, bf16[8,4,4,16,128]{4,3,1,2,0:T(8,128)(2,1)S(1)}, u32[]{:S(2)}) copy-start(bf16[8,4,4,16,128]{4,3,1,2,0:T(8,128)(2,1)S(1)} %copy.19) | copy-start | bytes 1572868
  25.1 33.2 %collective-permute-start.15 = (bf16[8,4,64,128]{3,2,1,0:T(8,128)(2,1)S(1)}, bf16[8,4,64,128]{3,2,1,0:T(8,128)(2,1)}, u32[]{:S(2)}, u32[]{:S(2)}) collective-permute-start(bf16[8,4,64,128]{3,2,1,0:T(8,128)(2,1)S(1)} %bitcast.51), channel_id=1, source_target_pairs={{4,8},{5,9},{6,10},{7,11},{8,4},{9,5},{10,6},{11,7},{20,24},{21,25... | collective-permute-start | bytes 1572872 | tf_op jit(solution)/shard_map/ppermute | solution.py:485
  26.8 31.4 %copy-start.16 = (s32[16]{0:T(128)}, s32[16]{0:T(128)S(1)}, u32[]{:S(2)}) copy-start(s32[16]{0:T(128)S(1)} %broadcast_multiply_fusion) | copy-start | bytes 196
  37.9 20.3 %copy-start.2 = (bf16[2,16,8,512]{3,2,1,0:T(8,128)(2,1)}, bf16[2,16,8,512]{3,2,1,0:T(8,128)(2,1)S(1)}, u32[]{:S(2)}) copy-start(bf16[2,16,8,512]{3,2,1,0:T(8,128)(2,1)S(1)} %collective-permute-done.refs_0_) | copy-start | bytes 786436
  37.9 10.5 %collective-permute-start.12 = (bf16[2,16,8,512]{3,2,1,0:T(8,128)(2,1)}, bf16[2,16,8,512]{3,2,1,0:T(8,128)(2,1)S(1)}, u32[]{:S(2)}, u32[]{:S(2)}) collective-permute-start(bf16[2,16,8,512]{3,2,1,0:T(8,128)(2,1)} %get-tuple-element.79), channel_id=1, source_target_pairs={{0,1},{1,2},{2,3},{3,0},{4,5},{5,6},{6,7},{7,4},{8,9},{9,10},{10,1... | collective-permute-start | bytes 786440 | tf_op jit(solution)/shard_map/ppermute | solution.py:506
  38.0 20.3 %copy-start.3 = (bf16[2,16,8,512]{3,2,1,0:T(8,128)(2,1)}, bf16[2,16,8,512]{3,2,1,0:T(8,128)(2,1)S(1)}, u32[]{:S(2)}) copy-start(bf16[2,16,8,512]{3,2,1,0:T(8,128)(2,1)S(1)} %collective-permute-done.3.refs_1_) | copy-start | bytes 786436
  38.0 14.0 %collective-permute-start.13 = (bf16[2,16,8,512]{3,2,1,0:T(8,128)(2,1)}, bf16[2,16,8,512]{3,2,1,0:T(8,128)(2,1)S(1)}, u32[]{:S(2)}, u32[]{:S(2)}) collective-permute-start(bf16[2,16,8,512]{3,2,1,0:T(8,128)(2,1)} %get-tuple-element.80), channel_id=1, source_target_pairs={{0,2},{1,3},{2,0},{3,1},{4,6},{5,7},{6,4},{7,5},{8,10},{9,11},{10,... | collective-permute-start | bytes 786440 | tf_op jit(solution)/shard_map/ppermute | solution.py:506
  39.6 18.7 %copy-start.4 = (bf16[2,16,8,512]{3,2,1,0:T(8,128)(2,1)}, bf16[2,16,8,512]{3,2,1,0:T(8,128)(2,1)S(1)}, u32[]{:S(2)}) copy-start(bf16[2,16,8,512]{3,2,1,0:T(8,128)(2,1)S(1)} %collective-permute-done.6.refs_2_) | copy-start | bytes 786436
  39.6 13.0 %collective-permute-start.14 = (bf16[2,16,8,512]{3,2,1,0:T(8,128)(2,1)}, bf16[2,16,8,512]{3,2,1,0:T(8,128)(2,1)S(1)}, u32[]{:S(2)}, u32[]{:S(2)}) collective-permute-start(bf16[2,16,8,512]{3,2,1,0:T(8,128)(2,1)} %get-tuple-element.81), channel_id=1, source_target_pairs={{0,3},{1,0},{2,1},{3,2},{4,7},{5,4},{6,5},{7,6},{8,11},{9,8},{10,9... | collective-permute-start | bytes 786440 | tf_op jit(solution)/shard_map/ppermute | solution.py:506
  42.6 15.7 %copy-start.5 = (bf16[2,16,8,512]{3,2,1,0:T(8,128)(2,1)}, bf16[2,16,8,512]{3,2,1,0:T(8,128)(2,1)S(1)}, u32[]{:S(2)}) copy-start(bf16[2,16,8,512]{3,2,1,0:T(8,128)(2,1)S(1)} %collective-permute-done.9.refs_3_) | copy-start | bytes 786436
  42.6 20.7 %collective-permute-start.1 = (bf16[2,16,8,512]{3,2,1,0:T(8,128)(2,1)}, bf16[2,16,8,512]{3,2,1,0:T(8,128)(2,1)S(1)}, u32[]{:S(2)}, u32[]{:S(2)}) collective-permute-start(bf16[2,16,8,512]{3,2,1,0:T(8,128)(2,1)} %get-tuple-element.53), channel_id=1, source_target_pairs={{0,12},{1,13},{2,14},{3,15},{4,4},{5,5},{6,6},{7,7},{8,8},{9,9},{1... | collective-permute-start | bytes 786440 | tf_op jit(solution)/shard_map/ppermute | solution.py:506
  48.5 25.4 %collective-permute-start.4 = (bf16[2,16,8,512]{3,2,1,0:T(8,128)(2,1)}, bf16[2,16,8,512]{3,2,1,0:T(8,128)(2,1)S(1)}, u32[]{:S(2)}, u32[]{:S(2)}) collective-permute-start(bf16[2,16,8,512]{3,2,1,0:T(8,128)(2,1)} %get-tuple-element.58), channel_id=1, source_target_pairs={{0,13},{1,14},{2,15},{3,12},{4,5},{5,6},{6,7},{7,4},{8,9},{9,10},{... | collective-permute-start | bytes 786440 | tf_op jit(solution)/shard_map/ppermute | solution.py:506
  51.9 51.4 %collective-permute-start.7 = (bf16[2,16,8,512]{3,2,1,0:T(8,128)(2,1)}, bf16[2,16,8,512]{3,2,1,0:T(8,128)(2,1)}, u32[]{:S(2)}, u32[]{:S(2)}) collective-permute-start(bf16[2,16,8,512]{3,2,1,0:T(8,128)(2,1)} %get-tuple-element.63), channel_id=1, source_target_pairs={{0,14},{1,15},{2,12},{3,13},{4,6},{5,7},{6,4},{7,5},{8,10},{9,11},... | collective-permute-start | bytes 786440 | tf_op jit(solution)/shard_map/ppermute | solution.py:506
  52.6 50.7 %collective-permute-start.10 = (bf16[2,16,8,512]{3,2,1,0:T(8,128)(2,1)}, bf16[2,16,8,512]{3,2,1,0:T(8,128)(2,1)}, u32[]{:S(2)}, u32[]{:S(2)}) collective-permute-start(bf16[2,16,8,512]{3,2,1,0:T(8,128)(2,1)} %get-tuple-element.68), channel_id=1, source_target_pairs={{0,15},{1,12},{2,13},{3,14},{4,7},{5,4},{6,5},{7,6},{8,11},{9,8},{... | collective-permute-start | bytes 786440 | tf_op jit(solution)/shard_map/ppermute | solution.py:506
  62.6 66.6 %collective-permute-start.16 = (bf16[8,4,64,128]{3,2,1,0:T(8,128)(2,1)}, bf16[8,4,64,128]{3,2,1,0:T(8,128)(2,1)S(1)}, u32[]{:S(2)}, u32[]{:S(2)}) collective-permute-start(bf16[8,4,64,128]{3,2,1,0:T(8,128)(2,1)} %get-tuple-element.91), channel_id=1, source_target_pairs={{4,8},{5,9},{6,10},{7,11},{8,4},{9,5},{10,6},{11,7},{20,24},{21,25... | collective-permute-start | bytes 1572872 | tf_op jit(solution)/shard_map/ppermute | solution.py:612
  63.3 40.0 %copy-start.20 = (bf16[2,16,8,512]{3,2,1,0:T(8,128)(2,1)S(1)}, bf16[2,16,8,512]{3,2,1,0:T(8,128)(2,1)}, u32[]{:S(2)}) copy-start(bf16[2,16,8,512]{3,2,1,0:T(8,128)(2,1)} %get-tuple-element.59) | copy-start | bytes 786436
  63.3 40.0 %copy-start.19 = (bf16[2,16,8,512]{3,2,1,0:T(8,128)(2,1)S(1)}, bf16[2,16,8,512]{3,2,1,0:T(8,128)(2,1)}, u32[]{:S(2)}) copy-start(bf16[2,16,8,512]{3,2,1,0:T(8,128)(2,1)} %get-tuple-element.64) | copy-start | bytes 786436
  63.4 41.5 %copy-start.18 = (bf16[2,16,8,512]{3,2,1,0:T(8,128)(2,1)S(1)}, bf16[2,16,8,512]{3,2,1,0:T(8,128)(2,1)}, u32[]{:S(2)}) copy-start(bf16[2,16,8,512]{3,2,1,0:T(8,128)(2,1)} %get-tuple-element.69) | copy-start | bytes 786436
  63.4 41.4 %collective-permute-start.17 = (f32[8,4,2,64]{3,2,1,0:T(2,128)}, f32[8,4,2,64]{3,2,1,0:T(2,128)S(1)}, u32[]{:S(2)}, u32[]{:S(2)}) collective-permute-start(f32[8,4,2,64]{3,2,1,0:T(2,128)} %get-tuple-element.92), channel_id=1, source_target_pairs={{4,8},{5,9},{6,10},{7,11},{8,4},{9,5},{10,6},{11,7},{20,24},{21,25... | collective-permute-start | bytes 49160 | tf_op jit(solution)/shard_map/ppermute | solution.py:613
  73.9 46.1 %copy-start.10 = (bf16[2,16,8,512]{3,2,1,0:T(8,128)(2,1)}, bf16[2,16,8,512]{3,2,1,0:T(8,128)(2,1)S(1)}, u32[]{:S(2)}) copy-start(bf16[2,16,8,512]{3,2,1,0:T(8,128)(2,1)S(1)} %collective-permute-done.4.refs_1_) | copy-start | bytes 786436
  73.9 55.2 %collective-permute-start.2 = (bf16[2,16,8,512]{3,2,1,0:T(8,128)(2,1)S(1)}, bf16[2,16,8,512]{3,2,1,0:T(8,128)(2,1)S(1)}, u32[]{:S(2)}, u32[]{:S(2)}) collective-permute-start(bf16[2,16,8,512]{3,2,1,0:T(8,128)(2,1)S(1)} %copy-done.21), channel_id=1, source_target_pairs={{0,4},{1,5},{2,6},{3,7},{4,0},{5,1},{6,2},{7,3},{8,12},{9,13},{10,... | collective-permute-start | bytes 786440 | tf_op jit(solution)/shard_map/ppermute | solution.py:506
  103.3 25.8 %collective-permute-start.5 = (bf16[2,16,8,512]{3,2,1,0:T(8,128)(2,1)S(1)}, bf16[2,16,8,512]{3,2,1,0:T(8,128)(2,1)S(1)}, u32[]{:S(2)}, u32[]{:S(2)}) collective-permute-start(bf16[2,16,8,512]{3,2,1,0:T(8,128)(2,1)S(1)} %copy-done.20), channel_id=1, source_target_pairs={{0,5},{1,6},{2,7},{3,4},{4,1},{5,2},{6,3},{7,0},{8,13},{9,14},{10,... | collective-permute-start | bytes 786440 | tf_op jit(solution)/shard_map/ppermute | solution.py:506
  103.4 25.8 %collective-permute-start.8 = (bf16[2,16,8,512]{3,2,1,0:T(8,128)(2,1)S(1)}, bf16[2,16,8,512]{3,2,1,0:T(8,128)(2,1)S(1)}, u32[]{:S(2)}, u32[]{:S(2)}) collective-permute-start(bf16[2,16,8,512]{3,2,1,0:T(8,128)(2,1)S(1)} %copy-done.19), channel_id=1, source_target_pairs={{0,6},{1,7},{2,4},{3,5},{4,2},{5,3},{6,0},{7,1},{8,14},{9,15},{10,... | collective-permute-start | bytes 786440 | tf_op jit(solution)/shard_map/ppermute | solution.py:506
  104.8 24.3 %copy-start.15 = (f32[8,4,2,64]{3,2,1,0:T(2,128)}, f32[8,4,2,64]{3,2,1,0:T(2,128)S(1)}, u32[]{:S(2)}) copy-start(f32[8,4,2,64]{3,2,1,0:T(2,128)S(1)} %collective-permute-done.17.refs_8_) | copy-start | bytes 49156
  104.8 24.4 %collective-permute-start.11 = (bf16[2,16,8,512]{3,2,1,0:T(8,128)(2,1)S(1)}, bf16[2,16,8,512]{3,2,1,0:T(8,128)(2,1)S(1)}, u32[]{:S(2)}, u32[]{:S(2)}) collective-permute-start(bf16[2,16,8,512]{3,2,1,0:T(8,128)(2,1)S(1)} %copy-done.18), channel_id=1, source_target_pairs={{0,7},{1,4},{2,5},{3,6},{4,3},{5,0},{6,1},{7,2},{8,15},{9,12},{10,... | collective-permute-start | bytes 786440 | tf_op jit(solution)/shard_map/ppermute | solution.py:506
  (10 other events, 45.9 us)
where the time goes:
time: 141 us
  starting transfers between devices  61.5 us (44%)
  Pallas kernels  49.7 us (35%)
  other arithmetic  10.8 us (8%)
  local copies, waits for them, and re-layouts  10.7 us (8%)
  waiting for transfers between devices  5.17 us (4%)
  between operations  2.49 us (2%)
    ppermute x15, starting transfers between devices, send(): value = lax.ppermute(value, 'seq', pairs)  52.5 us
    pallas_call x4, Pallas kernels, span(): pl.pallas_call(functools.partial(span_kernel, kind, count, cap), out_shap...  35.8 us
    pallas_call x1, Pallas kernels, resident(): pl.pallas_call(resident_kernel, out_shape=state_shapes(rows, grouped.shap...  8.32 us
    all_to_all x1, starting transfers between devices, body(): lax.all_to_all(notes, 'seq', split_axis=0, concat_axis=0, tiled=True)  6.07 us
    pallas_call x1, Pallas kernels, pack(): pl.pallas_call(functools.partial(pack_kernel, n, cap), out_shape=(jax.Sha...  5.52 us
    ppermute x15, waiting for transfers between devices, send(): value = lax.ppermute(value, 'seq', pairs)  5.16 us
  transfers between devices with their start and end apart: 19, of which 4 were waited for; matrix products, arithmetic and copies ran while one was open for 11% of the time, Pallas kernels for 24%

commit v1 on v0

v1 whole, which is shorter than its diff:
```python
import functools

import jax
import jax.numpy as jnp
import numpy as np
from jax import lax
from jax.experimental import pallas as pl
from jax.experimental.pallas import tpu as pltpu
from jax.sharding import PartitionSpec as P


KVH = 4
QH = 64
HD = 128
BLK = 8
PLANES = 4
CHUNK = 256
SPAN = 128
LANES = 128
GRANT = 20 * 2**20
UNROLL = 4
NEG = -1e30


def frequencies(half_width):
    freq_index = jnp.arange(half_width, dtype=jnp.float32)
    base_freq = 1.0 / 500000.0 ** (freq_index / half_width)
    wavelen = 2.0 * jnp.pi / base_freq
    smooth = (8192.0 / wavelen - 1.0) / 3.0
    blended = (1.0 - smooth) * base_freq / 8.0 + smooth * base_freq
    scaled = jnp.where(wavelen > 8192.0, base_freq / 8.0, blended)
    return jnp.where(wavelen < 2048.0, base_freq, scaled)


def turn_tables(positions):
    freq = frequencies(HD // 2)
    angles = positions.astype(jnp.float32)[..., None] * jnp.concatenate([freq, freq])
    sign = jnp.where(jnp.arange(HD) < HD // 2, -1.0, 1.0).astype(jnp.float32)
    return jnp.cos(angles), jnp.sin(angles) * sign


def pack_kernel(n, cap, phase_table, target, rows, lens, keys, values, *refs):
    notes = refs[0]
    outs = refs[1 : 1 + n]
    slots, fill, rel, sems = refs[1 + n :]
    blocks = keys.shape[0]
    in_plane = n // PLANES
    me = lax.axis_index("seq")
    plane, place = me // in_plane, me % in_plane

    def clear(i, _):
        fill[i] = 0
        offset = (i % in_plane - place + in_plane) % in_plane
        rel[i] = phase_table[plane, i // in_plane] * in_plane + offset
        for k in range(cap):
            notes[i, k] = -1
            notes[i, LANES + k] = -1
        for k in range(lens.shape[0]):
            notes[i, 2 * LANES + k] = lens[k]
        return 0

    lax.fori_loop(0, n, clear, 0)

    def put(b, _):
        dest = target[b]
        slot = fill[dest]
        fill[dest] = slot + 1
        row = rows[b]
        dest_plane = dest // in_plane
        inner = (dest_plane > 0) & (dest_plane < PLANES - 1)
        twin = jnp.where(inner, (PLANES - 1 - 2 * dest_plane) * in_plane + dest, dest)
        notes[dest, slot] = row
        notes[twin, LANES + slot] = row
        message = rel[dest]
        slots[message, 0, slot] = keys[b]
        slots[message, 1, slot] = values[b]
        return 0

    lax.fori_loop(0, blocks, put, 0, unroll=4)
    copies = [pltpu.make_async_copy(slots.at[i], outs[i], sems.at[i]) for i in range(n)]
    for copy in copies:
        copy.start()
    for copy in copies:
        copy.wait()


def pack(n, cap, phase_table, target, rows, lens, keys, values):
    width = keys.shape[-1]
    message = jax.ShapeDtypeStruct((2, cap, BLK, width), jnp.bfloat16)
    smem = pl.BlockSpec(memory_space=pltpu.SMEM)
    vmem = pl.BlockSpec(memory_space=pltpu.VMEM)
    return pl.pallas_call(
        functools.partial(pack_kernel, n, cap),
        out_shape=(jax.ShapeDtypeStruct((n, 3 * LANES), jnp.int32),) + (message,) * n,
        in_specs=[smem] * 4 + [vmem] * 2,
        out_specs=(smem,) + (pl.BlockSpec(memory_space=pl.ANY),) * n,
        scratch_shapes=[
            pltpu.VMEM((n, 2, cap, BLK, width), jnp.bfloat16),
            pltpu.SMEM((n,), jnp.int32),
            pltpu.SMEM((n,), jnp.int32),
            pltpu.SemaphoreType.DMA((n,)),
        ],
        compiler_params=pltpu.CompilerParams(vmem_limit_bytes=GRANT),
        name="pack",
    )(phase_table, target, rows, lens, keys, values)


def index_kernel(n, cap, rows, notes, stages, place, row_of, rank_of, used, tally):
    f32 = jnp.float32

    def iotas(shape):
        return [lax.broadcasted_iota(jnp.int32, shape, d) for d in (0, 1)]

    a, b = iotas((cap, cap))
    before = (a < b).astype(f32)
    a, b = iotas((n, n))
    sooner = (b < a).astype(f32)
    lines = [jnp.broadcast_to(stages[i : i + 1, :n], (n, n)) for i in range(2)]
    posts = [
        jnp.sum(jnp.where(a == b, line, 0), axis=1, keepdims=True) for line in lines
    ]
    mates = [jnp.where(line == post, sooner, 0.0) for line, post in zip(lines, posts)]
    kernel, lane = iotas((8, LANES))
    counts = jnp.zeros((8, LANES), f32)
    for side in range(2):
        rows_here = notes[:, side * LANES : side * LANES + cap]
        rank = jnp.zeros((n, cap), f32)
        local = jnp.zeros((n, cap), f32)
        for r in range(rows):
            hit = (rows_here == r).astype(f32)
            inside = jnp.dot(hit, before, preferred_element_type=f32)
            ahead = jnp.dot(sooner, hit, preferred_element_type=f32)
            near = jnp.dot(mates[side], hit, preferred_element_type=f32)
            rank += hit * (inside + jnp.sum(ahead, axis=1, keepdims=True))
            local += hit * (inside + jnp.sum(near, axis=1, keepdims=True))
            per_source = jnp.sum(hit, axis=1, keepdims=True)
            for stage in range(3):
                if (stage == 0) == (side == 1):
                    number = jnp.sum(
                        jnp.where(posts[side] == stage, per_source, 0.0), axis=0, keepdims=True
                    )
                    counts += jnp.where((kernel == stage) & (lane == r), number, 0.0)
        span = slice(side * n, side * n + n)
        valid = rows_here >= 0
        place[span, :] = jnp.where(valid, local, -1.0).astype(jnp.int32)
        row_of[span, :] = jnp.maximum(rows_here, 0)
        rank_of[span, :] = rank.astype(jnp.int32)
        filled = jnp.sum(valid.astype(f32), axis=1, keepdims=True)
        used[span, :] = jnp.broadcast_to(filled, (n, cap)).astype(jnp.int32)
    a, b = iotas((LANES, LANES))
    begin = jnp.dot(counts, (a < b).astype(f32), preferred_element_type=f32)
    tally[0:8, :] = begin.astype(jnp.int32)
    tally[8:16, :] = (counts * BLK).astype(jnp.int32)


def index(n, cap, rows, notes, stages):
    vmem = pl.BlockSpec(memory_space=pltpu.VMEM)
    slots = jax.ShapeDtypeStruct((2 * n, cap), jnp.int32)
    return pl.pallas_call(
        functools.partial(index_kernel, n, cap, rows),
        out_shape=(slots,) * 4 + (jax.ShapeDtypeStruct((16, LANES), jnp.int32),),
        in_specs=[vmem] * 2,
        out_specs=(vmem,) * 5,
        compiler_params=pltpu.CompilerParams(vmem_limit_bytes=GRANT),
        name="index",
    )(notes, stages)


def blend(queries, pieces, old, guard=False):
    scale = HD ** (-0.5)
    heads = range(KVH)
    scores = [
        [
            jnp.where(
                piece[2],
                lax.dot_general(
                    queries[head],
                    piece[0][head],
                    (((1,), (1,)), ((), ())),
                    preferred_element_type=jnp.float32,
                )
                * scale,
                NEG,
            )
            for piece in pieces
        ]
        for head in heads
    ]
    new = []
    for head in heads:
        peak = functools.reduce(
            jnp.maximum, [jnp.max(one, axis=-1, keepdims=True) for one in scores[head]]
        )
        if old is None:
            new_top = jnp.broadcast_to(peak, (peak.shape[0], HD))
        else:
            old_acc, old_top, old_total = old[head]
            new_top = jnp.maximum(old_top, peak)
        raw = [jnp.exp(one - new_top[:, :1]) for one in scores[head]]
        if guard:
            raw = [jnp.where(piece[2], one, 0.0) for piece, one in zip(pieces, raw)]
        added = sum(jnp.sum(one, axis=-1, keepdims=True) for one in raw)
        mixed = sum(
            jnp.dot(one.astype(jnp.bfloat16), piece[1][head], preferred_element_type=jnp.float32)
            for one, piece in zip(raw, pieces)
        )
        if old is None:
            new.append((mixed, new_top, jnp.broadcast_to(added, new_top.shape)))
        else:
            factor = jnp.exp(old_top - new_top)
            new.append((old_acc * factor + mixed, new_top, old_total * factor + added))
    return new


def held(row, state):
    return [tuple(one[row, head] for one in state) for head in range(KVH)]


def hold(row, state, new):
    for head in range(KVH):
        for one, value in zip(state, new[head]):
            one[row, head] = value


def row_queries(row, q_ref):
    return [q_ref[row, head] for head in range(KVH)]


def resident_kernel(
    lens, q_ref, step_k, step_v, keys, values, acc, top, total, kbuf, vbuf, sems
):
    rows, slot_count = kbuf.shape[0], kbuf.shape[1]
    piece = min(CHUNK, slot_count)
    pieces = slot_count // piece
    steps = step_k.shape[1]
    width = q_ref.shape[2]
    group = width // steps

    def copies(r, i):
        part = pl.ds(i * piece, piece)
        return (
            pltpu.make_async_copy(keys.at[r, part], kbuf.at[r, part], sems.at[0, r, i]),
            pltpu.make_async_copy(values.at[r, part], vbuf.at[r, part], sems.at[1, r, i]),
        )

    def fetch(r, _):
        for i in range(pieces):

            @pl.when((i == 0) | (i * piece < lens[r]))
            def _():
                for copy in copies(r, i):
                    copy.start()

        return 0

    lax.fori_loop(0, rows, fetch, 0)
    lane = lax.broadcasted_iota(jnp.int32, (width, piece), 1)
    causal = (
        lax.broadcasted_iota(jnp.int32, (width, steps), 1)
        <= lax.broadcasted_iota(jnp.int32, (width, steps), 0) // group
    )

    def one_row(r, _):
        def part(i):
            span = pl.ds(i * piece, piece)
            return (
                [kbuf[r, span, head * HD : (head + 1) * HD] for head in range(KVH)],
                [vbuf[r, span, head * HD : (head + 1) * HD] for head in range(KVH)],
                lane + i * piece < lens[r],
            )

        own = (
            [step_k[r, :, head * HD : (head + 1) * HD] for head in range(KVH)],
            [step_v[r, :, head * HD : (head + 1) * HD] for head in range(KVH)],
            causal,
        )
        state = (acc, top, total)
        for copy in copies(r, 0):
            copy.wait()
        hold(r, state, blend(row_queries(r, q_ref), [own, part(0)], None))
        for i in range(1, pieces):

            @pl.when(i * piece < lens[r])
            def _():
                for copy in copies(r, i):
                    copy.wait()
                hold(r, state, blend(row_queries(r, q_ref), [part(i)], held(r, state)))

        return 0

    lax.fori_loop(0, rows, one_row, 0)


def state_shapes(rows, width):
    shape = jax.ShapeDtypeStruct((rows, KVH, width, HD), jnp.float32)
    return (shape,) * 3


def resident(lens, grouped, step_k, step_v, keys, values):
    rows, slot_count, feature = keys.shape
    pieces = slot_count // min(CHUNK, slot_count)
    vmem = pl.BlockSpec(memory_space=pltpu.VMEM)
    hbm = pl.BlockSpec(memory_space=pl.ANY)
    return pl.pallas_call(
        resident_kernel,
        out_shape=state_shapes(rows, grouped.shape[2]),
        in_specs=[pl.BlockSpec(memory_space=pltpu.SMEM), vmem, vmem, vmem, hbm, hbm],
        out_specs=(vmem,) * 3,
        scratch_shapes=[
            pltpu.VMEM((rows, slot_count, feature), jnp.bfloat16),
            pltpu.VMEM((rows, slot_count, feature), jnp.bfloat16),
            pltpu.SemaphoreType.DMA((2, rows, pieces)),
        ],
        compiler_params=pltpu.CompilerParams(vmem_limit_bytes=GRANT),
        cost_estimate=pl.CostEstimate(
            flops=2 * 10**9, bytes_accessed=16 * 2**20, transcendentals=10**6
        ),
        name="resident",
    )(lens, grouped, step_k, step_v, keys, values)


def span_kernel(
    kind, kernel, count, cap, entry, stage, place_of, row_of, rank_of, used, tally,
    q_ref, ca, sa, cb, sb, *refs,
):
    messages = refs[:count]
    refs = refs[count:]
    if kind == "partial":
        out, stats, acc, top, total, got, kbuf, vbuf, sems = refs
        loads = []
    elif kind == "state":
        *before, acc, top, total, got, kbuf, vbuf, sems = refs
        loads = list(zip(before, (acc, top, total)))
    else:
        *before, part, stats, out, acc, top, total, scr, got, kbuf, vbuf, sems = refs
        loads = list(zip(before, (acc, top, total)))
    state = (acc, top, total)
    rows = q_ref.shape[0]
    width = q_ref.shape[2]
    feature = kbuf.shape[1]
    fetches = [pltpu.make_async_copy(messages[j], got.at[j], sems.at[j]) for j in range(count)]
    for j in range(count):

        @pl.when(stage[j] == kernel)
        def _():
            fetches[j].start()

    loads = [
        pltpu.make_async_copy(a, b, sems.at[count + i]) for i, (a, b) in enumerate(loads)
    ]
    for load in loads:
        load.start()
    last = tally[kernel, rows - 1] * BLK + tally[8 + kernel, rows - 1]
    tail = pl.ds(pl.multiple_of(last, BLK), SPAN)
    vbuf[tail, :] = jnp.zeros((SPAN, feature), jnp.float32)
    unroll = min(UNROLL, cap)
    trash = count * cap + SPAN // BLK
    for j in range(count):

        @pl.when(stage[j] == kernel)
        def _():
            source = entry[j]
            fetches[j].wait()

            def place(step, _):
                ready = []
                for u in range(unroll):
                    k = step * unroll + u
                    r = row_of[source, k]
                    rank = rank_of[source, k]
                    local = place_of[source, k]
                    slot = jnp.where(local < 0, trash, tally[kernel, r] + local)
                    c_a, s_a = ca[r], sa[r]
                    c_b, s_b = cb[pl.ds(rank, 1), :], sb[pl.ds(rank, 1), :]
                    cosine = c_a * c_b - s_a * s_b
                    sine = s_a * c_b + c_a * s_b
                    where = pl.ds(pl.multiple_of(slot * BLK, BLK), BLK)
                    value = got[j, 1, k].astype(jnp.float32)
                    key = got[j, 0, k].astype(jnp.float32)
                    turned = []
                    for head in range(KVH):
                        piece = key[:, head * HD : (head + 1) * HD]
                        turned.append(piece * cosine + pltpu.roll(piece, HD // 2, 1) * sine)
                    ready.append((where, turned, value))
                for where, turned, value in ready:
                    vbuf[where, :] = value
                    for head in range(KVH):
                        kbuf[where, head * HD : (head + 1) * HD] = turned[head]
                return 0

            lax.fori_loop(0, (used[source, 0] + unroll - 1) // unroll, place, 0)

    for load in loads:
        load.wait()
    lane = lax.broadcasted_iota(jnp.int32, (width, SPAN), 1)
    eye = lax.broadcasted_iota(jnp.int32, (width, width), 0) == lax.broadcasted_iota(
        jnp.int32, (width, width), 1
    )

    def block(r, i):
        where = pl.ds(pl.multiple_of(tally[kernel, r] * BLK + i * SPAN, BLK), SPAN)
        return (
            [kbuf[where, h * HD : (h + 1) * HD].astype(jnp.bfloat16) for h in range(KVH)],
            [vbuf[where, h * HD : (h + 1) * HD].astype(jnp.bfloat16) for h in range(KVH)],
            lane + i * SPAN < tally[8 + kernel, r],
        )

    def beyond(r):
        def piece(i, _):
            hold(r, state, blend(row_queries(r, q_ref), [block(r, i)], held(r, state)))
            return 0

        lax.fori_loop(1, (tally[8 + kernel, r] + SPAN - 1) // SPAN, piece, 0)

    def partial_rows(pair):
        new = [blend(row_queries(r, q_ref), [block(r, 0)], None, guard=True) for r in pair]
        for r, one in zip(pair, new):
            hold(r, state, one)
        for r in pair:
            beyond(r)
        done = []
        for r in pair:
            for head in range(KVH):
                amount = total[r, head]
                safe = jnp.where(amount > 0.0, amount, 1.0)
                lines = [
                    jnp.sum(jnp.where(eye, one[:, :width], 0.0), axis=0, keepdims=True)
                    for one in (top[r, head], amount)
                ]
                done.append((r, head, (acc[r, head] / safe).astype(jnp.bfloat16), lines))
        for r, head, value, lines in done:
            out[r, head] = value
            for i in range(2):
                stats[r, head, pl.ds(i, 1), :] = lines[i]

    def state_rows(pair):
        for r in pair:
            beyond(r)
        new = [blend(row_queries(r, q_ref), [block(r, 0)], held(r, state)) for r in pair]
        for r, one in zip(pair, new):
            hold(r, state, one)

    def final_rows(pair):
        for r in pair:
            beyond(r)
        done = []
        for r in pair:
            new = blend(row_queries(r, q_ref), [block(r, 0)], held(r, state))
            for head in range(KVH):
                lines = []
                for i in range(2):
                    line = jnp.broadcast_to(stats[r, head, pl.ds(i, 1), :], (width, width))
                    lines.append(jnp.sum(jnp.where(eye, line, 0.0), axis=1, keepdims=True))
                other_top, other_total = lines
                other_top = jnp.where(other_total > 0.0, other_top, NEG)
                value, old_top, amount = new[head]
                new_top = jnp.maximum(old_top, other_top)
                mine = jnp.exp(old_top - new_top)
                theirs = jnp.exp(other_top - new_top) * other_total
                whole = amount * mine + theirs
                merged = value * mine + part[r, head].astype(jnp.float32) * theirs
                done.append(merged / whole)
        for i, value in enumerate(done):
            scr[i] = value
        steps = out.shape[1]
        group = width // steps
        for i, r in enumerate(pair):
            for head in range(KVH):
                for g in range(group):
                    column = (head * group + g) * HD
                    out[r, :, column : column + HD] = scr[
                        i * KVH + head, pl.ds(g, steps, stride=group), :
                    ].astype(jnp.bfloat16)

    run = {"partial": partial_rows, "state": state_rows, "final": final_rows}[kind]
    together = 2 if rows % 2 == 0 else 1

    def some_rows(i, _):
        run([i * together + u for u in range(together)])
        return 0

    lax.fori_loop(0, rows // together, some_rows, 0)


def span(kind, kernel, cap, scalars, grouped, tables, messages, state, extra, steps):
    rows, _, width, _ = grouped.shape
    feature = messages[0].shape[-1]
    count = len(messages)
    room = (count * cap + 1) * BLK + SPAN
    smem = pl.BlockSpec(memory_space=pltpu.SMEM)
    vmem = pl.BlockSpec(memory_space=pltpu.VMEM)
    hbm = pl.BlockSpec(memory_space=pl.ANY)
    running = [pltpu.VMEM((rows, KVH, width, HD), jnp.float32)] * 3
    scratch = []
    if kind == "partial":
        out_shape = (
            jax.ShapeDtypeStruct((rows, KVH, width, HD), jnp.bfloat16),
            jax.ShapeDtypeStruct((rows, KVH, 2, width), jnp.float32),
        )
        scratch += running
    elif kind == "state":
        out_shape = state_shapes(rows, width)
    else:
        out_shape = jax.ShapeDtypeStruct((rows, steps, QH * HD), jnp.bfloat16)
        scratch += running + [pltpu.VMEM((2 * KVH, width, HD), jnp.float32)]
    scratch += [
        pltpu.VMEM((count, 2, cap, BLK, feature), jnp.bfloat16),
        pltpu.VMEM((room, feature), jnp.float32),
        pltpu.VMEM((room, feature), jnp.float32),
        pltpu.SemaphoreType.DMA((count + 3,)),
    ]
    return pl.pallas_call(
        functools.partial(span_kernel, kind, kernel, count, cap),
        out_shape=out_shape,
        in_specs=[smem] * 7 + [vmem] * 5 + [hbm] * (count + len(state)) + [vmem] * len(extra),
        out_specs=jax.tree.map(lambda _: vmem, out_shape),
        scratch_shapes=scratch,
        compiler_params=pltpu.CompilerParams(vmem_limit_bytes=GRANT),
        cost_estimate=pl.CostEstimate(
            flops=10**9, bytes_accessed=12 * 2**20, transcendentals=10**6
        ),
    )(*scalars, grouped, *tables, *messages, *state, *extra)


PHASES = {"d": (2, 2, 2, 2), "f": (0, 3, 3, 0), "g": (3, 0, 0, 3), "b": (1, 1, 1, 1)}


def site_plane(plane, flip):
    dest = plane ^ flip
    half = PLANES // 2
    if (plane < half) != (dest < half) and dest in (half - 1, half):
        return PLANES - 1 - dest
    return dest


def came_from(phase, plane):
    flips = PHASES[phase]
    return next(s for s in range(PLANES) if site_plane(s, flips[s]) == plane)


def for_mirror(phase, plane):
    source = came_from(phase, plane)
    return int(source ^ PHASES[phase][source] != plane)


def route(n, phase, offset):
    in_plane = n // PLANES
    return [
        (
            plane * in_plane + place,
            site_plane(plane, flip) * in_plane + (place + offset) % in_plane,
        )
        for plane, flip in enumerate(PHASES[phase])
        for place in range(in_plane)
    ]


STAGE = {"d": 1, "f": 1, "g": 1, "b": 2}


def device_tables(n):
    in_plane = n // PLANES
    lines = []
    for me in range(n):
        plane, place = me // in_plane, me % in_plane
        entry, stage = [], []
        post = [[-1] * n, [-1] * n]
        for phase in PHASES:
            mirror = for_mirror(phase, plane)
            for offset in range(in_plane):
                source = came_from(phase, plane) * in_plane + (place - offset) % in_plane
                entry.append(mirror * n + source)
                stage.append(0 if mirror else STAGE[phase])
                post[mirror][source] = stage[-1]
        lines.append((entry, stage, post[0], post[1]))
    return np.array(lines, np.int32)


def body(
    span_keys,
    span_values,
    block_device,
    block_row,
    cache_len,
    cache_keys,
    cache_values,
    queries,
    step_keys,
    step_values,
):
    n = lax.axis_size("seq")
    in_plane = n // PLANES
    me = lax.axis_index("seq").astype(jnp.int32)
    rows = cache_len.shape[0]
    feature = span_keys.shape[1]
    blocks = span_keys.shape[0] // BLK
    cap = max(2, (2 * blocks + n - 1) // n)
    steps = queries.shape[1]
    group = QH // KVH
    names = list(PHASES)

    phase_table = jnp.array(
        [
            [next(i for i, p in enumerate(names) if PHASES[p][z] == z ^ d) for d in range(PLANES)]
            for z in range(PLANES)
        ],
        jnp.int32,
    )
    notes, *messages = pack(
        n,
        cap,
        phase_table,
        block_device[:, 0],
        block_row,
        cache_len,
        span_keys.reshape(blocks, BLK, feature),
        span_values.reshape(blocks, BLK, feature),
    )
    packed = {p: messages[i * in_plane : (i + 1) * in_plane] for i, p in enumerate(names)}

    grouped = (
        queries.reshape(rows, steps, KVH, group, HD)
        .transpose(0, 2, 1, 3, 4)
        .reshape(rows, KVH, steps * group, HD)
    )
    half = PLANES // 2
    swap = [
        (a * in_plane + i, b * in_plane + i)
        for a, b in ((half - 1, half), (half, half - 1))
        for i in range(in_plane)
    ]
    mirrored = lax.ppermute(grouped, "seq", swap)

    def send(phase, after=None):
        out = []
        for offset in range(in_plane):
            value = packed[phase][offset]
            if after is not None:
                value, after[offset] = lax.optimization_barrier((value, after[offset]))
            pairs = route(n, phase, offset)
            if any(a != b for a, b in pairs):
                value = lax.ppermute(value, "seq", pairs)
            out.append(value)
        return out

    got = {}
    got["d"] = send("d")
    got["f"] = send("f")
    got["g"] = send("g")
    got["b"] = send("b", got["d"])

    notes = lax.all_to_all(notes, "seq", split_axis=0, concat_axis=0, tiled=True)
    mine = lax.dynamic_index_in_dim(jnp.array(device_tables(n)), me, 0, keepdims=False)
    *slots, tally = index(n, cap, rows, notes, mine[2:])
    twin = [m if m // in_plane in (0, PLANES - 1) else (PLANES - 1 - m // in_plane) * in_plane
            + m % in_plane for m in range(n)]
    twin = jnp.sum(jnp.where(jnp.arange(n) == me, jnp.array(twin, jnp.int32), 0))
    mirror_len = lax.dynamic_index_in_dim(notes, twin, 0, keepdims=False)
    mirror_len = mirror_len[2 * LANES : 2 * LANES + rows]

    own_tables = turn_tables(cache_len[:, None] + jnp.arange(BLK, dtype=jnp.int32)[None])
    mirror_tables = turn_tables(mirror_len[:, None] + jnp.arange(BLK, dtype=jnp.int32)[None])
    rank_tables = turn_tables(jnp.arange(n * cap, dtype=jnp.int32) * BLK)

    def scalars(phases):
        first = names.index(phases[0]) * in_plane
        picked = mine[:2, first : first + len(phases) * in_plane]
        return (picked[0], picked[1], *slots, tally)

    state = resident(cache_len, grouped, step_keys, step_values, cache_keys, cache_values)
    partial, stats = span(
        "partial", 0, cap, scalars("df"), mirrored,
        mirror_tables + rank_tables, got["d"] + got["f"], (), (), steps,
    )
    partial = lax.ppermute(partial, "seq", swap)
    stats = lax.ppermute(stats, "seq", swap)
    state = span(
        "state", 1, cap, scalars("dfg"), grouped,
        own_tables + rank_tables, got["d"] + got["f"] + got["g"], tuple(state), (), steps,
    )
    return span(
        "final", 2, cap, scalars("b"), grouped,
        own_tables + rank_tables, got["b"], tuple(state), (partial, stats), steps,
    )


def solution(mesh):
    placed = (
        P(("groups", "seq"), None),
        P(("groups", "seq"), None),
        P(("groups", "seq"), None),
        P(("groups", "seq")),
        P(("groups", "seq")),
        P(("groups", "seq"), None, None),
        P(("groups", "seq"), None, None),
        P(("groups", "seq"), None, None),
        P(("groups", "seq"), None, None),
        P(("groups", "seq"), None, None),
    )

    return jax.shard_map(
        body,
        mesh=mesh,
        in_specs=placed,
        out_specs=P(("groups", "seq"), None, None),
        check_vma=False,
    )
```

time: 141 us -> 132 us (0.936)
  the two profiles are of different devices: /device:TPU:26 before, /device:TPU:27 now
where the time goes in v1:
time: 132 us
  starting transfers between devices  57.2 us (43%)
  Pallas kernels  39.1 us (30%)
  local copies, waits for them, and re-layouts  18.2 us (14%)
  waiting for transfers between devices  13.2 us (10%)
  between operations  2.13 us (2%)
  other arithmetic  1.78 us (1%)
    ppermute x15, starting transfers between devices, send(): value = lax.ppermute(value, 'seq', pairs)  48.8 us
    pallas_call x3, Pallas kernels, span(): pl.pallas_call(functools.partial(span_kernel, kind, kernel, count, cap),...  27.5 us
    unnamed x41, local copies, waits for them, and re-layouts  15.2 us
    ppermute x15, waiting for transfers between devices, send(): value = lax.ppermute(value, 'seq', pairs)  13.2 us
    all_to_all x1, starting transfers between devices, body(): lax.all_to_all(notes, 'seq', split_axis=0, concat_axis=0, tiled=True)  6.35 us
    pallas_call x1, Pallas kernels, pack(): pl.pallas_call(functools.partial(pack_kernel, n, cap), out_shape=(jax.Sha...  5.7 us
    pallas_call x1, Pallas kernels, resident(): pl.pallas_call(resident_kernel, out_shape=state_shapes(rows, grouped.shap...  5.56 us
  transfers between devices with their start and end apart: 19, of which 5 were waited for; matrix products, arithmetic and copies ran while one was open for 3% of the time, Pallas kernels for 19%

profile of v1, /device:TPU:27, one launch (start us, length us, event | category | flops | bytes accessed | tf_op | source)
XLA Modules:
  0.0 131.6 jit_solution(4770343385963673473)
XLA Ops:
  0.0 1.2 copy-done.2
  1.3 1.2 copy-done.3
  5.1 5.7 %pack.1 = (s32[16,384]{1,0:T(8,128)S(1)}, bf16[2,16,8,512]{3,2,1,0:T(8,128)(2,1)}, bf16[2,16,8,512]{3,2,1,0:T(8,128)(2,1)}, bf16[2,16,8,512]{3,2,1,0:T(8,128)(2,...) custom-call(s32[4,4]{1,0:T(4,128)S(1)} %copy-done.8, ...), custom_call_target="tpu_custom_call" | custom-call | tf_op jit(solution)/shard_map/pack/pallas_call | solution.py:92
  11.5 0.7 copy-done.12
  12.3 0.7 copy-done.13
  13.7 0.7 copy-done.15
  14.4 0.7 copy-done.16
  15.8 0.7 copy-done.18
  17.1 6.4 %all-to-all-start = ((s32[16,1,384]{2,1,0:T(1,128)}), s32[16,1,384]{2,1,0:T(1,128)S(1)}, u32[]{:S(2)}, u32[]{:S(2)}) async-start(s32[16,1,384]{2,1,0:T(1,128)} %copy.15), calls=%async_computation | async-start | bytes 49152 | tf_op jit(solution)/shard_map/all_to_all | solution.py:652
  23.8 1.7 %collective-permute-start.2 = (bf16[2,16,8,512]{3,2,1,0:T(8,128)(2,1)}, bf16[2,16,8,512]{3,2,1,0:T(8,128)(2,1)S(1)}, u32[]{:S(2)}, u32[]{:S(2)}) collective-permute-start(bf16[2,16,8,512]{3,2,1,0:T(8,128)(2,1)} %get-tuple-element.53), channel_id=1, source_target_pairs={{0,5},{1,6},{2,7},{3,4},{4,13},{5,14},{6,15},{7,12},{8,1},{9,2},{1... | collective-permute-start | bytes 786440 | tf_op jit(solution)/shard_map/ppermute | solution.py:642
  25.5 1.2 collective-permute-start.4
  26.7 2.1 %collective-permute-start.6 = (bf16[2,16,8,512]{3,2,1,0:T(8,128)(2,1)}, bf16[2,16,8,512]{3,2,1,0:T(8,128)(2,1)S(1)}, u32[]{:S(2)}, u32[]{:S(2)}) collective-permute-start(bf16[2,16,8,512]{3,2,1,0:T(8,128)(2,1)} %get-tuple-element.59), channel_id=1, source_target_pairs={{0,7},{1,4},{2,5},{3,6},{4,15},{5,12},{6,13},{7,14},{8,3},{9,0},{1... | collective-permute-start | bytes 786440 | tf_op jit(solution)/shard_map/ppermute | solution.py:642
  28.8 1.6 %reshape.84 = bf16[8,4,4,16,128]{4,3,2,1,0:T(8,128)(2,1)S(1)} reshape(bf16[8,4,8192]{2,1,0:T(4,128)(2,1)} %param.20) | data formatting | bytes 1048576 | tf_op jit(solution)/shard_map/reshape | solution.py:622
  35.2 1.5 %collective-permute-start.8 = (bf16[2,16,8,512]{3,2,1,0:T(8,128)(2,1)}, bf16[2,16,8,512]{3,2,1,0:T(8,128)(2,1)S(1)}, u32[]{:S(2)}, u32[]{:S(2)}) collective-permute-start(bf16[2,16,8,512]{3,2,1,0:T(8,128)(2,1)} %copy-done.18), channel_id=1, source_target_pairs={{0,1},{1,2},{2,3},{3,0},{4,5},{5,6},{6,7},{7,4},{8,9},{9,10},{10,1... | collective-permute-start | bytes 786440 | tf_op jit(solution)/shard_map/ppermute | solution.py:642
  36.7 2.4 %collective-permute-done.2.refs_1_ = bf16[2,16,8,512]{3,2,1,0:T(8,128)(2,1)S(1)} collective-permute-done((bf16[2,16,8,512]{3,2,1,0:T(8,128)(2,1)}, bf16[2,16,8,512]{3,2,1,0:T(8,128)(2,1)S(1)}, u32[]{:S(2)}, u32[]{:S(2)}) %collective-permute-start.2) | collective-permute-done | bytes 262176 | tf_op jit(solution)/shard_map/ppermute | solution.py:642
  39.1 1.2 collective-permute-start.9
  40.3 3.9 %collective-permute-done.4.refs_2_ = bf16[2,16,8,512]{3,2,1,0:T(8,128)(2,1)S(1)} collective-permute-done((bf16[2,16,8,512]{3,2,1,0:T(8,128)(2,1)}, bf16[2,16,8,512]{3,2,1,0:T(8,128)(2,1)S(1)}, u32[]{:S(2)}, u32[]{:S(2)}) %collective-permute-start.4) | collective-permute-done | bytes 262176 | tf_op jit(solution)/shard_map/ppermute | solution.py:642
  44.2 2.1 %collective-permute-start.10 = (bf16[2,16,8,512]{3,2,1,0:T(8,128)(2,1)}, bf16[2,16,8,512]{3,2,1,0:T(8,128)(2,1)S(1)}, u32[]{:S(2)}, u32[]{:S(2)}) collective-permute-start(bf16[2,16,8,512]{3,2,1,0:T(8,128)(2,1)} %copy-done.16), channel_id=1, source_target_pairs={{0,3},{1,0},{2,1},{3,2},{4,7},{5,4},{6,5},{7,6},{8,11},{9,8},{10,9... | collective-permute-start | bytes 786440 | tf_op jit(solution)/shard_map/ppermute | solution.py:642
  47.1 4.1 %collective-permute-done.6.refs_3_ = bf16[2,16,8,512]{3,2,1,0:T(8,128)(2,1)S(1)} collective-permute-done((bf16[2,16,8,512]{3,2,1,0:T(8,128)(2,1)}, bf16[2,16,8,512]{3,2,1,0:T(8,128)(2,1)S(1)}, u32[]{:S(2)}, u32[]{:S(2)}) %collective-permute-start.6) | collective-permute-done | bytes 262176 | tf_op jit(solution)/shard_map/ppermute | solution.py:642
  51.2 2.3 %collective-permute-start.11 = (bf16[2,16,8,512]{3,2,1,0:T(8,128)(2,1)}, bf16[2,16,8,512]{3,2,1,0:T(8,128)(2,1)S(1)}, u32[]{:S(2)}, u32[]{:S(2)}) collective-permute-start(bf16[2,16,8,512]{3,2,1,0:T(8,128)(2,1)} %copy-done.15), channel_id=1, source_target_pairs={{0,12},{1,13},{2,14},{3,15},{4,4},{5,5},{6,6},{7,7},{8,8},{9,9},{1... | collective-permute-start | bytes 786440 | tf_op jit(solution)/shard_map/ppermute | solution.py:642
  53.6 2.1 %collective-permute-start.12 = (bf16[2,16,8,512]{3,2,1,0:T(8,128)(2,1)}, bf16[2,16,8,512]{3,2,1,0:T(8,128)(2,1)S(1)}, u32[]{:S(2)}, u32[]{:S(2)}) collective-permute-start(bf16[2,16,8,512]{3,2,1,0:T(8,128)(2,1)} %copy-done.14), channel_id=1, source_target_pairs={{0,13},{1,14},{2,15},{3,12},{4,5},{5,6},{6,7},{7,4},{8,9},{9,10},{... | collective-permute-start | bytes 786440 | tf_op jit(solution)/shard_map/ppermute | solution.py:642
  55.7 2.4 %collective-permute-done.9.refs_6_ = bf16[2,16,8,512]{3,2,1,0:T(8,128)(2,1)S(1)} collective-permute-done((bf16[2,16,8,512]{3,2,1,0:T(8,128)(2,1)}, bf16[2,16,8,512]{3,2,1,0:T(8,128)(2,1)S(1)}, u32[]{:S(2)}, u32[]{:S(2)}) %collective-permute-start.9) | collective-permute-done | bytes 262176 | tf_op jit(solution)/shard_map/ppermute | solution.py:642
  58.6 1.7 %collective-permute-start.14 = (bf16[2,16,8,512]{3,2,1,0:T(8,128)(2,1)}, bf16[2,16,8,512]{3,2,1,0:T(8,128)(2,1)S(1)}, u32[]{:S(2)}, u32[]{:S(2)}) collective-permute-start(bf16[2,16,8,512]{3,2,1,0:T(8,128)(2,1)} %copy-done.12), channel_id=1, source_target_pairs={{0,15},{1,12},{2,13},{3,14},{4,7},{5,4},{6,5},{7,6},{8,11},{9,8},{... | collective-permute-start | bytes 786440 | tf_op jit(solution)/shard_map/ppermute | solution.py:642
  60.3 5.2 %shard_map.128 = (bf16[8,4,64,128]{3,2,1,0:T(8,128)(2,1)S(1)}, f32[8,4,2,64]{3,2,1,0:T(2,128)S(1)}) custom-call(s32[8]{0:T(128)S(1)} %get-tuple-element.88.entry, s32[8]{0:T(128)S(1)} %get-tuple-element.87.stage, s32[32,16]{1,0:T(8,128)S(1)} %get-tuple-element.44.place_of, s32[32,16]{1,0:T(8,128)S(1)} %get-tuple-element.45.row_of, ...), custom_call_target="tpu_custom_call" | custom-call | flops 1000000000 | bytes 12582912 | tf_op jit(solution)/shard_map/pallas_call | solution.py:512
  66.3 25.2 %collective-permute-start.1 = (bf16[2,16,8,512]{3,2,1,0:T(8,128)(2,1)}, bf16[2,16,8,512]{3,2,1,0:T(8,128)(2,1)S(1)}, u32[]{:S(2)}, u32[]{:S(2)}) collective-permute-start(bf16[2,16,8,512]{3,2,1,0:T(8,128)(2,1)} %copy-done.11), channel_id=1, source_target_pairs={{0,4},{1,5},{2,6},{3,7},{4,0},{5,1},{6,2},{7,3},{8,12},{9,13},{10,... | collective-permute-start | bytes 786440 | tf_op jit(solution)/shard_map/ppermute | solution.py:642
  91.5 5.1 %collective-permute-start.3 = (bf16[2,16,8,512]{3,2,1,0:T(8,128)(2,1)S(1)}, bf16[2,16,8,512]{3,2,1,0:T(8,128)(2,1)S(1)}, u32[]{:S(2)}, u32[]{:S(2)}) collective-permute-start(bf16[2,16,8,512]{3,2,1,0:T(8,128)(2,1)S(1)} %get-tuple-element.54), channel_id=1, source_target_pairs={{0,5},{1,6},{2,7},{3,4},{4,1},{5,2},{6,3},{7,0},{8,13},{9,14},{10,... | collective-permute-start | bytes 786440 | tf_op jit(solution)/shard_map/ppermute | solution.py:642
  96.6 2.0 %collective-permute-start.7 = (bf16[2,16,8,512]{3,2,1,0:T(8,128)(2,1)S(1)}, bf16[2,16,8,512]{3,2,1,0:T(8,128)(2,1)S(1)}, u32[]{:S(2)}, u32[]{:S(2)}) collective-permute-start(bf16[2,16,8,512]{3,2,1,0:T(8,128)(2,1)S(1)} %get-tuple-element.60), channel_id=1, source_target_pairs={{0,7},{1,4},{2,5},{3,6},{4,3},{5,0},{6,1},{7,2},{8,15},{9,12},{10,... | collective-permute-start | bytes 786440 | tf_op jit(solution)/shard_map/ppermute | solution.py:642
  98.6 2.2 %copy-done = bf16[8,512,512]{2,1,0:T(8,128)(2,1)S(1)} copy-done((bf16[8,512,512]{2,1,0:T(8,128)(2,1)S(1)}, bf16[8,512,512]{2,1,0:T(8,128)(2,1)}, u32[]{:S(2)}) %copy-start) | copy-done | bytes 4194328
  100.8 2.2 %copy-done.1 = bf16[8,512,512]{2,1,0:T(8,128)(2,1)S(1)} copy-done((bf16[8,512,512]{2,1,0:T(8,128)(2,1)S(1)}, bf16[8,512,512]{2,1,0:T(8,128)(2,1)}, u32[]{:S(2)}) %copy-start.1) | copy-done | bytes 4194328
  103.0 5.6 %resident.1 = (f32[8,4,64,128]{3,2,1,0:T(8,128)S(1)}, f32[8,4,64,128]{3,2,1,0:T(8,128)S(1)}, f32[8,4,64,128]{3,2,1,0:T(8,128)S(1)}) custom-call(s32[8]{0:T(128)S(1)} %copy-done.7, bf16[8,4,64,128]{3,2,1,0:T(8,128)(2,1)S(1)} %bitcast.31, bf16[8,4,512]{2,1,0:T(4,128)(2,1)S(1)} %copy-done.4, bf16[8,4,512]{2,1,0:T(4,128)(2,1)S(1)} %copy-done.5, ...), custom_call_target="tpu_custom_call" | custom-call | flops 2000000000 | bytes 16777216 | tf_op jit(solution)/shard_map/resident/pallas_call | solution.py:304
  109.3 13.9 %shard_map.127 = (f32[8,4,64,128]{3,2,1,0:T(8,128)S(1)}, f32[8,4,64,128]{3,2,1,0:T(8,128)S(1)}, f32[8,4,64,128]{3,2,1,0:T(8,128)S(1)}) custom-call(s32[12]{0:T(128)S(1)} %get-tuple-element.90.entry, s32[12]{0:T(128)S(1)} %get-tuple-element.89.stage, s32[32,16]{1,0:T(8,128)S(1)} %get-tuple-element.44.place_of, s32[32,16]{1,0:T(8,128)S(1)} %get-tuple-element.45.row_of, ...), custom_call_target="tpu_custom_call" | custom-call | flops 1000000000 | bytes 12582912 | tf_op jit(solution)/shard_map/pallas_call | solution.py:512
  123.2 8.4 %shard_map.129 = bf16[8,4,8192]{2,1,0:T(4,128)(2,1)} custom-call(s32[4]{0:T(128)S(1)} %get-tuple-element.92.entry, s32[4]{0:T(128)S(1)} %get-tuple-element.91.stage, s32[32,16]{1,0:T(8,128)S(1)} %get-tuple-element.44.place_of, s32[32,16]{1,0:T(8,128)S(1)} %get-tuple-element.45.row_of, s32[32,16]{1,0:T(8,128)S(1)} %get-tuple-element.46.rank_of, ...), custom_call_target="tpu_custom_call" | custom-call | flops 1000000000 | bytes 12582912 | tf_op jit(solution)/shard_map/pallas_call | solution.py:512
  (71 shorter events, 11.3 us)
Async XLA Ops:
  0.0 32.6 %copy-start.19 = (s32[16]{0:T(128)S(1)}, s32[16]{0:T(128)}, u32[]{:S(2)}) copy-start(s32[16]{0:T(128)} %constant.54.clone) | copy-start | bytes 196
  0.0 31.2 %copy-start.7 = (s32[8]{0:T(128)S(1)}, s32[8]{0:T(128)}, u32[]{:S(2)}) copy-start(s32[8]{0:T(128)} %lens.3) | copy-start | bytes 100
  0.0 1.3 copy-start.2
  1.3 1.2 copy-start.3
  5.1 93.5 %copy-start.4 = (bf16[8,4,512]{2,1,0:T(4,128)(2,1)S(1)}, bf16[8,4,512]{2,1,0:T(4,128)(2,1)}, u32[]{:S(2)}) copy-start(bf16[8,4,512]{2,1,0:T(4,128)(2,1)} %step_k.1) | copy-start | bytes 98308
  5.1 93.5 %copy-start.5 = (bf16[8,4,512]{2,1,0:T(4,128)(2,1)S(1)}, bf16[8,4,512]{2,1,0:T(4,128)(2,1)}, u32[]{:S(2)}) copy-start(bf16[8,4,512]{2,1,0:T(4,128)(2,1)} %step_v.1) | copy-start | bytes 98308
  10.8 0.7 copy-start.11
  11.5 0.7 copy-start.12
  12.3 0.7 copy-start.13
  13.7 0.7 copy-start.15
  14.4 0.7 copy-start.16
  17.1 18.0 %all-to-all-start = ((s32[16,1,384]{2,1,0:T(1,128)}), s32[16,1,384]{2,1,0:T(1,128)S(1)}, u32[]{:S(2)}, u32[]{:S(2)}) async-start(s32[16,1,384]{2,1,0:T(1,128)} %copy.15), calls=%async_computation | async-start | bytes 49152 | tf_op jit(solution)/shard_map/all_to_all | solution.py:652
  23.5 11.7 %collective-permute-start = (bf16[2,16,8,512]{3,2,1,0:T(8,128)(2,1)}, bf16[2,16,8,512]{3,2,1,0:T(8,128)(2,1)S(1)}, u32[]{:S(2)}, u32[]{:S(2)}) collective-permute-start(bf16[2,16,8,512]{3,2,1,0:T(8,128)(2,1)} %get-tuple-element.50), channel_id=1, source_target_pairs={{0,4},{1,5},{2,6},{3,7},{4,12},{5,13},{6,14},{7,15},{8,0},{9,1},{1... | collective-permute-start | bytes 786440 | tf_op jit(solution)/shard_map/ppermute | solution.py:642
  23.8 15.3 %collective-permute-start.2 = (bf16[2,16,8,512]{3,2,1,0:T(8,128)(2,1)}, bf16[2,16,8,512]{3,2,1,0:T(8,128)(2,1)S(1)}, u32[]{:S(2)}, u32[]{:S(2)}) collective-permute-start(bf16[2,16,8,512]{3,2,1,0:T(8,128)(2,1)} %get-tuple-element.53), channel_id=1, source_target_pairs={{0,5},{1,6},{2,7},{3,4},{4,13},{5,14},{6,15},{7,12},{8,1},{9,2},{1... | collective-permute-start | bytes 786440 | tf_op jit(solution)/shard_map/ppermute | solution.py:642
  25.5 18.7 %collective-permute-start.4 = (bf16[2,16,8,512]{3,2,1,0:T(8,128)(2,1)}, bf16[2,16,8,512]{3,2,1,0:T(8,128)(2,1)S(1)}, u32[]{:S(2)}, u32[]{:S(2)}) collective-permute-start(bf16[2,16,8,512]{3,2,1,0:T(8,128)(2,1)} %get-tuple-element.56), channel_id=1, source_target_pairs={{0,6},{1,7},{2,4},{3,5},{4,14},{5,15},{6,12},{7,13},{8,2},{9,3},{1... | collective-permute-start | bytes 786440 | tf_op jit(solution)/shard_map/ppermute | solution.py:642
  26.7 24.5 %collective-permute-start.6 = (bf16[2,16,8,512]{3,2,1,0:T(8,128)(2,1)}, bf16[2,16,8,512]{3,2,1,0:T(8,128)(2,1)S(1)}, u32[]{:S(2)}, u32[]{:S(2)}) collective-permute-start(bf16[2,16,8,512]{3,2,1,0:T(8,128)(2,1)} %get-tuple-element.59), channel_id=1, source_target_pairs={{0,7},{1,4},{2,5},{3,6},{4,15},{5,12},{6,13},{7,14},{8,3},{9,0},{1... | collective-permute-start | bytes 786440 | tf_op jit(solution)/shard_map/ppermute | solution.py:642
  30.4 29.9 %collective-permute-start.15 = (bf16[8,4,64,128]{3,2,1,0:T(8,128)(2,1)S(1)}, bf16[8,4,64,128]{3,2,1,0:T(8,128)(2,1)S(1)}, u32[]{:S(2)}, u32[]{:S(2)}) collective-permute-start(bf16[8,4,64,128]{3,2,1,0:T(8,128)(2,1)S(1)} %bitcast.30), channel_id=1, source_target_pairs={{4,8},{5,9},{6,10},{7,11},{8,4},{9,5},{10,6},{11,7},{20,24},{21,25... | collective-permute-start | bytes 1572872 | tf_op jit(solution)/shard_map/ppermute | solution.py:632
  35.2 18.4 %collective-permute-start.8 = (bf16[2,16,8,512]{3,2,1,0:T(8,128)(2,1)}, bf16[2,16,8,512]{3,2,1,0:T(8,128)(2,1)S(1)}, u32[]{:S(2)}, u32[]{:S(2)}) collective-permute-start(bf16[2,16,8,512]{3,2,1,0:T(8,128)(2,1)} %copy-done.18), channel_id=1, source_target_pairs={{0,1},{1,2},{2,3},{3,0},{4,5},{5,6},{6,7},{7,4},{8,9},{9,10},{10,1... | collective-permute-start | bytes 786440 | tf_op jit(solution)/shard_map/ppermute | solution.py:642
  39.1 18.9 %collective-permute-start.9 = (bf16[2,16,8,512]{3,2,1,0:T(8,128)(2,1)}, bf16[2,16,8,512]{3,2,1,0:T(8,128)(2,1)S(1)}, u32[]{:S(2)}, u32[]{:S(2)}) collective-permute-start(bf16[2,16,8,512]{3,2,1,0:T(8,128)(2,1)} %copy-done.17), channel_id=1, source_target_pairs={{0,2},{1,3},{2,0},{3,1},{4,6},{5,7},{6,4},{7,5},{8,10},{9,11},{10,... | collective-permute-start | bytes 786440 | tf_op jit(solution)/shard_map/ppermute | solution.py:642
  44.2 14.4 %collective-permute-start.10 = (bf16[2,16,8,512]{3,2,1,0:T(8,128)(2,1)}, bf16[2,16,8,512]{3,2,1,0:T(8,128)(2,1)S(1)}, u32[]{:S(2)}, u32[]{:S(2)}) collective-permute-start(bf16[2,16,8,512]{3,2,1,0:T(8,128)(2,1)} %copy-done.16), channel_id=1, source_target_pairs={{0,3},{1,0},{2,1},{3,2},{4,7},{5,4},{6,5},{7,6},{8,11},{9,8},{10,9... | collective-permute-start | bytes 786440 | tf_op jit(solution)/shard_map/ppermute | solution.py:642
  51.2 15.1 %collective-permute-start.11 = (bf16[2,16,8,512]{3,2,1,0:T(8,128)(2,1)}, bf16[2,16,8,512]{3,2,1,0:T(8,128)(2,1)S(1)}, u32[]{:S(2)}, u32[]{:S(2)}) collective-permute-start(bf16[2,16,8,512]{3,2,1,0:T(8,128)(2,1)} %copy-done.15), channel_id=1, source_target_pairs={{0,12},{1,13},{2,14},{3,15},{4,4},{5,5},{6,6},{7,7},{8,8},{9,9},{1... | collective-permute-start | bytes 786440 | tf_op jit(solution)/shard_map/ppermute | solution.py:642
  53.6 38.0 %collective-permute-start.12 = (bf16[2,16,8,512]{3,2,1,0:T(8,128)(2,1)}, bf16[2,16,8,512]{3,2,1,0:T(8,128)(2,1)S(1)}, u32[]{:S(2)}, u32[]{:S(2)}) collective-permute-start(bf16[2,16,8,512]{3,2,1,0:T(8,128)(2,1)} %copy-done.14), channel_id=1, source_target_pairs={{0,13},{1,14},{2,15},{3,12},{4,5},{5,6},{6,7},{7,4},{8,9},{9,10},{... | collective-permute-start | bytes 786440 | tf_op jit(solution)/shard_map/ppermute | solution.py:642
  58.1 38.5 %collective-permute-start.13 = (bf16[2,16,8,512]{3,2,1,0:T(8,128)(2,1)}, bf16[2,16,8,512]{3,2,1,0:T(8,128)(2,1)S(1)}, u32[]{:S(2)}, u32[]{:S(2)}) collective-permute-start(bf16[2,16,8,512]{3,2,1,0:T(8,128)(2,1)} %copy-done.13), channel_id=1, source_target_pairs={{0,14},{1,15},{2,12},{3,13},{4,6},{5,7},{6,4},{7,5},{8,10},{9,11},... | collective-permute-start | bytes 786440 | tf_op jit(solution)/shard_map/ppermute | solution.py:642
  58.6 38.0 %collective-permute-start.14 = (bf16[2,16,8,512]{3,2,1,0:T(8,128)(2,1)}, bf16[2,16,8,512]{3,2,1,0:T(8,128)(2,1)S(1)}, u32[]{:S(2)}, u32[]{:S(2)}) collective-permute-start(bf16[2,16,8,512]{3,2,1,0:T(8,128)(2,1)} %copy-done.12), channel_id=1, source_target_pairs={{0,15},{1,12},{2,13},{3,14},{4,7},{5,4},{6,5},{7,6},{8,11},{9,8},{... | collective-permute-start | bytes 786440 | tf_op jit(solution)/shard_map/ppermute | solution.py:642
  65.6 57.6 %collective-permute-start.16 = (bf16[8,4,64,128]{3,2,1,0:T(8,128)(2,1)S(1)}, bf16[8,4,64,128]{3,2,1,0:T(8,128)(2,1)S(1)}, u32[]{:S(2)}, u32[]{:S(2)}) collective-permute-start(bf16[8,4,64,128]{3,2,1,0:T(8,128)(2,1)S(1)} %get-tuple-element.79), channel_id=1, source_target_pairs={{4,8},{5,9},{6,10},{7,11},{8,4},{9,5},{10,6},{11,7},{20,24},{21,25... | collective-permute-start | bytes 1572872 | tf_op jit(solution)/shard_map/ppermute | solution.py:675
  66.3 42.2 %collective-permute-start.1 = (bf16[2,16,8,512]{3,2,1,0:T(8,128)(2,1)}, bf16[2,16,8,512]{3,2,1,0:T(8,128)(2,1)S(1)}, u32[]{:S(2)}, u32[]{:S(2)}) collective-permute-start(bf16[2,16,8,512]{3,2,1,0:T(8,128)(2,1)} %copy-done.11), channel_id=1, source_target_pairs={{0,4},{1,5},{2,6},{3,7},{4,0},{5,1},{6,2},{7,3},{8,12},{9,13},{10,... | collective-permute-start | bytes 786440 | tf_op jit(solution)/shard_map/ppermute | solution.py:642
  91.5 31.6 %collective-permute-start.3 = (bf16[2,16,8,512]{3,2,1,0:T(8,128)(2,1)S(1)}, bf16[2,16,8,512]{3,2,1,0:T(8,128)(2,1)S(1)}, u32[]{:S(2)}, u32[]{:S(2)}) collective-permute-start(bf16[2,16,8,512]{3,2,1,0:T(8,128)(2,1)S(1)} %get-tuple-element.54), channel_id=1, source_target_pairs={{0,5},{1,6},{2,7},{3,4},{4,1},{5,2},{6,3},{7,0},{8,13},{9,14},{10,... | collective-permute-start | bytes 786440 | tf_op jit(solution)/shard_map/ppermute | solution.py:642
  96.6 26.6 %collective-permute-start.5 = (bf16[2,16,8,512]{3,2,1,0:T(8,128)(2,1)S(1)}, bf16[2,16,8,512]{3,2,1,0:T(8,128)(2,1)S(1)}, u32[]{:S(2)}, u32[]{:S(2)}) collective-permute-start(bf16[2,16,8,512]{3,2,1,0:T(8,128)(2,1)S(1)} %get-tuple-element.57), channel_id=1, source_target_pairs={{0,6},{1,7},{2,4},{3,5},{4,2},{5,3},{6,0},{7,1},{8,14},{9,15},{10,... | collective-permute-start | bytes 786440 | tf_op jit(solution)/shard_map/ppermute | solution.py:642
  96.6 26.6 %collective-permute-start.7 = (bf16[2,16,8,512]{3,2,1,0:T(8,128)(2,1)S(1)}, bf16[2,16,8,512]{3,2,1,0:T(8,128)(2,1)S(1)}, u32[]{:S(2)}, u32[]{:S(2)}) collective-permute-start(bf16[2,16,8,512]{3,2,1,0:T(8,128)(2,1)S(1)} %get-tuple-element.60), channel_id=1, source_target_pairs={{0,7},{1,4},{2,5},{3,6},{4,3},{5,0},{6,1},{7,2},{8,15},{9,12},{10,... | collective-permute-start | bytes 786440 | tf_op jit(solution)/shard_map/ppermute | solution.py:642
  98.6 2.2 %copy-start = (bf16[8,512,512]{2,1,0:T(8,128)(2,1)S(1)}, bf16[8,512,512]{2,1,0:T(8,128)(2,1)}, u32[]{:S(2)}) copy-start(bf16[8,512,512]{2,1,0:T(8,128)(2,1)} %keys.1) | copy-start | bytes 12582916
  100.8 2.2 %copy-start.1 = (bf16[8,512,512]{2,1,0:T(8,128)(2,1)S(1)}, bf16[8,512,512]{2,1,0:T(8,128)(2,1)}, u32[]{:S(2)}) copy-start(bf16[8,512,512]{2,1,0:T(8,128)(2,1)} %values.1) | copy-start | bytes 12582916
  108.6 14.6 %collective-permute-start.17 = (f32[8,4,2,64]{3,2,1,0:T(2,128)S(1)}, f32[8,4,2,64]{3,2,1,0:T(2,128)S(1)}, u32[]{:S(2)}, u32[]{:S(2)}) collective-permute-start(f32[8,4,2,64]{3,2,1,0:T(2,128)S(1)} %get-tuple-element.80), channel_id=1, source_target_pairs={{4,8},{5,9},{6,10},{7,11},{8,4},{9,5},{10,6},{11,7},{20,24},{21,25... | collective-permute-start | bytes 49160 | tf_op jit(solution)/shard_map/ppermute | solution.py:676
  (7 other events, 4.7 us)

commit v2 on v1

--- a/solution.py
+++ b/solution.py
@@ -100,7 +100,6 @@
             pltpu.SMEM((n,), jnp.int32),
             pltpu.SemaphoreType.DMA((n,)),
         ],
-        compiler_params=pltpu.CompilerParams(vmem_limit_bytes=GRANT),
         name="pack",
     )(phase_table, target, rows, lens, keys, values)
 
@@ -325,31 +324,17 @@
 ):
     messages = refs[:count]
     refs = refs[count:]
+    before = refs[:3]
     if kind == "partial":
-        out, stats, acc, top, total, got, kbuf, vbuf, sems = refs
-        loads = []
+        out, stats, acc, top, total, kbuf, vbuf = refs
     elif kind == "state":
-        *before, acc, top, total, got, kbuf, vbuf, sems = refs
-        loads = list(zip(before, (acc, top, total)))
+        part, stats, acc, top, total, kbuf, vbuf = refs[3:]
     else:
-        *before, part, stats, out, acc, top, total, scr, got, kbuf, vbuf, sems = refs
-        loads = list(zip(before, (acc, top, total)))
+        out, acc, top, total, scr, kbuf, vbuf = refs[3:]
     state = (acc, top, total)
     rows = q_ref.shape[0]
     width = q_ref.shape[2]
     feature = kbuf.shape[1]
-    fetches = [pltpu.make_async_copy(messages[j], got.at[j], sems.at[j]) for j in range(count)]
-    for j in range(count):
-
-        @pl.when(stage[j] == kernel)
-        def _():
-            fetches[j].start()
-
-    loads = [
-        pltpu.make_async_copy(a, b, sems.at[count + i]) for i, (a, b) in enumerate(loads)
-    ]
-    for load in loads:
-        load.start()
     last = tally[kernel, rows - 1] * BLK + tally[8 + kernel, rows - 1]
     tail = pl.ds(pl.multiple_of(last, BLK), SPAN)
     vbuf[tail, :] = jnp.zeros((SPAN, feature), jnp.float32)
@@ -360,7 +345,7 @@
         @pl.when(stage[j] == kernel)
         def _():
             source = entry[j]
-            fetches[j].wait()
+            message = messages[j]
 
             def place(step, _):
                 ready = []
@@ -375,8 +360,8 @@
                     cosine = c_a * c_b - s_a * s_b
                     sine = s_a * c_b + c_a * s_b
                     where = pl.ds(pl.multiple_of(slot * BLK, BLK), BLK)
-                    value = got[j, 1, k].astype(jnp.float32)
-                    key = got[j, 0, k].astype(jnp.float32)
+                    value = message[1, k].astype(jnp.float32)
+                    key = message[0, k].astype(jnp.float32)
                     turned = []
                     for head in range(KVH):
                         piece = key[:, head * HD : (head + 1) * HD]
@@ -390,8 +375,6 @@
 
             lax.fori_loop(0, (used[source, 0] + unroll - 1) // unroll, place, 0)
 
-    for load in loads:
-        load.wait()
     lane = lax.broadcasted_iota(jnp.int32, (width, SPAN), 1)
     eye = lax.broadcasted_iota(jnp.int32, (width, width), 0) == lax.broadcasted_iota(
         jnp.int32, (width, width), 1
@@ -433,33 +416,38 @@
             for i in range(2):
                 stats[r, head, pl.ds(i, 1), :] = lines[i]
 
+    def with_part(r, new):
+        merged = []
+        for head in range(KVH):
+            lines = []
+            for i in range(2):
+                line = jnp.broadcast_to(stats[r, head, pl.ds(i, 1), :], (width, width))
+                lines.append(jnp.sum(jnp.where(eye, line, 0.0), axis=1, keepdims=True))
+            other_top, other_total = lines
+            other_top = jnp.where(other_total > 0.0, other_top, NEG)
+            value, old_top, amount = new[head]
+            new_top = jnp.maximum(old_top, other_top)
+            mine = jnp.exp(old_top - new_top)
+            theirs = jnp.exp(other_top - new_top) * other_total
+            merged.append(
+                (
+                    value * mine + part[r, head].astype(jnp.float32) * theirs,
+                    new_top,
+                    amount * mine + theirs,
+                )
+            )
+        return merged
+
     def state_rows(pair):
+        new = [blend(row_queries(r, q_ref), [block(r, 0)], held(r, before)) for r in pair]
+        new = [with_part(r, one) for r, one in zip(pair, new)]
+        for r, one in zip(pair, new):
+            hold(r, state, one)
         for r in pair:
             beyond(r)
-        new = [blend(row_queries(r, q_ref), [block(r, 0)], held(r, state)) for r in pair]
-        for r, one in zip(pair, new):
-            hold(r, state, one)
-
-    def final_rows(pair):
-        for r in pair:
-            beyond(r)
-        done = []
-        for r in pair:
-            new = blend(row_queries(r, q_ref), [block(r, 0)], held(r, state))
-            for head in range(KVH):
-                lines = []
-                for i in range(2):
-                    line = jnp.broadcast_to(stats[r, head, pl.ds(i, 1), :], (width, width))
-                    lines.append(jnp.sum(jnp.where(eye, line, 0.0), axis=1, keepdims=True))
-                other_top, other_total = lines
-                other_top = jnp.where(other_total > 0.0, other_top, NEG)
-                value, old_top, amount = new[head]
-                new_top = jnp.maximum(old_top, other_top)
-                mine = jnp.exp(old_top - new_top)
-                theirs = jnp.exp(other_top - new_top) * other_total
-                whole = amount * mine + theirs
-                merged = value * mine + part[r, head].astype(jnp.float32) * theirs
-                done.append(merged / whole)
+
+    def put_out(pair, new):
+        done = [value / amount for one in new for value, _, amount in one]
         for i, value in enumerate(done):
             scr[i] = value
         steps = out.shape[1]
@@ -472,6 +460,19 @@
                         i * KVH + head, pl.ds(g, steps, stride=group), :
                     ].astype(jnp.bfloat16)
 
+    def final_rows(pair):
+        new = [blend(row_queries(r, q_ref), [block(r, 0)], held(r, before)) for r in pair]
+        put_out(pair, new)
+        longest = functools.reduce(jnp.maximum, [tally[8 + kernel, r] for r in pair])
+
+        @pl.when(longest > SPAN)
+        def _():
+            for r, one in zip(pair, new):
+                hold(r, state, one)
+            for r in pair:
+                beyond(r)
+            put_out(pair, [held(r, state) for r in pair])
+
     run = {"partial": partial_rows, "state": state_rows, "final": final_rows}[kind]
     together = 2 if rows % 2 == 0 else 1
 
@@ -489,7 +490,6 @@
     room = (count * cap + 1) * BLK + SPAN
     smem = pl.BlockSpec(memory_space=pltpu.SMEM)
     vmem = pl.BlockSpec(memory_space=pltpu.VMEM)
-    hbm = pl.BlockSpec(memory_space=pl.ANY)
     running = [pltpu.VMEM((rows, KVH, width, HD), jnp.float32)] * 3
     scratch = []
     if kind == "partial":
@@ -503,16 +503,11 @@
     else:
         out_shape = jax.ShapeDtypeStruct((rows, steps, QH * HD), jnp.bfloat16)
         scratch += running + [pltpu.VMEM((2 * KVH, width, HD), jnp.float32)]
-    scratch += [
-        pltpu.VMEM((count, 2, cap, BLK, feature), jnp.bfloat16),
-        pltpu.VMEM((room, feature), jnp.float32),
-        pltpu.VMEM((room, feature), jnp.float32),
-        pltpu.SemaphoreType.DMA((count + 3,)),
-    ]
+    scratch += [pltpu.VMEM((room, feature), jnp.float32)] * 2
     return pl.pallas_call(
         functools.partial(span_kernel, kind, kernel, count, cap),
         out_shape=out_shape,
-        in_specs=[smem] * 7 + [vmem] * 5 + [hbm] * (count + len(state)) + [vmem] * len(extra),
+        in_specs=[smem] * 7 + [vmem] * (5 + count + len(state) + len(extra)),
         out_specs=jax.tree.map(lambda _: vmem, out_shape),
         scratch_shapes=scratch,
         compiler_params=pltpu.CompilerParams(vmem_limit_bytes=GRANT),
@@ -676,11 +671,12 @@
     stats = lax.ppermute(stats, "seq", swap)
     state = span(
         "state", 1, cap, scalars("dfg"), grouped,
-        own_tables + rank_tables, got["d"] + got["f"] + got["g"], tuple(state), (), steps,
+        own_tables + rank_tables, got["d"] + got["f"] + got["g"], tuple(state),
+        (partial, stats), steps,
     )
     return span(
         "final", 2, cap, scalars("b"), grouped,
-        own_tables + rank_tables, got["b"], tuple(state), (partial, stats), steps,
+        own_tables + rank_tables, got["b"], tuple(state), (), steps,
     )
 
 

time: 132 us -> 118 us (0.89)
  starting transfers between devices: 57.2 us -> 46.5 us
  local copies, waits for them, and re-layouts: 18.2 us -> 9.23 us
  waiting for transfers between devices: 13.2 us -> 18.5 us
    ppermute x15, starting transfers between devices: 48.8 us -> 37.3 us  [send(): value = lax.ppermute(value, 'seq', pairs)]
    unnamed x41 -> x21, local copies, waits for them, and re-layouts: 15.2 us -> 5.36 us
    ppermute x15, waiting for transfers between devices: 13.2 us -> 18.5 us  [send(): value = lax.ppermute(value, 'seq', pairs)]
    pallas_call x1, Pallas kernels: 5.7 us -> 7.62 us  [pack(): pl.pallas_call(functools.partial(pack_kernel, n, cap), out_shape=(jax.Sha...]
    pallas_call x3, Pallas kernels: 27.5 us -> 26.1 us  [span(): pl.pallas_call(functools.partial(span_kernel, kind, kernel, count, cap),...]
  transfers between devices with their start and end apart: 19 -> 19, of which waited for: 5 -> 7; matrix products, arithmetic and copies ran while one was open for 3% -> 3% of each run, Pallas kernels for 19% -> 27%
where the time goes in v2:
time: 118 us
  starting transfers between devices  46.5 us (39%)
  Pallas kernels  39.6 us (34%)
  waiting for transfers between devices  18.5 us (16%)
  local copies, waits for them, and re-layouts  9.23 us (8%)
  between operations  1.96 us (2%)
  other arithmetic  1.71 us (1%)
    ppermute x15, starting transfers between devices, send(): value = lax.ppermute(value, 'seq', pairs)  37.3 us
    pallas_call x3, Pallas kernels, span(): pl.pallas_call(functools.partial(span_kernel, kind, kernel, count, cap),...  26.1 us
    ppermute x15, waiting for transfers between devices, send(): value = lax.ppermute(value, 'seq', pairs)  18.5 us
    pallas_call x1, Pallas kernels, pack(): pl.pallas_call(functools.partial(pack_kernel, n, cap), out_shape=(jax.Sha...  7.62 us
    all_to_all x1, starting transfers between devices, body(): lax.all_to_all(notes, 'seq', split_axis=0, concat_axis=0, tiled=True)  7.12 us
    pallas_call x1, Pallas kernels, resident(): pl.pallas_call(resident_kernel, out_shape=state_shapes(rows, grouped.shap...  5.52 us
    unnamed x21, local copies, waits for them, and re-layouts  5.36 us
  transfers between devices with their start and end apart: 19, of which 7 were waited for; matrix products, arithmetic and copies ran while one was open for 3% of the time, Pallas kernels for 27%

profile of v2, /device:TPU:27, one launch (start us, length us, event | category | flops | bytes accessed | tf_op | source)
XLA Modules:
  0.0 117.5 jit_solution(12943811134134059598)
XLA Ops:
  0.0 1.6 %reshape.84 = bf16[8,4,4,16,128]{4,3,2,1,0:T(8,128)(2,1)S(1)} reshape(bf16[8,4,8192]{2,1,0:T(4,128)(2,1)} %param.20) | data formatting | bytes 1048576 | tf_op jit(solution)/shard_map/reshape | solution.py:617
  1.7 0.7 collective-permute-start.15
  2.4 7.6 %pack.1 = (s32[16,384]{1,0:T(8,128)}, bf16[2,16,8,512]{3,2,1,0:T(8,128)(2,1)}, bf16[2,16,8,512]{3,2,1,0:T(8,128)(2,1)}, bf16[2,16,8,512]{3,2,1,0:T(8,128)(2,1)},...) custom-call(s32[4,4]{1,0:T(4,128)} %constant.52.clone.phase_table, ...), custom_call_target="tpu_custom_call" | custom-call | tf_op jit(solution)/shard_map/pack/pallas_call | solution.py:92
  10.1 1.4 %copy.15 = s32[16,1,384]{2,1,0:T(1,128)} copy(s32[16,1,384]{2,0,1:T(8,128)} %bitcast.37) | data formatting | bytes 49152 | tf_op jit(solution)/shard_map/all_to_all | solution.py:647
  11.5 7.1 %all-to-all-start = ((s32[16,1,384]{2,1,0:T(1,128)}), s32[16,1,384]{2,1,0:T(1,128)S(1)}, u32[]{:S(2)}, u32[]{:S(2)}) async-start(s32[16,1,384]{2,1,0:T(1,128)} %copy.15), calls=%async_computation | async-start | bytes 49152 | tf_op jit(solution)/shard_map/all_to_all | solution.py:647
  18.9 1.7 %collective-permute-start.2 = (bf16[2,16,8,512]{3,2,1,0:T(8,128)(2,1)}, bf16[2,16,8,512]{3,2,1,0:T(8,128)(2,1)S(1)}, u32[]{:S(2)}, u32[]{:S(2)}) collective-permute-start(bf16[2,16,8,512]{3,2,1,0:T(8,128)(2,1)} %get-tuple-element.53), channel_id=1, source_target_pairs={{0,5},{1,6},{2,7},{3,4},{4,13},{5,14},{6,15},{7,12},{8,1},{9,2},{1... | collective-permute-start | bytes 786440 | tf_op jit(solution)/shard_map/ppermute | solution.py:637
  20.6 1.2 %collective-permute-start.4 = (bf16[2,16,8,512]{3,2,1,0:T(8,128)(2,1)}, bf16[2,16,8,512]{3,2,1,0:T(8,128)(2,1)S(1)}, u32[]{:S(2)}, u32[]{:S(2)}) collective-permute-start(bf16[2,16,8,512]{3,2,1,0:T(8,128)(2,1)} %get-tuple-element.56), channel_id=1, source_target_pairs={{0,6},{1,7},{2,4},{3,5},{4,14},{5,15},{6,12},{7,13},{8,2},{9,3},{1... | collective-permute-start | bytes 786440 | tf_op jit(solution)/shard_map/ppermute | solution.py:637
  21.8 2.1 %collective-permute-start.6 = (bf16[2,16,8,512]{3,2,1,0:T(8,128)(2,1)}, bf16[2,16,8,512]{3,2,1,0:T(8,128)(2,1)S(1)}, u32[]{:S(2)}, u32[]{:S(2)}) collective-permute-start(bf16[2,16,8,512]{3,2,1,0:T(8,128)(2,1)} %get-tuple-element.59), channel_id=1, source_target_pairs={{0,7},{1,4},{2,5},{3,6},{4,15},{5,12},{6,13},{7,14},{8,3},{9,0},{1... | collective-permute-start | bytes 786440 | tf_op jit(solution)/shard_map/ppermute | solution.py:637
  24.1 0.7 constant_dynamic-slice_fusion
  27.7 2.7 %collective-permute-start.8 = (bf16[2,16,8,512]{3,2,1,0:T(8,128)(2,1)}, bf16[2,16,8,512]{3,2,1,0:T(8,128)(2,1)S(1)}, u32[]{:S(2)}, u32[]{:S(2)}) collective-permute-start(bf16[2,16,8,512]{3,2,1,0:T(8,128)(2,1)} %get-tuple-element.66), channel_id=1, source_target_pairs={{0,1},{1,2},{2,3},{3,0},{4,5},{5,6},{6,7},{7,4},{8,9},{9,10},{10,1... | collective-permute-start | bytes 786440 | tf_op jit(solution)/shard_map/ppermute | solution.py:637
  30.3 3.9 %collective-permute-done.2.refs_1_ = bf16[2,16,8,512]{3,2,1,0:T(8,128)(2,1)S(1)} collective-permute-done((bf16[2,16,8,512]{3,2,1,0:T(8,128)(2,1)}, bf16[2,16,8,512]{3,2,1,0:T(8,128)(2,1)S(1)}, u32[]{:S(2)}, u32[]{:S(2)}) %collective-permute-start.2) | collective-permute-done | bytes 262176 | tf_op jit(solution)/shard_map/ppermute | solution.py:637
  34.2 1.2 %collective-permute-start.9 = (bf16[2,16,8,512]{3,2,1,0:T(8,128)(2,1)}, bf16[2,16,8,512]{3,2,1,0:T(8,128)(2,1)S(1)}, u32[]{:S(2)}, u32[]{:S(2)}) collective-permute-start(bf16[2,16,8,512]{3,2,1,0:T(8,128)(2,1)} %get-tuple-element.67), channel_id=1, source_target_pairs={{0,2},{1,3},{2,0},{3,1},{4,6},{5,7},{6,4},{7,5},{8,10},{9,11},{10,... | collective-permute-start | bytes 786440 | tf_op jit(solution)/shard_map/ppermute | solution.py:637
  35.4 3.9 %collective-permute-done.4.refs_2_ = bf16[2,16,8,512]{3,2,1,0:T(8,128)(2,1)S(1)} collective-permute-done((bf16[2,16,8,512]{3,2,1,0:T(8,128)(2,1)}, bf16[2,16,8,512]{3,2,1,0:T(8,128)(2,1)S(1)}, u32[]{:S(2)}, u32[]{:S(2)}) %collective-permute-start.4) | collective-permute-done | bytes 262176 | tf_op jit(solution)/shard_map/ppermute | solution.py:637
  39.3 2.1 %collective-permute-start.10 = (bf16[2,16,8,512]{3,2,1,0:T(8,128)(2,1)}, bf16[2,16,8,512]{3,2,1,0:T(8,128)(2,1)S(1)}, u32[]{:S(2)}, u32[]{:S(2)}) collective-permute-start(bf16[2,16,8,512]{3,2,1,0:T(8,128)(2,1)} %get-tuple-element.68), channel_id=1, source_target_pairs={{0,3},{1,0},{2,1},{3,2},{4,7},{5,4},{6,5},{7,6},{8,11},{9,8},{10,9... | collective-permute-start | bytes 786440 | tf_op jit(solution)/shard_map/ppermute | solution.py:637
  42.2 3.3 %collective-permute-done.6.refs_3_ = bf16[2,16,8,512]{3,2,1,0:T(8,128)(2,1)S(1)} collective-permute-done((bf16[2,16,8,512]{3,2,1,0:T(8,128)(2,1)}, bf16[2,16,8,512]{3,2,1,0:T(8,128)(2,1)S(1)}, u32[]{:S(2)}, u32[]{:S(2)}) %collective-permute-start.6) | collective-permute-done | bytes 262176 | tf_op jit(solution)/shard_map/ppermute | solution.py:637
  45.5 2.6 %collective-permute-start.11 = (bf16[2,16,8,512]{3,2,1,0:T(8,128)(2,1)}, bf16[2,16,8,512]{3,2,1,0:T(8,128)(2,1)S(1)}, u32[]{:S(2)}, u32[]{:S(2)}) collective-permute-start(bf16[2,16,8,512]{3,2,1,0:T(8,128)(2,1)} %get-tuple-element.69), channel_id=1, source_target_pairs={{0,12},{1,13},{2,14},{3,15},{4,4},{5,5},{6,6},{7,7},{8,8},{9,9},{1... | collective-permute-start | bytes 786440 | tf_op jit(solution)/shard_map/ppermute | solution.py:637
  48.1 2.6 %collective-permute-start.12 = (bf16[2,16,8,512]{3,2,1,0:T(8,128)(2,1)}, bf16[2,16,8,512]{3,2,1,0:T(8,128)(2,1)S(1)}, u32[]{:S(2)}, u32[]{:S(2)}) collective-permute-start(bf16[2,16,8,512]{3,2,1,0:T(8,128)(2,1)} %get-tuple-element.70), channel_id=1, source_target_pairs={{0,13},{1,14},{2,15},{3,12},{4,5},{5,6},{6,7},{7,4},{8,9},{9,10},{... | collective-permute-start | bytes 786440 | tf_op jit(solution)/shard_map/ppermute | solution.py:637
  50.8 1.3 %collective-permute-start.13 = (bf16[2,16,8,512]{3,2,1,0:T(8,128)(2,1)}, bf16[2,16,8,512]{3,2,1,0:T(8,128)(2,1)S(1)}, u32[]{:S(2)}, u32[]{:S(2)}) collective-permute-start(bf16[2,16,8,512]{3,2,1,0:T(8,128)(2,1)} %get-tuple-element.71), channel_id=1, source_target_pairs={{0,14},{1,15},{2,12},{3,13},{4,6},{5,7},{6,4},{7,5},{8,10},{9,11},... | collective-permute-start | bytes 786440 | tf_op jit(solution)/shard_map/ppermute | solution.py:637
  52.6 2.0 %collective-permute-start.14 = (bf16[2,16,8,512]{3,2,1,0:T(8,128)(2,1)}, bf16[2,16,8,512]{3,2,1,0:T(8,128)(2,1)S(1)}, u32[]{:S(2)}, u32[]{:S(2)}) collective-permute-start(bf16[2,16,8,512]{3,2,1,0:T(8,128)(2,1)} %get-tuple-element.72), channel_id=1, source_target_pairs={{0,15},{1,12},{2,13},{3,14},{4,7},{5,4},{6,5},{7,6},{8,11},{9,8},{... | collective-permute-start | bytes 786440 | tf_op jit(solution)/shard_map/ppermute | solution.py:637
  54.6 0.9 copy-done.2
  55.6 5.1 %shard_map.127 = (bf16[8,4,64,128]{3,2,1,0:T(8,128)(2,1)S(1)}, f32[8,4,2,64]{3,2,1,0:T(2,128)S(1)}) custom-call(s32[8]{0:T(128)S(1)} %get-tuple-element.88.entry, s32[8]{0:T(128)S(1)} %get-tuple-element.87.stage, s32[32,16]{1,0:T(8,128)S(1)} %get-tuple-element.44.place_of, s32[32,16]{1,0:T(8,128)S(1)} %get-tuple-element.45.row_of, ...), custom_call_target="tpu_custom_call" | custom-call | flops 1000000000 | bytes 12582912 | tf_op jit(solution)/shard_map/pallas_call | solution.py:507
  60.6 0.7 collective-permute-start.16
  62.2 4.4 %collective-permute-start.1 = (bf16[2,16,8,512]{3,2,1,0:T(8,128)(2,1)}, bf16[2,16,8,512]{3,2,1,0:T(8,128)(2,1)S(1)}, u32[]{:S(2)}, u32[]{:S(2)}) collective-permute-start(bf16[2,16,8,512]{3,2,1,0:T(8,128)(2,1)} %get-tuple-element.51), channel_id=1, source_target_pairs={{0,4},{1,5},{2,6},{3,7},{4,0},{5,1},{6,2},{7,3},{8,12},{9,13},{10,... | collective-permute-start | bytes 786440 | tf_op jit(solution)/shard_map/ppermute | solution.py:637
  66.6 2.1 %collective-permute-done.13.refs_10_ = bf16[2,16,8,512]{3,2,1,0:T(8,128)(2,1)S(1)} collective-permute-done((bf16[2,16,8,512]{3,2,1,0:T(8,128)(2,1)}, bf16[2,16,8,512]{3,2,1,0:T(8,128)(2,1)S(1)}, u32[]{:S(2)}, u32[]{:S(2)}) %collective-permute-start.13) | collective-permute-done | bytes 262176 | tf_op jit(solution)/shard_map/ppermute | solution.py:637
  68.7 1.2 %collective-permute-start.3 = (bf16[2,16,8,512]{3,2,1,0:T(8,128)(2,1)}, bf16[2,16,8,512]{3,2,1,0:T(8,128)(2,1)S(1)}, u32[]{:S(2)}, u32[]{:S(2)}) collective-permute-start(bf16[2,16,8,512]{3,2,1,0:T(8,128)(2,1)} %get-tuple-element.54), channel_id=1, source_target_pairs={{0,5},{1,6},{2,7},{3,4},{4,1},{5,2},{6,3},{7,0},{8,13},{9,14},{10,... | collective-permute-start | bytes 786440 | tf_op jit(solution)/shard_map/ppermute | solution.py:637
  70.0 4.7 %collective-permute-done.14.refs_11_ = bf16[2,16,8,512]{3,2,1,0:T(8,128)(2,1)S(1)} collective-permute-done((bf16[2,16,8,512]{3,2,1,0:T(8,128)(2,1)}, bf16[2,16,8,512]{3,2,1,0:T(8,128)(2,1)S(1)}, u32[]{:S(2)}, u32[]{:S(2)}) %collective-permute-start.14) | collective-permute-done | bytes 262176 | tf_op jit(solution)/shard_map/ppermute | solution.py:637
  74.7 11.8 %collective-permute-start.7 = (bf16[2,16,8,512]{3,2,1,0:T(8,128)(2,1)S(1)}, bf16[2,16,8,512]{3,2,1,0:T(8,128)(2,1)S(1)}, u32[]{:S(2)}, u32[]{:S(2)}) collective-permute-start(bf16[2,16,8,512]{3,2,1,0:T(8,128)(2,1)S(1)} %copy-done.7), channel_id=1, source_target_pairs={{0,7},{1,4},{2,5},{3,6},{4,3},{5,0},{6,1},{7,2},{8,15},{9,12},{10,... | collective-permute-start | bytes 786440 | tf_op jit(solution)/shard_map/ppermute | solution.py:637
  86.5 2.2 %copy-done = bf16[8,512,512]{2,1,0:T(8,128)(2,1)S(1)} copy-done((bf16[8,512,512]{2,1,0:T(8,128)(2,1)S(1)}, bf16[8,512,512]{2,1,0:T(8,128)(2,1)}, u32[]{:S(2)}) %copy-start) | copy-done | bytes 4194328
  88.7 2.2 %copy-done.1 = bf16[8,512,512]{2,1,0:T(8,128)(2,1)S(1)} copy-done((bf16[8,512,512]{2,1,0:T(8,128)(2,1)S(1)}, bf16[8,512,512]{2,1,0:T(8,128)(2,1)}, u32[]{:S(2)}) %copy-start.1) | copy-done | bytes 4194328
  90.9 5.5 %resident.1 = (f32[8,4,64,128]{3,2,1,0:T(8,128)S(1)}, f32[8,4,64,128]{3,2,1,0:T(8,128)S(1)}, f32[8,4,64,128]{3,2,1,0:T(8,128)S(1)}) custom-call(s32[8]{0:T(128)S(1)} %copy-done.6, bf16[8,4,64,128]{3,2,1,0:T(8,128)(2,1)S(1)} %bitcast.31, bf16[8,4,512]{2,1,0:T(4,128)(2,1)S(1)} %copy-done.4, bf16[8,4,512]{2,1,0:T(4,128)(2,1)S(1)} %copy-done.5, ...), custom_call_target="tpu_custom_call" | custom-call | flops 2000000000 | bytes 16777216 | tf_op jit(solution)/shard_map/resident/pallas_call | solution.py:303
  96.4 13.4 %shard_map.128 = (f32[8,4,64,128]{3,2,1,0:T(8,128)S(1)}, f32[8,4,64,128]{3,2,1,0:T(8,128)S(1)}, f32[8,4,64,128]{3,2,1,0:T(8,128)S(1)}) custom-call(s32[12]{0:T(128)S(1)} %get-tuple-element.90.entry, s32[12]{0:T(128)S(1)} %get-tuple-element.89.stage, s32[32,16]{1,0:T(8,128)S(1)} %get-tuple-element.44.place_of, s32[32,16]{1,0:T(8,128)S(1)} %get-tuple-element.45.row_of, ...), custom_call_target="tpu_custom_call" | custom-call | flops 1000000000 | bytes 12582912 | tf_op jit(solution)/shard_map/pallas_call | solution.py:507
  109.9 7.7 %shard_map.129 = bf16[8,4,8192]{2,1,0:T(4,128)(2,1)} custom-call(s32[4]{0:T(128)S(1)} %get-tuple-element.92.entry, s32[4]{0:T(128)S(1)} %get-tuple-element.91.stage, s32[32,16]{1,0:T(8,128)S(1)} %get-tuple-element.44.place_of, s32[32,16]{1,0:T(8,128)S(1)} %get-tuple-element.45.row_of, s32[32,16]{1,0:T(8,128)S(1)} %get-tuple-element.46.rank_of, ...), custom_call_target="tpu_custom_call" | custom-call | flops 1000000000 | bytes 12582912 | tf_op jit(solution)/shard_map/pallas_call | solution.py:507
  (51 shorter events, 3.8 us)
Async XLA Ops:
  0.0 25.3 %copy-start.9 = (s32[16]{0:T(128)S(1)}, s32[16]{0:T(128)}, u32[]{:S(2)}) copy-start(s32[16]{0:T(128)} %constant.54.clone) | copy-start | bytes 196
  0.0 23.9 %copy-start.6 = (s32[8]{0:T(128)S(1)}, s32[8]{0:T(128)}, u32[]{:S(2)}) copy-start(s32[8]{0:T(128)} %lens.3) | copy-start | bytes 100
  0.0 86.5 %copy-start.5 = (bf16[8,4,512]{2,1,0:T(4,128)(2,1)S(1)}, bf16[8,4,512]{2,1,0:T(4,128)(2,1)}, u32[]{:S(2)}) copy-start(bf16[8,4,512]{2,1,0:T(4,128)(2,1)} %step_v.1) | copy-start | bytes 98308
  0.0 86.5 %copy-start.4 = (bf16[8,4,512]{2,1,0:T(4,128)(2,1)S(1)}, bf16[8,4,512]{2,1,0:T(4,128)(2,1)}, u32[]{:S(2)}) copy-start(bf16[8,4,512]{2,1,0:T(4,128)(2,1)} %step_k.1) | copy-start | bytes 98308
  1.7 52.9 %collective-permute-start.15 = (bf16[8,4,64,128]{3,2,1,0:T(8,128)(2,1)S(1)}, bf16[8,4,64,128]{3,2,1,0:T(8,128)(2,1)S(1)}, u32[]{:S(2)}, u32[]{:S(2)}) collective-permute-start(bf16[8,4,64,128]{3,2,1,0:T(8,128)(2,1)S(1)} %bitcast.30), channel_id=1, source_target_pairs={{4,8},{5,9},{6,10},{7,11},{8,4},{9,5},{10,6},{11,7},{20,24},{21,25... | collective-permute-start | bytes 1572872 | tf_op jit(solution)/shard_map/ppermute | solution.py:627
  10.0 64.7 %copy-start.8 = (bf16[2,16,8,512]{3,2,1,0:T(8,128)(2,1)S(1)}, bf16[2,16,8,512]{3,2,1,0:T(8,128)(2,1)}, u32[]{:S(2)}) copy-start(bf16[2,16,8,512]{3,2,1,0:T(8,128)(2,1)} %get-tuple-element.57) | copy-start | bytes 786436
  10.0 64.7 %copy-start.7 = (bf16[2,16,8,512]{3,2,1,0:T(8,128)(2,1)S(1)}, bf16[2,16,8,512]{3,2,1,0:T(8,128)(2,1)}, u32[]{:S(2)}) copy-start(bf16[2,16,8,512]{3,2,1,0:T(8,128)(2,1)} %get-tuple-element.60) | copy-start | bytes 786436
  11.5 16.2 %all-to-all-start = ((s32[16,1,384]{2,1,0:T(1,128)}), s32[16,1,384]{2,1,0:T(1,128)S(1)}, u32[]{:S(2)}, u32[]{:S(2)}) async-start(s32[16,1,384]{2,1,0:T(1,128)} %copy.15), calls=%async_computation | async-start | bytes 49152 | tf_op jit(solution)/shard_map/all_to_all | solution.py:647
  18.6 9.1 %collective-permute-start = (bf16[2,16,8,512]{3,2,1,0:T(8,128)(2,1)}, bf16[2,16,8,512]{3,2,1,0:T(8,128)(2,1)S(1)}, u32[]{:S(2)}, u32[]{:S(2)}) collective-permute-start(bf16[2,16,8,512]{3,2,1,0:T(8,128)(2,1)} %get-tuple-element.50), channel_id=1, source_target_pairs={{0,4},{1,5},{2,6},{3,7},{4,12},{5,13},{6,14},{7,15},{8,0},{9,1},{1... | collective-permute-start | bytes 786440 | tf_op jit(solution)/shard_map/ppermute | solution.py:637
  18.9 15.3 %collective-permute-start.2 = (bf16[2,16,8,512]{3,2,1,0:T(8,128)(2,1)}, bf16[2,16,8,512]{3,2,1,0:T(8,128)(2,1)S(1)}, u32[]{:S(2)}, u32[]{:S(2)}) collective-permute-start(bf16[2,16,8,512]{3,2,1,0:T(8,128)(2,1)} %get-tuple-element.53), channel_id=1, source_target_pairs={{0,5},{1,6},{2,7},{3,4},{4,13},{5,14},{6,15},{7,12},{8,1},{9,2},{1... | collective-permute-start | bytes 786440 | tf_op jit(solution)/shard_map/ppermute | solution.py:637
  20.6 18.7 %collective-permute-start.4 = (bf16[2,16,8,512]{3,2,1,0:T(8,128)(2,1)}, bf16[2,16,8,512]{3,2,1,0:T(8,128)(2,1)S(1)}, u32[]{:S(2)}, u32[]{:S(2)}) collective-permute-start(bf16[2,16,8,512]{3,2,1,0:T(8,128)(2,1)} %get-tuple-element.56), channel_id=1, source_target_pairs={{0,6},{1,7},{2,4},{3,5},{4,14},{5,15},{6,12},{7,13},{8,2},{9,3},{1... | collective-permute-start | bytes 786440 | tf_op jit(solution)/shard_map/ppermute | solution.py:637
  21.8 23.7 %collective-permute-start.6 = (bf16[2,16,8,512]{3,2,1,0:T(8,128)(2,1)}, bf16[2,16,8,512]{3,2,1,0:T(8,128)(2,1)S(1)}, u32[]{:S(2)}, u32[]{:S(2)}) collective-permute-start(bf16[2,16,8,512]{3,2,1,0:T(8,128)(2,1)} %get-tuple-element.59), channel_id=1, source_target_pairs={{0,7},{1,4},{2,5},{3,6},{4,15},{5,12},{6,13},{7,14},{8,3},{9,0},{1... | collective-permute-start | bytes 786440 | tf_op jit(solution)/shard_map/ppermute | solution.py:637
  27.7 20.4 %collective-permute-start.8 = (bf16[2,16,8,512]{3,2,1,0:T(8,128)(2,1)}, bf16[2,16,8,512]{3,2,1,0:T(8,128)(2,1)S(1)}, u32[]{:S(2)}, u32[]{:S(2)}) collective-permute-start(bf16[2,16,8,512]{3,2,1,0:T(8,128)(2,1)} %get-tuple-element.66), channel_id=1, source_target_pairs={{0,1},{1,2},{2,3},{3,0},{4,5},{5,6},{6,7},{7,4},{8,9},{9,10},{10,1... | collective-permute-start | bytes 786440 | tf_op jit(solution)/shard_map/ppermute | solution.py:637
  34.2 16.6 %collective-permute-start.9 = (bf16[2,16,8,512]{3,2,1,0:T(8,128)(2,1)}, bf16[2,16,8,512]{3,2,1,0:T(8,128)(2,1)S(1)}, u32[]{:S(2)}, u32[]{:S(2)}) collective-permute-start(bf16[2,16,8,512]{3,2,1,0:T(8,128)(2,1)} %get-tuple-element.67), channel_id=1, source_target_pairs={{0,2},{1,3},{2,0},{3,1},{4,6},{5,7},{6,4},{7,5},{8,10},{9,11},{10,... | collective-permute-start | bytes 786440 | tf_op jit(solution)/shard_map/ppermute | solution.py:637
  39.3 13.2 %collective-permute-start.10 = (bf16[2,16,8,512]{3,2,1,0:T(8,128)(2,1)}, bf16[2,16,8,512]{3,2,1,0:T(8,128)(2,1)S(1)}, u32[]{:S(2)}, u32[]{:S(2)}) collective-permute-start(bf16[2,16,8,512]{3,2,1,0:T(8,128)(2,1)} %get-tuple-element.68), channel_id=1, source_target_pairs={{0,3},{1,0},{2,1},{3,2},{4,7},{5,4},{6,5},{7,6},{8,11},{9,8},{10,9... | collective-permute-start | bytes 786440 | tf_op jit(solution)/shard_map/ppermute | solution.py:637
  45.5 15.9 %collective-permute-start.11 = (bf16[2,16,8,512]{3,2,1,0:T(8,128)(2,1)}, bf16[2,16,8,512]{3,2,1,0:T(8,128)(2,1)S(1)}, u32[]{:S(2)}, u32[]{:S(2)}) collective-permute-start(bf16[2,16,8,512]{3,2,1,0:T(8,128)(2,1)} %get-tuple-element.69), channel_id=1, source_target_pairs={{0,12},{1,13},{2,14},{3,15},{4,4},{5,5},{6,6},{7,7},{8,8},{9,9},{1... | collective-permute-start | bytes 786440 | tf_op jit(solution)/shard_map/ppermute | solution.py:637
  48.1 14.0 %collective-permute-start.12 = (bf16[2,16,8,512]{3,2,1,0:T(8,128)(2,1)}, bf16[2,16,8,512]{3,2,1,0:T(8,128)(2,1)S(1)}, u32[]{:S(2)}, u32[]{:S(2)}) collective-permute-start(bf16[2,16,8,512]{3,2,1,0:T(8,128)(2,1)} %get-tuple-element.70), channel_id=1, source_target_pairs={{0,13},{1,14},{2,15},{3,12},{4,5},{5,6},{6,7},{7,4},{8,9},{9,10},{... | collective-permute-start | bytes 786440 | tf_op jit(solution)/shard_map/ppermute | solution.py:637
  50.8 18.0 %collective-permute-start.13 = (bf16[2,16,8,512]{3,2,1,0:T(8,128)(2,1)}, bf16[2,16,8,512]{3,2,1,0:T(8,128)(2,1)S(1)}, u32[]{:S(2)}, u32[]{:S(2)}) collective-permute-start(bf16[2,16,8,512]{3,2,1,0:T(8,128)(2,1)} %get-tuple-element.71), channel_id=1, source_target_pairs={{0,14},{1,15},{2,12},{3,13},{4,6},{5,7},{6,4},{7,5},{8,10},{9,11},... | collective-permute-start | bytes 786440 | tf_op jit(solution)/shard_map/ppermute | solution.py:637
  52.6 22.1 %collective-permute-start.14 = (bf16[2,16,8,512]{3,2,1,0:T(8,128)(2,1)}, bf16[2,16,8,512]{3,2,1,0:T(8,128)(2,1)S(1)}, u32[]{:S(2)}, u32[]{:S(2)}) collective-permute-start(bf16[2,16,8,512]{3,2,1,0:T(8,128)(2,1)} %get-tuple-element.72), channel_id=1, source_target_pairs={{0,15},{1,12},{2,13},{3,14},{4,7},{5,4},{6,5},{7,6},{8,11},{9,8},{... | collective-permute-start | bytes 786440 | tf_op jit(solution)/shard_map/ppermute | solution.py:637
  54.6 1.0 copy-start.2
  60.6 35.8 %collective-permute-start.16 = (bf16[8,4,64,128]{3,2,1,0:T(8,128)(2,1)S(1)}, bf16[8,4,64,128]{3,2,1,0:T(8,128)(2,1)S(1)}, u32[]{:S(2)}, u32[]{:S(2)}) collective-permute-start(bf16[8,4,64,128]{3,2,1,0:T(8,128)(2,1)S(1)} %get-tuple-element.76), channel_id=1, source_target_pairs={{4,8},{5,9},{6,10},{7,11},{8,4},{9,5},{10,6},{11,7},{20,24},{21,25... | collective-permute-start | bytes 1572872 | tf_op jit(solution)/shard_map/ppermute | solution.py:670
  61.4 13.3 %collective-permute-start.17 = (f32[8,4,2,64]{3,2,1,0:T(2,128)S(1)}, f32[8,4,2,64]{3,2,1,0:T(2,128)S(1)}, u32[]{:S(2)}, u32[]{:S(2)}) collective-permute-start(f32[8,4,2,64]{3,2,1,0:T(2,128)S(1)} %get-tuple-element.77), channel_id=1, source_target_pairs={{4,8},{5,9},{6,10},{7,11},{8,4},{9,5},{10,6},{11,7},{20,24},{21,25... | collective-permute-start | bytes 49160 | tf_op jit(solution)/shard_map/ppermute | solution.py:671
  62.2 47.7 %collective-permute-start.1 = (bf16[2,16,8,512]{3,2,1,0:T(8,128)(2,1)}, bf16[2,16,8,512]{3,2,1,0:T(8,128)(2,1)S(1)}, u32[]{:S(2)}, u32[]{:S(2)}) collective-permute-start(bf16[2,16,8,512]{3,2,1,0:T(8,128)(2,1)} %get-tuple-element.51), channel_id=1, source_target_pairs={{0,4},{1,5},{2,6},{3,7},{4,0},{5,1},{6,2},{7,3},{8,12},{9,13},{10,... | collective-permute-start | bytes 786440 | tf_op jit(solution)/shard_map/ppermute | solution.py:637
  68.7 41.1 %collective-permute-start.3 = (bf16[2,16,8,512]{3,2,1,0:T(8,128)(2,1)}, bf16[2,16,8,512]{3,2,1,0:T(8,128)(2,1)S(1)}, u32[]{:S(2)}, u32[]{:S(2)}) collective-permute-start(bf16[2,16,8,512]{3,2,1,0:T(8,128)(2,1)} %get-tuple-element.54), channel_id=1, source_target_pairs={{0,5},{1,6},{2,7},{3,4},{4,1},{5,2},{6,3},{7,0},{8,13},{9,14},{10,... | collective-permute-start | bytes 786440 | tf_op jit(solution)/shard_map/ppermute | solution.py:637
  74.7 35.2 %collective-permute-start.5 = (bf16[2,16,8,512]{3,2,1,0:T(8,128)(2,1)S(1)}, bf16[2,16,8,512]{3,2,1,0:T(8,128)(2,1)S(1)}, u32[]{:S(2)}, u32[]{:S(2)}) collective-permute-start(bf16[2,16,8,512]{3,2,1,0:T(8,128)(2,1)S(1)} %copy-done.8), channel_id=1, source_target_pairs={{0,6},{1,7},{2,4},{3,5},{4,2},{5,3},{6,0},{7,1},{8,14},{9,15},{10,... | collective-permute-start | bytes 786440 | tf_op jit(solution)/shard_map/ppermute | solution.py:637
  74.7 35.1 %collective-permute-start.7 = (bf16[2,16,8,512]{3,2,1,0:T(8,128)(2,1)S(1)}, bf16[2,16,8,512]{3,2,1,0:T(8,128)(2,1)S(1)}, u32[]{:S(2)}, u32[]{:S(2)}) collective-permute-start(bf16[2,16,8,512]{3,2,1,0:T(8,128)(2,1)S(1)} %copy-done.7), channel_id=1, source_target_pairs={{0,7},{1,4},{2,5},{3,6},{4,3},{5,0},{6,1},{7,2},{8,15},{9,12},{10,... | collective-permute-start | bytes 786440 | tf_op jit(solution)/shard_map/ppermute | solution.py:637
  86.5 2.2 %copy-start = (bf16[8,512,512]{2,1,0:T(8,128)(2,1)S(1)}, bf16[8,512,512]{2,1,0:T(8,128)(2,1)}, u32[]{:S(2)}) copy-start(bf16[8,512,512]{2,1,0:T(8,128)(2,1)} %keys.1) | copy-start | bytes 12582916
  88.7 2.2 %copy-start.1 = (bf16[8,512,512]{2,1,0:T(8,128)(2,1)S(1)}, bf16[8,512,512]{2,1,0:T(8,128)(2,1)}, u32[]{:S(2)}) copy-start(bf16[8,512,512]{2,1,0:T(8,128)(2,1)} %values.1) | copy-start | bytes 12582916
  90.9 5.5 %copy-start.3 = (bf16[2,16,8,512]{3,2,1,0:T(8,128)(2,1)S(1)}, bf16[2,16,8,512]{3,2,1,0:T(8,128)(2,1)}, u32[]{:S(2)}) copy-start(bf16[2,16,8,512]{3,2,1,0:T(8,128)(2,1)} %get-tuple-element.65.refs_4_) | copy-start | bytes 786436

commit v3 on v2

--- a/solution.py
+++ b/solution.py
@@ -19,6 +19,7 @@
 LANES = 128
 GRANT = 20 * 2**20
 UNROLL = 4
+PACKED = 4
 NEG = -1e30
 
 
@@ -39,19 +40,70 @@
     return jnp.cos(angles), jnp.sin(angles) * sign
 
 
-def pack_kernel(n, cap, phase_table, target, rows, lens, keys, values, *refs):
-    notes = refs[0]
-    outs = refs[1 : 1 + n]
-    slots, fill, rel, sems = refs[1 + n :]
+def pack_kernel(n, phase_table, target, keys, values, *refs):
+    outs = refs[:n]
+    slots, fill, rel, sems = refs[n:]
     blocks = keys.shape[0]
     in_plane = n // PLANES
     me = lax.axis_index("seq")
     plane, place = me // in_plane, me % in_plane
 
+    def clear(p, _):
+        for i in range(in_plane):
+            fill[p * in_plane + i] = 0
+            offset = i - place
+            offset = jnp.where(offset < 0, offset + in_plane, offset)
+            rel[p * in_plane + i] = phase_table[plane, p] * in_plane + offset
+        return 0
+
+    lax.fori_loop(0, PLANES, clear, 0)
+
+    def put(step, _):
+        ready = []
+        for u in range(PACKED):
+            b = step * PACKED + u
+            dest = target[b]
+            slot = fill[dest]
+            fill[dest] = slot + 1
+            ready.append((b, rel[dest], slot))
+        for b, message, slot in ready:
+            slots[message, 0, slot] = keys[b]
+            slots[message, 1, slot] = values[b]
+        return 0
+
+    lax.fori_loop(0, blocks // PACKED, put, 0)
+    copies = [pltpu.make_async_copy(slots.at[i], outs[i], sems.at[i]) for i in range(n)]
+    for copy in copies:
+        copy.start()
+    for copy in copies:
+        copy.wait()
+
+
+def pack(n, cap, phase_table, target, keys, values):
+    width = keys.shape[-1]
+    message = jax.ShapeDtypeStruct((2, cap, BLK, width), jnp.bfloat16)
+    smem = pl.BlockSpec(memory_space=pltpu.SMEM)
+    vmem = pl.BlockSpec(memory_space=pltpu.VMEM)
+    return pl.pallas_call(
+        functools.partial(pack_kernel, n),
+        out_shape=(message,) * n,
+        in_specs=[smem] * 2 + [vmem] * 2,
+        out_specs=(pl.BlockSpec(memory_space=pl.ANY),) * n,
+        scratch_shapes=[
+            pltpu.VMEM((n, 2, cap, BLK, width), jnp.bfloat16),
+            pltpu.SMEM((n,), jnp.int32),
+            pltpu.SMEM((n,), jnp.int32),
+            pltpu.SemaphoreType.DMA((n,)),
+        ],
+        name="pack",
+    )(phase_table, target, keys, values)
+
+
+def note_kernel(n, cap, target, rows, lens, notes, fill):
+    in_plane = n // PLANES
+
     def clear(i, _):
         fill[i] = 0
-        offset = (i % in_plane - place + in_plane) % in_plane
-        rel[i] = phase_table[plane, i // in_plane] * in_plane + offset
         for k in range(cap):
             notes[i, k] = -1
             notes[i, LANES + k] = -1
@@ -71,37 +123,22 @@
         twin = jnp.where(inner, (PLANES - 1 - 2 * dest_plane) * in_plane + dest, dest)
         notes[dest, slot] = row
         notes[twin, LANES + slot] = row
-        message = rel[dest]
-        slots[message, 0, slot] = keys[b]
-        slots[message, 1, slot] = values[b]
         return 0
 
-    lax.fori_loop(0, blocks, put, 0, unroll=4)
-    copies = [pltpu.make_async_copy(slots.at[i], outs[i], sems.at[i]) for i in range(n)]
-    for copy in copies:
-        copy.start()
-    for copy in copies:
-        copy.wait()
-
-
-def pack(n, cap, phase_table, target, rows, lens, keys, values):
-    width = keys.shape[-1]
-    message = jax.ShapeDtypeStruct((2, cap, BLK, width), jnp.bfloat16)
+    lax.fori_loop(0, rows.shape[0], put, 0, unroll=4)
+
+
+def note(n, cap, target, rows, lens):
     smem = pl.BlockSpec(memory_space=pltpu.SMEM)
-    vmem = pl.BlockSpec(memory_space=pltpu.VMEM)
     return pl.pallas_call(
-        functools.partial(pack_kernel, n, cap),
-        out_shape=(jax.ShapeDtypeStruct((n, 3 * LANES), jnp.int32),) + (message,) * n,
-        in_specs=[smem] * 4 + [vmem] * 2,
-        out_specs=(smem,) + (pl.BlockSpec(memory_space=pl.ANY),) * n,
-        scratch_shapes=[
-            pltpu.VMEM((n, 2, cap, BLK, width), jnp.bfloat16),
-            pltpu.SMEM((n,), jnp.int32),
-            pltpu.SMEM((n,), jnp.int32),
-            pltpu.SemaphoreType.DMA((n,)),
-        ],
-        name="pack",
-    )(phase_table, target, rows, lens, keys, values)
+        functools.partial(note_kernel, n, cap),
+        out_shape=jax.ShapeDtypeStruct((n, 3 * LANES), jnp.int32),
+        in_specs=[smem] * 3,
+        out_specs=smem,
+        scratch_shapes=[pltpu.SMEM((n,), jnp.int32)],
+        compiler_params=pltpu.CompilerParams(vmem_limit_bytes=GRANT),
+        name="note",
+    )(target, rows, lens)
 
 
 def index_kernel(n, cap, rows, notes, stages, place, row_of, rank_of, used, tally):
@@ -165,6 +202,12 @@
     )(notes, stages)
 
 
+def as_wide(line, width):
+    if width % HD == 0:
+        return jnp.concatenate([line] * (width // HD), axis=1)
+    return line[:, :width]
+
+
 def blend(queries, pieces, old, guard=False):
     scale = HD ** (-0.5)
     heads = range(KVH)
@@ -195,7 +238,7 @@
         else:
             old_acc, old_top, old_total = old[head]
             new_top = jnp.maximum(old_top, peak)
-        raw = [jnp.exp(one - new_top[:, :1]) for one in scores[head]]
+        raw = [jnp.exp(one - as_wide(new_top, one.shape[1])) for one in scores[head]]
         if guard:
             raw = [jnp.where(piece[2], one, 0.0) for piece, one in zip(pieces, raw)]
         added = sum(jnp.sum(one, axis=-1, keepdims=True) for one in raw)
@@ -601,49 +644,43 @@
         ],
         jnp.int32,
     )
-    notes, *messages = pack(
-        n,
-        cap,
-        phase_table,
-        block_device[:, 0],
-        block_row,
-        cache_len,
-        span_keys.reshape(blocks, BLK, feature),
-        span_values.reshape(blocks, BLK, feature),
-    )
-    packed = {p: messages[i * in_plane : (i + 1) * in_plane] for i, p in enumerate(names)}
-
-    grouped = (
-        queries.reshape(rows, steps, KVH, group, HD)
-        .transpose(0, 2, 1, 3, 4)
-        .reshape(rows, KVH, steps * group, HD)
-    )
     half = PLANES // 2
     swap = [
         (a * in_plane + i, b * in_plane + i)
         for a, b in ((half - 1, half), (half, half - 1))
         for i in range(in_plane)
     ]
-    mirrored = lax.ppermute(grouped, "seq", swap)
-
-    def send(phase, after=None):
+    mirrored = lax.ppermute(queries, "seq", swap)
+    messages = pack(
+        n,
+        cap,
+        phase_table,
+        block_device[:, 0],
+        span_keys.reshape(blocks, BLK, feature),
+        span_values.reshape(blocks, BLK, feature),
+    )
+    packed = {p: messages[i * in_plane : (i + 1) * in_plane] for i, p in enumerate(names)}
+
+    def send(phase):
         out = []
         for offset in range(in_plane):
             value = packed[phase][offset]
-            if after is not None:
-                value, after[offset] = lax.optimization_barrier((value, after[offset]))
             pairs = route(n, phase, offset)
             if any(a != b for a, b in pairs):
                 value = lax.ppermute(value, "seq", pairs)
             out.append(value)
         return out
 
-    got = {}
-    got["d"] = send("d")
-    got["f"] = send("f")
-    got["g"] = send("g")
-    got["b"] = send("b", got["d"])
-
+    got = {phase: send(phase) for phase in names}
+
+    def regroup(value):
+        value = value.reshape(rows, steps, KVH, group, HD).transpose(0, 2, 1, 3, 4)
+        return value.reshape(rows, KVH, steps * group, HD)
+
+    queries, mirrored = lax.optimization_barrier((queries, mirrored))
+    grouped, mirrored = regroup(queries), regroup(mirrored)
+
+    notes = note(n, cap, block_device[:, 0], block_row, cache_len)
     notes = lax.all_to_all(notes, "seq", split_axis=0, concat_axis=0, tiled=True)
     mine = lax.dynamic_index_in_dim(jnp.array(device_tables(n)), me, 0, keepdims=False)
     *slots, tally = index(n, cap, rows, notes, mine[2:])

time: 118 us -> 119 us (level)
  local copies, waits for them, and re-layouts: 9.23 us -> 17.3 us
  starting transfers between devices: 46.5 us -> 38.7 us
  other arithmetic: 1.71 us -> 3.11 us
    ppermute x15, starting transfers between devices: 37.3 us -> 29.8 us  [send(): value = lax.ppermute(value, 'seq', pairs)]
    unnamed x21 -> x33, local copies, waits for them, and re-layouts: 5.36 us -> 9.63 us
    reshape x2 -> x4, local copies, waits for them, and re-layouts: 1.67 us -> 5.1 us  [regroup(): value = value.reshape(rows, steps, KVH, group, HD).transpose(0, 2, 1, 3, 4)]
    pallas_call x1 -> x2, Pallas kernels: 7.62 us -> 8.57 us  [the longest x1 4.53 us: pack(): pl.pallas_call(functools.partial(pack_kernel, n), out_shape=(message,) *...]
  transfers between devices with their start and end apart: 19 -> 19, of which waited for: 7 -> 6; matrix products, arithmetic and copies ran while one was open for 3% -> 9% of each run, Pallas kernels for 27% -> 24%
where the time goes in v3:
time: 119 us; the launch traced here: 118 us
  Pallas kernels  39.4 us (33%)
  starting transfers between devices  38.7 us (33%)
  waiting for transfers between devices  17.5 us (15%)
  local copies, waits for them, and re-layouts  17.3 us (15%)
  other arithmetic  3.11 us (3%)
  between operations  2.19 us (2%)
    ppermute x15, starting transfers between devices, send(): value = lax.ppermute(value, 'seq', pairs)  29.8 us
    pallas_call x3, Pallas kernels, span(): pl.pallas_call(functools.partial(span_kernel, kind, kernel, count, cap),...  25 us
    ppermute x15, waiting for transfers between devices, send(): value = lax.ppermute(value, 'seq', pairs)  17.4 us
    unnamed x33, local copies, waits for them, and re-layouts  9.63 us
    all_to_all x1, starting transfers between devices, body(): lax.all_to_all(notes, 'seq', split_axis=0, concat_axis=0, tiled=True)  6.35 us
    pallas_call x1, Pallas kernels, resident(): pl.pallas_call(resident_kernel, out_shape=state_shapes(rows, grouped.shap...  5.47 us
    reshape x4, local copies, waits for them, and re-layouts, regroup(): value = value.reshape(rows, steps, KVH, group, HD).transpose(0, 2, 1, 3, 4)  5.1 us
    pallas_call x1, Pallas kernels, pack(): pl.pallas_call(functools.partial(pack_kernel, n), out_shape=(message,) *...  4.53 us
  transfers between devices with their start and end apart: 19, of which 6 were waited for; matrix products, arithmetic and copies ran while one was open for 9% of the time, Pallas kernels for 24%

profile of v3, /device:TPU:27, one launch (start us, length us, event | category | flops | bytes accessed | tf_op | source)
XLA Modules:
  0.0 118.2 jit_solution(18271922902017585745)
XLA Ops:
  2.0 4.0 %note.1 = s32[16,384]{1,0:T(8,128)S(1)} custom-call(s32[128]{0:T(128)S(1)} %bitcast.40, s32[128]{0:T(128)S(1)} %copy-done.12, s32[8]{0:T(128)S(1)} %copy-done.6), custom_call_target="tpu_custom_call" | custom-call | tf_op jit(solution)/shard_map/note/pallas_call | solution.py:133
  6.6 6.4 %all-to-all-start = ((s32[16,1,384]{2,1,0:T(1,128)}), s32[16,1,384]{2,1,0:T(1,128)S(1)}, u32[]{:S(2)}, u32[]{:S(2)}) async-start(s32[16,1,384]{2,1,0:T(1,128)} %copy.16), calls=%async_computation | async-start | bytes 49152 | tf_op jit(solution)/shard_map/all_to_all | solution.py:684
  13.7 4.5 %pack.1 = (bf16[2,16,8,512]{3,2,1,0:T(8,128)(2,1)}, bf16[2,16,8,512]{3,2,1,0:T(8,128)(2,1)}, bf16[2,16,8,512]{3,2,1,0:T(8,128)(2,1)}, bf16[2,16,8,512]{3,2,1,0:T...) custom-call(s32[4,4]{1,0:T(4,128)} %constant.52.clone.phase_table, ...), custom_call_target="tpu_custom_call" | custom-call | tf_op jit(solution)/shard_map/pack/pallas_call | solution.py:87
  18.2 1.8 %collective-permute-start.5 = (bf16[2,16,8,512]{3,2,1,0:T(8,128)(2,1)}, bf16[2,16,8,512]{3,2,1,0:T(8,128)(2,1)S(1)}, u32[]{:S(2)}, u32[]{:S(2)}) collective-permute-start(bf16[2,16,8,512]{3,2,1,0:T(8,128)(2,1)} %get-tuple-element.46), channel_id=1, source_target_pairs={{0,4},{1,5},{2,6},{3,7},{4,12},{5,13},{6,14},{7,15},{8,0},{9,1},{1... | collective-permute-start | bytes 786440 | tf_op jit(solution)/shard_map/ppermute | solution.py:670
  20.1 1.5 %collective-permute-start.6 = (bf16[2,16,8,512]{3,2,1,0:T(8,128)(2,1)}, bf16[2,16,8,512]{3,2,1,0:T(8,128)(2,1)S(1)}, u32[]{:S(2)}, u32[]{:S(2)}) collective-permute-start(bf16[2,16,8,512]{3,2,1,0:T(8,128)(2,1)} %get-tuple-element.47), channel_id=1, source_target_pairs={{0,5},{1,6},{2,7},{3,4},{4,13},{5,14},{6,15},{7,12},{8,1},{9,2},{1... | collective-permute-start | bytes 786440 | tf_op jit(solution)/shard_map/ppermute | solution.py:670
  21.6 2.6 %collective-permute-start.7 = (bf16[2,16,8,512]{3,2,1,0:T(8,128)(2,1)}, bf16[2,16,8,512]{3,2,1,0:T(8,128)(2,1)S(1)}, u32[]{:S(2)}, u32[]{:S(2)}) collective-permute-start(bf16[2,16,8,512]{3,2,1,0:T(8,128)(2,1)} %get-tuple-element.48), channel_id=1, source_target_pairs={{0,6},{1,7},{2,4},{3,5},{4,14},{5,15},{6,12},{7,13},{8,2},{9,3},{1... | collective-permute-start | bytes 786440 | tf_op jit(solution)/shard_map/ppermute | solution.py:670
  26.5 1.4 %fusion.3 = s32[]{:T(128)} fusion(s32[16]{0:T(128)} %constant.54.clone, s32[]{:T(128)S(6)} %axis_index.12), kind=kLoop, calls=%fused_computation.20 | loop fusion | flops 47 | bytes 72 | tf_op jit(solution)/shard_map/reduce_sum | solution.py:689
  29.8 4.0 %collective-permute-done.5.refs_0_ = bf16[2,16,8,512]{3,2,1,0:T(8,128)(2,1)S(1)} collective-permute-done((bf16[2,16,8,512]{3,2,1,0:T(8,128)(2,1)}, bf16[2,16,8,512]{3,2,1,0:T(8,128)(2,1)S(1)}, u32[]{:S(2)}, u32[]{:S(2)}) %collective-permute-start.5) | collective-permute-done | bytes 262176 | tf_op jit(solution)/shard_map/ppermute | solution.py:670
  33.8 3.2 %collective-permute-start.9 = (bf16[2,16,8,512]{3,2,1,0:T(8,128)(2,1)}, bf16[2,16,8,512]{3,2,1,0:T(8,128)(2,1)S(1)}, u32[]{:S(2)}, u32[]{:S(2)}) collective-permute-start(bf16[2,16,8,512]{3,2,1,0:T(8,128)(2,1)} %get-tuple-element.51), channel_id=1, source_target_pairs={{0,1},{1,2},{2,3},{3,0},{4,5},{5,6},{6,7},{7,4},{8,9},{9,10},{10,1... | collective-permute-start | bytes 786440 | tf_op jit(solution)/shard_map/ppermute | solution.py:670
  37.0 3.9 %collective-permute-done.6.refs_1_ = bf16[2,16,8,512]{3,2,1,0:T(8,128)(2,1)S(1)} collective-permute-done((bf16[2,16,8,512]{3,2,1,0:T(8,128)(2,1)}, bf16[2,16,8,512]{3,2,1,0:T(8,128)(2,1)S(1)}, u32[]{:S(2)}, u32[]{:S(2)}) %collective-permute-start.6) | collective-permute-done | bytes 262176 | tf_op jit(solution)/shard_map/ppermute | solution.py:670
  40.8 1.2 %collective-permute-start.10 = (bf16[2,16,8,512]{3,2,1,0:T(8,128)(2,1)}, bf16[2,16,8,512]{3,2,1,0:T(8,128)(2,1)S(1)}, u32[]{:S(2)}, u32[]{:S(2)}) collective-permute-start(bf16[2,16,8,512]{3,2,1,0:T(8,128)(2,1)} %get-tuple-element.52), channel_id=1, source_target_pairs={{0,2},{1,3},{2,0},{3,1},{4,6},{5,7},{6,4},{7,5},{8,10},{9,11},{10,... | collective-permute-start | bytes 786440 | tf_op jit(solution)/shard_map/ppermute | solution.py:670
  42.0 0.8 copy-done.13
  43.6 1.6 %reshape.92 = bf16[8,4,4,16,128]{4,3,2,1,0:T(8,128)(2,1)S(1)} reshape(bf16[8,4,8192]{2,1,0:T(4,128)(2,1)} %copy-done.13) | data formatting | bytes 1048576 | tf_op jit(solution)/shard_map/reshape | solution.py:677
  45.9 3.1 %collective-permute-start.12 = (bf16[2,16,8,512]{3,2,1,0:T(8,128)(2,1)}, bf16[2,16,8,512]{3,2,1,0:T(8,128)(2,1)S(1)}, u32[]{:S(2)}, u32[]{:S(2)}) collective-permute-start(bf16[2,16,8,512]{3,2,1,0:T(8,128)(2,1)} %get-tuple-element.54), channel_id=1, source_target_pairs={{0,12},{1,13},{2,14},{3,15},{4,4},{5,5},{6,6},{7,7},{8,8},{9,9},{1... | collective-permute-start | bytes 786440 | tf_op jit(solution)/shard_map/ppermute | solution.py:670
  49.0 3.1 %collective-permute-done.8.refs_3_ = bf16[2,16,8,512]{3,2,1,0:T(8,128)(2,1)S(1)} collective-permute-done((bf16[2,16,8,512]{3,2,1,0:T(8,128)(2,1)}, bf16[2,16,8,512]{3,2,1,0:T(8,128)(2,1)S(1)}, u32[]{:S(2)}, u32[]{:S(2)}) %collective-permute-start.8) | collective-permute-done | bytes 262176 | tf_op jit(solution)/shard_map/ppermute | solution.py:670
  52.2 1.3 %collective-permute-start.13 = (bf16[2,16,8,512]{3,2,1,0:T(8,128)(2,1)}, bf16[2,16,8,512]{3,2,1,0:T(8,128)(2,1)S(1)}, u32[]{:S(2)}, u32[]{:S(2)}) collective-permute-start(bf16[2,16,8,512]{3,2,1,0:T(8,128)(2,1)} %get-tuple-element.55), channel_id=1, source_target_pairs={{0,13},{1,14},{2,15},{3,12},{4,5},{5,6},{6,7},{7,4},{8,9},{9,10},{... | collective-permute-start | bytes 786440 | tf_op jit(solution)/shard_map/ppermute | solution.py:670
  53.5 2.1 %collective-permute-start.14 = (bf16[2,16,8,512]{3,2,1,0:T(8,128)(2,1)}, bf16[2,16,8,512]{3,2,1,0:T(8,128)(2,1)S(1)}, u32[]{:S(2)}, u32[]{:S(2)}) collective-permute-start(bf16[2,16,8,512]{3,2,1,0:T(8,128)(2,1)} %get-tuple-element.56), channel_id=1, source_target_pairs={{0,14},{1,15},{2,12},{3,13},{4,6},{5,7},{6,4},{7,5},{8,10},{9,11},... | collective-permute-start | bytes 786440 | tf_op jit(solution)/shard_map/ppermute | solution.py:670
  55.6 2.2 %collective-permute-done.10.refs_6_ = bf16[2,16,8,512]{3,2,1,0:T(8,128)(2,1)S(1)} collective-permute-done((bf16[2,16,8,512]{3,2,1,0:T(8,128)(2,1)}, bf16[2,16,8,512]{3,2,1,0:T(8,128)(2,1)S(1)}, u32[]{:S(2)}, u32[]{:S(2)}) %collective-permute-start.10) | collective-permute-done | bytes 262176 | tf_op jit(solution)/shard_map/ppermute | solution.py:670
  57.8 3.5 %collective-permute-done.11.refs_7_ = bf16[2,16,8,512]{3,2,1,0:T(8,128)(2,1)S(1)} collective-permute-done((bf16[2,16,8,512]{3,2,1,0:T(8,128)(2,1)}, bf16[2,16,8,512]{3,2,1,0:T(8,128)(2,1)S(1)}, u32[]{:S(2)}, u32[]{:S(2)}) %collective-permute-start.11) | collective-permute-done | bytes 262176 | tf_op jit(solution)/shard_map/ppermute | solution.py:670
  61.3 0.9 copy-done.2
  62.3 5.9 %shard_map.127 = (bf16[8,4,64,128]{3,2,1,0:T(8,128)(2,1)}, f32[8,4,2,64]{3,2,1,0:T(2,128)}) custom-call(s32[8]{0:T(128)S(1)} %get-tuple-element.74.entry, s32[8]{0:T(128)S(1)} %get-tuple-element.73.stage, s32[32,16]{1,0:T(8,128)S(1)} %get-tuple-element.36.place_of, s32[32,16]{1,0:T(8,128)S(1)} %get-tuple-element.37.row_of, ...), custom_call_target="tpu_custom_call" | custom-call | flops 1000000000 | bytes 12582912 | tf_op jit(solution)/shard_map/pallas_call | solution.py:550
  69.5 1.3 %collective-permute-start.17 = (f32[8,4,2,64]{3,2,1,0:T(2,128)}, f32[8,4,2,64]{3,2,1,0:T(2,128)}, u32[]{:S(2)}, u32[]{:S(2)}) collective-permute-start(f32[8,4,2,64]{3,2,1,0:T(2,128)} %get-tuple-element.63), channel_id=1, source_target_pairs={{4,8},{5,9},{6,10},{7,11},{8,4},{9,5},{10,6},{11,7},{20,24},{21,25... | collective-permute-start | bytes 49160 | tf_op jit(solution)/shard_map/ppermute | solution.py:708
  71.3 2.4 %reshape.88 = bf16[8,4,4,16,128]{4,3,2,1,0:T(8,128)(2,1)} reshape(bf16[8,4,8192]{2,1,0:T(4,128)(2,1)} %param.20) | data formatting | bytes 1048576 | tf_op jit(solution)/shard_map/reshape | solution.py:677
  73.7 1.1 copy.17
  74.9 1.7 %collective-permute-start.2 = (bf16[2,16,8,512]{3,2,1,0:T(8,128)(2,1)}, bf16[2,16,8,512]{3,2,1,0:T(8,128)(2,1)S(1)}, u32[]{:S(2)}, u32[]{:S(2)}) collective-permute-start(bf16[2,16,8,512]{3,2,1,0:T(8,128)(2,1)} %get-tuple-element.43), channel_id=1, source_target_pairs={{0,5},{1,6},{2,7},{3,4},{4,1},{5,2},{6,3},{7,0},{8,13},{9,14},{10,... | collective-permute-start | bytes 786440 | tf_op jit(solution)/shard_map/ppermute | solution.py:670
  76.8 10.7 %collective-permute-start.4 = (bf16[2,16,8,512]{3,2,1,0:T(8,128)(2,1)}, bf16[2,16,8,512]{3,2,1,0:T(8,128)(2,1)S(1)}, u32[]{:S(2)}, u32[]{:S(2)}) collective-permute-start(bf16[2,16,8,512]{3,2,1,0:T(8,128)(2,1)} %get-tuple-element.45), channel_id=1, source_target_pairs={{0,7},{1,4},{2,5},{3,6},{4,3},{5,0},{6,1},{7,2},{8,15},{9,12},{10,... | collective-permute-start | bytes 786440 | tf_op jit(solution)/shard_map/ppermute | solution.py:670
  87.5 2.2 %copy-done = bf16[8,512,512]{2,1,0:T(8,128)(2,1)S(1)} copy-done((bf16[8,512,512]{2,1,0:T(8,128)(2,1)S(1)}, bf16[8,512,512]{2,1,0:T(8,128)(2,1)}, u32[]{:S(2)}) %copy-start) | copy-done | bytes 4194328
  89.7 2.2 %copy-done.1 = bf16[8,512,512]{2,1,0:T(8,128)(2,1)S(1)} copy-done((bf16[8,512,512]{2,1,0:T(8,128)(2,1)S(1)}, bf16[8,512,512]{2,1,0:T(8,128)(2,1)}, u32[]{:S(2)}) %copy-start.1) | copy-done | bytes 4194328
  91.9 0.8 copy-done.4
  93.4 5.5 %resident.1 = (f32[8,4,64,128]{3,2,1,0:T(8,128)S(1)}, f32[8,4,64,128]{3,2,1,0:T(8,128)S(1)}, f32[8,4,64,128]{3,2,1,0:T(8,128)S(1)}) custom-call(s32[8]{0:T(128)S(1)} %copy-done.7, bf16[8,4,64,128]{3,2,1,0:T(8,128)(2,1)S(1)} %bitcast.33, bf16[8,4,512]{2,1,0:T(4,128)(2,1)S(1)} %copy-done.4, bf16[8,4,512]{2,1,0:T(4,128)(2,1)S(1)} %copy-done.5, ...), custom_call_target="tpu_custom_call" | custom-call | flops 2000000000 | bytes 16777216 | tf_op jit(solution)/shard_map/resident/pallas_call | solution.py:346
  98.9 12.1 %shard_map.128 = (f32[8,4,64,128]{3,2,1,0:T(8,128)S(1)}, f32[8,4,64,128]{3,2,1,0:T(8,128)S(1)}, f32[8,4,64,128]{3,2,1,0:T(8,128)S(1)}) custom-call(s32[12]{0:T(128)S(1)} %copy-done.10, s32[12]{0:T(128)S(1)} %copy-done.9, s32[32,16]{1,0:T(8,128)S(1)} %get-tuple-element.36.place_of, s32[32,16]{1,0:T(8,128)S(1)} %get-tuple-element.37.row_of, ...), custom_call_target="tpu_custom_call" | custom-call | flops 1000000000 | bytes 12582912 | tf_op jit(solution)/shard_map/pallas_call | solution.py:550
  111.1 7.0 %shard_map.129 = bf16[8,4,8192]{2,1,0:T(4,128)(2,1)} custom-call(s32[4]{0:T(128)S(1)} %copy-done.8, s32[4]{0:T(128)S(1)} %get-tuple-element.77.stage, s32[32,16]{1,0:T(8,128)S(1)} %get-tuple-element.36.place_of, s32[32,16]{1,0:T(8,128)S(1)} %get-tuple-element.37.row_of, s32[32,16]{1,0:T(8,128)S(1)} %get-tuple-element.38.rank_of, ...), custom_call_target="tpu_custom_call" | custom-call | flops 1000000000 | bytes 12582912 | tf_op jit(solution)/shard_map/pallas_call | solution.py:550
  (66 shorter events, 10.1 us)
Async XLA Ops:
  6.6 23.2 %all-to-all-start = ((s32[16,1,384]{2,1,0:T(1,128)}), s32[16,1,384]{2,1,0:T(1,128)S(1)}, u32[]{:S(2)}, u32[]{:S(2)}) async-start(s32[16,1,384]{2,1,0:T(1,128)} %copy.16), calls=%async_computation | async-start | bytes 49152 | tf_op jit(solution)/shard_map/all_to_all | solution.py:684
  13.0 29.0 %collective-permute-start = (bf16[8,4,8192]{2,1,0:T(4,128)(2,1)}, bf16[8,4,8192]{2,1,0:T(4,128)(2,1)S(1)}, u32[]{:S(2)}, u32[]{:S(2)}) collective-permute-start(bf16[8,4,8192]{2,1,0:T(4,128)(2,1)} %param.20), channel_id=1, source_target_pairs={{4,8},{5,9},{6,10},{7,11},{8,4},{9,5},{10,6},{11,7},{20,24},{21,25... | collective-permute-start | bytes 1572872 | tf_op jit(solution)/shard_map/ppermute | solution.py:653
  18.2 15.6 %collective-permute-start.5 = (bf16[2,16,8,512]{3,2,1,0:T(8,128)(2,1)}, bf16[2,16,8,512]{3,2,1,0:T(8,128)(2,1)S(1)}, u32[]{:S(2)}, u32[]{:S(2)}) collective-permute-start(bf16[2,16,8,512]{3,2,1,0:T(8,128)(2,1)} %get-tuple-element.46), channel_id=1, source_target_pairs={{0,4},{1,5},{2,6},{3,7},{4,12},{5,13},{6,14},{7,15},{8,0},{9,1},{1... | collective-permute-start | bytes 786440 | tf_op jit(solution)/shard_map/ppermute | solution.py:670
  20.1 20.8 %collective-permute-start.6 = (bf16[2,16,8,512]{3,2,1,0:T(8,128)(2,1)}, bf16[2,16,8,512]{3,2,1,0:T(8,128)(2,1)S(1)}, u32[]{:S(2)}, u32[]{:S(2)}) collective-permute-start(bf16[2,16,8,512]{3,2,1,0:T(8,128)(2,1)} %get-tuple-element.47), channel_id=1, source_target_pairs={{0,5},{1,6},{2,7},{3,4},{4,13},{5,14},{6,15},{7,12},{8,1},{9,2},{1... | collective-permute-start | bytes 786440 | tf_op jit(solution)/shard_map/ppermute | solution.py:670
  21.6 24.3 %collective-permute-start.7 = (bf16[2,16,8,512]{3,2,1,0:T(8,128)(2,1)}, bf16[2,16,8,512]{3,2,1,0:T(8,128)(2,1)S(1)}, u32[]{:S(2)}, u32[]{:S(2)}) collective-permute-start(bf16[2,16,8,512]{3,2,1,0:T(8,128)(2,1)} %get-tuple-element.48), channel_id=1, source_target_pairs={{0,6},{1,7},{2,4},{3,5},{4,14},{5,15},{6,12},{7,13},{8,2},{9,3},{1... | collective-permute-start | bytes 786440 | tf_op jit(solution)/shard_map/ppermute | solution.py:670
  24.2 28.0 %collective-permute-start.8 = (bf16[2,16,8,512]{3,2,1,0:T(8,128)(2,1)}, bf16[2,16,8,512]{3,2,1,0:T(8,128)(2,1)S(1)}, u32[]{:S(2)}, u32[]{:S(2)}) collective-permute-start(bf16[2,16,8,512]{3,2,1,0:T(8,128)(2,1)} %get-tuple-element.49), channel_id=1, source_target_pairs={{0,7},{1,4},{2,5},{3,6},{4,15},{5,12},{6,13},{7,14},{8,3},{9,0},{1... | collective-permute-start | bytes 786440 | tf_op jit(solution)/shard_map/ppermute | solution.py:670
  26.0 16.8 %copy-start.14 = (s32[4,16]{1,0:T(4,128)}, s32[4,16]{1,0:T(4,128)S(1)}, u32[]{:S(2)}) copy-start(s32[4,16]{1,0:T(4,128)S(1)} %get-tuple-element.68) | copy-start | bytes 772
  26.0 61.5 %copy-start.7 = (s32[8]{0:T(128)S(1)}, s32[8]{0:T(128)}, u32[]{:S(2)}) copy-start(s32[8]{0:T(128)} %lens.3) | copy-start | bytes 100
  33.8 19.7 %collective-permute-start.9 = (bf16[2,16,8,512]{3,2,1,0:T(8,128)(2,1)}, bf16[2,16,8,512]{3,2,1,0:T(8,128)(2,1)S(1)}, u32[]{:S(2)}, u32[]{:S(2)}) collective-permute-start(bf16[2,16,8,512]{3,2,1,0:T(8,128)(2,1)} %get-tuple-element.51), channel_id=1, source_target_pairs={{0,1},{1,2},{2,3},{3,0},{4,5},{5,6},{6,7},{7,4},{8,9},{9,10},{10,1... | collective-permute-start | bytes 786440 | tf_op jit(solution)/shard_map/ppermute | solution.py:670
  40.8 17.0 %collective-permute-start.10 = (bf16[2,16,8,512]{3,2,1,0:T(8,128)(2,1)}, bf16[2,16,8,512]{3,2,1,0:T(8,128)(2,1)S(1)}, u32[]{:S(2)}, u32[]{:S(2)}) collective-permute-start(bf16[2,16,8,512]{3,2,1,0:T(8,128)(2,1)} %get-tuple-element.52), channel_id=1, source_target_pairs={{0,2},{1,3},{2,0},{3,1},{4,6},{5,7},{6,4},{7,5},{8,10},{9,11},{10,... | collective-permute-start | bytes 786440 | tf_op jit(solution)/shard_map/ppermute | solution.py:670
  42.0 0.8 copy-start.13
  42.8 18.5 %collective-permute-start.11 = (bf16[2,16,8,512]{3,2,1,0:T(8,128)(2,1)}, bf16[2,16,8,512]{3,2,1,0:T(8,128)(2,1)S(1)}, u32[]{:S(2)}, u32[]{:S(2)}) collective-permute-start(bf16[2,16,8,512]{3,2,1,0:T(8,128)(2,1)} %get-tuple-element.53), channel_id=1, source_target_pairs={{0,3},{1,0},{2,1},{3,2},{4,7},{5,4},{6,5},{7,6},{8,11},{9,8},{10,9... | collective-permute-start | bytes 786440 | tf_op jit(solution)/shard_map/ppermute | solution.py:670
  45.2 23.7 %copy-start.15 = (s32[4,16]{1,0:T(4,128)S(1)}, s32[4,16]{1,0:T(4,128)}, u32[]{:S(2)}) copy-start(s32[4,16]{1,0:T(4,128)} %copy-done.14) | copy-start | bytes 772
  45.9 23.5 %collective-permute-start.12 = (bf16[2,16,8,512]{3,2,1,0:T(8,128)(2,1)}, bf16[2,16,8,512]{3,2,1,0:T(8,128)(2,1)S(1)}, u32[]{:S(2)}, u32[]{:S(2)}) collective-permute-start(bf16[2,16,8,512]{3,2,1,0:T(8,128)(2,1)} %get-tuple-element.54), channel_id=1, source_target_pairs={{0,12},{1,13},{2,14},{3,15},{4,4},{5,5},{6,6},{7,7},{8,8},{9,9},{1... | collective-permute-start | bytes 786440 | tf_op jit(solution)/shard_map/ppermute | solution.py:670
  52.2 22.6 %collective-permute-start.13 = (bf16[2,16,8,512]{3,2,1,0:T(8,128)(2,1)}, bf16[2,16,8,512]{3,2,1,0:T(8,128)(2,1)S(1)}, u32[]{:S(2)}, u32[]{:S(2)}) collective-permute-start(bf16[2,16,8,512]{3,2,1,0:T(8,128)(2,1)} %get-tuple-element.55), channel_id=1, source_target_pairs={{0,13},{1,14},{2,15},{3,12},{4,5},{5,6},{6,7},{7,4},{8,9},{9,10},{... | collective-permute-start | bytes 786440 | tf_op jit(solution)/shard_map/ppermute | solution.py:670
  53.5 21.4 %collective-permute-start.14 = (bf16[2,16,8,512]{3,2,1,0:T(8,128)(2,1)}, bf16[2,16,8,512]{3,2,1,0:T(8,128)(2,1)S(1)}, u32[]{:S(2)}, u32[]{:S(2)}) collective-permute-start(bf16[2,16,8,512]{3,2,1,0:T(8,128)(2,1)} %get-tuple-element.56), channel_id=1, source_target_pairs={{0,14},{1,15},{2,12},{3,13},{4,6},{5,7},{6,4},{7,5},{8,10},{9,11},... | collective-permute-start | bytes 786440 | tf_op jit(solution)/shard_map/ppermute | solution.py:670
  57.8 18.8 %collective-permute-start.15 = (bf16[2,16,8,512]{3,2,1,0:T(8,128)(2,1)}, bf16[2,16,8,512]{3,2,1,0:T(8,128)(2,1)}, u32[]{:S(2)}, u32[]{:S(2)}) collective-permute-start(bf16[2,16,8,512]{3,2,1,0:T(8,128)(2,1)} %get-tuple-element.57), channel_id=1, source_target_pairs={{0,15},{1,12},{2,13},{3,14},{4,7},{5,4},{6,5},{7,6},{8,11},{9,8},{... | collective-permute-start | bytes 786440 | tf_op jit(solution)/shard_map/ppermute | solution.py:670
  61.3 1.0 copy-start.2
  68.1 30.8 %collective-permute-start.16 = (bf16[8,4,64,128]{3,2,1,0:T(8,128)(2,1)}, bf16[8,4,64,128]{3,2,1,0:T(8,128)(2,1)S(1)}, u32[]{:S(2)}, u32[]{:S(2)}) collective-permute-start(bf16[8,4,64,128]{3,2,1,0:T(8,128)(2,1)} %get-tuple-element.62), channel_id=1, source_target_pairs={{4,8},{5,9},{6,10},{7,11},{8,4},{9,5},{10,6},{11,7},{20,24},{21,25... | collective-permute-start | bytes 1572872 | tf_op jit(solution)/shard_map/ppermute | solution.py:707
  69.5 7.4 %collective-permute-start.17 = (f32[8,4,2,64]{3,2,1,0:T(2,128)}, f32[8,4,2,64]{3,2,1,0:T(2,128)}, u32[]{:S(2)}, u32[]{:S(2)}) collective-permute-start(f32[8,4,2,64]{3,2,1,0:T(2,128)} %get-tuple-element.63), channel_id=1, source_target_pairs={{4,8},{5,9},{6,10},{7,11},{8,4},{9,5},{10,6},{11,7},{20,24},{21,25... | collective-permute-start | bytes 49160 | tf_op jit(solution)/shard_map/ppermute | solution.py:708
  74.8 36.3 %collective-permute-start.1 = (bf16[2,16,8,512]{3,2,1,0:T(8,128)(2,1)}, bf16[2,16,8,512]{3,2,1,0:T(8,128)(2,1)S(1)}, u32[]{:S(2)}, u32[]{:S(2)}) collective-permute-start(bf16[2,16,8,512]{3,2,1,0:T(8,128)(2,1)} %get-tuple-element.42), channel_id=1, source_target_pairs={{0,4},{1,5},{2,6},{3,7},{4,0},{5,1},{6,2},{7,3},{8,12},{9,13},{10,... | collective-permute-start | bytes 786440 | tf_op jit(solution)/shard_map/ppermute | solution.py:670
  74.9 36.2 %collective-permute-start.2 = (bf16[2,16,8,512]{3,2,1,0:T(8,128)(2,1)}, bf16[2,16,8,512]{3,2,1,0:T(8,128)(2,1)S(1)}, u32[]{:S(2)}, u32[]{:S(2)}) collective-permute-start(bf16[2,16,8,512]{3,2,1,0:T(8,128)(2,1)} %get-tuple-element.43), channel_id=1, source_target_pairs={{0,5},{1,6},{2,7},{3,4},{4,1},{5,2},{6,3},{7,0},{8,13},{9,14},{10,... | collective-permute-start | bytes 786440 | tf_op jit(solution)/shard_map/ppermute | solution.py:670
  76.6 34.5 %collective-permute-start.3 = (bf16[2,16,8,512]{3,2,1,0:T(8,128)(2,1)}, bf16[2,16,8,512]{3,2,1,0:T(8,128)(2,1)S(1)}, u32[]{:S(2)}, u32[]{:S(2)}) collective-permute-start(bf16[2,16,8,512]{3,2,1,0:T(8,128)(2,1)} %get-tuple-element.44), channel_id=1, source_target_pairs={{0,6},{1,7},{2,4},{3,5},{4,2},{5,3},{6,0},{7,1},{8,14},{9,15},{10,... | collective-permute-start | bytes 786440 | tf_op jit(solution)/shard_map/ppermute | solution.py:670
  76.8 34.3 %collective-permute-start.4 = (bf16[2,16,8,512]{3,2,1,0:T(8,128)(2,1)}, bf16[2,16,8,512]{3,2,1,0:T(8,128)(2,1)S(1)}, u32[]{:S(2)}, u32[]{:S(2)}) collective-permute-start(bf16[2,16,8,512]{3,2,1,0:T(8,128)(2,1)} %get-tuple-element.45), channel_id=1, source_target_pairs={{0,7},{1,4},{2,5},{3,6},{4,3},{5,0},{6,1},{7,2},{8,15},{9,12},{10,... | collective-permute-start | bytes 786440 | tf_op jit(solution)/shard_map/ppermute | solution.py:670
  87.5 2.2 %copy-start = (bf16[8,512,512]{2,1,0:T(8,128)(2,1)S(1)}, bf16[8,512,512]{2,1,0:T(8,128)(2,1)}, u32[]{:S(2)}) copy-start(bf16[8,512,512]{2,1,0:T(8,128)(2,1)} %keys.1) | copy-start | bytes 12582916
  89.7 2.2 %copy-start.1 = (bf16[8,512,512]{2,1,0:T(8,128)(2,1)S(1)}, bf16[8,512,512]{2,1,0:T(8,128)(2,1)}, u32[]{:S(2)}) copy-start(bf16[8,512,512]{2,1,0:T(8,128)(2,1)} %values.1) | copy-start | bytes 12582916
  91.9 0.8 copy-start.4
  92.6 0.8 copy-start.5
  93.4 5.5 %copy-start.3 = (bf16[2,16,8,512]{3,2,1,0:T(8,128)(2,1)S(1)}, bf16[2,16,8,512]{3,2,1,0:T(8,128)(2,1)}, u32[]{:S(2)}) copy-start(bf16[2,16,8,512]{3,2,1,0:T(8,128)(2,1)} %get-tuple-element.50.refs_4_) | copy-start | bytes 786436
  93.4 5.5 %copy-start.9 = (s32[12]{0:T(128)S(1)}, s32[12]{0:T(128)}, u32[]{:S(2)}) copy-start(s32[12]{0:T(128)} %get-tuple-element.75.stage) | copy-start | bytes 148
  93.4 5.5 %copy-start.10 = (s32[12]{0:T(128)S(1)}, s32[12]{0:T(128)}, u32[]{:S(2)}) copy-start(s32[12]{0:T(128)} %get-tuple-element.76.entry) | copy-start | bytes 148
  98.9 12.2 %copy-start.8 = (s32[4]{0:T(128)S(1)}, s32[4]{0:T(128)}, u32[]{:S(2)}) copy-start(s32[4]{0:T(128)} %get-tuple-element.78.entry) | copy-start | bytes 52
  (3 other events, 2.0 us)

commit v4 on v3

--- a/solution.py
+++ b/solution.py
@@ -99,39 +99,49 @@
     )(phase_table, target, keys, values)
 
 
-def note_kernel(n, cap, target, rows, lens, notes, fill):
+def note_kernel(n, target, rows, lens, notes, fill):
     in_plane = n // PLANES
 
     def clear(i, _):
         fill[i] = 0
-        for k in range(cap):
-            notes[i, k] = -1
-            notes[i, LANES + k] = -1
         for k in range(lens.shape[0]):
             notes[i, 2 * LANES + k] = lens[k]
         return 0
 
     lax.fori_loop(0, n, clear, 0)
 
-    def put(b, _):
-        dest = target[b]
-        slot = fill[dest]
-        fill[dest] = slot + 1
-        row = rows[b]
-        dest_plane = dest // in_plane
-        inner = (dest_plane > 0) & (dest_plane < PLANES - 1)
-        twin = jnp.where(inner, (PLANES - 1 - 2 * dest_plane) * in_plane + dest, dest)
-        notes[dest, slot] = row
-        notes[twin, LANES + slot] = row
+    def twin_of(dest):
+        plane = dest // in_plane
+        inner = (plane > 0) & (plane < PLANES - 1)
+        return jnp.where(inner, (PLANES - 1 - 2 * plane) * in_plane + dest, dest)
+
+    def put(step, _):
+        ready = []
+        for u in range(PACKED):
+            b = step * PACKED + u
+            dest = target[b]
+            slot = fill[dest]
+            fill[dest] = slot + 1
+            ready.append((dest, twin_of(dest), slot, rows[b]))
+        for dest, twin, slot, row in ready:
+            notes[dest, slot] = row
+            notes[twin, LANES + slot] = row
         return 0
 
-    lax.fori_loop(0, rows.shape[0], put, 0, unroll=4)
-
-
-def note(n, cap, target, rows, lens):
+    lax.fori_loop(0, rows.shape[0] // PACKED, put, 0)
+
+    def close(i, _):
+        notes[i, LANES - 1] = fill[i]
+        notes[twin_of(i), 2 * LANES - 1] = fill[i]
+        return 0
+
+    lax.fori_loop(0, n, close, 0)
+
+
+def note(n, target, rows, lens):
     smem = pl.BlockSpec(memory_space=pltpu.SMEM)
     return pl.pallas_call(
-        functools.partial(note_kernel, n, cap),
+        functools.partial(note_kernel, n),
         out_shape=jax.ShapeDtypeStruct((n, 3 * LANES), jnp.int32),
         in_specs=[smem] * 3,
         out_specs=smem,
@@ -159,7 +169,9 @@
     kernel, lane = iotas((8, LANES))
     counts = jnp.zeros((8, LANES), f32)
     for side in range(2):
-        rows_here = notes[:, side * LANES : side * LANES + cap]
+        there = notes[:, side * LANES : (side + 1) * LANES]
+        valid = lax.broadcasted_iota(jnp.int32, (n, cap), 1) < there[:, LANES - 1 :]
+        rows_here = jnp.where(valid, there[:, :cap], -1)
         rank = jnp.zeros((n, cap), f32)
         local = jnp.zeros((n, cap), f32)
         for r in range(rows):
@@ -177,7 +189,6 @@
                     )
                     counts += jnp.where((kernel == stage) & (lane == r), number, 0.0)
         span = slice(side * n, side * n + n)
-        valid = rows_here >= 0
         place[span, :] = jnp.where(valid, local, -1.0).astype(jnp.int32)
         row_of[span, :] = jnp.maximum(rows_here, 0)
         rank_of[span, :] = rank.astype(jnp.int32)
@@ -342,7 +353,7 @@
     rows, slot_count, feature = keys.shape
     pieces = slot_count // min(CHUNK, slot_count)
     vmem = pl.BlockSpec(memory_space=pltpu.VMEM)
-    hbm = pl.BlockSpec(memory_space=pl.ANY)
+    hbm = pl.BlockSpec(memory_space=pltpu.HBM)
     return pl.pallas_call(
         resident_kernel,
         out_shape=state_shapes(rows, grouped.shape[2]),
@@ -677,10 +688,9 @@
         value = value.reshape(rows, steps, KVH, group, HD).transpose(0, 2, 1, 3, 4)
         return value.reshape(rows, KVH, steps * group, HD)
 
-    queries, mirrored = lax.optimization_barrier((queries, mirrored))
-    grouped, mirrored = regroup(queries), regroup(mirrored)
-
-    notes = note(n, cap, block_device[:, 0], block_row, cache_len)
+    mirrored = regroup(mirrored)
+
+    notes = note(n, block_device[:, 0], block_row, cache_len)
     notes = lax.all_to_all(notes, "seq", split_axis=0, concat_axis=0, tiled=True)
     mine = lax.dynamic_index_in_dim(jnp.array(device_tables(n)), me, 0, keepdims=False)
     *slots, tally = index(n, cap, rows, notes, mine[2:])
@@ -699,11 +709,13 @@
         picked = mine[:2, first : first + len(phases) * in_plane]
         return (picked[0], picked[1], *slots, tally)
 
-    state = resident(cache_len, grouped, step_keys, step_values, cache_keys, cache_values)
     partial, stats = span(
         "partial", 0, cap, scalars("df"), mirrored,
         mirror_tables + rank_tables, got["d"] + got["f"], (), (), steps,
     )
+    queries, partial = lax.optimization_barrier((queries, partial))
+    grouped = regroup(queries)
+    state = resident(cache_len, grouped, step_keys, step_values, cache_keys, cache_values)
     partial = lax.ppermute(partial, "seq", swap)
     stats = lax.ppermute(stats, "seq", swap)
     state = span(

time: 119 us -> 119 us (level)
  transfers between devices with their start and end apart: 19 -> 19, of which waited for: 6 -> 6; matrix products, arithmetic and copies ran while one was open for 9% -> 8% of each run, Pallas kernels for 24% -> 24%
where the time goes in v4:
time: 119 us; the launch traced here: 118 us
  Pallas kernels  39.7 us (33%)
  starting transfers between devices  38.8 us (33%)
  waiting for transfers between devices  17.4 us (15%)
  local copies, waits for them, and re-layouts  17.2 us (14%)
  other arithmetic  3.11 us (3%)
  between operations  2.19 us (2%)
    ppermute x15, starting transfers between devices, send(): value = lax.ppermute(value, 'seq', pairs)  29.8 us
    pallas_call x3, Pallas kernels, span(): pl.pallas_call(functools.partial(span_kernel, kind, kernel, count, cap),...  25 us
    ppermute x15, waiting for transfers between devices, send(): value = lax.ppermute(value, 'seq', pairs)  17.4 us
    unnamed x33, local copies, waits for them, and re-layouts  9.63 us
    all_to_all x1, starting transfers between devices, body(): lax.all_to_all(notes, 'seq', split_axis=0, concat_axis=0, tiled=True)  6.35 us
    pallas_call x1, Pallas kernels, resident(): pl.pallas_call(resident_kernel, out_shape=state_shapes(rows, grouped.shap...  5.46 us
    reshape x4, local copies, waits for them, and re-layouts, regroup(): value = value.reshape(rows, steps, KVH, group, HD).transpose(0, 2, 1, 3, 4)  5.1 us
    pallas_call x1, Pallas kernels, pack(): pl.pallas_call(functools.partial(pack_kernel, n), out_shape=(message,) *...  4.53 us
  transfers between devices with their start and end apart: 19, of which 6 were waited for; matrix products, arithmetic and copies ran while one was open for 8% of the time, Pallas kernels for 24%

profile of v4, /device:TPU:27, one launch (start us, length us, event | category | flops | bytes accessed | tf_op | source)
XLA Modules:
  0.0 118.4 jit_solution(10828040549817606830)
XLA Ops:
  2.0 4.3 %note.1 = s32[16,384]{1,0:T(8,128)S(1)} custom-call(s32[128]{0:T(128)S(1)} %bitcast.40, s32[128]{0:T(128)S(1)} %copy-done.12, s32[8]{0:T(128)S(1)} %copy-done.6), custom_call_target="tpu_custom_call" | custom-call | tf_op jit(solution)/shard_map/note/pallas_call | solution.py:143
  6.9 6.4 %all-to-all-start = ((s32[16,1,384]{2,1,0:T(1,128)}), s32[16,1,384]{2,1,0:T(1,128)S(1)}, u32[]{:S(2)}, u32[]{:S(2)}) async-start(s32[16,1,384]{2,1,0:T(1,128)} %copy.16), calls=%async_computation | async-start | bytes 49152 | tf_op jit(solution)/shard_map/all_to_all | solution.py:694
  13.9 4.5 %pack.1 = (bf16[2,16,8,512]{3,2,1,0:T(8,128)(2,1)}, bf16[2,16,8,512]{3,2,1,0:T(8,128)(2,1)}, bf16[2,16,8,512]{3,2,1,0:T(8,128)(2,1)}, bf16[2,16,8,512]{3,2,1,0:T...) custom-call(s32[4,4]{1,0:T(4,128)} %constant.52.clone.phase_table, ...), custom_call_target="tpu_custom_call" | custom-call | tf_op jit(solution)/shard_map/pack/pallas_call | solution.py:87
  18.4 1.8 %collective-permute-start.1 = (bf16[2,16,8,512]{3,2,1,0:T(8,128)(2,1)}, bf16[2,16,8,512]{3,2,1,0:T(8,128)(2,1)S(1)}, u32[]{:S(2)}, u32[]{:S(2)}) collective-permute-start(bf16[2,16,8,512]{3,2,1,0:T(8,128)(2,1)} %get-tuple-element.41), channel_id=1, source_target_pairs={{0,4},{1,5},{2,6},{3,7},{4,12},{5,13},{6,14},{7,15},{8,0},{9,1},{1... | collective-permute-start | bytes 786440 | tf_op jit(solution)/shard_map/ppermute | solution.py:681
  20.3 1.5 %collective-permute-start.2 = (bf16[2,16,8,512]{3,2,1,0:T(8,128)(2,1)}, bf16[2,16,8,512]{3,2,1,0:T(8,128)(2,1)S(1)}, u32[]{:S(2)}, u32[]{:S(2)}) collective-permute-start(bf16[2,16,8,512]{3,2,1,0:T(8,128)(2,1)} %get-tuple-element.42), channel_id=1, source_target_pairs={{0,5},{1,6},{2,7},{3,4},{4,13},{5,14},{6,15},{7,12},{8,1},{9,2},{1... | collective-permute-start | bytes 786440 | tf_op jit(solution)/shard_map/ppermute | solution.py:681
  21.8 2.6 %collective-permute-start.3 = (bf16[2,16,8,512]{3,2,1,0:T(8,128)(2,1)}, bf16[2,16,8,512]{3,2,1,0:T(8,128)(2,1)S(1)}, u32[]{:S(2)}, u32[]{:S(2)}) collective-permute-start(bf16[2,16,8,512]{3,2,1,0:T(8,128)(2,1)} %get-tuple-element.43), channel_id=1, source_target_pairs={{0,6},{1,7},{2,4},{3,5},{4,14},{5,15},{6,12},{7,13},{8,2},{9,3},{1... | collective-permute-start | bytes 786440 | tf_op jit(solution)/shard_map/ppermute | solution.py:681
  26.8 1.4 %fusion.3 = s32[]{:T(128)} fusion(s32[16]{0:T(128)} %constant.54.clone, s32[]{:T(128)S(6)} %axis_index.12), kind=kLoop, calls=%fused_computation.20 | loop fusion | flops 47 | bytes 72 | tf_op jit(solution)/shard_map/reduce_sum | solution.py:699
  30.1 4.0 %collective-permute-done.1.refs_0_ = bf16[2,16,8,512]{3,2,1,0:T(8,128)(2,1)S(1)} collective-permute-done((bf16[2,16,8,512]{3,2,1,0:T(8,128)(2,1)}, bf16[2,16,8,512]{3,2,1,0:T(8,128)(2,1)S(1)}, u32[]{:S(2)}, u32[]{:S(2)}) %collective-permute-start.1) | collective-permute-done | bytes 262176 | tf_op jit(solution)/shard_map/ppermute | solution.py:681
  34.0 3.2 %collective-permute-start.5 = (bf16[2,16,8,512]{3,2,1,0:T(8,128)(2,1)}, bf16[2,16,8,512]{3,2,1,0:T(8,128)(2,1)S(1)}, u32[]{:S(2)}, u32[]{:S(2)}) collective-permute-start(bf16[2,16,8,512]{3,2,1,0:T(8,128)(2,1)} %get-tuple-element.46), channel_id=1, source_target_pairs={{0,1},{1,2},{2,3},{3,0},{4,5},{5,6},{6,7},{7,4},{8,9},{9,10},{10,1... | collective-permute-start | bytes 786440 | tf_op jit(solution)/shard_map/ppermute | solution.py:681
  37.2 3.9 %collective-permute-done.2.refs_1_ = bf16[2,16,8,512]{3,2,1,0:T(8,128)(2,1)S(1)} collective-permute-done((bf16[2,16,8,512]{3,2,1,0:T(8,128)(2,1)}, bf16[2,16,8,512]{3,2,1,0:T(8,128)(2,1)S(1)}, u32[]{:S(2)}, u32[]{:S(2)}) %collective-permute-start.2) | collective-permute-done | bytes 262176 | tf_op jit(solution)/shard_map/ppermute | solution.py:681
  41.0 1.2 collective-permute-start.6
  42.2 0.8 copy-done.13
  43.8 1.6 %reshape.88 = bf16[8,4,4,16,128]{4,3,2,1,0:T(8,128)(2,1)S(1)} reshape(bf16[8,4,8192]{2,1,0:T(4,128)(2,1)} %copy-done.13) | data formatting | bytes 1048576 | tf_op jit(solution)/shard_map/reshape | solution.py:688
  46.2 3.1 %collective-permute-start.12 = (bf16[2,16,8,512]{3,2,1,0:T(8,128)(2,1)}, bf16[2,16,8,512]{3,2,1,0:T(8,128)(2,1)S(1)}, u32[]{:S(2)}, u32[]{:S(2)}) collective-permute-start(bf16[2,16,8,512]{3,2,1,0:T(8,128)(2,1)} %get-tuple-element.55), channel_id=1, source_target_pairs={{0,12},{1,13},{2,14},{3,15},{4,4},{5,5},{6,6},{7,7},{8,8},{9,9},{1... | collective-permute-start | bytes 786440 | tf_op jit(solution)/shard_map/ppermute | solution.py:681
  49.2 3.1 %collective-permute-done.4.refs_3_ = bf16[2,16,8,512]{3,2,1,0:T(8,128)(2,1)S(1)} collective-permute-done((bf16[2,16,8,512]{3,2,1,0:T(8,128)(2,1)}, bf16[2,16,8,512]{3,2,1,0:T(8,128)(2,1)S(1)}, u32[]{:S(2)}, u32[]{:S(2)}) %collective-permute-start.4) | collective-permute-done | bytes 262176 | tf_op jit(solution)/shard_map/ppermute | solution.py:681
  52.4 1.3 %collective-permute-start.13 = (bf16[2,16,8,512]{3,2,1,0:T(8,128)(2,1)}, bf16[2,16,8,512]{3,2,1,0:T(8,128)(2,1)S(1)}, u32[]{:S(2)}, u32[]{:S(2)}) collective-permute-start(bf16[2,16,8,512]{3,2,1,0:T(8,128)(2,1)} %get-tuple-element.56), channel_id=1, source_target_pairs={{0,13},{1,14},{2,15},{3,12},{4,5},{5,6},{6,7},{7,4},{8,9},{9,10},{... | collective-permute-start | bytes 786440 | tf_op jit(solution)/shard_map/ppermute | solution.py:681
  53.7 2.1 %collective-permute-start.14 = (bf16[2,16,8,512]{3,2,1,0:T(8,128)(2,1)}, bf16[2,16,8,512]{3,2,1,0:T(8,128)(2,1)S(1)}, u32[]{:S(2)}, u32[]{:S(2)}) collective-permute-start(bf16[2,16,8,512]{3,2,1,0:T(8,128)(2,1)} %get-tuple-element.57), channel_id=1, source_target_pairs={{0,14},{1,15},{2,12},{3,13},{4,6},{5,7},{6,4},{7,5},{8,10},{9,11},... | collective-permute-start | bytes 786440 | tf_op jit(solution)/shard_map/ppermute | solution.py:681
  55.8 2.2 %collective-permute-done.6.refs_6_ = bf16[2,16,8,512]{3,2,1,0:T(8,128)(2,1)S(1)} collective-permute-done((bf16[2,16,8,512]{3,2,1,0:T(8,128)(2,1)}, bf16[2,16,8,512]{3,2,1,0:T(8,128)(2,1)S(1)}, u32[]{:S(2)}, u32[]{:S(2)}) %collective-permute-start.6) | collective-permute-done | bytes 262176 | tf_op jit(solution)/shard_map/ppermute | solution.py:681
  58.0 3.5 %collective-permute-done.7.refs_7_ = bf16[2,16,8,512]{3,2,1,0:T(8,128)(2,1)S(1)} collective-permute-done((bf16[2,16,8,512]{3,2,1,0:T(8,128)(2,1)}, bf16[2,16,8,512]{3,2,1,0:T(8,128)(2,1)S(1)}, u32[]{:S(2)}, u32[]{:S(2)}) %collective-permute-start.7) | collective-permute-done | bytes 262176 | tf_op jit(solution)/shard_map/ppermute | solution.py:681
  61.5 0.9 copy-done.2
  62.5 5.9 %shard_map.127 = (bf16[8,4,64,128]{3,2,1,0:T(8,128)(2,1)}, f32[8,4,2,64]{3,2,1,0:T(2,128)}) custom-call(s32[8]{0:T(128)S(1)} %get-tuple-element.76.entry, s32[8]{0:T(128)S(1)} %get-tuple-element.75.stage, s32[32,16]{1,0:T(8,128)S(1)} %get-tuple-element.36.place_of, s32[32,16]{1,0:T(8,128)S(1)} %get-tuple-element.37.row_of, ...), custom_call_target="tpu_custom_call" | custom-call | flops 1000000000 | bytes 12582912 | tf_op jit(solution)/shard_map/pallas_call | solution.py:561
  69.6 1.3 %collective-permute-start.17 = (f32[8,4,2,64]{3,2,1,0:T(2,128)}, f32[8,4,2,64]{3,2,1,0:T(2,128)}, u32[]{:S(2)}, u32[]{:S(2)}) collective-permute-start(f32[8,4,2,64]{3,2,1,0:T(2,128)} %get-tuple-element.63), channel_id=1, source_target_pairs={{4,8},{5,9},{6,10},{7,11},{8,4},{9,5},{10,6},{11,7},{20,24},{21,25... | collective-permute-start | bytes 49160 | tf_op jit(solution)/shard_map/ppermute | solution.py:720
  71.5 2.4 %reshape.92 = bf16[8,4,4,16,128]{4,3,2,1,0:T(8,128)(2,1)} reshape(bf16[8,4,8192]{2,1,0:T(4,128)(2,1)} %param.20) | data formatting | bytes 1048576 | tf_op jit(solution)/shard_map/reshape | solution.py:688
  73.8 1.1 copy.18
  75.0 1.7 %collective-permute-start.9 = (bf16[2,16,8,512]{3,2,1,0:T(8,128)(2,1)}, bf16[2,16,8,512]{3,2,1,0:T(8,128)(2,1)S(1)}, u32[]{:S(2)}, u32[]{:S(2)}) collective-permute-start(bf16[2,16,8,512]{3,2,1,0:T(8,128)(2,1)} %get-tuple-element.52), channel_id=1, source_target_pairs={{0,5},{1,6},{2,7},{3,4},{4,1},{5,2},{6,3},{7,0},{8,13},{9,14},{10,... | collective-permute-start | bytes 786440 | tf_op jit(solution)/shard_map/ppermute | solution.py:681
  77.0 10.8 %collective-permute-start.11 = (bf16[2,16,8,512]{3,2,1,0:T(8,128)(2,1)}, bf16[2,16,8,512]{3,2,1,0:T(8,128)(2,1)S(1)}, u32[]{:S(2)}, u32[]{:S(2)}) collective-permute-start(bf16[2,16,8,512]{3,2,1,0:T(8,128)(2,1)} %get-tuple-element.54), channel_id=1, source_target_pairs={{0,7},{1,4},{2,5},{3,6},{4,3},{5,0},{6,1},{7,2},{8,15},{9,12},{10,... | collective-permute-start | bytes 786440 | tf_op jit(solution)/shard_map/ppermute | solution.py:681
  87.7 2.2 %copy-done = bf16[8,512,512]{2,1,0:T(8,128)(2,1)S(1)} copy-done((bf16[8,512,512]{2,1,0:T(8,128)(2,1)S(1)}, bf16[8,512,512]{2,1,0:T(8,128)(2,1)}, u32[]{:S(2)}) %copy-start) | copy-done | bytes 4194328
  89.9 2.2 %copy-done.1 = bf16[8,512,512]{2,1,0:T(8,128)(2,1)S(1)} copy-done((bf16[8,512,512]{2,1,0:T(8,128)(2,1)S(1)}, bf16[8,512,512]{2,1,0:T(8,128)(2,1)}, u32[]{:S(2)}) %copy-start.1) | copy-done | bytes 4194328
  92.1 0.8 copy-done.4
  93.6 5.5 %resident.1 = (f32[8,4,64,128]{3,2,1,0:T(8,128)S(1)}, f32[8,4,64,128]{3,2,1,0:T(8,128)S(1)}, f32[8,4,64,128]{3,2,1,0:T(8,128)S(1)}) custom-call(s32[8]{0:T(128)S(1)} %copy-done.7, bf16[8,4,64,128]{3,2,1,0:T(8,128)(2,1)S(1)} %bitcast.33, bf16[8,4,512]{2,1,0:T(4,128)(2,1)S(1)} %copy-done.4, bf16[8,4,512]{2,1,0:T(4,128)(2,1)S(1)} %copy-done.5, ...), custom_call_target="tpu_custom_call" | custom-call | flops 2000000000 | bytes 16777216 | tf_op jit(solution)/shard_map/resident/pallas_call | solution.py:357
  99.2 12.1 %shard_map.128 = (f32[8,4,64,128]{3,2,1,0:T(8,128)S(1)}, f32[8,4,64,128]{3,2,1,0:T(8,128)S(1)}, f32[8,4,64,128]{3,2,1,0:T(8,128)S(1)}) custom-call(s32[12]{0:T(128)S(1)} %copy-done.10, s32[12]{0:T(128)S(1)} %copy-done.9, s32[32,16]{1,0:T(8,128)S(1)} %get-tuple-element.36.place_of, s32[32,16]{1,0:T(8,128)S(1)} %get-tuple-element.37.row_of, ...), custom_call_target="tpu_custom_call" | custom-call | flops 1000000000 | bytes 12582912 | tf_op jit(solution)/shard_map/pallas_call | solution.py:561
  111.3 7.0 %shard_map.129 = bf16[8,4,8192]{2,1,0:T(4,128)(2,1)} custom-call(s32[4]{0:T(128)S(1)} %copy-done.8, s32[4]{0:T(128)S(1)} %get-tuple-element.77.stage, s32[32,16]{1,0:T(8,128)S(1)} %get-tuple-element.36.place_of, s32[32,16]{1,0:T(8,128)S(1)} %get-tuple-element.37.row_of, s32[32,16]{1,0:T(8,128)S(1)} %get-tuple-element.38.rank_of, ...), custom_call_target="tpu_custom_call" | custom-call | flops 1000000000 | bytes 12582912 | tf_op jit(solution)/shard_map/pallas_call | solution.py:561
  (66 shorter events, 10.1 us)
Async XLA Ops:
  6.9 23.2 %all-to-all-start = ((s32[16,1,384]{2,1,0:T(1,128)}), s32[16,1,384]{2,1,0:T(1,128)S(1)}, u32[]{:S(2)}, u32[]{:S(2)}) async-start(s32[16,1,384]{2,1,0:T(1,128)} %copy.16), calls=%async_computation | async-start | bytes 49152 | tf_op jit(solution)/shard_map/all_to_all | solution.py:694
  13.2 29.0 %collective-permute-start = (bf16[8,4,8192]{2,1,0:T(4,128)(2,1)}, bf16[8,4,8192]{2,1,0:T(4,128)(2,1)S(1)}, u32[]{:S(2)}, u32[]{:S(2)}) collective-permute-start(bf16[8,4,8192]{2,1,0:T(4,128)(2,1)} %param.20), channel_id=1, source_target_pairs={{4,8},{5,9},{6,10},{7,11},{8,4},{9,5},{10,6},{11,7},{20,24},{21,25... | collective-permute-start | bytes 1572872 | tf_op jit(solution)/shard_map/ppermute | solution.py:664
  18.4 15.6 %collective-permute-start.1 = (bf16[2,16,8,512]{3,2,1,0:T(8,128)(2,1)}, bf16[2,16,8,512]{3,2,1,0:T(8,128)(2,1)S(1)}, u32[]{:S(2)}, u32[]{:S(2)}) collective-permute-start(bf16[2,16,8,512]{3,2,1,0:T(8,128)(2,1)} %get-tuple-element.41), channel_id=1, source_target_pairs={{0,4},{1,5},{2,6},{3,7},{4,12},{5,13},{6,14},{7,15},{8,0},{9,1},{1... | collective-permute-start | bytes 786440 | tf_op jit(solution)/shard_map/ppermute | solution.py:681
  20.3 20.8 %collective-permute-start.2 = (bf16[2,16,8,512]{3,2,1,0:T(8,128)(2,1)}, bf16[2,16,8,512]{3,2,1,0:T(8,128)(2,1)S(1)}, u32[]{:S(2)}, u32[]{:S(2)}) collective-permute-start(bf16[2,16,8,512]{3,2,1,0:T(8,128)(2,1)} %get-tuple-element.42), channel_id=1, source_target_pairs={{0,5},{1,6},{2,7},{3,4},{4,13},{5,14},{6,15},{7,12},{8,1},{9,2},{1... | collective-permute-start | bytes 786440 | tf_op jit(solution)/shard_map/ppermute | solution.py:681
  21.8 24.3 %collective-permute-start.3 = (bf16[2,16,8,512]{3,2,1,0:T(8,128)(2,1)}, bf16[2,16,8,512]{3,2,1,0:T(8,128)(2,1)S(1)}, u32[]{:S(2)}, u32[]{:S(2)}) collective-permute-start(bf16[2,16,8,512]{3,2,1,0:T(8,128)(2,1)} %get-tuple-element.43), channel_id=1, source_target_pairs={{0,6},{1,7},{2,4},{3,5},{4,14},{5,15},{6,12},{7,13},{8,2},{9,3},{1... | collective-permute-start | bytes 786440 | tf_op jit(solution)/shard_map/ppermute | solution.py:681
  24.4 28.0 %collective-permute-start.4 = (bf16[2,16,8,512]{3,2,1,0:T(8,128)(2,1)}, bf16[2,16,8,512]{3,2,1,0:T(8,128)(2,1)S(1)}, u32[]{:S(2)}, u32[]{:S(2)}) collective-permute-start(bf16[2,16,8,512]{3,2,1,0:T(8,128)(2,1)} %get-tuple-element.44), channel_id=1, source_target_pairs={{0,7},{1,4},{2,5},{3,6},{4,15},{5,12},{6,13},{7,14},{8,3},{9,0},{1... | collective-permute-start | bytes 786440 | tf_op jit(solution)/shard_map/ppermute | solution.py:681
  26.2 16.8 %copy-start.14 = (s32[4,16]{1,0:T(4,128)}, s32[4,16]{1,0:T(4,128)S(1)}, u32[]{:S(2)}) copy-start(s32[4,16]{1,0:T(4,128)S(1)} %get-tuple-element.68) | copy-start | bytes 772
  26.2 61.5 %copy-start.7 = (s32[8]{0:T(128)S(1)}, s32[8]{0:T(128)}, u32[]{:S(2)}) copy-start(s32[8]{0:T(128)} %lens.3) | copy-start | bytes 100
  34.0 19.7 %collective-permute-start.5 = (bf16[2,16,8,512]{3,2,1,0:T(8,128)(2,1)}, bf16[2,16,8,512]{3,2,1,0:T(8,128)(2,1)S(1)}, u32[]{:S(2)}, u32[]{:S(2)}) collective-permute-start(bf16[2,16,8,512]{3,2,1,0:T(8,128)(2,1)} %get-tuple-element.46), channel_id=1, source_target_pairs={{0,1},{1,2},{2,3},{3,0},{4,5},{5,6},{6,7},{7,4},{8,9},{9,10},{10,1... | collective-permute-start | bytes 786440 | tf_op jit(solution)/shard_map/ppermute | solution.py:681
  41.0 17.0 %collective-permute-start.6 = (bf16[2,16,8,512]{3,2,1,0:T(8,128)(2,1)}, bf16[2,16,8,512]{3,2,1,0:T(8,128)(2,1)S(1)}, u32[]{:S(2)}, u32[]{:S(2)}) collective-permute-start(bf16[2,16,8,512]{3,2,1,0:T(8,128)(2,1)} %get-tuple-element.47), channel_id=1, source_target_pairs={{0,2},{1,3},{2,0},{3,1},{4,6},{5,7},{6,4},{7,5},{8,10},{9,11},{10,... | collective-permute-start | bytes 786440 | tf_op jit(solution)/shard_map/ppermute | solution.py:681
  42.2 0.8 copy-start.13
  43.0 18.5 %collective-permute-start.7 = (bf16[2,16,8,512]{3,2,1,0:T(8,128)(2,1)}, bf16[2,16,8,512]{3,2,1,0:T(8,128)(2,1)S(1)}, u32[]{:S(2)}, u32[]{:S(2)}) collective-permute-start(bf16[2,16,8,512]{3,2,1,0:T(8,128)(2,1)} %get-tuple-element.48), channel_id=1, source_target_pairs={{0,3},{1,0},{2,1},{3,2},{4,7},{5,4},{6,5},{7,6},{8,11},{9,8},{10,9... | collective-permute-start | bytes 786440 | tf_op jit(solution)/shard_map/ppermute | solution.py:681
  45.4 23.7 %copy-start.15 = (s32[4,16]{1,0:T(4,128)S(1)}, s32[4,16]{1,0:T(4,128)}, u32[]{:S(2)}) copy-start(s32[4,16]{1,0:T(4,128)} %copy-done.14) | copy-start | bytes 772
  46.2 23.5 %collective-permute-start.12 = (bf16[2,16,8,512]{3,2,1,0:T(8,128)(2,1)}, bf16[2,16,8,512]{3,2,1,0:T(8,128)(2,1)S(1)}, u32[]{:S(2)}, u32[]{:S(2)}) collective-permute-start(bf16[2,16,8,512]{3,2,1,0:T(8,128)(2,1)} %get-tuple-element.55), channel_id=1, source_target_pairs={{0,12},{1,13},{2,14},{3,15},{4,4},{5,5},{6,6},{7,7},{8,8},{9,9},{1... | collective-permute-start | bytes 786440 | tf_op jit(solution)/shard_map/ppermute | solution.py:681
  52.4 22.6 %collective-permute-start.13 = (bf16[2,16,8,512]{3,2,1,0:T(8,128)(2,1)}, bf16[2,16,8,512]{3,2,1,0:T(8,128)(2,1)S(1)}, u32[]{:S(2)}, u32[]{:S(2)}) collective-permute-start(bf16[2,16,8,512]{3,2,1,0:T(8,128)(2,1)} %get-tuple-element.56), channel_id=1, source_target_pairs={{0,13},{1,14},{2,15},{3,12},{4,5},{5,6},{6,7},{7,4},{8,9},{9,10},{... | collective-permute-start | bytes 786440 | tf_op jit(solution)/shard_map/ppermute | solution.py:681
  53.7 21.3 %collective-permute-start.14 = (bf16[2,16,8,512]{3,2,1,0:T(8,128)(2,1)}, bf16[2,16,8,512]{3,2,1,0:T(8,128)(2,1)S(1)}, u32[]{:S(2)}, u32[]{:S(2)}) collective-permute-start(bf16[2,16,8,512]{3,2,1,0:T(8,128)(2,1)} %get-tuple-element.57), channel_id=1, source_target_pairs={{0,14},{1,15},{2,12},{3,13},{4,6},{5,7},{6,4},{7,5},{8,10},{9,11},... | collective-permute-start | bytes 786440 | tf_op jit(solution)/shard_map/ppermute | solution.py:681
  58.0 18.7 %collective-permute-start.15 = (bf16[2,16,8,512]{3,2,1,0:T(8,128)(2,1)}, bf16[2,16,8,512]{3,2,1,0:T(8,128)(2,1)}, u32[]{:S(2)}, u32[]{:S(2)}) collective-permute-start(bf16[2,16,8,512]{3,2,1,0:T(8,128)(2,1)} %get-tuple-element.58), channel_id=1, source_target_pairs={{0,15},{1,12},{2,13},{3,14},{4,7},{5,4},{6,5},{7,6},{8,11},{9,8},{... | collective-permute-start | bytes 786440 | tf_op jit(solution)/shard_map/ppermute | solution.py:681
  61.5 1.0 copy-start.2
  68.4 30.8 %collective-permute-start.16 = (bf16[8,4,64,128]{3,2,1,0:T(8,128)(2,1)}, bf16[8,4,64,128]{3,2,1,0:T(8,128)(2,1)S(1)}, u32[]{:S(2)}, u32[]{:S(2)}) collective-permute-start(bf16[8,4,64,128]{3,2,1,0:T(8,128)(2,1)} %get-tuple-element.62), channel_id=1, source_target_pairs={{4,8},{5,9},{6,10},{7,11},{8,4},{9,5},{10,6},{11,7},{20,24},{21,25... | collective-permute-start | bytes 1572872 | tf_op jit(solution)/shard_map/ppermute | solution.py:719
  69.6 7.4 %collective-permute-start.17 = (f32[8,4,2,64]{3,2,1,0:T(2,128)}, f32[8,4,2,64]{3,2,1,0:T(2,128)}, u32[]{:S(2)}, u32[]{:S(2)}) collective-permute-start(f32[8,4,2,64]{3,2,1,0:T(2,128)} %get-tuple-element.63), channel_id=1, source_target_pairs={{4,8},{5,9},{6,10},{7,11},{8,4},{9,5},{10,6},{11,7},{20,24},{21,25... | collective-permute-start | bytes 49160 | tf_op jit(solution)/shard_map/ppermute | solution.py:720
  74.9 36.4 %collective-permute-start.8 = (bf16[2,16,8,512]{3,2,1,0:T(8,128)(2,1)}, bf16[2,16,8,512]{3,2,1,0:T(8,128)(2,1)S(1)}, u32[]{:S(2)}, u32[]{:S(2)}) collective-permute-start(bf16[2,16,8,512]{3,2,1,0:T(8,128)(2,1)} %get-tuple-element.51), channel_id=1, source_target_pairs={{0,4},{1,5},{2,6},{3,7},{4,0},{5,1},{6,2},{7,3},{8,12},{9,13},{10,... | collective-permute-start | bytes 786440 | tf_op jit(solution)/shard_map/ppermute | solution.py:681
  75.0 36.3 %collective-permute-start.9 = (bf16[2,16,8,512]{3,2,1,0:T(8,128)(2,1)}, bf16[2,16,8,512]{3,2,1,0:T(8,128)(2,1)S(1)}, u32[]{:S(2)}, u32[]{:S(2)}) collective-permute-start(bf16[2,16,8,512]{3,2,1,0:T(8,128)(2,1)} %get-tuple-element.52), channel_id=1, source_target_pairs={{0,5},{1,6},{2,7},{3,4},{4,1},{5,2},{6,3},{7,0},{8,13},{9,14},{10,... | collective-permute-start | bytes 786440 | tf_op jit(solution)/shard_map/ppermute | solution.py:681
  76.8 34.6 %collective-permute-start.10 = (bf16[2,16,8,512]{3,2,1,0:T(8,128)(2,1)}, bf16[2,16,8,512]{3,2,1,0:T(8,128)(2,1)S(1)}, u32[]{:S(2)}, u32[]{:S(2)}) collective-permute-start(bf16[2,16,8,512]{3,2,1,0:T(8,128)(2,1)} %get-tuple-element.53), channel_id=1, source_target_pairs={{0,6},{1,7},{2,4},{3,5},{4,2},{5,3},{6,0},{7,1},{8,14},{9,15},{10,... | collective-permute-start | bytes 786440 | tf_op jit(solution)/shard_map/ppermute | solution.py:681
  77.0 34.4 %collective-permute-start.11 = (bf16[2,16,8,512]{3,2,1,0:T(8,128)(2,1)}, bf16[2,16,8,512]{3,2,1,0:T(8,128)(2,1)S(1)}, u32[]{:S(2)}, u32[]{:S(2)}) collective-permute-start(bf16[2,16,8,512]{3,2,1,0:T(8,128)(2,1)} %get-tuple-element.54), channel_id=1, source_target_pairs={{0,7},{1,4},{2,5},{3,6},{4,3},{5,0},{6,1},{7,2},{8,15},{9,12},{10,... | collective-permute-start | bytes 786440 | tf_op jit(solution)/shard_map/ppermute | solution.py:681
  87.7 2.2 %copy-start = (bf16[8,512,512]{2,1,0:T(8,128)(2,1)S(1)}, bf16[8,512,512]{2,1,0:T(8,128)(2,1)}, u32[]{:S(2)}) copy-start(bf16[8,512,512]{2,1,0:T(8,128)(2,1)} %keys.1) | copy-start | bytes 12582916
  89.9 2.2 %copy-start.1 = (bf16[8,512,512]{2,1,0:T(8,128)(2,1)S(1)}, bf16[8,512,512]{2,1,0:T(8,128)(2,1)}, u32[]{:S(2)}) copy-start(bf16[8,512,512]{2,1,0:T(8,128)(2,1)} %values.1) | copy-start | bytes 12582916
  92.1 0.8 copy-start.4
  92.9 0.8 copy-start.5
  93.6 5.5 %copy-start.3 = (bf16[2,16,8,512]{3,2,1,0:T(8,128)(2,1)S(1)}, bf16[2,16,8,512]{3,2,1,0:T(8,128)(2,1)}, u32[]{:S(2)}) copy-start(bf16[2,16,8,512]{3,2,1,0:T(8,128)(2,1)} %get-tuple-element.45.refs_4_) | copy-start | bytes 786436
  93.6 5.5 %copy-start.9 = (s32[12]{0:T(128)S(1)}, s32[12]{0:T(128)}, u32[]{:S(2)}) copy-start(s32[12]{0:T(128)} %get-tuple-element.73.stage) | copy-start | bytes 148
  93.6 5.5 %copy-start.10 = (s32[12]{0:T(128)S(1)}, s32[12]{0:T(128)}, u32[]{:S(2)}) copy-start(s32[12]{0:T(128)} %get-tuple-element.74.entry) | copy-start | bytes 148
  99.1 12.2 %copy-start.8 = (s32[4]{0:T(128)S(1)}, s32[4]{0:T(128)}, u32[]{:S(2)}) copy-start(s32[4]{0:T(128)} %get-tuple-element.78.entry) | copy-start | bytes 52
  (3 other events, 2.0 us)

commit v5 on v4

--- a/solution.py
+++ b/solution.py
@@ -18,26 +18,27 @@
 SPAN = 128
 LANES = 128
 GRANT = 20 * 2**20
+WIDE = 52 * 2**20
 UNROLL = 4
 PACKED = 4
 NEG = -1e30
 
 
 def frequencies(half_width):
-    freq_index = jnp.arange(half_width, dtype=jnp.float32)
-    base_freq = 1.0 / 500000.0 ** (freq_index / half_width)
-    wavelen = 2.0 * jnp.pi / base_freq
+    index = np.arange(half_width, dtype=np.float64)
+    base = 1.0 / 500000.0 ** (index / half_width)
+    wavelen = 2.0 * np.pi / base
     smooth = (8192.0 / wavelen - 1.0) / 3.0
-    blended = (1.0 - smooth) * base_freq / 8.0 + smooth * base_freq
-    scaled = jnp.where(wavelen > 8192.0, base_freq / 8.0, blended)
-    return jnp.where(wavelen < 2048.0, base_freq, scaled)
+    blended = (1.0 - smooth) * base / 8.0 + smooth * base
+    scaled = np.where(wavelen > 8192.0, base / 8.0, blended)
+    return np.where(wavelen < 2048.0, base, scaled)
 
 
 def turn_tables(positions):
     freq = frequencies(HD // 2)
-    angles = positions.astype(jnp.float32)[..., None] * jnp.concatenate([freq, freq])
-    sign = jnp.where(jnp.arange(HD) < HD // 2, -1.0, 1.0).astype(jnp.float32)
-    return jnp.cos(angles), jnp.sin(angles) * sign
+    angles = np.asarray(positions, np.float64)[:, None] * np.concatenate([freq, freq])[None]
+    sign = np.where(np.arange(HD) < HD // 2, -1.0, 1.0)
+    return jnp.array(np.cos(angles), jnp.float32), jnp.array(np.sin(angles) * sign, jnp.float32)
 
 
 def pack_kernel(n, phase_table, target, keys, values, *refs):
@@ -99,21 +100,24 @@
     )(phase_table, target, keys, values)
 
 
+def twin_index(in_plane, index):
+    plane = index // in_plane
+    inner = (plane > 0) & (plane < PLANES - 1)
+    return jnp.where(inner, (PLANES - 1 - 2 * plane) * in_plane + index, index)
+
+
 def note_kernel(n, target, rows, lens, notes, fill):
     in_plane = n // PLANES
 
     def clear(i, _):
         fill[i] = 0
-        for k in range(lens.shape[0]):
-            notes[i, 2 * LANES + k] = lens[k]
         return 0
 
-    lax.fori_loop(0, n, clear, 0)
-
-    def twin_of(dest):
-        plane = dest // in_plane
-        inner = (plane > 0) & (plane < PLANES - 1)
-        return jnp.where(inner, (PLANES - 1 - 2 * plane) * in_plane + dest, dest)
+    lax.fori_loop(0, n, clear, 0, unroll=min(n, 16))
+    twin_of = functools.partial(twin_index, in_plane)
+    my_twin = twin_of(lax.axis_index("seq"))
+    for k in range(lens.shape[0]):
+        notes[my_twin, 2 * LANES + k] = lens[k]
 
     def put(step, _):
         ready = []
@@ -135,7 +139,7 @@
         notes[twin_of(i), 2 * LANES - 1] = fill[i]
         return 0
 
-    lax.fori_loop(0, n, close, 0)
+    lax.fori_loop(0, n, close, 0, unroll=min(n, 4))
 
 
 def note(n, target, rows, lens):
@@ -146,7 +150,6 @@
         in_specs=[smem] * 3,
         out_specs=smem,
         scratch_shapes=[pltpu.SMEM((n,), jnp.int32)],
-        compiler_params=pltpu.CompilerParams(vmem_limit_bytes=GRANT),
         name="note",
     )(target, rows, lens)
 
@@ -161,7 +164,7 @@
     before = (a < b).astype(f32)
     a, b = iotas((n, n))
     sooner = (b < a).astype(f32)
-    lines = [jnp.broadcast_to(stages[i : i + 1, :n], (n, n)) for i in range(2)]
+    lines = [jnp.broadcast_to(stages[i : i + 1, :n], (n, n)) for i in (2, 3)]
     posts = [
         jnp.sum(jnp.where(a == b, line, 0), axis=1, keepdims=True) for line in lines
     ]
@@ -196,7 +199,12 @@
         used[span, :] = jnp.broadcast_to(filled, (n, cap)).astype(jnp.int32)
     a, b = iotas((LANES, LANES))
     begin = jnp.dot(counts, (a < b).astype(f32), preferred_element_type=f32)
-    tally[0:8, :] = begin.astype(jnp.int32)
+    twin = twin_index(n // PLANES, lax.axis_index("seq"))
+    source = lax.broadcasted_iota(jnp.int32, (n, LANES), 0)
+    lens = jnp.sum(
+        jnp.where(source == twin, notes[:, 2 * LANES :], 0), axis=0, keepdims=True
+    )
+    tally[0:8, :] = jnp.where(kernel == 3, lens, begin.astype(jnp.int32))
     tally[8:16, :] = (counts * BLK).astype(jnp.int32)
 
 
@@ -364,7 +372,7 @@
             pltpu.VMEM((rows, slot_count, feature), jnp.bfloat16),
             pltpu.SemaphoreType.DMA((2, rows, pieces)),
         ],
-        compiler_params=pltpu.CompilerParams(vmem_limit_bytes=GRANT),
+        compiler_params=pltpu.CompilerParams(vmem_limit_bytes=WIDE),
         cost_estimate=pl.CostEstimate(
             flops=2 * 10**9, bytes_accessed=16 * 2**20, transcendentals=10**6
         ),
@@ -373,7 +381,7 @@
 
 
 def span_kernel(
-    kind, kernel, count, cap, entry, stage, place_of, row_of, rank_of, used, tally,
+    kind, kernel, first, count, cap, mine, place_of, row_of, rank_of, used, tally, lens,
     q_ref, ca, sa, cb, sb, *refs,
 ):
     messages = refs[:count]
@@ -396,9 +404,9 @@
     trash = count * cap + SPAN // BLK
     for j in range(count):
 
-        @pl.when(stage[j] == kernel)
+        @pl.when(mine[1, first + j] == kernel)
         def _():
-            source = entry[j]
+            source = mine[0, first + j]
             message = messages[j]
 
             def place(step, _):
@@ -409,8 +417,10 @@
                     rank = rank_of[source, k]
                     local = place_of[source, k]
                     slot = jnp.where(local < 0, trash, tally[kernel, r] + local)
-                    c_a, s_a = ca[r], sa[r]
-                    c_b, s_b = cb[pl.ds(rank, 1), :], sb[pl.ds(rank, 1), :]
+                    length = tally[3, r] if kind == "partial" else lens[r]
+                    fine, coarse = pl.ds(length % BLK, BLK), pl.ds(length // BLK + rank, 1)
+                    c_a, s_a = ca[fine, :], sa[fine, :]
+                    c_b, s_b = cb[coarse, :], sb[coarse, :]
                     cosine = c_a * c_b - s_a * s_b
                     sine = s_a * c_b + c_a * s_b
                     where = pl.ds(pl.multiple_of(slot * BLK, BLK), BLK)
@@ -537,7 +547,7 @@
     lax.fori_loop(0, rows // together, some_rows, 0)
 
 
-def span(kind, kernel, cap, scalars, grouped, tables, messages, state, extra, steps):
+def span(kind, kernel, first, cap, scalars, grouped, tables, messages, state, extra, steps):
     rows, _, width, _ = grouped.shape
     feature = messages[0].shape[-1]
     count = len(messages)
@@ -559,7 +569,7 @@
         scratch += running + [pltpu.VMEM((2 * KVH, width, HD), jnp.float32)]
     scratch += [pltpu.VMEM((room, feature), jnp.float32)] * 2
     return pl.pallas_call(
-        functools.partial(span_kernel, kind, kernel, count, cap),
+        functools.partial(span_kernel, kind, kernel, first, count, cap),
         out_shape=out_shape,
         in_specs=[smem] * 7 + [vmem] * (5 + count + len(state) + len(extra)),
         out_specs=jax.tree.map(lambda _: vmem, out_shape),
@@ -693,25 +703,14 @@
     notes = note(n, block_device[:, 0], block_row, cache_len)
     notes = lax.all_to_all(notes, "seq", split_axis=0, concat_axis=0, tiled=True)
     mine = lax.dynamic_index_in_dim(jnp.array(device_tables(n)), me, 0, keepdims=False)
-    *slots, tally = index(n, cap, rows, notes, mine[2:])
-    twin = [m if m // in_plane in (0, PLANES - 1) else (PLANES - 1 - m // in_plane) * in_plane
-            + m % in_plane for m in range(n)]
-    twin = jnp.sum(jnp.where(jnp.arange(n) == me, jnp.array(twin, jnp.int32), 0))
-    mirror_len = lax.dynamic_index_in_dim(notes, twin, 0, keepdims=False)
-    mirror_len = mirror_len[2 * LANES : 2 * LANES + rows]
-
-    own_tables = turn_tables(cache_len[:, None] + jnp.arange(BLK, dtype=jnp.int32)[None])
-    mirror_tables = turn_tables(mirror_len[:, None] + jnp.arange(BLK, dtype=jnp.int32)[None])
-    rank_tables = turn_tables(jnp.arange(n * cap, dtype=jnp.int32) * BLK)
-
-    def scalars(phases):
-        first = names.index(phases[0]) * in_plane
-        picked = mine[:2, first : first + len(phases) * in_plane]
-        return (picked[0], picked[1], *slots, tally)
+    *slots, tally = index(n, cap, rows, notes, mine)
+    reach = cache_keys.shape[1] // BLK + n * cap + 1
+    tables = turn_tables(np.arange(2 * BLK)) + turn_tables(np.arange(reach) * BLK)
+    scalars = (mine, *slots, tally, cache_len)
 
     partial, stats = span(
-        "partial", 0, cap, scalars("df"), mirrored,
-        mirror_tables + rank_tables, got["d"] + got["f"], (), (), steps,
+        "partial", 0, 0, cap, scalars, mirrored, tables,
+        got["d"] + got["f"], (), (), steps,
     )
     queries, partial = lax.optimization_barrier((queries, partial))
     grouped = regroup(queries)
@@ -719,13 +718,12 @@
     partial = lax.ppermute(partial, "seq", swap)
     stats = lax.ppermute(stats, "seq", swap)
     state = span(
-        "state", 1, cap, scalars("dfg"), grouped,
-        own_tables + rank_tables, got["d"] + got["f"] + got["g"], tuple(state),
-        (partial, stats), steps,
+        "state", 1, 0, cap, scalars, grouped, tables,
+        got["d"] + got["f"] + got["g"], tuple(state), (partial, stats), steps,
     )
     return span(
-        "final", 2, cap, scalars("b"), grouped,
-        own_tables + rank_tables, got["b"], tuple(state), (), steps,
+        "final", 2, 3 * in_plane, cap, scalars, grouped, tables,
+        got["b"], tuple(state), (), steps,
     )
 
 

time: 119 us -> 128 us (1.076)
  waiting for transfers between devices: 17.4 us -> 33.3 us
  local copies, waits for them, and re-layouts: 17.2 us -> 12.8 us
  other arithmetic: 3.11 us -> 0 us
  between operations: 2.19 us -> 0.3 us
  Pallas kernels: 39.7 us -> 41.3 us
    ppermute x15, waiting for transfers between devices: 17.4 us -> 28.9 us  [send(): value = lax.ppermute(value, 'seq', pairs)]
    all_to_all x1, waiting for transfers between devices: 0.01 us -> 4.4 us  [body(): lax.all_to_all(notes, 'seq', split_axis=0, concat_axis=0, tiled=True)]
    unnamed x33 -> x35, local copies, waits for them, and re-layouts: 9.63 us -> 5.6 us
    pallas_call x1, Pallas kernels: 5.46 us -> 7.36 us  [resident(): pl.pallas_call(resident_kernel, out_shape=state_shapes(rows, grouped.shap...]
    reduce_sum x1 -> x0, other arithmetic: 1.36 us -> none  [body(): jnp.sum(jnp.where(jnp.arange(n) == me, jnp.array(twin, jnp.int32), 0))]
  transfers between devices with their start and end apart: 19 -> 19, of which waited for: 6 -> 7; matrix products, arithmetic and copies ran while one was open for 8% -> 6% of each run, Pallas kernels for 24% -> 22%
where the time goes in v5:
time: 128 us; the launch traced here: 127 us
  Pallas kernels  41.3 us (32%)
  starting transfers between devices  39.4 us (31%)
  waiting for transfers between devices  33.3 us (26%)
  local copies, waits for them, and re-layouts  12.8 us (10%)
    ppermute x15, starting transfers between devices, send(): value = lax.ppermute(value, 'seq', pairs)  29.5 us
    ppermute x15, waiting for transfers between devices, send(): value = lax.ppermute(value, 'seq', pairs)  28.9 us
    pallas_call x3, Pallas kernels, span(): pl.pallas_call(functools.partial(span_kernel, kind, kernel, first, count,...  25.1 us
    pallas_call x1, Pallas kernels, resident(): pl.pallas_call(resident_kernel, out_shape=state_shapes(rows, grouped.shap...  7.36 us
    all_to_all x1, starting transfers between devices, body(): lax.all_to_all(notes, 'seq', split_axis=0, concat_axis=0, tiled=True)  6.3 us
    unnamed x35, local copies, waits for them, and re-layouts  5.6 us
    reshape x4, local copies, waits for them, and re-layouts, regroup(): value = value.reshape(rows, steps, KVH, group, HD).transpose(0, 2, 1, 3, 4)  5.1 us
    pallas_call x1, Pallas kernels, pack(): pl.pallas_call(functools.partial(pack_kernel, n), out_shape=(message,) *...  4.48 us
  transfers between devices with their start and end apart: 19, of which 7 were waited for; matrix products, arithmetic and copies ran while one was open for 6% of the time, Pallas kernels for 22%

profile of v5, /device:TPU:27, one launch (start us, length us, event | category | flops | bytes accessed | tf_op | source)
XLA Modules:
  0.0 127.0 jit_solution(6101780529987464933)
XLA Ops:
  0.0 1.6 %collective-permute-start = (bf16[8,4,8192]{2,1,0:T(4,128)(2,1)}, bf16[8,4,8192]{2,1,0:T(4,128)(2,1)}, u32[]{:S(2)}, u32[]{:S(2)}) collective-permute-start(bf16[8,4,8192]{2,1,0:T(4,128)(2,1)} %param.23), channel_id=1, source_target_pairs={{4,8},{5,9},{6,10},{7,11},{8,4},{9,5},{10,6},{11,7},{20,24},{21,25... | collective-permute-start | bytes 1572872 | tf_op jit(solution)/shard_map/ppermute | solution.py:674
  1.6 4.5 %pack.1 = (bf16[2,16,8,512]{3,2,1,0:T(8,128)(2,1)}, bf16[2,16,8,512]{3,2,1,0:T(8,128)(2,1)}, bf16[2,16,8,512]{3,2,1,0:T(8,128)(2,1)}, bf16[2,16,8,512]{3,2,1,0:T...) custom-call(s32[4,4]{1,0:T(4,128)} %constant.22.clone.phase_table, ...), custom_call_target="tpu_custom_call" | custom-call | tf_op jit(solution)/shard_map/pack/pallas_call | solution.py:88
  7.0 1.9 %collective-permute-start.2 = (bf16[2,16,8,512]{3,2,1,0:T(8,128)(2,1)}, bf16[2,16,8,512]{3,2,1,0:T(8,128)(2,1)S(1)}, u32[]{:S(2)}, u32[]{:S(2)}) collective-permute-start(bf16[2,16,8,512]{3,2,1,0:T(8,128)(2,1)} %get-tuple-element.42), channel_id=1, source_target_pairs={{0,5},{1,6},{2,7},{3,4},{4,13},{5,14},{6,15},{7,12},{8,1},{9,2},{1... | collective-permute-start | bytes 786440 | tf_op jit(solution)/shard_map/ppermute | solution.py:691
  8.8 2.6 %collective-permute-start.3 = (bf16[2,16,8,512]{3,2,1,0:T(8,128)(2,1)}, bf16[2,16,8,512]{3,2,1,0:T(8,128)(2,1)S(1)}, u32[]{:S(2)}, u32[]{:S(2)}) collective-permute-start(bf16[2,16,8,512]{3,2,1,0:T(8,128)(2,1)} %get-tuple-element.43), channel_id=1, source_target_pairs={{0,6},{1,7},{2,4},{3,5},{4,14},{5,15},{6,12},{7,13},{8,2},{9,3},{1... | collective-permute-start | bytes 786440 | tf_op jit(solution)/shard_map/ppermute | solution.py:691
  11.8 8.8 %collective-permute-done.1.refs_0_ = bf16[2,16,8,512]{3,2,1,0:T(8,128)(2,1)S(1)} collective-permute-done((bf16[2,16,8,512]{3,2,1,0:T(8,128)(2,1)}, bf16[2,16,8,512]{3,2,1,0:T(8,128)(2,1)S(1)}, u32[]{:S(2)}, u32[]{:S(2)}) %collective-permute-start.1) | collective-permute-done | bytes 262176 | tf_op jit(solution)/shard_map/ppermute | solution.py:691
  20.6 3.8 %collective-permute-start.5 = (bf16[2,16,8,512]{3,2,1,0:T(8,128)(2,1)}, bf16[2,16,8,512]{3,2,1,0:T(8,128)(2,1)S(1)}, u32[]{:S(2)}, u32[]{:S(2)}) collective-permute-start(bf16[2,16,8,512]{3,2,1,0:T(8,128)(2,1)} %get-tuple-element.46), channel_id=1, source_target_pairs={{0,1},{1,2},{2,3},{3,0},{4,5},{5,6},{6,7},{7,4},{8,9},{9,10},{10,1... | collective-permute-start | bytes 786440 | tf_op jit(solution)/shard_map/ppermute | solution.py:691
  24.4 3.8 %collective-permute-done.2.refs_1_ = bf16[2,16,8,512]{3,2,1,0:T(8,128)(2,1)S(1)} collective-permute-done((bf16[2,16,8,512]{3,2,1,0:T(8,128)(2,1)}, bf16[2,16,8,512]{3,2,1,0:T(8,128)(2,1)S(1)}, u32[]{:S(2)}, u32[]{:S(2)}) %collective-permute-start.2) | collective-permute-done | bytes 262176 | tf_op jit(solution)/shard_map/ppermute | solution.py:691
  28.2 1.5 %collective-permute-start.6 = (bf16[2,16,8,512]{3,2,1,0:T(8,128)(2,1)}, bf16[2,16,8,512]{3,2,1,0:T(8,128)(2,1)S(1)}, u32[]{:S(2)}, u32[]{:S(2)}) collective-permute-start(bf16[2,16,8,512]{3,2,1,0:T(8,128)(2,1)} %get-tuple-element.47), channel_id=1, source_target_pairs={{0,2},{1,3},{2,0},{3,1},{4,6},{5,7},{6,4},{7,5},{8,10},{9,11},{10,... | collective-permute-start | bytes 786440 | tf_op jit(solution)/shard_map/ppermute | solution.py:691
  29.7 4.0 %note.1 = s32[16,384]{1,0:T(8,128)} custom-call(s32[128]{0:T(128)} %bitcast.24, s32[128]{0:T(128)} %rows.1, s32[8]{0:T(128)} %lens.9), custom_call_target="tpu_custom_call" | custom-call | tf_op jit(solution)/shard_map/note/pallas_call | solution.py:147
  33.8 1.4 %copy.19 = s32[16,1,384]{2,1,0:T(1,128)} copy(s32[16,1,384]{2,0,1:T(8,128)} %bitcast.22) | data formatting | bytes 49152 | tf_op jit(solution)/shard_map/all_to_all | solution.py:704
  35.1 6.3 %all-to-all-start = ((s32[16,1,384]{2,1,0:T(1,128)}), s32[16,1,384]{2,1,0:T(1,128)S(1)}, u32[]{:S(2)}, u32[]{:S(2)}) async-start(s32[16,1,384]{2,1,0:T(1,128)} %copy.19), calls=%async_computation | async-start | bytes 49152 | tf_op jit(solution)/shard_map/all_to_all | solution.py:704
  42.1 4.4 %all-to-all-done = s32[16,1,384]{2,1,0:T(1,128)S(1)} async-done(((s32[16,1,384]{2,1,0:T(1,128)}), s32[16,1,384]{2,1,0:T(1,128)S(1)}, u32[]{:S(2)}, u32[]{:S(2)}) %all-to-all-start) | async-done | bytes 24608 | tf_op jit(solution)/shard_map/all_to_all | solution.py:704
  46.9 1.6 %reshape.20 = bf16[8,4,4,16,128]{4,3,2,1,0:T(8,128)(2,1)S(1)} reshape(bf16[8,4,8192]{2,1,0:T(4,128)(2,1)} %collective-permute-done) | data formatting | bytes 1048576 | tf_op jit(solution)/shard_map/reshape | solution.py:698
  48.7 0.9 copy-done.4
  49.6 5.9 %shard_map.154 = (bf16[8,4,64,128]{3,2,1,0:T(8,128)(2,1)}, f32[8,4,2,64]{3,2,1,0:T(2,128)}) custom-call(s32[4,16]{1,0:T(4,128)S(1)} %dynamic-slice_bitcast_fusion.stages.mine, s32[32,16]{1,0:T(8,128)S(1)} %get-tuple-element.36.place_of, s32[32,16]{1,0:T(8,128)S(1)} %get-tuple-element.37.row_of, s32[32,16]{1,0:T(8,128)S(1)} %get-tuple-element.38.rank_of, ...), custom_call_target="tpu_custom_call" | custom-call | flops 1000000000 | bytes 12582912 | tf_op jit(solution)/shard_map/pallas_call | solution.py:571
  56.2 3.0 %collective-permute-start.12 = (bf16[2,16,8,512]{3,2,1,0:T(8,128)(2,1)}, bf16[2,16,8,512]{3,2,1,0:T(8,128)(2,1)S(1)}, u32[]{:S(2)}, u32[]{:S(2)}) collective-permute-start(bf16[2,16,8,512]{3,2,1,0:T(8,128)(2,1)} %get-tuple-element.55), channel_id=1, source_target_pairs={{0,12},{1,13},{2,14},{3,15},{4,4},{5,5},{6,6},{7,7},{8,8},{9,9},{1... | collective-permute-start | bytes 786440 | tf_op jit(solution)/shard_map/ppermute | solution.py:691
  59.2 3.3 %collective-permute-start.13 = (bf16[2,16,8,512]{3,2,1,0:T(8,128)(2,1)}, bf16[2,16,8,512]{3,2,1,0:T(8,128)(2,1)S(1)}, u32[]{:S(2)}, u32[]{:S(2)}) collective-permute-start(bf16[2,16,8,512]{3,2,1,0:T(8,128)(2,1)} %get-tuple-element.56), channel_id=1, source_target_pairs={{0,13},{1,14},{2,15},{3,12},{4,5},{5,6},{6,7},{7,4},{8,9},{9,10},{... | collective-permute-start | bytes 786440 | tf_op jit(solution)/shard_map/ppermute | solution.py:691
  62.5 1.7 %collective-permute-start.14 = (bf16[2,16,8,512]{3,2,1,0:T(8,128)(2,1)}, bf16[2,16,8,512]{3,2,1,0:T(8,128)(2,1)S(1)}, u32[]{:S(2)}, u32[]{:S(2)}) collective-permute-start(bf16[2,16,8,512]{3,2,1,0:T(8,128)(2,1)} %get-tuple-element.57), channel_id=1, source_target_pairs={{0,14},{1,15},{2,12},{3,13},{4,6},{5,7},{6,4},{7,5},{8,10},{9,11},... | collective-permute-start | bytes 786440 | tf_op jit(solution)/shard_map/ppermute | solution.py:691
  64.2 1.2 collective-permute-start.15
  65.5 2.2 %collective-permute-done.12.refs_8_ = bf16[2,16,8,512]{3,2,1,0:T(8,128)(2,1)S(1)} collective-permute-done((bf16[2,16,8,512]{3,2,1,0:T(8,128)(2,1)}, bf16[2,16,8,512]{3,2,1,0:T(8,128)(2,1)S(1)}, u32[]{:S(2)}, u32[]{:S(2)}) %collective-permute-start.12) | collective-permute-done | bytes 262176 | tf_op jit(solution)/shard_map/ppermute | solution.py:691
  67.6 1.3 collective-permute-start.17
  68.9 2.4 %reshape.24 = bf16[8,4,4,16,128]{4,3,2,1,0:T(8,128)(2,1)} reshape(bf16[8,4,8192]{2,1,0:T(4,128)(2,1)} %param.23) | data formatting | bytes 1048576 | tf_op jit(solution)/shard_map/reshape | solution.py:698
  71.3 1.1 copy.21
  72.4 2.4 %collective-permute-done.13.refs_9_ = bf16[2,16,8,512]{3,2,1,0:T(8,128)(2,1)S(1)} collective-permute-done((bf16[2,16,8,512]{3,2,1,0:T(8,128)(2,1)}, bf16[2,16,8,512]{3,2,1,0:T(8,128)(2,1)S(1)}, u32[]{:S(2)}, u32[]{:S(2)}) %collective-permute-start.13) | collective-permute-done | bytes 262176 | tf_op jit(solution)/shard_map/ppermute | solution.py:691
  74.7 4.1 %collective-permute-done.14.refs_10_ = bf16[2,16,8,512]{3,2,1,0:T(8,128)(2,1)S(1)} collective-permute-done((bf16[2,16,8,512]{3,2,1,0:T(8,128)(2,1)}, bf16[2,16,8,512]{3,2,1,0:T(8,128)(2,1)S(1)}, u32[]{:S(2)}, u32[]{:S(2)}) %collective-permute-start.14) | collective-permute-done | bytes 262176 | tf_op jit(solution)/shard_map/ppermute | solution.py:691
  78.8 7.6 %collective-permute-done.15.refs_11_ = bf16[2,16,8,512]{3,2,1,0:T(8,128)(2,1)} collective-permute-done((bf16[2,16,8,512]{3,2,1,0:T(8,128)(2,1)}, bf16[2,16,8,512]{3,2,1,0:T(8,128)(2,1)}, u32[]{:S(2)}, u32[]{:S(2)}) %collective-permute-start.15) | collective-permute-done | bytes 262176 | tf_op jit(solution)/shard_map/ppermute | solution.py:691
  86.5 9.2 %collective-permute-start.11 = (bf16[2,16,8,512]{3,2,1,0:T(8,128)(2,1)}, bf16[2,16,8,512]{3,2,1,0:T(8,128)(2,1)S(1)}, u32[]{:S(2)}, u32[]{:S(2)}) collective-permute-start(bf16[2,16,8,512]{3,2,1,0:T(8,128)(2,1)} %get-tuple-element.54), channel_id=1, source_target_pairs={{0,7},{1,4},{2,5},{3,6},{4,3},{5,0},{6,1},{7,2},{8,15},{9,12},{10,... | collective-permute-start | bytes 786440 | tf_op jit(solution)/shard_map/ppermute | solution.py:691
  97.9 7.4 %resident.1 = (f32[8,4,64,128]{3,2,1,0:T(8,128)S(1)}, f32[8,4,64,128]{3,2,1,0:T(8,128)}, f32[8,4,64,128]{3,2,1,0:T(8,128)}) custom-call(s32[8]{0:T(128)S(1)} %copy-done.16, bf16[8,4,64,128]{3,2,1,0:T(8,128)(2,1)S(1)} %bitcast.15, bf16[8,4,512]{2,1,0:T(4,128)(2,1)S(1)} %copy-done.6, bf16[8,4,512]{2,1,0:T(4,128)(2,1)S(1)} %copy-done.7, ...), custom_call_target="tpu_custom_call" | custom-call | flops 2000000000 | bytes 16777216 | tf_op jit(solution)/shard_map/resident/pallas_call | solution.py:365
  105.3 1.2 copy-done
  106.6 1.2 copy-done.1
  107.8 12.1 %shard_map.155 = (f32[8,4,64,128]{3,2,1,0:T(8,128)S(1)}, f32[8,4,64,128]{3,2,1,0:T(8,128)S(1)}, f32[8,4,64,128]{3,2,1,0:T(8,128)S(1)}) custom-call(s32[4,16]{1,0:T(4,128)S(1)} %copy-done.14, s32[32,16]{1,0:T(8,128)S(1)} %get-tuple-element.36.place_of, s32[32,16]{1,0:T(8,128)S(1)} %get-tuple-element.37.row_of, s32[32,16]{1,0:T(8,128)S(1)} %get-tuple-element.38.rank_of, ...), custom_call_target="tpu_custom_call" | custom-call | flops 1000000000 | bytes 12582912 | tf_op jit(solution)/shard_map/pallas_call | solution.py:571
  119.9 7.1 %shard_map.156 = bf16[8,4,8192]{2,1,0:T(4,128)(2,1)} custom-call(s32[4,16]{1,0:T(4,128)S(1)} %copy-done.14, s32[32,16]{1,0:T(8,128)S(1)} %get-tuple-element.36.place_of, s32[32,16]{1,0:T(8,128)S(1)} %get-tuple-element.37.row_of, s32[32,16]{1,0:T(8,128)S(1)} %get-tuple-element.38.rank_of, s32[32,16]{1,0:T(8,128)S(1)} %get-tuple-element.39.used, ...), custom_call_target="tpu_custom_call" | custom-call | flops 1000000000 | bytes 12582912 | tf_op jit(solution)/shard_map/pallas_call | solution.py:571
  (54 shorter events, 5.3 us)
Async XLA Ops:
  0.0 48.6 %copy-start.2 = (f32[321,128]{1,0:T(8,128)S(1)}, f32[321,128]{1,0:T(8,128)}, u32[]{:S(2)}) copy-start(f32[321,128]{1,0:T(8,128)} %constant.27.clone.sb) | copy-start | bytes 493060
  0.0 48.6 %copy-start.3 = (f32[321,128]{1,0:T(8,128)S(1)}, f32[321,128]{1,0:T(8,128)}, u32[]{:S(2)}) copy-start(f32[321,128]{1,0:T(8,128)} %constant.26.clone.cb) | copy-start | bytes 493060
  0.0 48.6 %copy-start.8 = (f32[16,128]{1,0:T(8,128)S(1)}, f32[16,128]{1,0:T(8,128)}, u32[]{:S(2)}) copy-start(f32[16,128]{1,0:T(8,128)} %constant.25.clone.sa) | copy-start | bytes 24580
  0.0 48.6 %copy-start.9 = (f32[16,128]{1,0:T(8,128)S(1)}, f32[16,128]{1,0:T(8,128)}, u32[]{:S(2)}) copy-start(f32[16,128]{1,0:T(8,128)} %constant.24.clone.ca) | copy-start | bytes 24580
  0.0 48.6 %copy-start.15 = (s32[8]{0:T(128)S(1)}, s32[8]{0:T(128)}, u32[]{:S(2)}) copy-start(s32[8]{0:T(128)} %lens.9) | copy-start | bytes 100
  0.0 29.7 %collective-permute-start = (bf16[8,4,8192]{2,1,0:T(4,128)(2,1)}, bf16[8,4,8192]{2,1,0:T(4,128)(2,1)}, u32[]{:S(2)}, u32[]{:S(2)}) collective-permute-start(bf16[8,4,8192]{2,1,0:T(4,128)(2,1)} %param.23), channel_id=1, source_target_pairs={{4,8},{5,9},{6,10},{7,11},{8,4},{9,5},{10,6},{11,7},{20,24},{21,25... | collective-permute-start | bytes 1572872 | tf_op jit(solution)/shard_map/ppermute | solution.py:674
  6.1 14.5 %collective-permute-start.1 = (bf16[2,16,8,512]{3,2,1,0:T(8,128)(2,1)}, bf16[2,16,8,512]{3,2,1,0:T(8,128)(2,1)S(1)}, u32[]{:S(2)}, u32[]{:S(2)}) collective-permute-start(bf16[2,16,8,512]{3,2,1,0:T(8,128)(2,1)} %get-tuple-element.41), channel_id=1, source_target_pairs={{0,4},{1,5},{2,6},{3,7},{4,12},{5,13},{6,14},{7,15},{8,0},{9,1},{1... | collective-permute-start | bytes 786440 | tf_op jit(solution)/shard_map/ppermute | solution.py:691
  7.0 21.2 %collective-permute-start.2 = (bf16[2,16,8,512]{3,2,1,0:T(8,128)(2,1)}, bf16[2,16,8,512]{3,2,1,0:T(8,128)(2,1)S(1)}, u32[]{:S(2)}, u32[]{:S(2)}) collective-permute-start(bf16[2,16,8,512]{3,2,1,0:T(8,128)(2,1)} %get-tuple-element.42), channel_id=1, source_target_pairs={{0,5},{1,6},{2,7},{3,4},{4,13},{5,14},{6,15},{7,12},{8,1},{9,2},{1... | collective-permute-start | bytes 786440 | tf_op jit(solution)/shard_map/ppermute | solution.py:691
  8.8 39.7 %collective-permute-start.3 = (bf16[2,16,8,512]{3,2,1,0:T(8,128)(2,1)}, bf16[2,16,8,512]{3,2,1,0:T(8,128)(2,1)S(1)}, u32[]{:S(2)}, u32[]{:S(2)}) collective-permute-start(bf16[2,16,8,512]{3,2,1,0:T(8,128)(2,1)} %get-tuple-element.43), channel_id=1, source_target_pairs={{0,6},{1,7},{2,4},{3,5},{4,14},{5,15},{6,12},{7,13},{8,2},{9,3},{1... | collective-permute-start | bytes 786440 | tf_op jit(solution)/shard_map/ppermute | solution.py:691
  11.5 37.1 %collective-permute-start.4 = (bf16[2,16,8,512]{3,2,1,0:T(8,128)(2,1)}, bf16[2,16,8,512]{3,2,1,0:T(8,128)(2,1)S(1)}, u32[]{:S(2)}, u32[]{:S(2)}) collective-permute-start(bf16[2,16,8,512]{3,2,1,0:T(8,128)(2,1)} %get-tuple-element.44), channel_id=1, source_target_pairs={{0,7},{1,4},{2,5},{3,6},{4,15},{5,12},{6,13},{7,14},{8,3},{9,0},{1... | collective-permute-start | bytes 786440 | tf_op jit(solution)/shard_map/ppermute | solution.py:691
  20.6 28.0 %collective-permute-start.5 = (bf16[2,16,8,512]{3,2,1,0:T(8,128)(2,1)}, bf16[2,16,8,512]{3,2,1,0:T(8,128)(2,1)S(1)}, u32[]{:S(2)}, u32[]{:S(2)}) collective-permute-start(bf16[2,16,8,512]{3,2,1,0:T(8,128)(2,1)} %get-tuple-element.46), channel_id=1, source_target_pairs={{0,1},{1,2},{2,3},{3,0},{4,5},{5,6},{6,7},{7,4},{8,9},{9,10},{10,1... | collective-permute-start | bytes 786440 | tf_op jit(solution)/shard_map/ppermute | solution.py:691
  28.2 20.4 %collective-permute-start.6 = (bf16[2,16,8,512]{3,2,1,0:T(8,128)(2,1)}, bf16[2,16,8,512]{3,2,1,0:T(8,128)(2,1)S(1)}, u32[]{:S(2)}, u32[]{:S(2)}) collective-permute-start(bf16[2,16,8,512]{3,2,1,0:T(8,128)(2,1)} %get-tuple-element.47), channel_id=1, source_target_pairs={{0,2},{1,3},{2,0},{3,1},{4,6},{5,7},{6,4},{7,5},{8,10},{9,11},{10,... | collective-permute-start | bytes 786440 | tf_op jit(solution)/shard_map/ppermute | solution.py:691
  29.7 18.9 %collective-permute-start.7 = (bf16[2,16,8,512]{3,2,1,0:T(8,128)(2,1)}, bf16[2,16,8,512]{3,2,1,0:T(8,128)(2,1)S(1)}, u32[]{:S(2)}, u32[]{:S(2)}) collective-permute-start(bf16[2,16,8,512]{3,2,1,0:T(8,128)(2,1)} %get-tuple-element.48), channel_id=1, source_target_pairs={{0,3},{1,0},{2,1},{3,2},{4,7},{5,4},{6,5},{7,6},{8,11},{9,8},{10,9... | collective-permute-start | bytes 786440 | tf_op jit(solution)/shard_map/ppermute | solution.py:691
  35.1 11.4 %all-to-all-start = ((s32[16,1,384]{2,1,0:T(1,128)}), s32[16,1,384]{2,1,0:T(1,128)S(1)}, u32[]{:S(2)}, u32[]{:S(2)}) async-start(s32[16,1,384]{2,1,0:T(1,128)} %copy.19), calls=%async_computation | async-start | bytes 49152 | tf_op jit(solution)/shard_map/all_to_all | solution.py:704
  42.1 13.4 %copy-start.13 = (s32[4,16]{1,0:T(4,128)}, s32[4,16]{1,0:T(4,128)S(1)}, u32[]{:S(2)}) copy-start(s32[4,16]{1,0:T(4,128)S(1)} %dynamic-slice_bitcast_fusion.stages.mine) | copy-start | bytes 772
  46.9 8.6 %copy-start.11 = (s32[16,128]{1,0:T(8,128)}, s32[16,128]{1,0:T(8,128)S(1)}, u32[]{:S(2)}) copy-start(s32[16,128]{1,0:T(8,128)S(1)} %get-tuple-element.40.tally) | copy-start | bytes 24580
  55.5 49.8 %collective-permute-start.16 = (bf16[8,4,64,128]{3,2,1,0:T(8,128)(2,1)}, bf16[8,4,64,128]{3,2,1,0:T(8,128)(2,1)S(1)}, u32[]{:S(2)}, u32[]{:S(2)}) collective-permute-start(bf16[8,4,64,128]{3,2,1,0:T(8,128)(2,1)} %get-tuple-element.62), channel_id=1, source_target_pairs={{4,8},{5,9},{6,10},{7,11},{8,4},{9,5},{10,6},{11,7},{20,24},{21,25... | collective-permute-start | bytes 1572872 | tf_op jit(solution)/shard_map/ppermute | solution.py:718
  56.2 11.4 %collective-permute-start.12 = (bf16[2,16,8,512]{3,2,1,0:T(8,128)(2,1)}, bf16[2,16,8,512]{3,2,1,0:T(8,128)(2,1)S(1)}, u32[]{:S(2)}, u32[]{:S(2)}) collective-permute-start(bf16[2,16,8,512]{3,2,1,0:T(8,128)(2,1)} %get-tuple-element.55), channel_id=1, source_target_pairs={{0,12},{1,13},{2,14},{3,15},{4,4},{5,5},{6,6},{7,7},{8,8},{9,9},{1... | collective-permute-start | bytes 786440 | tf_op jit(solution)/shard_map/ppermute | solution.py:691
  59.2 15.5 %collective-permute-start.13 = (bf16[2,16,8,512]{3,2,1,0:T(8,128)(2,1)}, bf16[2,16,8,512]{3,2,1,0:T(8,128)(2,1)S(1)}, u32[]{:S(2)}, u32[]{:S(2)}) collective-permute-start(bf16[2,16,8,512]{3,2,1,0:T(8,128)(2,1)} %get-tuple-element.56), channel_id=1, source_target_pairs={{0,13},{1,14},{2,15},{3,12},{4,5},{5,6},{6,7},{7,4},{8,9},{9,10},{... | collective-permute-start | bytes 786440 | tf_op jit(solution)/shard_map/ppermute | solution.py:691
  62.5 16.3 %collective-permute-start.14 = (bf16[2,16,8,512]{3,2,1,0:T(8,128)(2,1)}, bf16[2,16,8,512]{3,2,1,0:T(8,128)(2,1)S(1)}, u32[]{:S(2)}, u32[]{:S(2)}) collective-permute-start(bf16[2,16,8,512]{3,2,1,0:T(8,128)(2,1)} %get-tuple-element.57), channel_id=1, source_target_pairs={{0,14},{1,15},{2,12},{3,13},{4,6},{5,7},{6,4},{7,5},{8,10},{9,11},... | collective-permute-start | bytes 786440 | tf_op jit(solution)/shard_map/ppermute | solution.py:691
  64.2 22.3 %collective-permute-start.15 = (bf16[2,16,8,512]{3,2,1,0:T(8,128)(2,1)}, bf16[2,16,8,512]{3,2,1,0:T(8,128)(2,1)}, u32[]{:S(2)}, u32[]{:S(2)}) collective-permute-start(bf16[2,16,8,512]{3,2,1,0:T(8,128)(2,1)} %get-tuple-element.58), channel_id=1, source_target_pairs={{0,15},{1,12},{2,13},{3,14},{4,7},{5,4},{6,5},{7,6},{8,11},{9,8},{... | collective-permute-start | bytes 786440 | tf_op jit(solution)/shard_map/ppermute | solution.py:691
  67.6 18.8 %collective-permute-start.17 = (f32[8,4,2,64]{3,2,1,0:T(2,128)}, f32[8,4,2,64]{3,2,1,0:T(2,128)}, u32[]{:S(2)}, u32[]{:S(2)}) collective-permute-start(f32[8,4,2,64]{3,2,1,0:T(2,128)} %get-tuple-element.63), channel_id=1, source_target_pairs={{4,8},{5,9},{6,10},{7,11},{8,4},{9,5},{10,6},{11,7},{20,24},{21,25... | collective-permute-start | bytes 49160 | tf_op jit(solution)/shard_map/ppermute | solution.py:719
  74.7 45.2 %collective-permute-start.8 = (bf16[2,16,8,512]{3,2,1,0:T(8,128)(2,1)}, bf16[2,16,8,512]{3,2,1,0:T(8,128)(2,1)S(1)}, u32[]{:S(2)}, u32[]{:S(2)}) collective-permute-start(bf16[2,16,8,512]{3,2,1,0:T(8,128)(2,1)} %get-tuple-element.51), channel_id=1, source_target_pairs={{0,4},{1,5},{2,6},{3,7},{4,0},{5,1},{6,2},{7,3},{8,12},{9,13},{10,... | collective-permute-start | bytes 786440 | tf_op jit(solution)/shard_map/ppermute | solution.py:691
  78.8 41.1 %collective-permute-start.9 = (bf16[2,16,8,512]{3,2,1,0:T(8,128)(2,1)}, bf16[2,16,8,512]{3,2,1,0:T(8,128)(2,1)S(1)}, u32[]{:S(2)}, u32[]{:S(2)}) collective-permute-start(bf16[2,16,8,512]{3,2,1,0:T(8,128)(2,1)} %get-tuple-element.52), channel_id=1, source_target_pairs={{0,5},{1,6},{2,7},{3,4},{4,1},{5,2},{6,3},{7,0},{8,13},{9,14},{10,... | collective-permute-start | bytes 786440 | tf_op jit(solution)/shard_map/ppermute | solution.py:691
  86.5 33.5 %collective-permute-start.10 = (bf16[2,16,8,512]{3,2,1,0:T(8,128)(2,1)}, bf16[2,16,8,512]{3,2,1,0:T(8,128)(2,1)S(1)}, u32[]{:S(2)}, u32[]{:S(2)}) collective-permute-start(bf16[2,16,8,512]{3,2,1,0:T(8,128)(2,1)} %get-tuple-element.53), channel_id=1, source_target_pairs={{0,6},{1,7},{2,4},{3,5},{4,2},{5,3},{6,0},{7,1},{8,14},{9,15},{10,... | collective-permute-start | bytes 786440 | tf_op jit(solution)/shard_map/ppermute | solution.py:691
  86.5 33.5 %collective-permute-start.11 = (bf16[2,16,8,512]{3,2,1,0:T(8,128)(2,1)}, bf16[2,16,8,512]{3,2,1,0:T(8,128)(2,1)S(1)}, u32[]{:S(2)}, u32[]{:S(2)}) collective-permute-start(bf16[2,16,8,512]{3,2,1,0:T(8,128)(2,1)} %get-tuple-element.54), channel_id=1, source_target_pairs={{0,7},{1,4},{2,5},{3,6},{4,3},{5,0},{6,1},{7,2},{8,15},{9,12},{10,... | collective-permute-start | bytes 786440 | tf_op jit(solution)/shard_map/ppermute | solution.py:691
  97.9 7.4 %copy-start.5 = (bf16[2,16,8,512]{3,2,1,0:T(8,128)(2,1)S(1)}, bf16[2,16,8,512]{3,2,1,0:T(8,128)(2,1)}, u32[]{:S(2)}) copy-start(bf16[2,16,8,512]{3,2,1,0:T(8,128)(2,1)} %get-tuple-element.45.refs_4_) | copy-start | bytes 786436
  97.9 7.4 %copy-start.10 = (f32[16,128]{1,0:T(8,128)S(1)}, f32[16,128]{1,0:T(8,128)}, u32[]{:S(2)}) copy-start(f32[16,128]{1,0:T(8,128)} %constant.24.clone.ca) | copy-start | bytes 24580
  97.9 7.4 %copy-start.12 = (s32[16,128]{1,0:T(8,128)S(1)}, s32[16,128]{1,0:T(8,128)}, u32[]{:S(2)}) copy-start(s32[16,128]{1,0:T(8,128)} %copy-done.11) | copy-start | bytes 24580
  97.9 7.4 %copy-start.14 = (s32[4,16]{1,0:T(4,128)S(1)}, s32[4,16]{1,0:T(4,128)}, u32[]{:S(2)}) copy-start(s32[4,16]{1,0:T(4,128)} %copy-done.13) | copy-start | bytes 772
  105.3 1.2 copy-start
  106.6 1.2 copy-start.1
  (4 other events, 3.1 us)

commit v6 on v5

--- a/solution.py
+++ b/solution.py
@@ -106,16 +106,16 @@
     return jnp.where(inner, (PLANES - 1 - 2 * plane) * in_plane + index, index)
 
 
-def note_kernel(n, target, rows, lens, notes, fill):
+def note_kernel(n, target, rows, lens, notes, fill, twins):
     in_plane = n // PLANES
 
     def clear(i, _):
         fill[i] = 0
+        twins[i] = twin_index(in_plane, i)
         return 0
 
     lax.fori_loop(0, n, clear, 0, unroll=min(n, 16))
-    twin_of = functools.partial(twin_index, in_plane)
-    my_twin = twin_of(lax.axis_index("seq"))
+    my_twin = twins[lax.axis_index("seq")]
     for k in range(lens.shape[0]):
         notes[my_twin, 2 * LANES + k] = lens[k]
 
@@ -126,7 +126,7 @@
             dest = target[b]
             slot = fill[dest]
             fill[dest] = slot + 1
-            ready.append((dest, twin_of(dest), slot, rows[b]))
+            ready.append((dest, twins[dest], slot, rows[b]))
         for dest, twin, slot, row in ready:
             notes[dest, slot] = row
             notes[twin, LANES + slot] = row
@@ -136,7 +136,7 @@
 
     def close(i, _):
         notes[i, LANES - 1] = fill[i]
-        notes[twin_of(i), 2 * LANES - 1] = fill[i]
+        notes[twins[i], 2 * LANES - 1] = fill[i]
         return 0
 
     lax.fori_loop(0, n, close, 0, unroll=min(n, 4))
@@ -149,7 +149,7 @@
         out_shape=jax.ShapeDtypeStruct((n, 3 * LANES), jnp.int32),
         in_specs=[smem] * 3,
         out_specs=smem,
-        scratch_shapes=[pltpu.SMEM((n,), jnp.int32)],
+        scratch_shapes=[pltpu.SMEM((n,), jnp.int32), pltpu.SMEM((n,), jnp.int32)],
         name="note",
     )(target, rows, lens)
 
@@ -581,7 +581,7 @@
     )(*scalars, grouped, *tables, *messages, *state, *extra)
 
 
-PHASES = {"d": (2, 2, 2, 2), "f": (0, 3, 3, 0), "g": (3, 0, 0, 3), "b": (1, 1, 1, 1)}
+PHASES = {"e": (2, 1, 1, 2), "f": (0, 3, 3, 0), "g": (3, 0, 0, 3), "h": (1, 2, 2, 1)}
 
 
 def site_plane(plane, flip):
@@ -614,7 +614,7 @@
     ]
 
 
-STAGE = {"d": 1, "f": 1, "g": 1, "b": 2}
+STAGE = {"e": 1, "f": 1, "g": 1, "h": 2}
 
 
 def device_tables(n):
@@ -710,7 +710,7 @@
 
     partial, stats = span(
         "partial", 0, 0, cap, scalars, mirrored, tables,
-        got["d"] + got["f"], (), (), steps,
+        got["e"] + got["f"], (), (), steps,
     )
     queries, partial = lax.optimization_barrier((queries, partial))
     grouped = regroup(queries)
@@ -719,11 +719,11 @@
     stats = lax.ppermute(stats, "seq", swap)
     state = span(
         "state", 1, 0, cap, scalars, grouped, tables,
-        got["d"] + got["f"] + got["g"], tuple(state), (partial, stats), steps,
+        got["e"] + got["f"] + got["g"], tuple(state), (partial, stats), steps,
     )
     return span(
         "final", 2, 3 * in_plane, cap, scalars, grouped, tables,
-        got["b"], tuple(state), (), steps,
+        got["h"], tuple(state), (), steps,
     )
 
 

time: 128 us -> 123 us (0.961)
  waiting for transfers between devices: 33.3 us -> 28.6 us
  Pallas kernels: 41.3 us -> 39.9 us
    ppermute x15, waiting for transfers between devices: 28.9 us -> 23.1 us  [send(): value = lax.ppermute(value, 'seq', pairs)]
where the time goes in v6:
time: 123 us; the launch traced here: 122 us
  starting transfers between devices  40.4 us (33%)
  Pallas kernels  39.9 us (32%)
  waiting for transfers between devices  28.6 us (23%)
  local copies, waits for them, and re-layouts  12.8 us (10%)
    ppermute x15, starting transfers between devices, send(): value = lax.ppermute(value, 'seq', pairs)  30.5 us
    pallas_call x3, Pallas kernels, span(): pl.pallas_call(functools.partial(span_kernel, kind, kernel, first, count,...  24.7 us
    ppermute x15, waiting for transfers between devices, send(): value = lax.ppermute(value, 'seq', pairs)  23.1 us
    pallas_call x1, Pallas kernels, resident(): pl.pallas_call(resident_kernel, out_shape=state_shapes(rows, grouped.shap...  7.36 us
    all_to_all x1, starting transfers between devices, body(): lax.all_to_all(notes, 'seq', split_axis=0, concat_axis=0, tiled=True)  6.33 us
    unnamed x35, local copies, waits for them, and re-layouts  5.6 us
    all_to_all x1, waiting for transfers between devices, body(): lax.all_to_all(notes, 'seq', split_axis=0, concat_axis=0, tiled=True)  5.42 us
    reshape x4, local copies, waits for them, and re-layouts, regroup(): value = value.reshape(rows, steps, KVH, group, HD).transpose(0, 2, 1, 3, 4)  5.1 us
  transfers between devices with their start and end apart: 19, of which 7 were waited for; matrix products, arithmetic and copies ran while one was open for 6% of the time, Pallas kernels for 22%

profile of v6, /device:TPU:27, one launch (start us, length us, event | category | flops | bytes accessed | tf_op | source)
XLA Modules:
  0.0 121.9 jit_solution(4227828646845917835)
XLA Ops:
  0.0 1.6 %collective-permute-start = (bf16[8,4,8192]{2,1,0:T(4,128)(2,1)}, bf16[8,4,8192]{2,1,0:T(4,128)(2,1)}, u32[]{:S(2)}, u32[]{:S(2)}) collective-permute-start(bf16[8,4,8192]{2,1,0:T(4,128)(2,1)} %param.23), channel_id=1, source_target_pairs={{4,8},{5,9},{6,10},{7,11},{8,4},{9,5},{10,6},{11,7},{20,24},{21,25... | collective-permute-start | bytes 1572872 | tf_op jit(solution)/shard_map/ppermute | solution.py:674
  1.6 4.5 %pack.1 = (bf16[2,16,8,512]{3,2,1,0:T(8,128)(2,1)}, bf16[2,16,8,512]{3,2,1,0:T(8,128)(2,1)}, bf16[2,16,8,512]{3,2,1,0:T(8,128)(2,1)}, bf16[2,16,8,512]{3,2,1,0:T...) custom-call(s32[4,4]{1,0:T(4,128)} %constant.22.clone.phase_table, ...), custom_call_target="tpu_custom_call" | custom-call | tf_op jit(solution)/shard_map/pack/pallas_call | solution.py:88
  7.0 2.4 %collective-permute-start.2 = (bf16[2,16,8,512]{3,2,1,0:T(8,128)(2,1)}, bf16[2,16,8,512]{3,2,1,0:T(8,128)(2,1)S(1)}, u32[]{:S(2)}, u32[]{:S(2)}) collective-permute-start(bf16[2,16,8,512]{3,2,1,0:T(8,128)(2,1)} %get-tuple-element.42), channel_id=1, source_target_pairs={{0,5},{1,6},{2,7},{3,4},{4,1},{5,2},{6,3},{7,0},{8,13},{9,14},{10,... | collective-permute-start | bytes 786440 | tf_op jit(solution)/shard_map/ppermute | solution.py:691
  9.4 1.0 collective-permute-start.3
  10.8 2.7 %collective-permute-done.1.refs_0_ = bf16[2,16,8,512]{3,2,1,0:T(8,128)(2,1)S(1)} collective-permute-done((bf16[2,16,8,512]{3,2,1,0:T(8,128)(2,1)}, bf16[2,16,8,512]{3,2,1,0:T(8,128)(2,1)S(1)}, u32[]{:S(2)}, u32[]{:S(2)}) %collective-permute-start.1) | collective-permute-done | bytes 262176 | tf_op jit(solution)/shard_map/ppermute | solution.py:691
  13.6 3.8 %collective-permute-start.5 = (bf16[2,16,8,512]{3,2,1,0:T(8,128)(2,1)}, bf16[2,16,8,512]{3,2,1,0:T(8,128)(2,1)S(1)}, u32[]{:S(2)}, u32[]{:S(2)}) collective-permute-start(bf16[2,16,8,512]{3,2,1,0:T(8,128)(2,1)} %get-tuple-element.46), channel_id=1, source_target_pairs={{0,1},{1,2},{2,3},{3,0},{4,5},{5,6},{6,7},{7,4},{8,9},{9,10},{10,1... | collective-permute-start | bytes 786440 | tf_op jit(solution)/shard_map/ppermute | solution.py:691
  17.4 4.1 %collective-permute-done.2.refs_1_ = bf16[2,16,8,512]{3,2,1,0:T(8,128)(2,1)S(1)} collective-permute-done((bf16[2,16,8,512]{3,2,1,0:T(8,128)(2,1)}, bf16[2,16,8,512]{3,2,1,0:T(8,128)(2,1)S(1)}, u32[]{:S(2)}, u32[]{:S(2)}) %collective-permute-start.2) | collective-permute-done | bytes 262176 | tf_op jit(solution)/shard_map/ppermute | solution.py:691
  21.5 1.2 %collective-permute-start.6 = (bf16[2,16,8,512]{3,2,1,0:T(8,128)(2,1)}, bf16[2,16,8,512]{3,2,1,0:T(8,128)(2,1)S(1)}, u32[]{:S(2)}, u32[]{:S(2)}) collective-permute-start(bf16[2,16,8,512]{3,2,1,0:T(8,128)(2,1)} %get-tuple-element.47), channel_id=1, source_target_pairs={{0,2},{1,3},{2,0},{3,1},{4,6},{5,7},{6,4},{7,5},{8,10},{9,11},{10,... | collective-permute-start | bytes 786440 | tf_op jit(solution)/shard_map/ppermute | solution.py:691
  22.7 3.0 %note.1 = s32[16,384]{1,0:T(8,128)} custom-call(s32[128]{0:T(128)} %bitcast.24, s32[128]{0:T(128)} %rows.1, s32[8]{0:T(128)} %lens.9), custom_call_target="tpu_custom_call" | custom-call | tf_op jit(solution)/shard_map/note/pallas_call | solution.py:147
  25.7 1.4 %copy.19 = s32[16,1,384]{2,1,0:T(1,128)} copy(s32[16,1,384]{2,0,1:T(8,128)} %bitcast.22) | data formatting | bytes 49152 | tf_op jit(solution)/shard_map/all_to_all | solution.py:704
  27.1 6.3 %all-to-all-start = ((s32[16,1,384]{2,1,0:T(1,128)}), s32[16,1,384]{2,1,0:T(1,128)S(1)}, u32[]{:S(2)}, u32[]{:S(2)}) async-start(s32[16,1,384]{2,1,0:T(1,128)} %copy.19), calls=%async_computation | async-start | bytes 49152 | tf_op jit(solution)/shard_map/all_to_all | solution.py:704
  34.1 5.4 %all-to-all-done = s32[16,1,384]{2,1,0:T(1,128)S(1)} async-done(((s32[16,1,384]{2,1,0:T(1,128)}), s32[16,1,384]{2,1,0:T(1,128)S(1)}, u32[]{:S(2)}, u32[]{:S(2)}) %all-to-all-start) | async-done | bytes 24608 | tf_op jit(solution)/shard_map/all_to_all | solution.py:704
  39.9 1.6 %reshape.20 = bf16[8,4,4,16,128]{4,3,2,1,0:T(8,128)(2,1)S(1)} reshape(bf16[8,4,8192]{2,1,0:T(4,128)(2,1)} %collective-permute-done) | data formatting | bytes 1048576 | tf_op jit(solution)/shard_map/reshape | solution.py:698
  41.7 0.9 copy-done.4
  42.6 5.9 %shard_map.154 = (bf16[8,4,64,128]{3,2,1,0:T(8,128)(2,1)}, f32[8,4,2,64]{3,2,1,0:T(2,128)}) custom-call(s32[4,16]{1,0:T(4,128)S(1)} %dynamic-slice_bitcast_fusion.stages.mine, s32[32,16]{1,0:T(8,128)S(1)} %get-tuple-element.36.place_of, s32[32,16]{1,0:T(8,128)S(1)} %get-tuple-element.37.row_of, s32[32,16]{1,0:T(8,128)S(1)} %get-tuple-element.38.rank_of, ...), custom_call_target="tpu_custom_call" | custom-call | flops 1000000000 | bytes 12582912 | tf_op jit(solution)/shard_map/pallas_call | solution.py:571
  49.2 3.5 %collective-permute-start.12 = (bf16[2,16,8,512]{3,2,1,0:T(8,128)(2,1)}, bf16[2,16,8,512]{3,2,1,0:T(8,128)(2,1)S(1)}, u32[]{:S(2)}, u32[]{:S(2)}) collective-permute-start(bf16[2,16,8,512]{3,2,1,0:T(8,128)(2,1)} %get-tuple-element.55), channel_id=1, source_target_pairs={{0,12},{1,13},{2,14},{3,15},{4,4},{5,5},{6,6},{7,7},{8,8},{9,9},{1... | collective-permute-start | bytes 786440 | tf_op jit(solution)/shard_map/ppermute | solution.py:691
  52.7 2.8 %collective-permute-start.13 = (bf16[2,16,8,512]{3,2,1,0:T(8,128)(2,1)}, bf16[2,16,8,512]{3,2,1,0:T(8,128)(2,1)S(1)}, u32[]{:S(2)}, u32[]{:S(2)}) collective-permute-start(bf16[2,16,8,512]{3,2,1,0:T(8,128)(2,1)} %get-tuple-element.56), channel_id=1, source_target_pairs={{0,13},{1,14},{2,15},{3,12},{4,5},{5,6},{6,7},{7,4},{8,9},{9,10},{... | collective-permute-start | bytes 786440 | tf_op jit(solution)/shard_map/ppermute | solution.py:691
  55.5 2.0 %collective-permute-start.14 = (bf16[2,16,8,512]{3,2,1,0:T(8,128)(2,1)}, bf16[2,16,8,512]{3,2,1,0:T(8,128)(2,1)S(1)}, u32[]{:S(2)}, u32[]{:S(2)}) collective-permute-start(bf16[2,16,8,512]{3,2,1,0:T(8,128)(2,1)} %get-tuple-element.57), channel_id=1, source_target_pairs={{0,14},{1,15},{2,12},{3,13},{4,6},{5,7},{6,4},{7,5},{8,10},{9,11},... | collective-permute-start | bytes 786440 | tf_op jit(solution)/shard_map/ppermute | solution.py:691
  57.5 1.0 collective-permute-start.15
  58.4 2.2 %collective-permute-done.12.refs_8_ = bf16[2,16,8,512]{3,2,1,0:T(8,128)(2,1)S(1)} collective-permute-done((bf16[2,16,8,512]{3,2,1,0:T(8,128)(2,1)}, bf16[2,16,8,512]{3,2,1,0:T(8,128)(2,1)S(1)}, u32[]{:S(2)}, u32[]{:S(2)}) %collective-permute-start.12) | collective-permute-done | bytes 262176 | tf_op jit(solution)/shard_map/ppermute | solution.py:691
  60.6 1.3 %collective-permute-start.17 = (f32[8,4,2,64]{3,2,1,0:T(2,128)}, f32[8,4,2,64]{3,2,1,0:T(2,128)}, u32[]{:S(2)}, u32[]{:S(2)}) collective-permute-start(f32[8,4,2,64]{3,2,1,0:T(2,128)} %get-tuple-element.63), channel_id=1, source_target_pairs={{4,8},{5,9},{6,10},{7,11},{8,4},{9,5},{10,6},{11,7},{20,24},{21,25... | collective-permute-start | bytes 49160 | tf_op jit(solution)/shard_map/ppermute | solution.py:719
  61.9 2.4 %reshape.24 = bf16[8,4,4,16,128]{4,3,2,1,0:T(8,128)(2,1)} reshape(bf16[8,4,8192]{2,1,0:T(4,128)(2,1)} %param.23) | data formatting | bytes 1048576 | tf_op jit(solution)/shard_map/reshape | solution.py:698
  64.2 1.1 copy.21
  65.3 2.4 %collective-permute-done.13.refs_9_ = bf16[2,16,8,512]{3,2,1,0:T(8,128)(2,1)S(1)} collective-permute-done((bf16[2,16,8,512]{3,2,1,0:T(8,128)(2,1)}, bf16[2,16,8,512]{3,2,1,0:T(8,128)(2,1)S(1)}, u32[]{:S(2)}, u32[]{:S(2)}) %collective-permute-start.13) | collective-permute-done | bytes 262176 | tf_op jit(solution)/shard_map/ppermute | solution.py:691
  67.7 4.0 %collective-permute-done.14.refs_10_ = bf16[2,16,8,512]{3,2,1,0:T(8,128)(2,1)S(1)} collective-permute-done((bf16[2,16,8,512]{3,2,1,0:T(8,128)(2,1)}, bf16[2,16,8,512]{3,2,1,0:T(8,128)(2,1)S(1)}, u32[]{:S(2)}, u32[]{:S(2)}) %collective-permute-start.14) | collective-permute-done | bytes 262176 | tf_op jit(solution)/shard_map/ppermute | solution.py:691
  71.8 7.7 %collective-permute-done.15.refs_11_ = bf16[2,16,8,512]{3,2,1,0:T(8,128)(2,1)} collective-permute-done((bf16[2,16,8,512]{3,2,1,0:T(8,128)(2,1)}, bf16[2,16,8,512]{3,2,1,0:T(8,128)(2,1)}, u32[]{:S(2)}, u32[]{:S(2)}) %collective-permute-start.15) | collective-permute-done | bytes 262176 | tf_op jit(solution)/shard_map/ppermute | solution.py:691
  79.5 11.5 %collective-permute-start.11 = (bf16[2,16,8,512]{3,2,1,0:T(8,128)(2,1)}, bf16[2,16,8,512]{3,2,1,0:T(8,128)(2,1)S(1)}, u32[]{:S(2)}, u32[]{:S(2)}) collective-permute-start(bf16[2,16,8,512]{3,2,1,0:T(8,128)(2,1)} %get-tuple-element.54), channel_id=1, source_target_pairs={{0,7},{1,4},{2,5},{3,6},{4,15},{5,12},{6,13},{7,14},{8,3},{9,0},{1... | collective-permute-start | bytes 786440 | tf_op jit(solution)/shard_map/ppermute | solution.py:691
  93.2 7.4 %resident.1 = (f32[8,4,64,128]{3,2,1,0:T(8,128)S(1)}, f32[8,4,64,128]{3,2,1,0:T(8,128)}, f32[8,4,64,128]{3,2,1,0:T(8,128)}) custom-call(s32[8]{0:T(128)S(1)} %copy-done.16, bf16[8,4,64,128]{3,2,1,0:T(8,128)(2,1)S(1)} %bitcast.15, bf16[8,4,512]{2,1,0:T(4,128)(2,1)S(1)} %copy-done.6, bf16[8,4,512]{2,1,0:T(4,128)(2,1)S(1)} %copy-done.7, ...), custom_call_target="tpu_custom_call" | custom-call | flops 2000000000 | bytes 16777216 | tf_op jit(solution)/shard_map/resident/pallas_call | solution.py:365
  100.6 1.2 copy-done
  101.8 1.2 %copy-done.1 = f32[8,4,64,128]{3,2,1,0:T(8,128)S(1)} copy-done((f32[8,4,64,128]{3,2,1,0:T(8,128)S(1)}, f32[8,4,64,128]{3,2,1,0:T(8,128)}, u32[]{:S(2)}) %copy-start.1) | copy-done | bytes 1048600
  103.0 11.7 %shard_map.155 = (f32[8,4,64,128]{3,2,1,0:T(8,128)S(1)}, f32[8,4,64,128]{3,2,1,0:T(8,128)S(1)}, f32[8,4,64,128]{3,2,1,0:T(8,128)S(1)}) custom-call(s32[4,16]{1,0:T(4,128)S(1)} %copy-done.14, s32[32,16]{1,0:T(8,128)S(1)} %get-tuple-element.36.place_of, s32[32,16]{1,0:T(8,128)S(1)} %get-tuple-element.37.row_of, s32[32,16]{1,0:T(8,128)S(1)} %get-tuple-element.38.rank_of, ...), custom_call_target="tpu_custom_call" | custom-call | flops 1000000000 | bytes 12582912 | tf_op jit(solution)/shard_map/pallas_call | solution.py:571
  114.8 7.1 %shard_map.156 = bf16[8,4,8192]{2,1,0:T(4,128)(2,1)} custom-call(s32[4,16]{1,0:T(4,128)S(1)} %copy-done.14, s32[32,16]{1,0:T(8,128)S(1)} %get-tuple-element.36.place_of, s32[32,16]{1,0:T(8,128)S(1)} %get-tuple-element.37.row_of, s32[32,16]{1,0:T(8,128)S(1)} %get-tuple-element.38.rank_of, s32[32,16]{1,0:T(8,128)S(1)} %get-tuple-element.39.used, ...), custom_call_target="tpu_custom_call" | custom-call | flops 1000000000 | bytes 12582912 | tf_op jit(solution)/shard_map/pallas_call | solution.py:571
  (54 shorter events, 5.3 us)
Async XLA Ops:
  0.0 41.6 %copy-start.2 = (f32[321,128]{1,0:T(8,128)S(1)}, f32[321,128]{1,0:T(8,128)}, u32[]{:S(2)}) copy-start(f32[321,128]{1,0:T(8,128)} %constant.27.clone.sb) | copy-start | bytes 493060
  0.0 41.6 %copy-start.3 = (f32[321,128]{1,0:T(8,128)S(1)}, f32[321,128]{1,0:T(8,128)}, u32[]{:S(2)}) copy-start(f32[321,128]{1,0:T(8,128)} %constant.26.clone.cb) | copy-start | bytes 493060
  0.0 41.6 %copy-start.8 = (f32[16,128]{1,0:T(8,128)S(1)}, f32[16,128]{1,0:T(8,128)}, u32[]{:S(2)}) copy-start(f32[16,128]{1,0:T(8,128)} %constant.25.clone.sa) | copy-start | bytes 24580
  0.0 41.6 %copy-start.9 = (f32[16,128]{1,0:T(8,128)S(1)}, f32[16,128]{1,0:T(8,128)}, u32[]{:S(2)}) copy-start(f32[16,128]{1,0:T(8,128)} %constant.24.clone.ca) | copy-start | bytes 24580
  0.0 41.6 %copy-start.15 = (s32[8]{0:T(128)S(1)}, s32[8]{0:T(128)}, u32[]{:S(2)}) copy-start(s32[8]{0:T(128)} %lens.9) | copy-start | bytes 100
  0.0 22.7 %collective-permute-start = (bf16[8,4,8192]{2,1,0:T(4,128)(2,1)}, bf16[8,4,8192]{2,1,0:T(4,128)(2,1)}, u32[]{:S(2)}, u32[]{:S(2)}) collective-permute-start(bf16[8,4,8192]{2,1,0:T(4,128)(2,1)} %param.23), channel_id=1, source_target_pairs={{4,8},{5,9},{6,10},{7,11},{8,4},{9,5},{10,6},{11,7},{20,24},{21,25... | collective-permute-start | bytes 1572872 | tf_op jit(solution)/shard_map/ppermute | solution.py:674
  6.1 7.5 %collective-permute-start.1 = (bf16[2,16,8,512]{3,2,1,0:T(8,128)(2,1)}, bf16[2,16,8,512]{3,2,1,0:T(8,128)(2,1)S(1)}, u32[]{:S(2)}, u32[]{:S(2)}) collective-permute-start(bf16[2,16,8,512]{3,2,1,0:T(8,128)(2,1)} %get-tuple-element.41), channel_id=1, source_target_pairs={{0,4},{1,5},{2,6},{3,7},{4,0},{5,1},{6,2},{7,3},{8,12},{9,13},{10,... | collective-permute-start | bytes 786440 | tf_op jit(solution)/shard_map/ppermute | solution.py:691
  7.0 14.5 %collective-permute-start.2 = (bf16[2,16,8,512]{3,2,1,0:T(8,128)(2,1)}, bf16[2,16,8,512]{3,2,1,0:T(8,128)(2,1)S(1)}, u32[]{:S(2)}, u32[]{:S(2)}) collective-permute-start(bf16[2,16,8,512]{3,2,1,0:T(8,128)(2,1)} %get-tuple-element.42), channel_id=1, source_target_pairs={{0,5},{1,6},{2,7},{3,4},{4,1},{5,2},{6,3},{7,0},{8,13},{9,14},{10,... | collective-permute-start | bytes 786440 | tf_op jit(solution)/shard_map/ppermute | solution.py:691
  9.4 32.1 %collective-permute-start.3 = (bf16[2,16,8,512]{3,2,1,0:T(8,128)(2,1)}, bf16[2,16,8,512]{3,2,1,0:T(8,128)(2,1)S(1)}, u32[]{:S(2)}, u32[]{:S(2)}) collective-permute-start(bf16[2,16,8,512]{3,2,1,0:T(8,128)(2,1)} %get-tuple-element.43), channel_id=1, source_target_pairs={{0,6},{1,7},{2,4},{3,5},{4,2},{5,3},{6,0},{7,1},{8,14},{9,15},{10,... | collective-permute-start | bytes 786440 | tf_op jit(solution)/shard_map/ppermute | solution.py:691
  10.5 31.1 %collective-permute-start.4 = (bf16[2,16,8,512]{3,2,1,0:T(8,128)(2,1)}, bf16[2,16,8,512]{3,2,1,0:T(8,128)(2,1)S(1)}, u32[]{:S(2)}, u32[]{:S(2)}) collective-permute-start(bf16[2,16,8,512]{3,2,1,0:T(8,128)(2,1)} %get-tuple-element.44), channel_id=1, source_target_pairs={{0,7},{1,4},{2,5},{3,6},{4,3},{5,0},{6,1},{7,2},{8,15},{9,12},{10,... | collective-permute-start | bytes 786440 | tf_op jit(solution)/shard_map/ppermute | solution.py:691
  13.6 28.0 %collective-permute-start.5 = (bf16[2,16,8,512]{3,2,1,0:T(8,128)(2,1)}, bf16[2,16,8,512]{3,2,1,0:T(8,128)(2,1)S(1)}, u32[]{:S(2)}, u32[]{:S(2)}) collective-permute-start(bf16[2,16,8,512]{3,2,1,0:T(8,128)(2,1)} %get-tuple-element.46), channel_id=1, source_target_pairs={{0,1},{1,2},{2,3},{3,0},{4,5},{5,6},{6,7},{7,4},{8,9},{9,10},{10,1... | collective-permute-start | bytes 786440 | tf_op jit(solution)/shard_map/ppermute | solution.py:691
  21.5 20.1 %collective-permute-start.6 = (bf16[2,16,8,512]{3,2,1,0:T(8,128)(2,1)}, bf16[2,16,8,512]{3,2,1,0:T(8,128)(2,1)S(1)}, u32[]{:S(2)}, u32[]{:S(2)}) collective-permute-start(bf16[2,16,8,512]{3,2,1,0:T(8,128)(2,1)} %get-tuple-element.47), channel_id=1, source_target_pairs={{0,2},{1,3},{2,0},{3,1},{4,6},{5,7},{6,4},{7,5},{8,10},{9,11},{10,... | collective-permute-start | bytes 786440 | tf_op jit(solution)/shard_map/ppermute | solution.py:691
  22.7 18.9 %collective-permute-start.7 = (bf16[2,16,8,512]{3,2,1,0:T(8,128)(2,1)}, bf16[2,16,8,512]{3,2,1,0:T(8,128)(2,1)S(1)}, u32[]{:S(2)}, u32[]{:S(2)}) collective-permute-start(bf16[2,16,8,512]{3,2,1,0:T(8,128)(2,1)} %get-tuple-element.48), channel_id=1, source_target_pairs={{0,3},{1,0},{2,1},{3,2},{4,7},{5,4},{6,5},{7,6},{8,11},{9,8},{10,9... | collective-permute-start | bytes 786440 | tf_op jit(solution)/shard_map/ppermute | solution.py:691
  27.1 12.4 %all-to-all-start = ((s32[16,1,384]{2,1,0:T(1,128)}), s32[16,1,384]{2,1,0:T(1,128)S(1)}, u32[]{:S(2)}, u32[]{:S(2)}) async-start(s32[16,1,384]{2,1,0:T(1,128)} %copy.19), calls=%async_computation | async-start | bytes 49152 | tf_op jit(solution)/shard_map/all_to_all | solution.py:704
  34.1 14.4 %copy-start.13 = (s32[4,16]{1,0:T(4,128)}, s32[4,16]{1,0:T(4,128)S(1)}, u32[]{:S(2)}) copy-start(s32[4,16]{1,0:T(4,128)S(1)} %dynamic-slice_bitcast_fusion.stages.mine) | copy-start | bytes 772
  39.9 8.6 %copy-start.11 = (s32[16,128]{1,0:T(8,128)}, s32[16,128]{1,0:T(8,128)S(1)}, u32[]{:S(2)}) copy-start(s32[16,128]{1,0:T(8,128)S(1)} %get-tuple-element.40.tally) | copy-start | bytes 24580
  48.5 52.0 %collective-permute-start.16 = (bf16[8,4,64,128]{3,2,1,0:T(8,128)(2,1)}, bf16[8,4,64,128]{3,2,1,0:T(8,128)(2,1)S(1)}, u32[]{:S(2)}, u32[]{:S(2)}) collective-permute-start(bf16[8,4,64,128]{3,2,1,0:T(8,128)(2,1)} %get-tuple-element.62), channel_id=1, source_target_pairs={{4,8},{5,9},{6,10},{7,11},{8,4},{9,5},{10,6},{11,7},{20,24},{21,25... | collective-permute-start | bytes 1572872 | tf_op jit(solution)/shard_map/ppermute | solution.py:718
  49.2 11.4 %collective-permute-start.12 = (bf16[2,16,8,512]{3,2,1,0:T(8,128)(2,1)}, bf16[2,16,8,512]{3,2,1,0:T(8,128)(2,1)S(1)}, u32[]{:S(2)}, u32[]{:S(2)}) collective-permute-start(bf16[2,16,8,512]{3,2,1,0:T(8,128)(2,1)} %get-tuple-element.55), channel_id=1, source_target_pairs={{0,12},{1,13},{2,14},{3,15},{4,4},{5,5},{6,6},{7,7},{8,8},{9,9},{1... | collective-permute-start | bytes 786440 | tf_op jit(solution)/shard_map/ppermute | solution.py:691
  52.7 15.0 %collective-permute-start.13 = (bf16[2,16,8,512]{3,2,1,0:T(8,128)(2,1)}, bf16[2,16,8,512]{3,2,1,0:T(8,128)(2,1)S(1)}, u32[]{:S(2)}, u32[]{:S(2)}) collective-permute-start(bf16[2,16,8,512]{3,2,1,0:T(8,128)(2,1)} %get-tuple-element.56), channel_id=1, source_target_pairs={{0,13},{1,14},{2,15},{3,12},{4,5},{5,6},{6,7},{7,4},{8,9},{9,10},{... | collective-permute-start | bytes 786440 | tf_op jit(solution)/shard_map/ppermute | solution.py:691
  55.5 16.3 %collective-permute-start.14 = (bf16[2,16,8,512]{3,2,1,0:T(8,128)(2,1)}, bf16[2,16,8,512]{3,2,1,0:T(8,128)(2,1)S(1)}, u32[]{:S(2)}, u32[]{:S(2)}) collective-permute-start(bf16[2,16,8,512]{3,2,1,0:T(8,128)(2,1)} %get-tuple-element.57), channel_id=1, source_target_pairs={{0,14},{1,15},{2,12},{3,13},{4,6},{5,7},{6,4},{7,5},{8,10},{9,11},... | collective-permute-start | bytes 786440 | tf_op jit(solution)/shard_map/ppermute | solution.py:691
  57.5 22.0 %collective-permute-start.15 = (bf16[2,16,8,512]{3,2,1,0:T(8,128)(2,1)}, bf16[2,16,8,512]{3,2,1,0:T(8,128)(2,1)}, u32[]{:S(2)}, u32[]{:S(2)}) collective-permute-start(bf16[2,16,8,512]{3,2,1,0:T(8,128)(2,1)} %get-tuple-element.58), channel_id=1, source_target_pairs={{0,15},{1,12},{2,13},{3,14},{4,7},{5,4},{6,5},{7,6},{8,11},{9,8},{... | collective-permute-start | bytes 786440 | tf_op jit(solution)/shard_map/ppermute | solution.py:691
  60.6 18.8 %collective-permute-start.17 = (f32[8,4,2,64]{3,2,1,0:T(2,128)}, f32[8,4,2,64]{3,2,1,0:T(2,128)}, u32[]{:S(2)}, u32[]{:S(2)}) collective-permute-start(f32[8,4,2,64]{3,2,1,0:T(2,128)} %get-tuple-element.63), channel_id=1, source_target_pairs={{4,8},{5,9},{6,10},{7,11},{8,4},{9,5},{10,6},{11,7},{20,24},{21,25... | collective-permute-start | bytes 49160 | tf_op jit(solution)/shard_map/ppermute | solution.py:719
  67.7 47.0 %collective-permute-start.8 = (bf16[2,16,8,512]{3,2,1,0:T(8,128)(2,1)}, bf16[2,16,8,512]{3,2,1,0:T(8,128)(2,1)S(1)}, u32[]{:S(2)}, u32[]{:S(2)}) collective-permute-start(bf16[2,16,8,512]{3,2,1,0:T(8,128)(2,1)} %get-tuple-element.51), channel_id=1, source_target_pairs={{0,4},{1,5},{2,6},{3,7},{4,12},{5,13},{6,14},{7,15},{8,0},{9,1},{1... | collective-permute-start | bytes 786440 | tf_op jit(solution)/shard_map/ppermute | solution.py:691
  71.8 43.0 %collective-permute-start.9 = (bf16[2,16,8,512]{3,2,1,0:T(8,128)(2,1)}, bf16[2,16,8,512]{3,2,1,0:T(8,128)(2,1)S(1)}, u32[]{:S(2)}, u32[]{:S(2)}) collective-permute-start(bf16[2,16,8,512]{3,2,1,0:T(8,128)(2,1)} %get-tuple-element.52), channel_id=1, source_target_pairs={{0,5},{1,6},{2,7},{3,4},{4,13},{5,14},{6,15},{7,12},{8,1},{9,2},{1... | collective-permute-start | bytes 786440 | tf_op jit(solution)/shard_map/ppermute | solution.py:691
  79.5 35.3 %collective-permute-start.10 = (bf16[2,16,8,512]{3,2,1,0:T(8,128)(2,1)}, bf16[2,16,8,512]{3,2,1,0:T(8,128)(2,1)S(1)}, u32[]{:S(2)}, u32[]{:S(2)}) collective-permute-start(bf16[2,16,8,512]{3,2,1,0:T(8,128)(2,1)} %get-tuple-element.53), channel_id=1, source_target_pairs={{0,6},{1,7},{2,4},{3,5},{4,14},{5,15},{6,12},{7,13},{8,2},{9,3},{1... | collective-permute-start | bytes 786440 | tf_op jit(solution)/shard_map/ppermute | solution.py:691
  79.5 35.3 %collective-permute-start.11 = (bf16[2,16,8,512]{3,2,1,0:T(8,128)(2,1)}, bf16[2,16,8,512]{3,2,1,0:T(8,128)(2,1)S(1)}, u32[]{:S(2)}, u32[]{:S(2)}) collective-permute-start(bf16[2,16,8,512]{3,2,1,0:T(8,128)(2,1)} %get-tuple-element.54), channel_id=1, source_target_pairs={{0,7},{1,4},{2,5},{3,6},{4,15},{5,12},{6,13},{7,14},{8,3},{9,0},{1... | collective-permute-start | bytes 786440 | tf_op jit(solution)/shard_map/ppermute | solution.py:691
  93.2 7.4 %copy-start.5 = (bf16[2,16,8,512]{3,2,1,0:T(8,128)(2,1)S(1)}, bf16[2,16,8,512]{3,2,1,0:T(8,128)(2,1)}, u32[]{:S(2)}) copy-start(bf16[2,16,8,512]{3,2,1,0:T(8,128)(2,1)} %get-tuple-element.45.refs_4_) | copy-start | bytes 786436
  93.2 7.4 %copy-start.10 = (f32[16,128]{1,0:T(8,128)S(1)}, f32[16,128]{1,0:T(8,128)}, u32[]{:S(2)}) copy-start(f32[16,128]{1,0:T(8,128)} %constant.24.clone.ca) | copy-start | bytes 24580
  93.2 7.4 %copy-start.12 = (s32[16,128]{1,0:T(8,128)S(1)}, s32[16,128]{1,0:T(8,128)}, u32[]{:S(2)}) copy-start(s32[16,128]{1,0:T(8,128)} %copy-done.11) | copy-start | bytes 24580
  93.2 7.4 %copy-start.14 = (s32[4,16]{1,0:T(4,128)S(1)}, s32[4,16]{1,0:T(4,128)}, u32[]{:S(2)}) copy-start(s32[4,16]{1,0:T(4,128)} %copy-done.13) | copy-start | bytes 772
  100.6 1.2 %copy-start = (f32[8,4,64,128]{3,2,1,0:T(8,128)S(1)}, f32[8,4,64,128]{3,2,1,0:T(8,128)}, u32[]{:S(2)}) copy-start(f32[8,4,64,128]{3,2,1,0:T(8,128)} %get-tuple-element.60.refs_13_) | copy-start | bytes 3145732
  101.8 1.2 %copy-start.1 = (f32[8,4,64,128]{3,2,1,0:T(8,128)S(1)}, f32[8,4,64,128]{3,2,1,0:T(8,128)}, u32[]{:S(2)}) copy-start(f32[8,4,64,128]{3,2,1,0:T(8,128)} %get-tuple-element.61.refs_14_) | copy-start | bytes 3145732
  (4 other events, 3.1 us)

commit v7 on v6

--- a/solution.py
+++ b/solution.py
@@ -698,7 +698,9 @@
         value = value.reshape(rows, steps, KVH, group, HD).transpose(0, 2, 1, 3, 4)
         return value.reshape(rows, KVH, steps * group, HD)
 
-    mirrored = regroup(mirrored)
+    queries, mirrored = lax.optimization_barrier((queries, mirrored))
+    grouped, mirrored = regroup(queries), regroup(mirrored)
+    state = resident(cache_len, grouped, step_keys, step_values, cache_keys, cache_values)
 
     notes = note(n, block_device[:, 0], block_row, cache_len)
     notes = lax.all_to_all(notes, "seq", split_axis=0, concat_axis=0, tiled=True)
@@ -712,9 +714,6 @@
         "partial", 0, 0, cap, scalars, mirrored, tables,
         got["e"] + got["f"], (), (), steps,
     )
-    queries, partial = lax.optimization_barrier((queries, partial))
-    grouped = regroup(queries)
-    state = resident(cache_len, grouped, step_keys, step_values, cache_keys, cache_values)
     partial = lax.ppermute(partial, "seq", swap)
     stats = lax.ppermute(stats, "seq", swap)
     state = span(

time: 123 us -> 123 us (level)
  no operation moved by 1% of the time
where the time goes in v7:
time: 123 us; the launch traced here: 122 us
  starting transfers between devices  40.4 us (33%)
  Pallas kernels  39.9 us (32%)
  waiting for transfers between devices  28.6 us (23%)
  local copies, waits for them, and re-layouts  12.8 us (10%)
    ppermute x15, starting transfers between devices, send(): value = lax.ppermute(value, 'seq', pairs)  30.5 us
    pallas_call x3, Pallas kernels, span(): pl.pallas_call(functools.partial(span_kernel, kind, kernel, first, count,...  24.7 us
    ppermute x15, waiting for transfers between devices, send(): value = lax.ppermute(value, 'seq', pairs)  23.1 us
    pallas_call x1, Pallas kernels, resident(): pl.pallas_call(resident_kernel, out_shape=state_shapes(rows, grouped.shap...  7.36 us
    all_to_all x1, starting transfers between devices, body(): lax.all_to_all(notes, 'seq', split_axis=0, concat_axis=0, tiled=True)  6.33 us
    unnamed x35, local copies, waits for them, and re-layouts  5.6 us
    all_to_all x1, waiting for transfers between devices, body(): lax.all_to_all(notes, 'seq', split_axis=0, concat_axis=0, tiled=True)  5.42 us
    reshape x4, local copies, waits for them, and re-layouts, regroup(): value = value.reshape(rows, steps, KVH, group, HD).transpose(0, 2, 1, 3, 4)  5.1 us
  transfers between devices with their start and end apart: 19, of which 7 were waited for; matrix products, arithmetic and copies ran while one was open for 6% of the time, Pallas kernels for 22%

profile of v7, /device:TPU:27, one launch (start us, length us, event | category | flops | bytes accessed | tf_op | source)
XLA Modules:
  0.0 121.9 jit_solution(4227828646845917835)
XLA Ops:
  0.0 1.6 %collective-permute-start = (bf16[8,4,8192]{2,1,0:T(4,128)(2,1)}, bf16[8,4,8192]{2,1,0:T(4,128)(2,1)}, u32[]{:S(2)}, u32[]{:S(2)}) collective-permute-start(bf16[8,4,8192]{2,1,0:T(4,128)(2,1)} %param.23), channel_id=1, source_target_pairs={{4,8},{5,9},{6,10},{7,11},{8,4},{9,5},{10,6},{11,7},{20,24},{21,25... | collective-permute-start | bytes 1572872 | tf_op jit(solution)/shard_map/ppermute | solution.py:674
  1.6 4.5 %pack.1 = (bf16[2,16,8,512]{3,2,1,0:T(8,128)(2,1)}, bf16[2,16,8,512]{3,2,1,0:T(8,128)(2,1)}, bf16[2,16,8,512]{3,2,1,0:T(8,128)(2,1)}, bf16[2,16,8,512]{3,2,1,0:T...) custom-call(s32[4,4]{1,0:T(4,128)} %constant.22.clone.phase_table, ...), custom_call_target="tpu_custom_call" | custom-call | tf_op jit(solution)/shard_map/pack/pallas_call | solution.py:88
  7.0 2.4 %collective-permute-start.6 = (bf16[2,16,8,512]{3,2,1,0:T(8,128)(2,1)}, bf16[2,16,8,512]{3,2,1,0:T(8,128)(2,1)S(1)}, u32[]{:S(2)}, u32[]{:S(2)}) collective-permute-start(bf16[2,16,8,512]{3,2,1,0:T(8,128)(2,1)} %get-tuple-element.47), channel_id=1, source_target_pairs={{0,5},{1,6},{2,7},{3,4},{4,1},{5,2},{6,3},{7,0},{8,13},{9,14},{10,... | collective-permute-start | bytes 786440 | tf_op jit(solution)/shard_map/ppermute | solution.py:691
  9.4 1.0 collective-permute-start.7
  10.8 2.7 %collective-permute-done.5.refs_0_ = bf16[2,16,8,512]{3,2,1,0:T(8,128)(2,1)S(1)} collective-permute-done((bf16[2,16,8,512]{3,2,1,0:T(8,128)(2,1)}, bf16[2,16,8,512]{3,2,1,0:T(8,128)(2,1)S(1)}, u32[]{:S(2)}, u32[]{:S(2)}) %collective-permute-start.5) | collective-permute-done | bytes 262176 | tf_op jit(solution)/shard_map/ppermute | solution.py:691
  13.6 3.8 %collective-permute-start.9 = (bf16[2,16,8,512]{3,2,1,0:T(8,128)(2,1)}, bf16[2,16,8,512]{3,2,1,0:T(8,128)(2,1)S(1)}, u32[]{:S(2)}, u32[]{:S(2)}) collective-permute-start(bf16[2,16,8,512]{3,2,1,0:T(8,128)(2,1)} %get-tuple-element.51), channel_id=1, source_target_pairs={{0,1},{1,2},{2,3},{3,0},{4,5},{5,6},{6,7},{7,4},{8,9},{9,10},{10,1... | collective-permute-start | bytes 786440 | tf_op jit(solution)/shard_map/ppermute | solution.py:691
  17.4 4.1 %collective-permute-done.6.refs_1_ = bf16[2,16,8,512]{3,2,1,0:T(8,128)(2,1)S(1)} collective-permute-done((bf16[2,16,8,512]{3,2,1,0:T(8,128)(2,1)}, bf16[2,16,8,512]{3,2,1,0:T(8,128)(2,1)S(1)}, u32[]{:S(2)}, u32[]{:S(2)}) %collective-permute-start.6) | collective-permute-done | bytes 262176 | tf_op jit(solution)/shard_map/ppermute | solution.py:691
  21.5 1.2 %collective-permute-start.10 = (bf16[2,16,8,512]{3,2,1,0:T(8,128)(2,1)}, bf16[2,16,8,512]{3,2,1,0:T(8,128)(2,1)S(1)}, u32[]{:S(2)}, u32[]{:S(2)}) collective-permute-start(bf16[2,16,8,512]{3,2,1,0:T(8,128)(2,1)} %get-tuple-element.52), channel_id=1, source_target_pairs={{0,2},{1,3},{2,0},{3,1},{4,6},{5,7},{6,4},{7,5},{8,10},{9,11},{10,... | collective-permute-start | bytes 786440 | tf_op jit(solution)/shard_map/ppermute | solution.py:691
  22.7 3.0 %note.1 = s32[16,384]{1,0:T(8,128)} custom-call(s32[128]{0:T(128)} %bitcast.24, s32[128]{0:T(128)} %rows.1, s32[8]{0:T(128)} %lens.9), custom_call_target="tpu_custom_call" | custom-call | tf_op jit(solution)/shard_map/note/pallas_call | solution.py:147
  25.7 1.4 %copy.19 = s32[16,1,384]{2,1,0:T(1,128)} copy(s32[16,1,384]{2,0,1:T(8,128)} %bitcast.22) | data formatting | bytes 49152 | tf_op jit(solution)/shard_map/all_to_all | solution.py:706
  27.1 6.3 %all-to-all-start = ((s32[16,1,384]{2,1,0:T(1,128)}), s32[16,1,384]{2,1,0:T(1,128)S(1)}, u32[]{:S(2)}, u32[]{:S(2)}) async-start(s32[16,1,384]{2,1,0:T(1,128)} %copy.19), calls=%async_computation | async-start | bytes 49152 | tf_op jit(solution)/shard_map/all_to_all | solution.py:706
  34.1 5.4 %all-to-all-done = s32[16,1,384]{2,1,0:T(1,128)S(1)} async-done(((s32[16,1,384]{2,1,0:T(1,128)}), s32[16,1,384]{2,1,0:T(1,128)S(1)}, u32[]{:S(2)}, u32[]{:S(2)}) %all-to-all-start) | async-done | bytes 24608 | tf_op jit(solution)/shard_map/all_to_all | solution.py:706
  39.9 1.6 %reshape.24 = bf16[8,4,4,16,128]{4,3,2,1,0:T(8,128)(2,1)S(1)} reshape(bf16[8,4,8192]{2,1,0:T(4,128)(2,1)} %collective-permute-done) | data formatting | bytes 1048576 | tf_op jit(solution)/shard_map/reshape | solution.py:698
  41.7 0.9 copy-done.4
  42.6 5.9 %shard_map.154 = (bf16[8,4,64,128]{3,2,1,0:T(8,128)(2,1)}, f32[8,4,2,64]{3,2,1,0:T(2,128)}) custom-call(s32[4,16]{1,0:T(4,128)S(1)} %dynamic-slice_bitcast_fusion.stages.mine, s32[32,16]{1,0:T(8,128)S(1)} %get-tuple-element.36.place_of, s32[32,16]{1,0:T(8,128)S(1)} %get-tuple-element.37.row_of, s32[32,16]{1,0:T(8,128)S(1)} %get-tuple-element.38.rank_of, ...), custom_call_target="tpu_custom_call" | custom-call | flops 1000000000 | bytes 12582912 | tf_op jit(solution)/shard_map/pallas_call | solution.py:571
  49.2 3.5 %collective-permute-start.12 = (bf16[2,16,8,512]{3,2,1,0:T(8,128)(2,1)}, bf16[2,16,8,512]{3,2,1,0:T(8,128)(2,1)S(1)}, u32[]{:S(2)}, u32[]{:S(2)}) collective-permute-start(bf16[2,16,8,512]{3,2,1,0:T(8,128)(2,1)} %get-tuple-element.54), channel_id=1, source_target_pairs={{0,12},{1,13},{2,14},{3,15},{4,4},{5,5},{6,6},{7,7},{8,8},{9,9},{1... | collective-permute-start | bytes 786440 | tf_op jit(solution)/shard_map/ppermute | solution.py:691
  52.7 2.8 %collective-permute-start.13 = (bf16[2,16,8,512]{3,2,1,0:T(8,128)(2,1)}, bf16[2,16,8,512]{3,2,1,0:T(8,128)(2,1)S(1)}, u32[]{:S(2)}, u32[]{:S(2)}) collective-permute-start(bf16[2,16,8,512]{3,2,1,0:T(8,128)(2,1)} %get-tuple-element.55), channel_id=1, source_target_pairs={{0,13},{1,14},{2,15},{3,12},{4,5},{5,6},{6,7},{7,4},{8,9},{9,10},{... | collective-permute-start | bytes 786440 | tf_op jit(solution)/shard_map/ppermute | solution.py:691
  55.5 2.0 %collective-permute-start.14 = (bf16[2,16,8,512]{3,2,1,0:T(8,128)(2,1)}, bf16[2,16,8,512]{3,2,1,0:T(8,128)(2,1)S(1)}, u32[]{:S(2)}, u32[]{:S(2)}) collective-permute-start(bf16[2,16,8,512]{3,2,1,0:T(8,128)(2,1)} %get-tuple-element.56), channel_id=1, source_target_pairs={{0,14},{1,15},{2,12},{3,13},{4,6},{5,7},{6,4},{7,5},{8,10},{9,11},... | collective-permute-start | bytes 786440 | tf_op jit(solution)/shard_map/ppermute | solution.py:691
  57.5 1.0 collective-permute-start.15
  58.4 2.2 %collective-permute-done.12.refs_8_ = bf16[2,16,8,512]{3,2,1,0:T(8,128)(2,1)S(1)} collective-permute-done((bf16[2,16,8,512]{3,2,1,0:T(8,128)(2,1)}, bf16[2,16,8,512]{3,2,1,0:T(8,128)(2,1)S(1)}, u32[]{:S(2)}, u32[]{:S(2)}) %collective-permute-start.12) | collective-permute-done | bytes 262176 | tf_op jit(solution)/shard_map/ppermute | solution.py:691
  60.6 1.3 %collective-permute-start.17 = (f32[8,4,2,64]{3,2,1,0:T(2,128)}, f32[8,4,2,64]{3,2,1,0:T(2,128)}, u32[]{:S(2)}, u32[]{:S(2)}) collective-permute-start(f32[8,4,2,64]{3,2,1,0:T(2,128)} %get-tuple-element.63), channel_id=1, source_target_pairs={{4,8},{5,9},{6,10},{7,11},{8,4},{9,5},{10,6},{11,7},{20,24},{21,25... | collective-permute-start | bytes 49160 | tf_op jit(solution)/shard_map/ppermute | solution.py:718
  61.9 2.4 %reshape.20 = bf16[8,4,4,16,128]{4,3,2,1,0:T(8,128)(2,1)} reshape(bf16[8,4,8192]{2,1,0:T(4,128)(2,1)} %param.23) | data formatting | bytes 1048576 | tf_op jit(solution)/shard_map/reshape | solution.py:698
  64.2 1.1 copy.20
  65.3 2.4 %collective-permute-done.13.refs_9_ = bf16[2,16,8,512]{3,2,1,0:T(8,128)(2,1)S(1)} collective-permute-done((bf16[2,16,8,512]{3,2,1,0:T(8,128)(2,1)}, bf16[2,16,8,512]{3,2,1,0:T(8,128)(2,1)S(1)}, u32[]{:S(2)}, u32[]{:S(2)}) %collective-permute-start.13) | collective-permute-done | bytes 262176 | tf_op jit(solution)/shard_map/ppermute | solution.py:691
  67.7 4.0 %collective-permute-done.14.refs_10_ = bf16[2,16,8,512]{3,2,1,0:T(8,128)(2,1)S(1)} collective-permute-done((bf16[2,16,8,512]{3,2,1,0:T(8,128)(2,1)}, bf16[2,16,8,512]{3,2,1,0:T(8,128)(2,1)S(1)}, u32[]{:S(2)}, u32[]{:S(2)}) %collective-permute-start.14) | collective-permute-done | bytes 262176 | tf_op jit(solution)/shard_map/ppermute | solution.py:691
  71.8 7.7 %collective-permute-done.15.refs_11_ = bf16[2,16,8,512]{3,2,1,0:T(8,128)(2,1)} collective-permute-done((bf16[2,16,8,512]{3,2,1,0:T(8,128)(2,1)}, bf16[2,16,8,512]{3,2,1,0:T(8,128)(2,1)}, u32[]{:S(2)}, u32[]{:S(2)}) %collective-permute-start.15) | collective-permute-done | bytes 262176 | tf_op jit(solution)/shard_map/ppermute | solution.py:691
  79.5 11.5 %collective-permute-start.4 = (bf16[2,16,8,512]{3,2,1,0:T(8,128)(2,1)}, bf16[2,16,8,512]{3,2,1,0:T(8,128)(2,1)S(1)}, u32[]{:S(2)}, u32[]{:S(2)}) collective-permute-start(bf16[2,16,8,512]{3,2,1,0:T(8,128)(2,1)} %get-tuple-element.45), channel_id=1, source_target_pairs={{0,7},{1,4},{2,5},{3,6},{4,15},{5,12},{6,13},{7,14},{8,3},{9,0},{1... | collective-permute-start | bytes 786440 | tf_op jit(solution)/shard_map/ppermute | solution.py:691
  93.2 7.4 %resident.1 = (f32[8,4,64,128]{3,2,1,0:T(8,128)S(1)}, f32[8,4,64,128]{3,2,1,0:T(8,128)}, f32[8,4,64,128]{3,2,1,0:T(8,128)}) custom-call(s32[8]{0:T(128)S(1)} %copy-done.16, bf16[8,4,64,128]{3,2,1,0:T(8,128)(2,1)S(1)} %bitcast.15, bf16[8,4,512]{2,1,0:T(4,128)(2,1)S(1)} %copy-done.6, bf16[8,4,512]{2,1,0:T(4,128)(2,1)S(1)} %copy-done.7, ...), custom_call_target="tpu_custom_call" | custom-call | flops 2000000000 | bytes 16777216 | tf_op jit(solution)/shard_map/resident/pallas_call | solution.py:365
  100.6 1.2 copy-done
  101.8 1.2 %copy-done.1 = f32[8,4,64,128]{3,2,1,0:T(8,128)S(1)} copy-done((f32[8,4,64,128]{3,2,1,0:T(8,128)S(1)}, f32[8,4,64,128]{3,2,1,0:T(8,128)}, u32[]{:S(2)}) %copy-start.1) | copy-done | bytes 1048600
  103.0 11.7 %shard_map.155 = (f32[8,4,64,128]{3,2,1,0:T(8,128)S(1)}, f32[8,4,64,128]{3,2,1,0:T(8,128)S(1)}, f32[8,4,64,128]{3,2,1,0:T(8,128)S(1)}) custom-call(s32[4,16]{1,0:T(4,128)S(1)} %copy-done.14, s32[32,16]{1,0:T(8,128)S(1)} %get-tuple-element.36.place_of, s32[32,16]{1,0:T(8,128)S(1)} %get-tuple-element.37.row_of, s32[32,16]{1,0:T(8,128)S(1)} %get-tuple-element.38.rank_of, ...), custom_call_target="tpu_custom_call" | custom-call | flops 1000000000 | bytes 12582912 | tf_op jit(solution)/shard_map/pallas_call | solution.py:571
  114.8 7.1 %shard_map.156 = bf16[8,4,8192]{2,1,0:T(4,128)(2,1)} custom-call(s32[4,16]{1,0:T(4,128)S(1)} %copy-done.14, s32[32,16]{1,0:T(8,128)S(1)} %get-tuple-element.36.place_of, s32[32,16]{1,0:T(8,128)S(1)} %get-tuple-element.37.row_of, s32[32,16]{1,0:T(8,128)S(1)} %get-tuple-element.38.rank_of, s32[32,16]{1,0:T(8,128)S(1)} %get-tuple-element.39.used, ...), custom_call_target="tpu_custom_call" | custom-call | flops 1000000000 | bytes 12582912 | tf_op jit(solution)/shard_map/pallas_call | solution.py:571
  (54 shorter events, 5.3 us)
Async XLA Ops:
  0.0 41.6 %copy-start.2 = (f32[321,128]{1,0:T(8,128)S(1)}, f32[321,128]{1,0:T(8,128)}, u32[]{:S(2)}) copy-start(f32[321,128]{1,0:T(8,128)} %constant.27.clone.sb) | copy-start | bytes 493060
  0.0 41.6 %copy-start.3 = (f32[321,128]{1,0:T(8,128)S(1)}, f32[321,128]{1,0:T(8,128)}, u32[]{:S(2)}) copy-start(f32[321,128]{1,0:T(8,128)} %constant.26.clone.cb) | copy-start | bytes 493060
  0.0 41.6 %copy-start.8 = (f32[16,128]{1,0:T(8,128)S(1)}, f32[16,128]{1,0:T(8,128)}, u32[]{:S(2)}) copy-start(f32[16,128]{1,0:T(8,128)} %constant.25.clone.sa) | copy-start | bytes 24580
  0.0 41.6 %copy-start.9 = (f32[16,128]{1,0:T(8,128)S(1)}, f32[16,128]{1,0:T(8,128)}, u32[]{:S(2)}) copy-start(f32[16,128]{1,0:T(8,128)} %constant.24.clone.ca) | copy-start | bytes 24580
  0.0 41.6 %copy-start.15 = (s32[8]{0:T(128)S(1)}, s32[8]{0:T(128)}, u32[]{:S(2)}) copy-start(s32[8]{0:T(128)} %lens.9) | copy-start | bytes 100
  0.0 22.7 %collective-permute-start = (bf16[8,4,8192]{2,1,0:T(4,128)(2,1)}, bf16[8,4,8192]{2,1,0:T(4,128)(2,1)}, u32[]{:S(2)}, u32[]{:S(2)}) collective-permute-start(bf16[8,4,8192]{2,1,0:T(4,128)(2,1)} %param.23), channel_id=1, source_target_pairs={{4,8},{5,9},{6,10},{7,11},{8,4},{9,5},{10,6},{11,7},{20,24},{21,25... | collective-permute-start | bytes 1572872 | tf_op jit(solution)/shard_map/ppermute | solution.py:674
  6.1 7.5 %collective-permute-start.5 = (bf16[2,16,8,512]{3,2,1,0:T(8,128)(2,1)}, bf16[2,16,8,512]{3,2,1,0:T(8,128)(2,1)S(1)}, u32[]{:S(2)}, u32[]{:S(2)}) collective-permute-start(bf16[2,16,8,512]{3,2,1,0:T(8,128)(2,1)} %get-tuple-element.46), channel_id=1, source_target_pairs={{0,4},{1,5},{2,6},{3,7},{4,0},{5,1},{6,2},{7,3},{8,12},{9,13},{10,... | collective-permute-start | bytes 786440 | tf_op jit(solution)/shard_map/ppermute | solution.py:691
  7.0 14.5 %collective-permute-start.6 = (bf16[2,16,8,512]{3,2,1,0:T(8,128)(2,1)}, bf16[2,16,8,512]{3,2,1,0:T(8,128)(2,1)S(1)}, u32[]{:S(2)}, u32[]{:S(2)}) collective-permute-start(bf16[2,16,8,512]{3,2,1,0:T(8,128)(2,1)} %get-tuple-element.47), channel_id=1, source_target_pairs={{0,5},{1,6},{2,7},{3,4},{4,1},{5,2},{6,3},{7,0},{8,13},{9,14},{10,... | collective-permute-start | bytes 786440 | tf_op jit(solution)/shard_map/ppermute | solution.py:691
  9.4 32.1 %collective-permute-start.7 = (bf16[2,16,8,512]{3,2,1,0:T(8,128)(2,1)}, bf16[2,16,8,512]{3,2,1,0:T(8,128)(2,1)S(1)}, u32[]{:S(2)}, u32[]{:S(2)}) collective-permute-start(bf16[2,16,8,512]{3,2,1,0:T(8,128)(2,1)} %get-tuple-element.48), channel_id=1, source_target_pairs={{0,6},{1,7},{2,4},{3,5},{4,2},{5,3},{6,0},{7,1},{8,14},{9,15},{10,... | collective-permute-start | bytes 786440 | tf_op jit(solution)/shard_map/ppermute | solution.py:691
  10.5 31.1 %collective-permute-start.8 = (bf16[2,16,8,512]{3,2,1,0:T(8,128)(2,1)}, bf16[2,16,8,512]{3,2,1,0:T(8,128)(2,1)S(1)}, u32[]{:S(2)}, u32[]{:S(2)}) collective-permute-start(bf16[2,16,8,512]{3,2,1,0:T(8,128)(2,1)} %get-tuple-element.49), channel_id=1, source_target_pairs={{0,7},{1,4},{2,5},{3,6},{4,3},{5,0},{6,1},{7,2},{8,15},{9,12},{10,... | collective-permute-start | bytes 786440 | tf_op jit(solution)/shard_map/ppermute | solution.py:691
  13.6 28.0 %collective-permute-start.9 = (bf16[2,16,8,512]{3,2,1,0:T(8,128)(2,1)}, bf16[2,16,8,512]{3,2,1,0:T(8,128)(2,1)S(1)}, u32[]{:S(2)}, u32[]{:S(2)}) collective-permute-start(bf16[2,16,8,512]{3,2,1,0:T(8,128)(2,1)} %get-tuple-element.51), channel_id=1, source_target_pairs={{0,1},{1,2},{2,3},{3,0},{4,5},{5,6},{6,7},{7,4},{8,9},{9,10},{10,1... | collective-permute-start | bytes 786440 | tf_op jit(solution)/shard_map/ppermute | solution.py:691
  21.5 20.1 %collective-permute-start.10 = (bf16[2,16,8,512]{3,2,1,0:T(8,128)(2,1)}, bf16[2,16,8,512]{3,2,1,0:T(8,128)(2,1)S(1)}, u32[]{:S(2)}, u32[]{:S(2)}) collective-permute-start(bf16[2,16,8,512]{3,2,1,0:T(8,128)(2,1)} %get-tuple-element.52), channel_id=1, source_target_pairs={{0,2},{1,3},{2,0},{3,1},{4,6},{5,7},{6,4},{7,5},{8,10},{9,11},{10,... | collective-permute-start | bytes 786440 | tf_op jit(solution)/shard_map/ppermute | solution.py:691
  22.7 18.9 %collective-permute-start.11 = (bf16[2,16,8,512]{3,2,1,0:T(8,128)(2,1)}, bf16[2,16,8,512]{3,2,1,0:T(8,128)(2,1)S(1)}, u32[]{:S(2)}, u32[]{:S(2)}) collective-permute-start(bf16[2,16,8,512]{3,2,1,0:T(8,128)(2,1)} %get-tuple-element.53), channel_id=1, source_target_pairs={{0,3},{1,0},{2,1},{3,2},{4,7},{5,4},{6,5},{7,6},{8,11},{9,8},{10,9... | collective-permute-start | bytes 786440 | tf_op jit(solution)/shard_map/ppermute | solution.py:691
  27.1 12.4 %all-to-all-start = ((s32[16,1,384]{2,1,0:T(1,128)}), s32[16,1,384]{2,1,0:T(1,128)S(1)}, u32[]{:S(2)}, u32[]{:S(2)}) async-start(s32[16,1,384]{2,1,0:T(1,128)} %copy.19), calls=%async_computation | async-start | bytes 49152 | tf_op jit(solution)/shard_map/all_to_all | solution.py:706
  34.1 14.4 %copy-start.13 = (s32[4,16]{1,0:T(4,128)}, s32[4,16]{1,0:T(4,128)S(1)}, u32[]{:S(2)}) copy-start(s32[4,16]{1,0:T(4,128)S(1)} %dynamic-slice_bitcast_fusion.stages.mine) | copy-start | bytes 772
  39.9 8.6 %copy-start.11 = (s32[16,128]{1,0:T(8,128)}, s32[16,128]{1,0:T(8,128)S(1)}, u32[]{:S(2)}) copy-start(s32[16,128]{1,0:T(8,128)S(1)} %get-tuple-element.40.tally) | copy-start | bytes 24580
  48.5 52.0 %collective-permute-start.16 = (bf16[8,4,64,128]{3,2,1,0:T(8,128)(2,1)}, bf16[8,4,64,128]{3,2,1,0:T(8,128)(2,1)S(1)}, u32[]{:S(2)}, u32[]{:S(2)}) collective-permute-start(bf16[8,4,64,128]{3,2,1,0:T(8,128)(2,1)} %get-tuple-element.62), channel_id=1, source_target_pairs={{4,8},{5,9},{6,10},{7,11},{8,4},{9,5},{10,6},{11,7},{20,24},{21,25... | collective-permute-start | bytes 1572872 | tf_op jit(solution)/shard_map/ppermute | solution.py:717
  49.2 11.4 %collective-permute-start.12 = (bf16[2,16,8,512]{3,2,1,0:T(8,128)(2,1)}, bf16[2,16,8,512]{3,2,1,0:T(8,128)(2,1)S(1)}, u32[]{:S(2)}, u32[]{:S(2)}) collective-permute-start(bf16[2,16,8,512]{3,2,1,0:T(8,128)(2,1)} %get-tuple-element.54), channel_id=1, source_target_pairs={{0,12},{1,13},{2,14},{3,15},{4,4},{5,5},{6,6},{7,7},{8,8},{9,9},{1... | collective-permute-start | bytes 786440 | tf_op jit(solution)/shard_map/ppermute | solution.py:691
  52.7 15.0 %collective-permute-start.13 = (bf16[2,16,8,512]{3,2,1,0:T(8,128)(2,1)}, bf16[2,16,8,512]{3,2,1,0:T(8,128)(2,1)S(1)}, u32[]{:S(2)}, u32[]{:S(2)}) collective-permute-start(bf16[2,16,8,512]{3,2,1,0:T(8,128)(2,1)} %get-tuple-element.55), channel_id=1, source_target_pairs={{0,13},{1,14},{2,15},{3,12},{4,5},{5,6},{6,7},{7,4},{8,9},{9,10},{... | collective-permute-start | bytes 786440 | tf_op jit(solution)/shard_map/ppermute | solution.py:691
  55.5 16.3 %collective-permute-start.14 = (bf16[2,16,8,512]{3,2,1,0:T(8,128)(2,1)}, bf16[2,16,8,512]{3,2,1,0:T(8,128)(2,1)S(1)}, u32[]{:S(2)}, u32[]{:S(2)}) collective-permute-start(bf16[2,16,8,512]{3,2,1,0:T(8,128)(2,1)} %get-tuple-element.56), channel_id=1, source_target_pairs={{0,14},{1,15},{2,12},{3,13},{4,6},{5,7},{6,4},{7,5},{8,10},{9,11},... | collective-permute-start | bytes 786440 | tf_op jit(solution)/shard_map/ppermute | solution.py:691
  57.5 22.0 %collective-permute-start.15 = (bf16[2,16,8,512]{3,2,1,0:T(8,128)(2,1)}, bf16[2,16,8,512]{3,2,1,0:T(8,128)(2,1)}, u32[]{:S(2)}, u32[]{:S(2)}) collective-permute-start(bf16[2,16,8,512]{3,2,1,0:T(8,128)(2,1)} %get-tuple-element.57), channel_id=1, source_target_pairs={{0,15},{1,12},{2,13},{3,14},{4,7},{5,4},{6,5},{7,6},{8,11},{9,8},{... | collective-permute-start | bytes 786440 | tf_op jit(solution)/shard_map/ppermute | solution.py:691
  60.6 18.8 %collective-permute-start.17 = (f32[8,4,2,64]{3,2,1,0:T(2,128)}, f32[8,4,2,64]{3,2,1,0:T(2,128)}, u32[]{:S(2)}, u32[]{:S(2)}) collective-permute-start(f32[8,4,2,64]{3,2,1,0:T(2,128)} %get-tuple-element.63), channel_id=1, source_target_pairs={{4,8},{5,9},{6,10},{7,11},{8,4},{9,5},{10,6},{11,7},{20,24},{21,25... | collective-permute-start | bytes 49160 | tf_op jit(solution)/shard_map/ppermute | solution.py:718
  67.7 47.0 %collective-permute-start.1 = (bf16[2,16,8,512]{3,2,1,0:T(8,128)(2,1)}, bf16[2,16,8,512]{3,2,1,0:T(8,128)(2,1)S(1)}, u32[]{:S(2)}, u32[]{:S(2)}) collective-permute-start(bf16[2,16,8,512]{3,2,1,0:T(8,128)(2,1)} %get-tuple-element.42), channel_id=1, source_target_pairs={{0,4},{1,5},{2,6},{3,7},{4,12},{5,13},{6,14},{7,15},{8,0},{9,1},{1... | collective-permute-start | bytes 786440 | tf_op jit(solution)/shard_map/ppermute | solution.py:691
  71.8 43.0 %collective-permute-start.2 = (bf16[2,16,8,512]{3,2,1,0:T(8,128)(2,1)}, bf16[2,16,8,512]{3,2,1,0:T(8,128)(2,1)S(1)}, u32[]{:S(2)}, u32[]{:S(2)}) collective-permute-start(bf16[2,16,8,512]{3,2,1,0:T(8,128)(2,1)} %get-tuple-element.43), channel_id=1, source_target_pairs={{0,5},{1,6},{2,7},{3,4},{4,13},{5,14},{6,15},{7,12},{8,1},{9,2},{1... | collective-permute-start | bytes 786440 | tf_op jit(solution)/shard_map/ppermute | solution.py:691
  79.5 35.3 %collective-permute-start.3 = (bf16[2,16,8,512]{3,2,1,0:T(8,128)(2,1)}, bf16[2,16,8,512]{3,2,1,0:T(8,128)(2,1)S(1)}, u32[]{:S(2)}, u32[]{:S(2)}) collective-permute-start(bf16[2,16,8,512]{3,2,1,0:T(8,128)(2,1)} %get-tuple-element.44), channel_id=1, source_target_pairs={{0,6},{1,7},{2,4},{3,5},{4,14},{5,15},{6,12},{7,13},{8,2},{9,3},{1... | collective-permute-start | bytes 786440 | tf_op jit(solution)/shard_map/ppermute | solution.py:691
  79.5 35.3 %collective-permute-start.4 = (bf16[2,16,8,512]{3,2,1,0:T(8,128)(2,1)}, bf16[2,16,8,512]{3,2,1,0:T(8,128)(2,1)S(1)}, u32[]{:S(2)}, u32[]{:S(2)}) collective-permute-start(bf16[2,16,8,512]{3,2,1,0:T(8,128)(2,1)} %get-tuple-element.45), channel_id=1, source_target_pairs={{0,7},{1,4},{2,5},{3,6},{4,15},{5,12},{6,13},{7,14},{8,3},{9,0},{1... | collective-permute-start | bytes 786440 | tf_op jit(solution)/shard_map/ppermute | solution.py:691
  93.2 7.4 %copy-start.5 = (bf16[2,16,8,512]{3,2,1,0:T(8,128)(2,1)S(1)}, bf16[2,16,8,512]{3,2,1,0:T(8,128)(2,1)}, u32[]{:S(2)}) copy-start(bf16[2,16,8,512]{3,2,1,0:T(8,128)(2,1)} %get-tuple-element.50.refs_4_) | copy-start | bytes 786436
  93.2 7.4 %copy-start.10 = (f32[16,128]{1,0:T(8,128)S(1)}, f32[16,128]{1,0:T(8,128)}, u32[]{:S(2)}) copy-start(f32[16,128]{1,0:T(8,128)} %constant.24.clone.ca) | copy-start | bytes 24580
  93.2 7.4 %copy-start.12 = (s32[16,128]{1,0:T(8,128)S(1)}, s32[16,128]{1,0:T(8,128)}, u32[]{:S(2)}) copy-start(s32[16,128]{1,0:T(8,128)} %copy-done.11) | copy-start | bytes 24580
  93.2 7.4 %copy-start.14 = (s32[4,16]{1,0:T(4,128)S(1)}, s32[4,16]{1,0:T(4,128)}, u32[]{:S(2)}) copy-start(s32[4,16]{1,0:T(4,128)} %copy-done.13) | copy-start | bytes 772
  100.6 1.2 %copy-start = (f32[8,4,64,128]{3,2,1,0:T(8,128)S(1)}, f32[8,4,64,128]{3,2,1,0:T(8,128)}, u32[]{:S(2)}) copy-start(f32[8,4,64,128]{3,2,1,0:T(8,128)} %get-tuple-element.59.refs_13_) | copy-start | bytes 3145732
  101.8 1.2 %copy-start.1 = (f32[8,4,64,128]{3,2,1,0:T(8,128)S(1)}, f32[8,4,64,128]{3,2,1,0:T(8,128)}, u32[]{:S(2)}) copy-start(f32[8,4,64,128]{3,2,1,0:T(8,128)} %get-tuple-element.60.refs_14_) | copy-start | bytes 3145732
  (4 other events, 3.1 us)

commit v8 on v7

--- a/solution.py
+++ b/solution.py
@@ -390,9 +390,9 @@
     if kind == "partial":
         out, stats, acc, top, total, kbuf, vbuf = refs
     elif kind == "state":
-        part, stats, acc, top, total, kbuf, vbuf = refs[3:]
+        acc, top, total, kbuf, vbuf = refs[3:]
     else:
-        out, acc, top, total, scr, kbuf, vbuf = refs[3:]
+        part, stats, out, acc, top, total, scr, kbuf, vbuf = refs[3:]
     state = (acc, top, total)
     rows = q_ref.shape[0]
     width = q_ref.shape[2]
@@ -504,7 +504,6 @@
 
     def state_rows(pair):
         new = [blend(row_queries(r, q_ref), [block(r, 0)], held(r, before)) for r in pair]
-        new = [with_part(r, one) for r, one in zip(pair, new)]
         for r, one in zip(pair, new):
             hold(r, state, one)
         for r in pair:
@@ -526,6 +525,7 @@
 
     def final_rows(pair):
         new = [blend(row_queries(r, q_ref), [block(r, 0)], held(r, before)) for r in pair]
+        new = [with_part(r, one) for r, one in zip(pair, new)]
         put_out(pair, new)
         longest = functools.reduce(jnp.maximum, [tally[8 + kernel, r] for r in pair])
 
@@ -581,7 +581,7 @@
     )(*scalars, grouped, *tables, *messages, *state, *extra)
 
 
-PHASES = {"e": (2, 1, 1, 2), "f": (0, 3, 3, 0), "g": (3, 0, 0, 3), "h": (1, 2, 2, 1)}
+PHASES = {"d": (2, 2, 2, 2), "f": (0, 3, 3, 0), "g": (3, 0, 0, 3), "b": (1, 1, 1, 1)}
 
 
 def site_plane(plane, flip):
@@ -614,7 +614,7 @@
     ]
 
 
-STAGE = {"e": 1, "f": 1, "g": 1, "h": 2}
+STAGE = {"d": 1, "f": 1, "g": 1, "b": 2}
 
 
 def device_tables(n):
@@ -712,17 +712,17 @@
 
     partial, stats = span(
         "partial", 0, 0, cap, scalars, mirrored, tables,
-        got["e"] + got["f"], (), (), steps,
+        got["d"] + got["f"], (), (), steps,
     )
     partial = lax.ppermute(partial, "seq", swap)
     stats = lax.ppermute(stats, "seq", swap)
     state = span(
         "state", 1, 0, cap, scalars, grouped, tables,
-        got["e"] + got["f"] + got["g"], tuple(state), (partial, stats), steps,
+        got["d"] + got["f"] + got["g"], tuple(state), (), steps,
     )
     return span(
         "final", 2, 3 * in_plane, cap, scalars, grouped, tables,
-        got["h"], tuple(state), (), steps,
+        got["b"], tuple(state), (partial, stats), steps,
     )
 
 

time: 123 us -> 116 us (0.943)
  waiting for transfers between devices: 28.6 us -> 18 us
  starting transfers between devices: 40.4 us -> 43 us
    ppermute x15, waiting for transfers between devices: 23.1 us -> 12.6 us  [send(): value = lax.ppermute(value, 'seq', pairs)]
    ppermute x15, starting transfers between devices: 30.5 us -> 33.8 us  [send(): value = lax.ppermute(value, 'seq', pairs)]
    unnamed x35 -> x39, local copies, waits for them, and re-layouts: 5.6 us -> 6.2 us
  transfers between devices with their start and end apart: 19 -> 19, of which waited for: 7 -> 3; matrix products, arithmetic and copies ran while one was open for 6% -> 6% of each run, Pallas kernels for 22% -> 29%
where the time goes in v8:
time: 116 us; the launch traced here: 115 us
  starting transfers between devices  43 us (37%)
  Pallas kernels  40.4 us (35%)
  waiting for transfers between devices  18 us (16%)
  local copies, waits for them, and re-layouts  13.3 us (11%)
    ppermute x15, starting transfers between devices, send(): value = lax.ppermute(value, 'seq', pairs)  33.8 us
    pallas_call x3, Pallas kernels, span(): pl.pallas_call(functools.partial(span_kernel, kind, kernel, first, count,...  25.1 us
    ppermute x15, waiting for transfers between devices, send(): value = lax.ppermute(value, 'seq', pairs)  12.6 us
    pallas_call x1, Pallas kernels, resident(): pl.pallas_call(resident_kernel, out_shape=state_shapes(rows, grouped.shap...  7.37 us
    all_to_all x1, starting transfers between devices, body(): lax.all_to_all(notes, 'seq', split_axis=0, concat_axis=0, tiled=True)  6.3 us
    unnamed x39, local copies, waits for them, and re-layouts  6.2 us
    all_to_all x1, waiting for transfers between devices, body(): lax.all_to_all(notes, 'seq', split_axis=0, concat_axis=0, tiled=True)  5.46 us
    reshape x4, local copies, waits for them, and re-layouts, regroup(): value = value.reshape(rows, steps, KVH, group, HD).transpose(0, 2, 1, 3, 4)  5.1 us
  transfers between devices with their start and end apart: 19, of which 3 were waited for; matrix products, arithmetic and copies ran while one was open for 6% of the time, Pallas kernels for 29%

profile of v8, /device:TPU:27, one launch (start us, length us, event | category | flops | bytes accessed | tf_op | source)
XLA Modules:
  0.0 115.1 jit_solution(11174495293871830309)
XLA Ops:
  0.0 1.6 %collective-permute-start = (bf16[8,4,8192]{2,1,0:T(4,128)(2,1)}, bf16[8,4,8192]{2,1,0:T(4,128)(2,1)}, u32[]{:S(2)}, u32[]{:S(2)}) collective-permute-start(bf16[8,4,8192]{2,1,0:T(4,128)(2,1)} %param.23), channel_id=1, source_target_pairs={{4,8},{5,9},{6,10},{7,11},{8,4},{9,5},{10,6},{11,7},{20,24},{21,25... | collective-permute-start | bytes 1572872 | tf_op jit(solution)/shard_map/ppermute | solution.py:674
  1.6 4.5 %pack.1 = (bf16[2,16,8,512]{3,2,1,0:T(8,128)(2,1)}, bf16[2,16,8,512]{3,2,1,0:T(8,128)(2,1)}, bf16[2,16,8,512]{3,2,1,0:T(8,128)(2,1)}, bf16[2,16,8,512]{3,2,1,0:T...) custom-call(s32[4,4]{1,0:T(4,128)} %constant.22.clone.phase_table, ...), custom_call_target="tpu_custom_call" | custom-call | tf_op jit(solution)/shard_map/pack/pallas_call | solution.py:88
  6.1 0.9 collective-permute-start.5
  7.0 1.9 %collective-permute-start.6 = (bf16[2,16,8,512]{3,2,1,0:T(8,128)(2,1)}, bf16[2,16,8,512]{3,2,1,0:T(8,128)(2,1)S(1)}, u32[]{:S(2)}, u32[]{:S(2)}) collective-permute-start(bf16[2,16,8,512]{3,2,1,0:T(8,128)(2,1)} %get-tuple-element.47), channel_id=1, source_target_pairs={{0,5},{1,6},{2,7},{3,4},{4,13},{5,14},{6,15},{7,12},{8,1},{9,2},{1... | collective-permute-start | bytes 786440 | tf_op jit(solution)/shard_map/ppermute | solution.py:691
  8.9 2.6 %collective-permute-start.7 = (bf16[2,16,8,512]{3,2,1,0:T(8,128)(2,1)}, bf16[2,16,8,512]{3,2,1,0:T(8,128)(2,1)S(1)}, u32[]{:S(2)}, u32[]{:S(2)}) collective-permute-start(bf16[2,16,8,512]{3,2,1,0:T(8,128)(2,1)} %get-tuple-element.48), channel_id=1, source_target_pairs={{0,6},{1,7},{2,4},{3,5},{4,14},{5,15},{6,12},{7,13},{8,2},{9,3},{1... | collective-permute-start | bytes 786440 | tf_op jit(solution)/shard_map/ppermute | solution.py:691
  11.8 8.7 %collective-permute-done.5.refs_0_ = bf16[2,16,8,512]{3,2,1,0:T(8,128)(2,1)S(1)} collective-permute-done((bf16[2,16,8,512]{3,2,1,0:T(8,128)(2,1)}, bf16[2,16,8,512]{3,2,1,0:T(8,128)(2,1)S(1)}, u32[]{:S(2)}, u32[]{:S(2)}) %collective-permute-start.5) | collective-permute-done | bytes 262176 | tf_op jit(solution)/shard_map/ppermute | solution.py:691
  20.6 3.8 %collective-permute-start.9 = (bf16[2,16,8,512]{3,2,1,0:T(8,128)(2,1)}, bf16[2,16,8,512]{3,2,1,0:T(8,128)(2,1)S(1)}, u32[]{:S(2)}, u32[]{:S(2)}) collective-permute-start(bf16[2,16,8,512]{3,2,1,0:T(8,128)(2,1)} %get-tuple-element.51), channel_id=1, source_target_pairs={{0,1},{1,2},{2,3},{3,0},{4,5},{5,6},{6,7},{7,4},{8,9},{9,10},{10,1... | collective-permute-start | bytes 786440 | tf_op jit(solution)/shard_map/ppermute | solution.py:691
  24.4 3.8 %collective-permute-done.6.refs_1_ = bf16[2,16,8,512]{3,2,1,0:T(8,128)(2,1)S(1)} collective-permute-done((bf16[2,16,8,512]{3,2,1,0:T(8,128)(2,1)}, bf16[2,16,8,512]{3,2,1,0:T(8,128)(2,1)S(1)}, u32[]{:S(2)}, u32[]{:S(2)}) %collective-permute-start.6) | collective-permute-done | bytes 262176 | tf_op jit(solution)/shard_map/ppermute | solution.py:691
  28.2 1.5 %collective-permute-start.10 = (bf16[2,16,8,512]{3,2,1,0:T(8,128)(2,1)}, bf16[2,16,8,512]{3,2,1,0:T(8,128)(2,1)S(1)}, u32[]{:S(2)}, u32[]{:S(2)}) collective-permute-start(bf16[2,16,8,512]{3,2,1,0:T(8,128)(2,1)} %get-tuple-element.52), channel_id=1, source_target_pairs={{0,2},{1,3},{2,0},{3,1},{4,6},{5,7},{6,4},{7,5},{8,10},{9,11},{10,... | collective-permute-start | bytes 786440 | tf_op jit(solution)/shard_map/ppermute | solution.py:691
  29.7 3.0 %note.1 = s32[16,384]{1,0:T(8,128)} custom-call(s32[128]{0:T(128)} %bitcast.24, s32[128]{0:T(128)} %rows.1, s32[8]{0:T(128)} %lens.9), custom_call_target="tpu_custom_call" | custom-call | tf_op jit(solution)/shard_map/note/pallas_call | solution.py:147
  32.7 1.4 %copy.19 = s32[16,1,384]{2,1,0:T(1,128)} copy(s32[16,1,384]{2,0,1:T(8,128)} %bitcast.22) | data formatting | bytes 49152 | tf_op jit(solution)/shard_map/all_to_all | solution.py:706
  34.1 6.3 %all-to-all-start = ((s32[16,1,384]{2,1,0:T(1,128)}), s32[16,1,384]{2,1,0:T(1,128)S(1)}, u32[]{:S(2)}, u32[]{:S(2)}) async-start(s32[16,1,384]{2,1,0:T(1,128)} %copy.19), calls=%async_computation | async-start | bytes 49152 | tf_op jit(solution)/shard_map/all_to_all | solution.py:706
  41.1 5.5 %all-to-all-done = s32[16,1,384]{2,1,0:T(1,128)S(1)} async-done(((s32[16,1,384]{2,1,0:T(1,128)}), s32[16,1,384]{2,1,0:T(1,128)S(1)}, u32[]{:S(2)}, u32[]{:S(2)}) %all-to-all-start) | async-done | bytes 24608 | tf_op jit(solution)/shard_map/all_to_all | solution.py:706
  46.9 1.6 %reshape.24 = bf16[8,4,4,16,128]{4,3,2,1,0:T(8,128)(2,1)S(1)} reshape(bf16[8,4,8192]{2,1,0:T(4,128)(2,1)} %collective-permute-done) | data formatting | bytes 1048576 | tf_op jit(solution)/shard_map/reshape | solution.py:698
  48.7 3.0 %collective-permute-start.12 = (bf16[2,16,8,512]{3,2,1,0:T(8,128)(2,1)}, bf16[2,16,8,512]{3,2,1,0:T(8,128)(2,1)S(1)}, u32[]{:S(2)}, u32[]{:S(2)}) collective-permute-start(bf16[2,16,8,512]{3,2,1,0:T(8,128)(2,1)} %get-tuple-element.54), channel_id=1, source_target_pairs={{0,12},{1,13},{2,14},{3,15},{4,4},{5,5},{6,6},{7,7},{8,8},{9,9},{1... | collective-permute-start | bytes 786440 | tf_op jit(solution)/shard_map/ppermute | solution.py:691
  51.7 3.3 %collective-permute-start.13 = (bf16[2,16,8,512]{3,2,1,0:T(8,128)(2,1)}, bf16[2,16,8,512]{3,2,1,0:T(8,128)(2,1)S(1)}, u32[]{:S(2)}, u32[]{:S(2)}) collective-permute-start(bf16[2,16,8,512]{3,2,1,0:T(8,128)(2,1)} %get-tuple-element.55), channel_id=1, source_target_pairs={{0,13},{1,14},{2,15},{3,12},{4,5},{5,6},{6,7},{7,4},{8,9},{9,10},{... | collective-permute-start | bytes 786440 | tf_op jit(solution)/shard_map/ppermute | solution.py:691
  54.9 1.5 %collective-permute-start.14 = (bf16[2,16,8,512]{3,2,1,0:T(8,128)(2,1)}, bf16[2,16,8,512]{3,2,1,0:T(8,128)(2,1)}, u32[]{:S(2)}, u32[]{:S(2)}) collective-permute-start(bf16[2,16,8,512]{3,2,1,0:T(8,128)(2,1)} %get-tuple-element.56), channel_id=1, source_target_pairs={{0,14},{1,15},{2,12},{3,13},{4,6},{5,7},{6,4},{7,5},{8,10},{9,11},... | collective-permute-start | bytes 786440 | tf_op jit(solution)/shard_map/ppermute | solution.py:691
  56.5 0.9 copy-done.4
  57.4 5.9 %shard_map.155 = (bf16[8,4,64,128]{3,2,1,0:T(8,128)(2,1)}, f32[8,4,2,64]{3,2,1,0:T(2,128)S(1)}) custom-call(s32[4,16]{1,0:T(4,128)S(1)} %dynamic-slice_bitcast_fusion.stages.mine, s32[32,16]{1,0:T(8,128)S(1)} %get-tuple-element.36.place_of, s32[32,16]{1,0:T(8,128)S(1)} %get-tuple-element.37.row_of, s32[32,16]{1,0:T(8,128)S(1)} %get-tuple-element.38.rank_of, ...), custom_call_target="tpu_custom_call" | custom-call | flops 1000000000 | bytes 12582912 | tf_op jit(solution)/shard_map/pallas_call | solution.py:571
  63.9 0.7 collective-permute-start.16
  64.6 1.5 %collective-permute-start.15 = (bf16[2,16,8,512]{3,2,1,0:T(8,128)(2,1)}, bf16[2,16,8,512]{3,2,1,0:T(8,128)(2,1)}, u32[]{:S(2)}, u32[]{:S(2)}) collective-permute-start(bf16[2,16,8,512]{3,2,1,0:T(8,128)(2,1)} %get-tuple-element.57), channel_id=1, source_target_pairs={{0,15},{1,12},{2,13},{3,14},{4,7},{5,4},{6,5},{7,6},{8,11},{9,8},{... | collective-permute-start | bytes 786440 | tf_op jit(solution)/shard_map/ppermute | solution.py:691
  66.2 2.4 %reshape.20 = bf16[8,4,4,16,128]{4,3,2,1,0:T(8,128)(2,1)} reshape(bf16[8,4,8192]{2,1,0:T(4,128)(2,1)} %param.23) | data formatting | bytes 1048576 | tf_op jit(solution)/shard_map/reshape | solution.py:698
  68.5 1.1 copy.20
  69.7 10.6 %collective-permute-start.2 = (bf16[2,16,8,512]{3,2,1,0:T(8,128)(2,1)}, bf16[2,16,8,512]{3,2,1,0:T(8,128)(2,1)S(1)}, u32[]{:S(2)}, u32[]{:S(2)}) collective-permute-start(bf16[2,16,8,512]{3,2,1,0:T(8,128)(2,1)} %get-tuple-element.43), channel_id=1, source_target_pairs={{0,5},{1,6},{2,7},{3,4},{4,1},{5,2},{6,3},{7,0},{8,13},{9,14},{10,... | collective-permute-start | bytes 786440 | tf_op jit(solution)/shard_map/ppermute | solution.py:691
  80.2 2.8 %collective-permute-start.3 = (bf16[2,16,8,512]{3,2,1,0:T(8,128)(2,1)}, bf16[2,16,8,512]{3,2,1,0:T(8,128)(2,1)S(1)}, u32[]{:S(2)}, u32[]{:S(2)}) collective-permute-start(bf16[2,16,8,512]{3,2,1,0:T(8,128)(2,1)} %get-tuple-element.44), channel_id=1, source_target_pairs={{0,6},{1,7},{2,4},{3,5},{4,2},{5,3},{6,0},{7,1},{8,14},{9,15},{10,... | collective-permute-start | bytes 786440 | tf_op jit(solution)/shard_map/ppermute | solution.py:691
  83.0 0.8 copy-done.6
  83.8 0.8 copy-done.7
  85.2 7.4 %resident.1 = (f32[8,4,64,128]{3,2,1,0:T(8,128)S(1)}, f32[8,4,64,128]{3,2,1,0:T(8,128)}, f32[8,4,64,128]{3,2,1,0:T(8,128)}) custom-call(s32[8]{0:T(128)S(1)} %copy-done.16, bf16[8,4,64,128]{3,2,1,0:T(8,128)(2,1)S(1)} %bitcast.15, bf16[8,4,512]{2,1,0:T(4,128)(2,1)S(1)} %copy-done.6, bf16[8,4,512]{2,1,0:T(4,128)(2,1)S(1)} %copy-done.7, ...), custom_call_target="tpu_custom_call" | custom-call | flops 2000000000 | bytes 16777216 | tf_op jit(solution)/shard_map/resident/pallas_call | solution.py:365
  93.4 1.2 %copy-done = f32[8,4,64,128]{3,2,1,0:T(8,128)S(1)} copy-done((f32[8,4,64,128]{3,2,1,0:T(8,128)S(1)}, f32[8,4,64,128]{3,2,1,0:T(8,128)}, u32[]{:S(2)}) %copy-start) | copy-done | bytes 1048600
  94.6 1.2 %copy-done.1 = f32[8,4,64,128]{3,2,1,0:T(8,128)S(1)} copy-done((f32[8,4,64,128]{3,2,1,0:T(8,128)S(1)}, f32[8,4,64,128]{3,2,1,0:T(8,128)}, u32[]{:S(2)}) %copy-start.1) | copy-done | bytes 1048600
  95.8 12.0 %shard_map.154 = (f32[8,4,64,128]{3,2,1,0:T(8,128)S(1)}, f32[8,4,64,128]{3,2,1,0:T(8,128)S(1)}, f32[8,4,64,128]{3,2,1,0:T(8,128)S(1)}) custom-call(s32[4,16]{1,0:T(4,128)S(1)} %copy-done.14, s32[32,16]{1,0:T(8,128)S(1)} %get-tuple-element.36.place_of, s32[32,16]{1,0:T(8,128)S(1)} %get-tuple-element.37.row_of, s32[32,16]{1,0:T(8,128)S(1)} %get-tuple-element.38.rank_of, ...), custom_call_target="tpu_custom_call" | custom-call | flops 1000000000 | bytes 12582912 | tf_op jit(solution)/shard_map/pallas_call | solution.py:571
  107.8 7.2 %shard_map.156 = bf16[8,4,8192]{2,1,0:T(4,128)(2,1)} custom-call(s32[4,16]{1,0:T(4,128)S(1)} %copy-done.14, s32[32,16]{1,0:T(8,128)S(1)} %get-tuple-element.36.place_of, s32[32,16]{1,0:T(8,128)S(1)} %get-tuple-element.37.row_of, s32[32,16]{1,0:T(8,128)S(1)} %get-tuple-element.38.rank_of, s32[32,16]{1,0:T(8,128)S(1)} %get-tuple-element.39.used, ...), custom_call_target="tpu_custom_call" | custom-call | flops 1000000000 | bytes 12582912 | tf_op jit(solution)/shard_map/pallas_call | solution.py:571
  (58 shorter events, 3.5 us)
Async XLA Ops:
  0.0 56.4 %copy-start.8 = (f32[16,128]{1,0:T(8,128)S(1)}, f32[16,128]{1,0:T(8,128)}, u32[]{:S(2)}) copy-start(f32[16,128]{1,0:T(8,128)} %constant.24.clone.ca) | copy-start | bytes 24580
  0.0 56.4 %copy-start.9 = (f32[16,128]{1,0:T(8,128)S(1)}, f32[16,128]{1,0:T(8,128)}, u32[]{:S(2)}) copy-start(f32[16,128]{1,0:T(8,128)} %constant.25.clone.sa) | copy-start | bytes 24580
  0.0 56.4 %copy-start.2 = (f32[321,128]{1,0:T(8,128)S(1)}, f32[321,128]{1,0:T(8,128)}, u32[]{:S(2)}) copy-start(f32[321,128]{1,0:T(8,128)} %constant.26.clone.cb) | copy-start | bytes 493060
  0.0 56.4 %copy-start.3 = (f32[321,128]{1,0:T(8,128)S(1)}, f32[321,128]{1,0:T(8,128)}, u32[]{:S(2)}) copy-start(f32[321,128]{1,0:T(8,128)} %constant.27.clone.sb) | copy-start | bytes 493060
  0.0 56.4 %copy-start.15 = (s32[8]{0:T(128)S(1)}, s32[8]{0:T(128)}, u32[]{:S(2)}) copy-start(s32[8]{0:T(128)} %lens.9) | copy-start | bytes 100
  0.0 29.7 %collective-permute-start = (bf16[8,4,8192]{2,1,0:T(4,128)(2,1)}, bf16[8,4,8192]{2,1,0:T(4,128)(2,1)}, u32[]{:S(2)}, u32[]{:S(2)}) collective-permute-start(bf16[8,4,8192]{2,1,0:T(4,128)(2,1)} %param.23), channel_id=1, source_target_pairs={{4,8},{5,9},{6,10},{7,11},{8,4},{9,5},{10,6},{11,7},{20,24},{21,25... | collective-permute-start | bytes 1572872 | tf_op jit(solution)/shard_map/ppermute | solution.py:674
  6.1 14.5 %collective-permute-start.5 = (bf16[2,16,8,512]{3,2,1,0:T(8,128)(2,1)}, bf16[2,16,8,512]{3,2,1,0:T(8,128)(2,1)S(1)}, u32[]{:S(2)}, u32[]{:S(2)}) collective-permute-start(bf16[2,16,8,512]{3,2,1,0:T(8,128)(2,1)} %get-tuple-element.46), channel_id=1, source_target_pairs={{0,4},{1,5},{2,6},{3,7},{4,12},{5,13},{6,14},{7,15},{8,0},{9,1},{1... | collective-permute-start | bytes 786440 | tf_op jit(solution)/shard_map/ppermute | solution.py:691
  7.0 21.2 %collective-permute-start.6 = (bf16[2,16,8,512]{3,2,1,0:T(8,128)(2,1)}, bf16[2,16,8,512]{3,2,1,0:T(8,128)(2,1)S(1)}, u32[]{:S(2)}, u32[]{:S(2)}) collective-permute-start(bf16[2,16,8,512]{3,2,1,0:T(8,128)(2,1)} %get-tuple-element.47), channel_id=1, source_target_pairs={{0,5},{1,6},{2,7},{3,4},{4,13},{5,14},{6,15},{7,12},{8,1},{9,2},{1... | collective-permute-start | bytes 786440 | tf_op jit(solution)/shard_map/ppermute | solution.py:691
  8.9 39.7 %collective-permute-start.7 = (bf16[2,16,8,512]{3,2,1,0:T(8,128)(2,1)}, bf16[2,16,8,512]{3,2,1,0:T(8,128)(2,1)S(1)}, u32[]{:S(2)}, u32[]{:S(2)}) collective-permute-start(bf16[2,16,8,512]{3,2,1,0:T(8,128)(2,1)} %get-tuple-element.48), channel_id=1, source_target_pairs={{0,6},{1,7},{2,4},{3,5},{4,14},{5,15},{6,12},{7,13},{8,2},{9,3},{1... | collective-permute-start | bytes 786440 | tf_op jit(solution)/shard_map/ppermute | solution.py:691
  11.5 37.2 %collective-permute-start.8 = (bf16[2,16,8,512]{3,2,1,0:T(8,128)(2,1)}, bf16[2,16,8,512]{3,2,1,0:T(8,128)(2,1)S(1)}, u32[]{:S(2)}, u32[]{:S(2)}) collective-permute-start(bf16[2,16,8,512]{3,2,1,0:T(8,128)(2,1)} %get-tuple-element.49), channel_id=1, source_target_pairs={{0,7},{1,4},{2,5},{3,6},{4,15},{5,12},{6,13},{7,14},{8,3},{9,0},{1... | collective-permute-start | bytes 786440 | tf_op jit(solution)/shard_map/ppermute | solution.py:691
  20.6 31.1 %collective-permute-start.9 = (bf16[2,16,8,512]{3,2,1,0:T(8,128)(2,1)}, bf16[2,16,8,512]{3,2,1,0:T(8,128)(2,1)S(1)}, u32[]{:S(2)}, u32[]{:S(2)}) collective-permute-start(bf16[2,16,8,512]{3,2,1,0:T(8,128)(2,1)} %get-tuple-element.51), channel_id=1, source_target_pairs={{0,1},{1,2},{2,3},{3,0},{4,5},{5,6},{6,7},{7,4},{8,9},{9,10},{10,1... | collective-permute-start | bytes 786440 | tf_op jit(solution)/shard_map/ppermute | solution.py:691
  28.2 26.8 %collective-permute-start.10 = (bf16[2,16,8,512]{3,2,1,0:T(8,128)(2,1)}, bf16[2,16,8,512]{3,2,1,0:T(8,128)(2,1)S(1)}, u32[]{:S(2)}, u32[]{:S(2)}) collective-permute-start(bf16[2,16,8,512]{3,2,1,0:T(8,128)(2,1)} %get-tuple-element.52), channel_id=1, source_target_pairs={{0,2},{1,3},{2,0},{3,1},{4,6},{5,7},{6,4},{7,5},{8,10},{9,11},{10,... | collective-permute-start | bytes 786440 | tf_op jit(solution)/shard_map/ppermute | solution.py:691
  29.7 26.7 %collective-permute-start.11 = (bf16[2,16,8,512]{3,2,1,0:T(8,128)(2,1)}, bf16[2,16,8,512]{3,2,1,0:T(8,128)(2,1)S(1)}, u32[]{:S(2)}, u32[]{:S(2)}) collective-permute-start(bf16[2,16,8,512]{3,2,1,0:T(8,128)(2,1)} %get-tuple-element.53), channel_id=1, source_target_pairs={{0,3},{1,0},{2,1},{3,2},{4,7},{5,4},{6,5},{7,6},{8,11},{9,8},{10,9... | collective-permute-start | bytes 786440 | tf_op jit(solution)/shard_map/ppermute | solution.py:691
  34.1 12.4 %all-to-all-start = ((s32[16,1,384]{2,1,0:T(1,128)}), s32[16,1,384]{2,1,0:T(1,128)S(1)}, u32[]{:S(2)}, u32[]{:S(2)}) async-start(s32[16,1,384]{2,1,0:T(1,128)} %copy.19), calls=%async_computation | async-start | bytes 49152 | tf_op jit(solution)/shard_map/all_to_all | solution.py:706
  41.1 22.3 %copy-start.13 = (s32[4,16]{1,0:T(4,128)}, s32[4,16]{1,0:T(4,128)S(1)}, u32[]{:S(2)}) copy-start(s32[4,16]{1,0:T(4,128)S(1)} %dynamic-slice_bitcast_fusion.stages.mine) | copy-start | bytes 772
  46.9 16.4 %copy-start.11 = (s32[16,128]{1,0:T(8,128)}, s32[16,128]{1,0:T(8,128)S(1)}, u32[]{:S(2)}) copy-start(s32[16,128]{1,0:T(8,128)S(1)} %get-tuple-element.40.tally) | copy-start | bytes 24580
  48.6 16.1 %collective-permute-start.1 = (bf16[2,16,8,512]{3,2,1,0:T(8,128)(2,1)}, bf16[2,16,8,512]{3,2,1,0:T(8,128)(2,1)S(1)}, u32[]{:S(2)}, u32[]{:S(2)}) collective-permute-start(bf16[2,16,8,512]{3,2,1,0:T(8,128)(2,1)} %get-tuple-element.42), channel_id=1, source_target_pairs={{0,4},{1,5},{2,6},{3,7},{4,0},{5,1},{6,2},{7,3},{8,12},{9,13},{10,... | collective-permute-start | bytes 786440 | tf_op jit(solution)/shard_map/ppermute | solution.py:691
  48.7 21.0 %collective-permute-start.12 = (bf16[2,16,8,512]{3,2,1,0:T(8,128)(2,1)}, bf16[2,16,8,512]{3,2,1,0:T(8,128)(2,1)S(1)}, u32[]{:S(2)}, u32[]{:S(2)}) collective-permute-start(bf16[2,16,8,512]{3,2,1,0:T(8,128)(2,1)} %get-tuple-element.54), channel_id=1, source_target_pairs={{0,12},{1,13},{2,14},{3,15},{4,4},{5,5},{6,6},{7,7},{8,8},{9,9},{1... | collective-permute-start | bytes 786440 | tf_op jit(solution)/shard_map/ppermute | solution.py:691
  51.7 28.6 %collective-permute-start.13 = (bf16[2,16,8,512]{3,2,1,0:T(8,128)(2,1)}, bf16[2,16,8,512]{3,2,1,0:T(8,128)(2,1)S(1)}, u32[]{:S(2)}, u32[]{:S(2)}) collective-permute-start(bf16[2,16,8,512]{3,2,1,0:T(8,128)(2,1)} %get-tuple-element.55), channel_id=1, source_target_pairs={{0,13},{1,14},{2,15},{3,12},{4,5},{5,6},{6,7},{7,4},{8,9},{9,10},{... | collective-permute-start | bytes 786440 | tf_op jit(solution)/shard_map/ppermute | solution.py:691
  54.9 28.1 %collective-permute-start.14 = (bf16[2,16,8,512]{3,2,1,0:T(8,128)(2,1)}, bf16[2,16,8,512]{3,2,1,0:T(8,128)(2,1)}, u32[]{:S(2)}, u32[]{:S(2)}) collective-permute-start(bf16[2,16,8,512]{3,2,1,0:T(8,128)(2,1)} %get-tuple-element.56), channel_id=1, source_target_pairs={{0,14},{1,15},{2,12},{3,13},{4,6},{5,7},{6,4},{7,5},{8,10},{9,11},... | collective-permute-start | bytes 786440 | tf_op jit(solution)/shard_map/ppermute | solution.py:691
  63.9 43.9 %collective-permute-start.16 = (bf16[8,4,64,128]{3,2,1,0:T(8,128)(2,1)}, bf16[8,4,64,128]{3,2,1,0:T(8,128)(2,1)S(1)}, u32[]{:S(2)}, u32[]{:S(2)}) collective-permute-start(bf16[8,4,64,128]{3,2,1,0:T(8,128)(2,1)} %get-tuple-element.65), channel_id=1, source_target_pairs={{4,8},{5,9},{6,10},{7,11},{8,4},{9,5},{10,6},{11,7},{20,24},{21,25... | collective-permute-start | bytes 1572872 | tf_op jit(solution)/shard_map/ppermute | solution.py:717
  64.6 28.0 %collective-permute-start.15 = (bf16[2,16,8,512]{3,2,1,0:T(8,128)(2,1)}, bf16[2,16,8,512]{3,2,1,0:T(8,128)(2,1)}, u32[]{:S(2)}, u32[]{:S(2)}) collective-permute-start(bf16[2,16,8,512]{3,2,1,0:T(8,128)(2,1)} %get-tuple-element.57), channel_id=1, source_target_pairs={{0,15},{1,12},{2,13},{3,14},{4,7},{5,4},{6,5},{7,6},{8,11},{9,8},{... | collective-permute-start | bytes 786440 | tf_op jit(solution)/shard_map/ppermute | solution.py:691
  69.7 38.1 %collective-permute-start.2 = (bf16[2,16,8,512]{3,2,1,0:T(8,128)(2,1)}, bf16[2,16,8,512]{3,2,1,0:T(8,128)(2,1)S(1)}, u32[]{:S(2)}, u32[]{:S(2)}) collective-permute-start(bf16[2,16,8,512]{3,2,1,0:T(8,128)(2,1)} %get-tuple-element.43), channel_id=1, source_target_pairs={{0,5},{1,6},{2,7},{3,4},{4,1},{5,2},{6,3},{7,0},{8,13},{9,14},{10,... | collective-permute-start | bytes 786440 | tf_op jit(solution)/shard_map/ppermute | solution.py:691
  80.2 27.6 %collective-permute-start.3 = (bf16[2,16,8,512]{3,2,1,0:T(8,128)(2,1)}, bf16[2,16,8,512]{3,2,1,0:T(8,128)(2,1)S(1)}, u32[]{:S(2)}, u32[]{:S(2)}) collective-permute-start(bf16[2,16,8,512]{3,2,1,0:T(8,128)(2,1)} %get-tuple-element.44), channel_id=1, source_target_pairs={{0,6},{1,7},{2,4},{3,5},{4,2},{5,3},{6,0},{7,1},{8,14},{9,15},{10,... | collective-permute-start | bytes 786440 | tf_op jit(solution)/shard_map/ppermute | solution.py:691
  83.0 24.8 %collective-permute-start.4 = (bf16[2,16,8,512]{3,2,1,0:T(8,128)(2,1)}, bf16[2,16,8,512]{3,2,1,0:T(8,128)(2,1)S(1)}, u32[]{:S(2)}, u32[]{:S(2)}) collective-permute-start(bf16[2,16,8,512]{3,2,1,0:T(8,128)(2,1)} %get-tuple-element.45), channel_id=1, source_target_pairs={{0,7},{1,4},{2,5},{3,6},{4,3},{5,0},{6,1},{7,2},{8,15},{9,12},{10,... | collective-permute-start | bytes 786440 | tf_op jit(solution)/shard_map/ppermute | solution.py:691
  85.2 7.4 %copy-start.18 = (f32[8,4,2,64]{3,2,1,0:T(2,128)S(1)}, f32[8,4,2,64]{3,2,1,0:T(2,128)}, u32[]{:S(2)}) copy-start(f32[8,4,2,64]{3,2,1,0:T(2,128)} %copy-done.17) | copy-start | bytes 49156
  85.2 8.1 %copy-start.5 = (bf16[2,16,8,512]{3,2,1,0:T(8,128)(2,1)S(1)}, bf16[2,16,8,512]{3,2,1,0:T(8,128)(2,1)}, u32[]{:S(2)}) copy-start(bf16[2,16,8,512]{3,2,1,0:T(8,128)(2,1)} %get-tuple-element.50.refs_4_) | copy-start | bytes 786436
  85.2 8.1 %copy-start.10 = (f32[16,128]{1,0:T(8,128)S(1)}, f32[16,128]{1,0:T(8,128)}, u32[]{:S(2)}) copy-start(f32[16,128]{1,0:T(8,128)} %constant.25.clone.sa) | copy-start | bytes 24580
  85.2 8.1 %copy-start.12 = (s32[16,128]{1,0:T(8,128)S(1)}, s32[16,128]{1,0:T(8,128)}, u32[]{:S(2)}) copy-start(s32[16,128]{1,0:T(8,128)} %copy-done.11) | copy-start | bytes 24580
  85.2 8.1 %copy-start.14 = (s32[4,16]{1,0:T(4,128)S(1)}, s32[4,16]{1,0:T(4,128)}, u32[]{:S(2)}) copy-start(s32[4,16]{1,0:T(4,128)} %copy-done.13) | copy-start | bytes 772
  92.6 15.2 %collective-permute-start.17 = (f32[8,4,2,64]{3,2,1,0:T(2,128)S(1)}, f32[8,4,2,64]{3,2,1,0:T(2,128)S(1)}, u32[]{:S(2)}, u32[]{:S(2)}) collective-permute-start(f32[8,4,2,64]{3,2,1,0:T(2,128)S(1)} %copy-done.18), channel_id=1, source_target_pairs={{4,8},{5,9},{6,10},{7,11},{8,4},{9,5},{10,6},{11,7},{20,24},{21,25... | collective-permute-start | bytes 49160 | tf_op jit(solution)/shard_map/ppermute | solution.py:718
  93.3 1.2 %copy-start = (f32[8,4,64,128]{3,2,1,0:T(8,128)S(1)}, f32[8,4,64,128]{3,2,1,0:T(8,128)}, u32[]{:S(2)}) copy-start(f32[8,4,64,128]{3,2,1,0:T(8,128)} %get-tuple-element.59.refs_13_) | copy-start | bytes 3145732
  (6 other events, 4.9 us)

commit v9 on v8

--- a/solution.py
+++ b/solution.py
@@ -386,13 +386,13 @@
 ):
     messages = refs[:count]
     refs = refs[count:]
-    before = refs[:3]
+    before = refs[: 4 if kind == "final" else 3]
     if kind == "partial":
         out, stats, acc, top, total, kbuf, vbuf = refs
     elif kind == "state":
-        acc, top, total, kbuf, vbuf = refs[3:]
+        stats, acc, top, total, theirs, kbuf, vbuf = refs[3:]
     else:
-        part, stats, out, acc, top, total, scr, kbuf, vbuf = refs[3:]
+        part, out, acc, top, total, scr, kbuf, vbuf = refs[4:]
     state = (acc, top, total)
     rows = q_ref.shape[0]
     width = q_ref.shape[2]
@@ -480,8 +480,8 @@
             for i in range(2):
                 stats[r, head, pl.ds(i, 1), :] = lines[i]
 
-    def with_part(r, new):
-        merged = []
+    def with_stats(r, new):
+        merged, factors = [], []
         for head in range(KVH):
             lines = []
             for i in range(2):
@@ -492,22 +492,27 @@
             value, old_top, amount = new[head]
             new_top = jnp.maximum(old_top, other_top)
             mine = jnp.exp(old_top - new_top)
-            theirs = jnp.exp(other_top - new_top) * other_total
-            merged.append(
-                (
-                    value * mine + part[r, head].astype(jnp.float32) * theirs,
-                    new_top,
-                    amount * mine + theirs,
-                )
-            )
-        return merged
+            factor = jnp.exp(other_top - new_top) * other_total
+            merged.append((value * mine, new_top, amount * mine + factor))
+            factors.append(factor)
+        return merged, factors
 
     def state_rows(pair):
-        new = [blend(row_queries(r, q_ref), [block(r, 0)], held(r, before)) for r in pair]
-        for r, one in zip(pair, new):
+        for r in pair:
+            hold(r, state, held(r, before))
+            beyond(r)
+        new = [blend(row_queries(r, q_ref), [block(r, 0)], held(r, state)) for r in pair]
+        done = [with_stats(r, one) for r, one in zip(pair, new)]
+        for r, (one, factors) in zip(pair, done):
             hold(r, state, one)
-        for r in pair:
-            beyond(r)
+            for head in range(KVH):
+                theirs[r, head] = factors[head]
+
+    def with_values(r):
+        return [
+            (value + part[r, head].astype(jnp.float32) * before[3][r, head], old_top, amount)
+            for head, (value, old_top, amount) in enumerate(held(r, before[:3]))
+        ]
 
     def put_out(pair, new):
         done = [value / amount for one in new for value, _, amount in one]
@@ -524,8 +529,7 @@
                     ].astype(jnp.bfloat16)
 
     def final_rows(pair):
-        new = [blend(row_queries(r, q_ref), [block(r, 0)], held(r, before)) for r in pair]
-        new = [with_part(r, one) for r, one in zip(pair, new)]
+        new = [blend(row_queries(r, q_ref), [block(r, 0)], with_values(r)) for r in pair]
         put_out(pair, new)
         longest = functools.reduce(jnp.maximum, [tally[8 + kernel, r] for r in pair])
 
@@ -564,6 +568,7 @@
         scratch += running
     elif kind == "state":
         out_shape = state_shapes(rows, width)
+        out_shape += out_shape[:1]
     else:
         out_shape = jax.ShapeDtypeStruct((rows, steps, QH * HD), jnp.bfloat16)
         scratch += running + [pltpu.VMEM((2 * KVH, width, HD), jnp.float32)]
@@ -718,11 +723,11 @@
     stats = lax.ppermute(stats, "seq", swap)
     state = span(
         "state", 1, 0, cap, scalars, grouped, tables,
-        got["d"] + got["f"] + got["g"], tuple(state), (), steps,
+        got["d"] + got["f"] + got["g"], tuple(state), (stats,), steps,
     )
     return span(
         "final", 2, 3 * in_plane, cap, scalars, grouped, tables,
-        got["b"], tuple(state), (partial, stats), steps,
+        got["b"], tuple(state), (partial,), steps,
     )
 
 

time: 116 us -> 122 us (1.052)
  waiting for transfers between devices: 18 us -> 23.9 us
  starting transfers between devices: 43 us -> 44.3 us
    ppermute x15, waiting for transfers between devices: 12.6 us -> 18.4 us  [send(): value = lax.ppermute(value, 'seq', pairs)]
    unnamed x39 -> x35, local copies, waits for them, and re-layouts: 6.2 us -> 5.6 us
  transfers between devices with their start and end apart: 19 -> 19, of which waited for: 3 -> 5; matrix products, arithmetic and copies ran while one was open for 6% -> 6% of each run, Pallas kernels for 29% -> 27%
where the time goes in v9:
time: 122 us
  starting transfers between devices  44.3 us (36%)
  Pallas kernels  40.5 us (33%)
  waiting for transfers between devices  23.9 us (20%)
  local copies, waits for them, and re-layouts  12.8 us (10%)
    ppermute x15, starting transfers between devices, send(): value = lax.ppermute(value, 'seq', pairs)  34.5 us
    pallas_call x3, Pallas kernels, span(): pl.pallas_call(functools.partial(span_kernel, kind, kernel, first, count,...  25.3 us
    ppermute x15, waiting for transfers between devices, send(): value = lax.ppermute(value, 'seq', pairs)  18.4 us
    pallas_call x1, Pallas kernels, resident(): pl.pallas_call(resident_kernel, out_shape=state_shapes(rows, grouped.shap...  7.36 us
    all_to_all x1, starting transfers between devices, body(): lax.all_to_all(notes, 'seq', split_axis=0, concat_axis=0, tiled=True)  6.3 us
    unnamed x35, local copies, waits for them, and re-layouts  5.6 us
    all_to_all x1, waiting for transfers between devices, body(): lax.all_to_all(notes, 'seq', split_axis=0, concat_axis=0, tiled=True)  5.45 us
    reshape x4, local copies, waits for them, and re-layouts, regroup(): value = value.reshape(rows, steps, KVH, group, HD).transpose(0, 2, 1, 3, 4)  5.1 us
  transfers between devices with their start and end apart: 19, of which 5 were waited for; matrix products, arithmetic and copies ran while one was open for 6% of the time, Pallas kernels for 27%

profile of v9, /device:TPU:27, one launch (start us, length us, event | category | flops | bytes accessed | tf_op | source)
XLA Modules:
  0.0 121.7 jit_solution(3390713891149413582)
XLA Ops:
  0.0 1.6 %collective-permute-start = (bf16[8,4,8192]{2,1,0:T(4,128)(2,1)}, bf16[8,4,8192]{2,1,0:T(4,128)(2,1)}, u32[]{:S(2)}, u32[]{:S(2)}) collective-permute-start(bf16[8,4,8192]{2,1,0:T(4,128)(2,1)} %param.23), channel_id=1, source_target_pairs={{4,8},{5,9},{6,10},{7,11},{8,4},{9,5},{10,6},{11,7},{20,24},{21,25... | collective-permute-start | bytes 1572872 | tf_op jit(solution)/shard_map/ppermute | solution.py:679
  1.6 4.5 %pack.1 = (bf16[2,16,8,512]{3,2,1,0:T(8,128)(2,1)}, bf16[2,16,8,512]{3,2,1,0:T(8,128)(2,1)}, bf16[2,16,8,512]{3,2,1,0:T(8,128)(2,1)}, bf16[2,16,8,512]{3,2,1,0:T...) custom-call(s32[4,4]{1,0:T(4,128)} %constant.22.clone.phase_table, ...), custom_call_target="tpu_custom_call" | custom-call | tf_op jit(solution)/shard_map/pack/pallas_call | solution.py:88
  6.1 0.9 collective-permute-start.5
  7.0 1.9 %collective-permute-start.6 = (bf16[2,16,8,512]{3,2,1,0:T(8,128)(2,1)}, bf16[2,16,8,512]{3,2,1,0:T(8,128)(2,1)S(1)}, u32[]{:S(2)}, u32[]{:S(2)}) collective-permute-start(bf16[2,16,8,512]{3,2,1,0:T(8,128)(2,1)} %get-tuple-element.48), channel_id=1, source_target_pairs={{0,5},{1,6},{2,7},{3,4},{4,13},{5,14},{6,15},{7,12},{8,1},{9,2},{1... | collective-permute-start | bytes 786440 | tf_op jit(solution)/shard_map/ppermute | solution.py:696
  8.8 2.6 %collective-permute-start.7 = (bf16[2,16,8,512]{3,2,1,0:T(8,128)(2,1)}, bf16[2,16,8,512]{3,2,1,0:T(8,128)(2,1)S(1)}, u32[]{:S(2)}, u32[]{:S(2)}) collective-permute-start(bf16[2,16,8,512]{3,2,1,0:T(8,128)(2,1)} %get-tuple-element.49), channel_id=1, source_target_pairs={{0,6},{1,7},{2,4},{3,5},{4,14},{5,15},{6,12},{7,13},{8,2},{9,3},{1... | collective-permute-start | bytes 786440 | tf_op jit(solution)/shard_map/ppermute | solution.py:696
  11.8 8.8 %collective-permute-done.5.refs_0_ = bf16[2,16,8,512]{3,2,1,0:T(8,128)(2,1)S(1)} collective-permute-done((bf16[2,16,8,512]{3,2,1,0:T(8,128)(2,1)}, bf16[2,16,8,512]{3,2,1,0:T(8,128)(2,1)S(1)}, u32[]{:S(2)}, u32[]{:S(2)}) %collective-permute-start.5) | collective-permute-done | bytes 262176 | tf_op jit(solution)/shard_map/ppermute | solution.py:696
  20.6 3.8 %collective-permute-start.9 = (bf16[2,16,8,512]{3,2,1,0:T(8,128)(2,1)}, bf16[2,16,8,512]{3,2,1,0:T(8,128)(2,1)S(1)}, u32[]{:S(2)}, u32[]{:S(2)}) collective-permute-start(bf16[2,16,8,512]{3,2,1,0:T(8,128)(2,1)} %get-tuple-element.52), channel_id=1, source_target_pairs={{0,1},{1,2},{2,3},{3,0},{4,5},{5,6},{6,7},{7,4},{8,9},{9,10},{10,1... | collective-permute-start | bytes 786440 | tf_op jit(solution)/shard_map/ppermute | solution.py:696
  24.4 3.8 %collective-permute-done.6.refs_1_ = bf16[2,16,8,512]{3,2,1,0:T(8,128)(2,1)S(1)} collective-permute-done((bf16[2,16,8,512]{3,2,1,0:T(8,128)(2,1)}, bf16[2,16,8,512]{3,2,1,0:T(8,128)(2,1)S(1)}, u32[]{:S(2)}, u32[]{:S(2)}) %collective-permute-start.6) | collective-permute-done | bytes 262176 | tf_op jit(solution)/shard_map/ppermute | solution.py:696
  28.2 1.5 %collective-permute-start.10 = (bf16[2,16,8,512]{3,2,1,0:T(8,128)(2,1)}, bf16[2,16,8,512]{3,2,1,0:T(8,128)(2,1)S(1)}, u32[]{:S(2)}, u32[]{:S(2)}) collective-permute-start(bf16[2,16,8,512]{3,2,1,0:T(8,128)(2,1)} %get-tuple-element.53), channel_id=1, source_target_pairs={{0,2},{1,3},{2,0},{3,1},{4,6},{5,7},{6,4},{7,5},{8,10},{9,11},{10,... | collective-permute-start | bytes 786440 | tf_op jit(solution)/shard_map/ppermute | solution.py:696
  29.7 3.0 %note.1 = s32[16,384]{1,0:T(8,128)} custom-call(s32[128]{0:T(128)} %bitcast.24, s32[128]{0:T(128)} %rows.1, s32[8]{0:T(128)} %lens.9), custom_call_target="tpu_custom_call" | custom-call | tf_op jit(solution)/shard_map/note/pallas_call | solution.py:147
  32.7 1.4 %copy.19 = s32[16,1,384]{2,1,0:T(1,128)} copy(s32[16,1,384]{2,0,1:T(8,128)} %bitcast.22) | data formatting | bytes 49152 | tf_op jit(solution)/shard_map/all_to_all | solution.py:711
  34.1 6.3 %all-to-all-start = ((s32[16,1,384]{2,1,0:T(1,128)}), s32[16,1,384]{2,1,0:T(1,128)S(1)}, u32[]{:S(2)}, u32[]{:S(2)}) async-start(s32[16,1,384]{2,1,0:T(1,128)} %copy.19), calls=%async_computation | async-start | bytes 49152 | tf_op jit(solution)/shard_map/all_to_all | solution.py:711
  41.1 5.5 %all-to-all-done = s32[16,1,384]{2,1,0:T(1,128)S(1)} async-done(((s32[16,1,384]{2,1,0:T(1,128)}), s32[16,1,384]{2,1,0:T(1,128)S(1)}, u32[]{:S(2)}, u32[]{:S(2)}) %all-to-all-start) | async-done | bytes 24608 | tf_op jit(solution)/shard_map/all_to_all | solution.py:711
  46.9 1.6 %reshape.24 = bf16[8,4,4,16,128]{4,3,2,1,0:T(8,128)(2,1)S(1)} reshape(bf16[8,4,8192]{2,1,0:T(4,128)(2,1)} %collective-permute-done) | data formatting | bytes 1048576 | tf_op jit(solution)/shard_map/reshape | solution.py:703
  48.6 3.0 %collective-permute-start.12 = (bf16[2,16,8,512]{3,2,1,0:T(8,128)(2,1)}, bf16[2,16,8,512]{3,2,1,0:T(8,128)(2,1)S(1)}, u32[]{:S(2)}, u32[]{:S(2)}) collective-permute-start(bf16[2,16,8,512]{3,2,1,0:T(8,128)(2,1)} %get-tuple-element.55), channel_id=1, source_target_pairs={{0,12},{1,13},{2,14},{3,15},{4,4},{5,5},{6,6},{7,7},{8,8},{9,9},{1... | collective-permute-start | bytes 786440 | tf_op jit(solution)/shard_map/ppermute | solution.py:696
  51.6 3.3 %collective-permute-start.13 = (bf16[2,16,8,512]{3,2,1,0:T(8,128)(2,1)}, bf16[2,16,8,512]{3,2,1,0:T(8,128)(2,1)S(1)}, u32[]{:S(2)}, u32[]{:S(2)}) collective-permute-start(bf16[2,16,8,512]{3,2,1,0:T(8,128)(2,1)} %get-tuple-element.56), channel_id=1, source_target_pairs={{0,13},{1,14},{2,15},{3,12},{4,5},{5,6},{6,7},{7,4},{8,9},{9,10},{... | collective-permute-start | bytes 786440 | tf_op jit(solution)/shard_map/ppermute | solution.py:696
  54.8 1.5 %collective-permute-start.14 = (bf16[2,16,8,512]{3,2,1,0:T(8,128)(2,1)}, bf16[2,16,8,512]{3,2,1,0:T(8,128)(2,1)S(1)}, u32[]{:S(2)}, u32[]{:S(2)}) collective-permute-start(bf16[2,16,8,512]{3,2,1,0:T(8,128)(2,1)} %get-tuple-element.57), channel_id=1, source_target_pairs={{0,14},{1,15},{2,12},{3,13},{4,6},{5,7},{6,4},{7,5},{8,10},{9,11},... | collective-permute-start | bytes 786440 | tf_op jit(solution)/shard_map/ppermute | solution.py:696
  56.3 1.5 %collective-permute-start.15 = (bf16[2,16,8,512]{3,2,1,0:T(8,128)(2,1)}, bf16[2,16,8,512]{3,2,1,0:T(8,128)(2,1)}, u32[]{:S(2)}, u32[]{:S(2)}) collective-permute-start(bf16[2,16,8,512]{3,2,1,0:T(8,128)(2,1)} %get-tuple-element.58), channel_id=1, source_target_pairs={{0,15},{1,12},{2,13},{3,14},{4,7},{5,4},{6,5},{7,6},{8,11},{9,8},{... | collective-permute-start | bytes 786440 | tf_op jit(solution)/shard_map/ppermute | solution.py:696
  57.9 0.9 copy-done.4
  58.8 5.9 %shard_map.154 = (bf16[8,4,64,128]{3,2,1,0:T(8,128)(2,1)}, f32[8,4,2,64]{3,2,1,0:T(2,128)}) custom-call(s32[4,16]{1,0:T(4,128)S(1)} %dynamic-slice_bitcast_fusion.stages.mine, s32[32,16]{1,0:T(8,128)S(1)} %get-tuple-element.37.place_of, s32[32,16]{1,0:T(8,128)S(1)} %get-tuple-element.38.row_of, s32[32,16]{1,0:T(8,128)S(1)} %get-tuple-element.39.rank_of, ...), custom_call_target="tpu_custom_call" | custom-call | flops 1000000000 | bytes 12582912 | tf_op jit(solution)/shard_map/pallas_call | solution.py:576
  65.4 1.3 %collective-permute-start.16 = (f32[8,4,2,64]{3,2,1,0:T(2,128)}, f32[8,4,2,64]{3,2,1,0:T(2,128)}, u32[]{:S(2)}, u32[]{:S(2)}) collective-permute-start(f32[8,4,2,64]{3,2,1,0:T(2,128)} %get-tuple-element.63), channel_id=1, source_target_pairs={{4,8},{5,9},{6,10},{7,11},{8,4},{9,5},{10,6},{11,7},{20,24},{21,25... | collective-permute-start | bytes 49160 | tf_op jit(solution)/shard_map/ppermute | solution.py:723
  66.7 2.4 %reshape.20 = bf16[8,4,4,16,128]{4,3,2,1,0:T(8,128)(2,1)} reshape(bf16[8,4,8192]{2,1,0:T(4,128)(2,1)} %param.23) | data formatting | bytes 1048576 | tf_op jit(solution)/shard_map/reshape | solution.py:703
  69.1 1.1 copy.20
  70.3 0.9 collective-permute-done.14.refs_10_
  71.1 2.8 %collective-permute-start.2 = (bf16[2,16,8,512]{3,2,1,0:T(8,128)(2,1)}, bf16[2,16,8,512]{3,2,1,0:T(8,128)(2,1)S(1)}, u32[]{:S(2)}, u32[]{:S(2)}) collective-permute-start(bf16[2,16,8,512]{3,2,1,0:T(8,128)(2,1)} %get-tuple-element.44), channel_id=1, source_target_pairs={{0,5},{1,6},{2,7},{3,4},{4,1},{5,2},{6,3},{7,0},{8,13},{9,14},{10,... | collective-permute-start | bytes 786440 | tf_op jit(solution)/shard_map/ppermute | solution.py:696
  73.9 5.0 %collective-permute-done.15.refs_11_ = bf16[2,16,8,512]{3,2,1,0:T(8,128)(2,1)} collective-permute-done((bf16[2,16,8,512]{3,2,1,0:T(8,128)(2,1)}, bf16[2,16,8,512]{3,2,1,0:T(8,128)(2,1)}, u32[]{:S(2)}, u32[]{:S(2)}) %collective-permute-start.15) | collective-permute-done | bytes 262176 | tf_op jit(solution)/shard_map/ppermute | solution.py:696
  78.9 11.4 %collective-permute-start.4 = (bf16[2,16,8,512]{3,2,1,0:T(8,128)(2,1)}, bf16[2,16,8,512]{3,2,1,0:T(8,128)(2,1)S(1)}, u32[]{:S(2)}, u32[]{:S(2)}) collective-permute-start(bf16[2,16,8,512]{3,2,1,0:T(8,128)(2,1)} %get-tuple-element.46), channel_id=1, source_target_pairs={{0,7},{1,4},{2,5},{3,6},{4,3},{5,0},{6,1},{7,2},{8,15},{9,12},{10,... | collective-permute-start | bytes 786440 | tf_op jit(solution)/shard_map/ppermute | solution.py:696
  92.4 7.4 %resident.1 = (f32[8,4,64,128]{3,2,1,0:T(8,128)S(1)}, f32[8,4,64,128]{3,2,1,0:T(8,128)}, f32[8,4,64,128]{3,2,1,0:T(8,128)}) custom-call(s32[8]{0:T(128)S(1)} %copy-done.16, bf16[8,4,64,128]{3,2,1,0:T(8,128)(2,1)S(1)} %bitcast.15, bf16[8,4,512]{2,1,0:T(4,128)(2,1)S(1)} %copy-done.6, bf16[8,4,512]{2,1,0:T(4,128)(2,1)S(1)} %copy-done.7, ...), custom_call_target="tpu_custom_call" | custom-call | flops 2000000000 | bytes 16777216 | tf_op jit(solution)/shard_map/resident/pallas_call | solution.py:365
  99.9 1.2 copy-done
  101.1 1.2 %copy-done.1 = f32[8,4,64,128]{3,2,1,0:T(8,128)S(1)} copy-done((f32[8,4,64,128]{3,2,1,0:T(8,128)S(1)}, f32[8,4,64,128]{3,2,1,0:T(8,128)}, u32[]{:S(2)}) %copy-start.1) | copy-done | bytes 1048600
  102.3 12.3 %shard_map.155 = (f32[8,4,64,128]{3,2,1,0:T(8,128)S(1)}, f32[8,4,64,128]{3,2,1,0:T(8,128)S(1)}, f32[8,4,64,128]{3,2,1,0:T(8,128)S(1)}, f32[8,4,64,128]{3,2,1,0:T(8,128)S(1)}) custom-call(s32[4,16]{1,0:T(4,128)S(1)} %copy-done.14, s32[32,16]{1,0:T(8,128)S(1)} %get-tuple-element.37.place_of, s32[32,16]{1,0:T(8,128)S(1)} %get-tuple-element.38.row_of, ...), custom_call_target="tpu_custom_call" | custom-call | flops 1000000000 | bytes 12582912 | tf_op jit(solution)/shard_map/pallas_call | solution.py:576
  114.6 7.1 %shard_map.156 = bf16[8,4,8192]{2,1,0:T(4,128)(2,1)} custom-call(s32[4,16]{1,0:T(4,128)S(1)} %copy-done.14, s32[32,16]{1,0:T(8,128)S(1)} %get-tuple-element.37.place_of, s32[32,16]{1,0:T(8,128)S(1)} %get-tuple-element.38.row_of, s32[32,16]{1,0:T(8,128)S(1)} %get-tuple-element.39.rank_of, s32[32,16]{1,0:T(8,128)S(1)} %get-tuple-element.40.used, ...), custom_call_target="tpu_custom_call" | custom-call | flops 1000000000 | bytes 12582912 | tf_op jit(solution)/shard_map/pallas_call | solution.py:576
  (54 shorter events, 4.5 us)
Async XLA Ops:
  0.0 57.8 %copy-start.2 = (f32[321,128]{1,0:T(8,128)S(1)}, f32[321,128]{1,0:T(8,128)}, u32[]{:S(2)}) copy-start(f32[321,128]{1,0:T(8,128)} %constant.27.clone.sb) | copy-start | bytes 493060
  0.0 57.8 %copy-start.3 = (f32[321,128]{1,0:T(8,128)S(1)}, f32[321,128]{1,0:T(8,128)}, u32[]{:S(2)}) copy-start(f32[321,128]{1,0:T(8,128)} %constant.26.clone.cb) | copy-start | bytes 493060
  0.0 57.8 %copy-start.8 = (f32[16,128]{1,0:T(8,128)S(1)}, f32[16,128]{1,0:T(8,128)}, u32[]{:S(2)}) copy-start(f32[16,128]{1,0:T(8,128)} %constant.25.clone.sa) | copy-start | bytes 24580
  0.0 57.8 %copy-start.9 = (f32[16,128]{1,0:T(8,128)S(1)}, f32[16,128]{1,0:T(8,128)}, u32[]{:S(2)}) copy-start(f32[16,128]{1,0:T(8,128)} %constant.24.clone.ca) | copy-start | bytes 24580
  0.0 57.8 %copy-start.15 = (s32[8]{0:T(128)S(1)}, s32[8]{0:T(128)}, u32[]{:S(2)}) copy-start(s32[8]{0:T(128)} %lens.9) | copy-start | bytes 100
  0.0 29.7 %collective-permute-start = (bf16[8,4,8192]{2,1,0:T(4,128)(2,1)}, bf16[8,4,8192]{2,1,0:T(4,128)(2,1)}, u32[]{:S(2)}, u32[]{:S(2)}) collective-permute-start(bf16[8,4,8192]{2,1,0:T(4,128)(2,1)} %param.23), channel_id=1, source_target_pairs={{4,8},{5,9},{6,10},{7,11},{8,4},{9,5},{10,6},{11,7},{20,24},{21,25... | collective-permute-start | bytes 1572872 | tf_op jit(solution)/shard_map/ppermute | solution.py:679
  6.1 14.5 %collective-permute-start.5 = (bf16[2,16,8,512]{3,2,1,0:T(8,128)(2,1)}, bf16[2,16,8,512]{3,2,1,0:T(8,128)(2,1)S(1)}, u32[]{:S(2)}, u32[]{:S(2)}) collective-permute-start(bf16[2,16,8,512]{3,2,1,0:T(8,128)(2,1)} %get-tuple-element.47), channel_id=1, source_target_pairs={{0,4},{1,5},{2,6},{3,7},{4,12},{5,13},{6,14},{7,15},{8,0},{9,1},{1... | collective-permute-start | bytes 786440 | tf_op jit(solution)/shard_map/ppermute | solution.py:696
  7.0 21.2 %collective-permute-start.6 = (bf16[2,16,8,512]{3,2,1,0:T(8,128)(2,1)}, bf16[2,16,8,512]{3,2,1,0:T(8,128)(2,1)S(1)}, u32[]{:S(2)}, u32[]{:S(2)}) collective-permute-start(bf16[2,16,8,512]{3,2,1,0:T(8,128)(2,1)} %get-tuple-element.48), channel_id=1, source_target_pairs={{0,5},{1,6},{2,7},{3,4},{4,13},{5,14},{6,15},{7,12},{8,1},{9,2},{1... | collective-permute-start | bytes 786440 | tf_op jit(solution)/shard_map/ppermute | solution.py:696
  8.8 39.7 %collective-permute-start.7 = (bf16[2,16,8,512]{3,2,1,0:T(8,128)(2,1)}, bf16[2,16,8,512]{3,2,1,0:T(8,128)(2,1)S(1)}, u32[]{:S(2)}, u32[]{:S(2)}) collective-permute-start(bf16[2,16,8,512]{3,2,1,0:T(8,128)(2,1)} %get-tuple-element.49), channel_id=1, source_target_pairs={{0,6},{1,7},{2,4},{3,5},{4,14},{5,15},{6,12},{7,13},{8,2},{9,3},{1... | collective-permute-start | bytes 786440 | tf_op jit(solution)/shard_map/ppermute | solution.py:696
  11.5 40.1 %collective-permute-start.8 = (bf16[2,16,8,512]{3,2,1,0:T(8,128)(2,1)}, bf16[2,16,8,512]{3,2,1,0:T(8,128)(2,1)S(1)}, u32[]{:S(2)}, u32[]{:S(2)}) collective-permute-start(bf16[2,16,8,512]{3,2,1,0:T(8,128)(2,1)} %get-tuple-element.50), channel_id=1, source_target_pairs={{0,7},{1,4},{2,5},{3,6},{4,15},{5,12},{6,13},{7,14},{8,3},{9,0},{1... | collective-permute-start | bytes 786440 | tf_op jit(solution)/shard_map/ppermute | solution.py:696
  20.6 34.3 %collective-permute-start.9 = (bf16[2,16,8,512]{3,2,1,0:T(8,128)(2,1)}, bf16[2,16,8,512]{3,2,1,0:T(8,128)(2,1)S(1)}, u32[]{:S(2)}, u32[]{:S(2)}) collective-permute-start(bf16[2,16,8,512]{3,2,1,0:T(8,128)(2,1)} %get-tuple-element.52), channel_id=1, source_target_pairs={{0,1},{1,2},{2,3},{3,0},{4,5},{5,6},{6,7},{7,4},{8,9},{9,10},{10,1... | collective-permute-start | bytes 786440 | tf_op jit(solution)/shard_map/ppermute | solution.py:696
  28.2 28.2 %collective-permute-start.10 = (bf16[2,16,8,512]{3,2,1,0:T(8,128)(2,1)}, bf16[2,16,8,512]{3,2,1,0:T(8,128)(2,1)S(1)}, u32[]{:S(2)}, u32[]{:S(2)}) collective-permute-start(bf16[2,16,8,512]{3,2,1,0:T(8,128)(2,1)} %get-tuple-element.53), channel_id=1, source_target_pairs={{0,2},{1,3},{2,0},{3,1},{4,6},{5,7},{6,4},{7,5},{8,10},{9,11},{10,... | collective-permute-start | bytes 786440 | tf_op jit(solution)/shard_map/ppermute | solution.py:696
  29.7 28.1 %collective-permute-start.11 = (bf16[2,16,8,512]{3,2,1,0:T(8,128)(2,1)}, bf16[2,16,8,512]{3,2,1,0:T(8,128)(2,1)S(1)}, u32[]{:S(2)}, u32[]{:S(2)}) collective-permute-start(bf16[2,16,8,512]{3,2,1,0:T(8,128)(2,1)} %get-tuple-element.54), channel_id=1, source_target_pairs={{0,3},{1,0},{2,1},{3,2},{4,7},{5,4},{6,5},{7,6},{8,11},{9,8},{10,9... | collective-permute-start | bytes 786440 | tf_op jit(solution)/shard_map/ppermute | solution.py:696
  34.1 12.4 %all-to-all-start = ((s32[16,1,384]{2,1,0:T(1,128)}), s32[16,1,384]{2,1,0:T(1,128)S(1)}, u32[]{:S(2)}, u32[]{:S(2)}) async-start(s32[16,1,384]{2,1,0:T(1,128)} %copy.19), calls=%async_computation | async-start | bytes 49152 | tf_op jit(solution)/shard_map/all_to_all | solution.py:711
  41.1 23.7 %copy-start.13 = (s32[4,16]{1,0:T(4,128)}, s32[4,16]{1,0:T(4,128)S(1)}, u32[]{:S(2)}) copy-start(s32[4,16]{1,0:T(4,128)S(1)} %dynamic-slice_bitcast_fusion.stages.mine) | copy-start | bytes 772
  46.9 17.8 %copy-start.11 = (s32[16,128]{1,0:T(8,128)}, s32[16,128]{1,0:T(8,128)S(1)}, u32[]{:S(2)}) copy-start(s32[16,128]{1,0:T(8,128)S(1)} %get-tuple-element.41.tally) | copy-start | bytes 24580
  48.6 16.9 %collective-permute-start.12 = (bf16[2,16,8,512]{3,2,1,0:T(8,128)(2,1)}, bf16[2,16,8,512]{3,2,1,0:T(8,128)(2,1)S(1)}, u32[]{:S(2)}, u32[]{:S(2)}) collective-permute-start(bf16[2,16,8,512]{3,2,1,0:T(8,128)(2,1)} %get-tuple-element.55), channel_id=1, source_target_pairs={{0,12},{1,13},{2,14},{3,15},{4,4},{5,5},{6,6},{7,7},{8,8},{9,9},{1... | collective-permute-start | bytes 786440 | tf_op jit(solution)/shard_map/ppermute | solution.py:696
  51.6 18.6 %collective-permute-start.13 = (bf16[2,16,8,512]{3,2,1,0:T(8,128)(2,1)}, bf16[2,16,8,512]{3,2,1,0:T(8,128)(2,1)S(1)}, u32[]{:S(2)}, u32[]{:S(2)}) collective-permute-start(bf16[2,16,8,512]{3,2,1,0:T(8,128)(2,1)} %get-tuple-element.56), channel_id=1, source_target_pairs={{0,13},{1,14},{2,15},{3,12},{4,5},{5,6},{6,7},{7,4},{8,9},{9,10},{... | collective-permute-start | bytes 786440 | tf_op jit(solution)/shard_map/ppermute | solution.py:696
  54.8 16.3 %collective-permute-start.14 = (bf16[2,16,8,512]{3,2,1,0:T(8,128)(2,1)}, bf16[2,16,8,512]{3,2,1,0:T(8,128)(2,1)S(1)}, u32[]{:S(2)}, u32[]{:S(2)}) collective-permute-start(bf16[2,16,8,512]{3,2,1,0:T(8,128)(2,1)} %get-tuple-element.57), channel_id=1, source_target_pairs={{0,14},{1,15},{2,12},{3,13},{4,6},{5,7},{6,4},{7,5},{8,10},{9,11},... | collective-permute-start | bytes 786440 | tf_op jit(solution)/shard_map/ppermute | solution.py:696
  56.3 22.5 %collective-permute-start.15 = (bf16[2,16,8,512]{3,2,1,0:T(8,128)(2,1)}, bf16[2,16,8,512]{3,2,1,0:T(8,128)(2,1)}, u32[]{:S(2)}, u32[]{:S(2)}) collective-permute-start(bf16[2,16,8,512]{3,2,1,0:T(8,128)(2,1)} %get-tuple-element.58), channel_id=1, source_target_pairs={{0,15},{1,12},{2,13},{3,14},{4,7},{5,4},{6,5},{7,6},{8,11},{9,8},{... | collective-permute-start | bytes 786440 | tf_op jit(solution)/shard_map/ppermute | solution.py:696
  64.7 49.9 %collective-permute-start.17 = (bf16[8,4,64,128]{3,2,1,0:T(8,128)(2,1)}, bf16[8,4,64,128]{3,2,1,0:T(8,128)(2,1)S(1)}, u32[]{:S(2)}, u32[]{:S(2)}) collective-permute-start(bf16[8,4,64,128]{3,2,1,0:T(8,128)(2,1)} %get-tuple-element.68), channel_id=1, source_target_pairs={{4,8},{5,9},{6,10},{7,11},{8,4},{9,5},{10,6},{11,7},{20,24},{21,25... | collective-permute-start | bytes 1572872 | tf_op jit(solution)/shard_map/ppermute | solution.py:722
  65.4 13.4 %collective-permute-start.16 = (f32[8,4,2,64]{3,2,1,0:T(2,128)}, f32[8,4,2,64]{3,2,1,0:T(2,128)}, u32[]{:S(2)}, u32[]{:S(2)}) collective-permute-start(f32[8,4,2,64]{3,2,1,0:T(2,128)} %get-tuple-element.63), channel_id=1, source_target_pairs={{4,8},{5,9},{6,10},{7,11},{8,4},{9,5},{10,6},{11,7},{20,24},{21,25... | collective-permute-start | bytes 49160 | tf_op jit(solution)/shard_map/ppermute | solution.py:723
  70.2 44.4 %collective-permute-start.1 = (bf16[2,16,8,512]{3,2,1,0:T(8,128)(2,1)}, bf16[2,16,8,512]{3,2,1,0:T(8,128)(2,1)S(1)}, u32[]{:S(2)}, u32[]{:S(2)}) collective-permute-start(bf16[2,16,8,512]{3,2,1,0:T(8,128)(2,1)} %get-tuple-element.43), channel_id=1, source_target_pairs={{0,4},{1,5},{2,6},{3,7},{4,0},{5,1},{6,2},{7,3},{8,12},{9,13},{10,... | collective-permute-start | bytes 786440 | tf_op jit(solution)/shard_map/ppermute | solution.py:696
  71.1 43.5 %collective-permute-start.2 = (bf16[2,16,8,512]{3,2,1,0:T(8,128)(2,1)}, bf16[2,16,8,512]{3,2,1,0:T(8,128)(2,1)S(1)}, u32[]{:S(2)}, u32[]{:S(2)}) collective-permute-start(bf16[2,16,8,512]{3,2,1,0:T(8,128)(2,1)} %get-tuple-element.44), channel_id=1, source_target_pairs={{0,5},{1,6},{2,7},{3,4},{4,1},{5,2},{6,3},{7,0},{8,13},{9,14},{10,... | collective-permute-start | bytes 786440 | tf_op jit(solution)/shard_map/ppermute | solution.py:696
  78.9 35.7 %collective-permute-start.3 = (bf16[2,16,8,512]{3,2,1,0:T(8,128)(2,1)}, bf16[2,16,8,512]{3,2,1,0:T(8,128)(2,1)S(1)}, u32[]{:S(2)}, u32[]{:S(2)}) collective-permute-start(bf16[2,16,8,512]{3,2,1,0:T(8,128)(2,1)} %get-tuple-element.45), channel_id=1, source_target_pairs={{0,6},{1,7},{2,4},{3,5},{4,2},{5,3},{6,0},{7,1},{8,14},{9,15},{10,... | collective-permute-start | bytes 786440 | tf_op jit(solution)/shard_map/ppermute | solution.py:696
  78.9 35.7 %collective-permute-start.4 = (bf16[2,16,8,512]{3,2,1,0:T(8,128)(2,1)}, bf16[2,16,8,512]{3,2,1,0:T(8,128)(2,1)S(1)}, u32[]{:S(2)}, u32[]{:S(2)}) collective-permute-start(bf16[2,16,8,512]{3,2,1,0:T(8,128)(2,1)} %get-tuple-element.46), channel_id=1, source_target_pairs={{0,7},{1,4},{2,5},{3,6},{4,3},{5,0},{6,1},{7,2},{8,15},{9,12},{10,... | collective-permute-start | bytes 786440 | tf_op jit(solution)/shard_map/ppermute | solution.py:696
  92.4 7.4 %copy-start.5 = (bf16[2,16,8,512]{3,2,1,0:T(8,128)(2,1)S(1)}, bf16[2,16,8,512]{3,2,1,0:T(8,128)(2,1)}, u32[]{:S(2)}) copy-start(bf16[2,16,8,512]{3,2,1,0:T(8,128)(2,1)} %get-tuple-element.51.refs_4_) | copy-start | bytes 786436
  92.4 7.4 %copy-start.10 = (f32[16,128]{1,0:T(8,128)S(1)}, f32[16,128]{1,0:T(8,128)}, u32[]{:S(2)}) copy-start(f32[16,128]{1,0:T(8,128)} %constant.24.clone.ca) | copy-start | bytes 24580
  92.4 7.4 %copy-start.12 = (s32[16,128]{1,0:T(8,128)S(1)}, s32[16,128]{1,0:T(8,128)}, u32[]{:S(2)}) copy-start(s32[16,128]{1,0:T(8,128)} %copy-done.11) | copy-start | bytes 24580
  92.4 7.4 %copy-start.14 = (s32[4,16]{1,0:T(4,128)S(1)}, s32[4,16]{1,0:T(4,128)}, u32[]{:S(2)}) copy-start(s32[4,16]{1,0:T(4,128)} %copy-done.13) | copy-start | bytes 772
  99.9 1.2 %copy-start = (f32[8,4,64,128]{3,2,1,0:T(8,128)S(1)}, f32[8,4,64,128]{3,2,1,0:T(8,128)}, u32[]{:S(2)}) copy-start(f32[8,4,64,128]{3,2,1,0:T(8,128)} %get-tuple-element.60.refs_13_) | copy-start | bytes 3145732
  101.1 1.2 %copy-start.1 = (f32[8,4,64,128]{3,2,1,0:T(8,128)S(1)}, f32[8,4,64,128]{3,2,1,0:T(8,128)}, u32[]{:S(2)}) copy-start(f32[8,4,64,128]{3,2,1,0:T(8,128)} %get-tuple-element.61.refs_14_) | copy-start | bytes 3145732
  (4 other events, 3.1 us)

commit v10 on v9

--- a/solution.py
+++ b/solution.py
@@ -171,6 +171,7 @@
     mates = [jnp.where(line == post, sooner, 0.0) for line, post in zip(lines, posts)]
     kernel, lane = iotas((8, LANES))
     counts = jnp.zeros((8, LANES), f32)
+    locals_ = []
     for side in range(2):
         there = notes[:, side * LANES : (side + 1) * LANES]
         valid = lax.broadcasted_iota(jnp.int32, (n, cap), 1) < there[:, LANES - 1 :]
@@ -192,14 +193,27 @@
                     )
                     counts += jnp.where((kernel == stage) & (lane == r), number, 0.0)
         span = slice(side * n, side * n + n)
-        place[span, :] = jnp.where(valid, local, -1.0).astype(jnp.int32)
+        locals_.append((span, valid, rows_here, local))
         row_of[span, :] = jnp.maximum(rows_here, 0)
         rank_of[span, :] = rank.astype(jnp.int32)
         filled = jnp.sum(valid.astype(f32), axis=1, keepdims=True)
         used[span, :] = jnp.broadcast_to(filled, (n, cap)).astype(jnp.int32)
     a, b = iotas((LANES, LANES))
     begin = jnp.dot(counts, (a < b).astype(f32), preferred_element_type=f32)
-    twin = twin_index(n // PLANES, lax.axis_index("seq"))
+    in_plane = n // PLANES
+    messages = {0: 2 * in_plane, 1: 3 * in_plane, 2: in_plane}
+    for side, (span, valid, rows_here, local) in enumerate(locals_):
+        unfilled = jnp.zeros((n, 1), f32)
+        for stage in range(3):
+            if (stage == 0) != (side == 1):
+                continue
+            mine = posts[side] == stage
+            unfilled += jnp.where(mine, float(messages[stage] * cap + SPAN // BLK), 0.0)
+            for r in range(rows):
+                here = jnp.where(mine, begin[stage : stage + 1, r : r + 1], 0.0)
+                local += jnp.where(rows_here == r, here, 0.0)
+        place[span, :] = (jnp.where(valid, local, unfilled) * BLK).astype(jnp.int32)
+    twin = twin_index(in_plane, lax.axis_index("seq"))
     source = lax.broadcasted_iota(jnp.int32, (n, LANES), 0)
     lens = jnp.sum(
         jnp.where(source == twin, notes[:, 2 * LANES :], 0), axis=0, keepdims=True
@@ -401,7 +415,6 @@
     tail = pl.ds(pl.multiple_of(last, BLK), SPAN)
     vbuf[tail, :] = jnp.zeros((SPAN, feature), jnp.float32)
     unroll = min(UNROLL, cap)
-    trash = count * cap + SPAN // BLK
     for j in range(count):
 
         @pl.when(mine[1, first + j] == kernel)
@@ -415,15 +428,14 @@
                     k = step * unroll + u
                     r = row_of[source, k]
                     rank = rank_of[source, k]
-                    local = place_of[source, k]
-                    slot = jnp.where(local < 0, trash, tally[kernel, r] + local)
                     length = tally[3, r] if kind == "partial" else lens[r]
-                    fine, coarse = pl.ds(length % BLK, BLK), pl.ds(length // BLK + rank, 1)
+                    fine = pl.ds(length & (BLK - 1), BLK)
+                    coarse = pl.ds(lax.shift_right_logical(length, BLK.bit_length() - 1) + rank, 1)
                     c_a, s_a = ca[fine, :], sa[fine, :]
                     c_b, s_b = cb[coarse, :], sb[coarse, :]
                     cosine = c_a * c_b - s_a * s_b
                     sine = s_a * c_b + c_a * s_b
-                    where = pl.ds(pl.multiple_of(slot * BLK, BLK), BLK)
+                    where = pl.ds(pl.multiple_of(place_of[source, k], BLK), BLK)
                     value = message[1, k].astype(jnp.float32)
                     key = message[0, k].astype(jnp.float32)
                     turned = []

time: 122 us -> 123 us (level)
  no operation moved by 1% of the time
where the time goes in v10:
time: 123 us; the launch traced here: 122 us
  starting transfers between devices  44.3 us (36%)
  Pallas kernels  40.5 us (33%)
  waiting for transfers between devices  23.9 us (19%)
  local copies, waits for them, and re-layouts  12.8 us (10%)
    ppermute x15, starting transfers between devices, send(): value = lax.ppermute(value, 'seq', pairs)  34.5 us
    pallas_call x3, Pallas kernels, span(): pl.pallas_call(functools.partial(span_kernel, kind, kernel, first, count,...  25.2 us
    ppermute x15, waiting for transfers between devices, send(): value = lax.ppermute(value, 'seq', pairs)  18.4 us
    pallas_call x1, Pallas kernels, resident(): pl.pallas_call(resident_kernel, out_shape=state_shapes(rows, grouped.shap...  7.37 us
    all_to_all x1, starting transfers between devices, body(): lax.all_to_all(notes, 'seq', split_axis=0, concat_axis=0, tiled=True)  6.3 us
    unnamed x35, local copies, waits for them, and re-layouts  5.6 us
    all_to_all x1, waiting for transfers between devices, body(): lax.all_to_all(notes, 'seq', split_axis=0, concat_axis=0, tiled=True)  5.45 us
    reshape x4, local copies, waits for them, and re-layouts, regroup(): value = value.reshape(rows, steps, KVH, group, HD).transpose(0, 2, 1, 3, 4)  5.1 us
  transfers between devices with their start and end apart: 19, of which 5 were waited for; matrix products, arithmetic and copies ran while one was open for 6% of the time, Pallas kernels for 27%

profile of v10, /device:TPU:27, one launch (start us, length us, event | category | flops | bytes accessed | tf_op | source)
XLA Modules:
  0.0 121.8 jit_solution(17646994692916235755)
XLA Ops:
  0.0 1.6 %collective-permute-start = (bf16[8,4,8192]{2,1,0:T(4,128)(2,1)}, bf16[8,4,8192]{2,1,0:T(4,128)(2,1)}, u32[]{:S(2)}, u32[]{:S(2)}) collective-permute-start(bf16[8,4,8192]{2,1,0:T(4,128)(2,1)} %param.23), channel_id=1, source_target_pairs={{4,8},{5,9},{6,10},{7,11},{8,4},{9,5},{10,6},{11,7},{20,24},{21,25... | collective-permute-start | bytes 1572872 | tf_op jit(solution)/shard_map/ppermute | solution.py:691
  1.6 4.5 %pack.1 = (bf16[2,16,8,512]{3,2,1,0:T(8,128)(2,1)}, bf16[2,16,8,512]{3,2,1,0:T(8,128)(2,1)}, bf16[2,16,8,512]{3,2,1,0:T(8,128)(2,1)}, bf16[2,16,8,512]{3,2,1,0:T...) custom-call(s32[4,4]{1,0:T(4,128)} %constant.22.clone.phase_table, ...), custom_call_target="tpu_custom_call" | custom-call | tf_op jit(solution)/shard_map/pack/pallas_call | solution.py:88
  6.1 0.9 collective-permute-start.5
  7.0 1.9 %collective-permute-start.6 = (bf16[2,16,8,512]{3,2,1,0:T(8,128)(2,1)}, bf16[2,16,8,512]{3,2,1,0:T(8,128)(2,1)S(1)}, u32[]{:S(2)}, u32[]{:S(2)}) collective-permute-start(bf16[2,16,8,512]{3,2,1,0:T(8,128)(2,1)} %get-tuple-element.48), channel_id=1, source_target_pairs={{0,5},{1,6},{2,7},{3,4},{4,13},{5,14},{6,15},{7,12},{8,1},{9,2},{1... | collective-permute-start | bytes 786440 | tf_op jit(solution)/shard_map/ppermute | solution.py:708
  8.8 2.6 %collective-permute-start.7 = (bf16[2,16,8,512]{3,2,1,0:T(8,128)(2,1)}, bf16[2,16,8,512]{3,2,1,0:T(8,128)(2,1)S(1)}, u32[]{:S(2)}, u32[]{:S(2)}) collective-permute-start(bf16[2,16,8,512]{3,2,1,0:T(8,128)(2,1)} %get-tuple-element.49), channel_id=1, source_target_pairs={{0,6},{1,7},{2,4},{3,5},{4,14},{5,15},{6,12},{7,13},{8,2},{9,3},{1... | collective-permute-start | bytes 786440 | tf_op jit(solution)/shard_map/ppermute | solution.py:708
  11.8 8.8 %collective-permute-done.5.refs_0_ = bf16[2,16,8,512]{3,2,1,0:T(8,128)(2,1)S(1)} collective-permute-done((bf16[2,16,8,512]{3,2,1,0:T(8,128)(2,1)}, bf16[2,16,8,512]{3,2,1,0:T(8,128)(2,1)S(1)}, u32[]{:S(2)}, u32[]{:S(2)}) %collective-permute-start.5) | collective-permute-done | bytes 262176 | tf_op jit(solution)/shard_map/ppermute | solution.py:708
  20.6 3.8 %collective-permute-start.9 = (bf16[2,16,8,512]{3,2,1,0:T(8,128)(2,1)}, bf16[2,16,8,512]{3,2,1,0:T(8,128)(2,1)S(1)}, u32[]{:S(2)}, u32[]{:S(2)}) collective-permute-start(bf16[2,16,8,512]{3,2,1,0:T(8,128)(2,1)} %get-tuple-element.52), channel_id=1, source_target_pairs={{0,1},{1,2},{2,3},{3,0},{4,5},{5,6},{6,7},{7,4},{8,9},{9,10},{10,1... | collective-permute-start | bytes 786440 | tf_op jit(solution)/shard_map/ppermute | solution.py:708
  24.4 3.8 %collective-permute-done.6.refs_1_ = bf16[2,16,8,512]{3,2,1,0:T(8,128)(2,1)S(1)} collective-permute-done((bf16[2,16,8,512]{3,2,1,0:T(8,128)(2,1)}, bf16[2,16,8,512]{3,2,1,0:T(8,128)(2,1)S(1)}, u32[]{:S(2)}, u32[]{:S(2)}) %collective-permute-start.6) | collective-permute-done | bytes 262176 | tf_op jit(solution)/shard_map/ppermute | solution.py:708
  28.2 1.5 %collective-permute-start.10 = (bf16[2,16,8,512]{3,2,1,0:T(8,128)(2,1)}, bf16[2,16,8,512]{3,2,1,0:T(8,128)(2,1)S(1)}, u32[]{:S(2)}, u32[]{:S(2)}) collective-permute-start(bf16[2,16,8,512]{3,2,1,0:T(8,128)(2,1)} %get-tuple-element.53), channel_id=1, source_target_pairs={{0,2},{1,3},{2,0},{3,1},{4,6},{5,7},{6,4},{7,5},{8,10},{9,11},{10,... | collective-permute-start | bytes 786440 | tf_op jit(solution)/shard_map/ppermute | solution.py:708
  29.7 3.0 %note.1 = s32[16,384]{1,0:T(8,128)} custom-call(s32[128]{0:T(128)} %bitcast.24, s32[128]{0:T(128)} %rows.1, s32[8]{0:T(128)} %lens.9), custom_call_target="tpu_custom_call" | custom-call | tf_op jit(solution)/shard_map/note/pallas_call | solution.py:147
  32.7 1.4 %copy.19 = s32[16,1,384]{2,1,0:T(1,128)} copy(s32[16,1,384]{2,0,1:T(8,128)} %bitcast.22) | data formatting | bytes 49152 | tf_op jit(solution)/shard_map/all_to_all | solution.py:723
  34.1 6.3 %all-to-all-start = ((s32[16,1,384]{2,1,0:T(1,128)}), s32[16,1,384]{2,1,0:T(1,128)S(1)}, u32[]{:S(2)}, u32[]{:S(2)}) async-start(s32[16,1,384]{2,1,0:T(1,128)} %copy.19), calls=%async_computation | async-start | bytes 49152 | tf_op jit(solution)/shard_map/all_to_all | solution.py:723
  41.1 5.5 %all-to-all-done = s32[16,1,384]{2,1,0:T(1,128)S(1)} async-done(((s32[16,1,384]{2,1,0:T(1,128)}), s32[16,1,384]{2,1,0:T(1,128)S(1)}, u32[]{:S(2)}, u32[]{:S(2)}) %all-to-all-start) | async-done | bytes 24608 | tf_op jit(solution)/shard_map/all_to_all | solution.py:723
  47.0 1.6 %reshape.24 = bf16[8,4,4,16,128]{4,3,2,1,0:T(8,128)(2,1)S(1)} reshape(bf16[8,4,8192]{2,1,0:T(4,128)(2,1)} %collective-permute-done) | data formatting | bytes 1048576 | tf_op jit(solution)/shard_map/reshape | solution.py:715
  48.7 3.0 %collective-permute-start.12 = (bf16[2,16,8,512]{3,2,1,0:T(8,128)(2,1)}, bf16[2,16,8,512]{3,2,1,0:T(8,128)(2,1)S(1)}, u32[]{:S(2)}, u32[]{:S(2)}) collective-permute-start(bf16[2,16,8,512]{3,2,1,0:T(8,128)(2,1)} %get-tuple-element.55), channel_id=1, source_target_pairs={{0,12},{1,13},{2,14},{3,15},{4,4},{5,5},{6,6},{7,7},{8,8},{9,9},{1... | collective-permute-start | bytes 786440 | tf_op jit(solution)/shard_map/ppermute | solution.py:708
  51.7 3.3 %collective-permute-start.13 = (bf16[2,16,8,512]{3,2,1,0:T(8,128)(2,1)}, bf16[2,16,8,512]{3,2,1,0:T(8,128)(2,1)S(1)}, u32[]{:S(2)}, u32[]{:S(2)}) collective-permute-start(bf16[2,16,8,512]{3,2,1,0:T(8,128)(2,1)} %get-tuple-element.56), channel_id=1, source_target_pairs={{0,13},{1,14},{2,15},{3,12},{4,5},{5,6},{6,7},{7,4},{8,9},{9,10},{... | collective-permute-start | bytes 786440 | tf_op jit(solution)/shard_map/ppermute | solution.py:708
  55.0 1.5 %collective-permute-start.14 = (bf16[2,16,8,512]{3,2,1,0:T(8,128)(2,1)}, bf16[2,16,8,512]{3,2,1,0:T(8,128)(2,1)S(1)}, u32[]{:S(2)}, u32[]{:S(2)}) collective-permute-start(bf16[2,16,8,512]{3,2,1,0:T(8,128)(2,1)} %get-tuple-element.57), channel_id=1, source_target_pairs={{0,14},{1,15},{2,12},{3,13},{4,6},{5,7},{6,4},{7,5},{8,10},{9,11},... | collective-permute-start | bytes 786440 | tf_op jit(solution)/shard_map/ppermute | solution.py:708
  56.5 1.5 %collective-permute-start.15 = (bf16[2,16,8,512]{3,2,1,0:T(8,128)(2,1)}, bf16[2,16,8,512]{3,2,1,0:T(8,128)(2,1)}, u32[]{:S(2)}, u32[]{:S(2)}) collective-permute-start(bf16[2,16,8,512]{3,2,1,0:T(8,128)(2,1)} %get-tuple-element.58), channel_id=1, source_target_pairs={{0,15},{1,12},{2,13},{3,14},{4,7},{5,4},{6,5},{7,6},{8,11},{9,8},{... | collective-permute-start | bytes 786440 | tf_op jit(solution)/shard_map/ppermute | solution.py:708
  58.0 0.9 copy-done.4
  59.0 5.9 %shard_map.154 = (bf16[8,4,64,128]{3,2,1,0:T(8,128)(2,1)}, f32[8,4,2,64]{3,2,1,0:T(2,128)}) custom-call(s32[4,16]{1,0:T(4,128)S(1)} %dynamic-slice_bitcast_fusion.stages.mine, s32[32,16]{1,0:T(8,128)S(1)} %get-tuple-element.37.place_of, s32[32,16]{1,0:T(8,128)S(1)} %get-tuple-element.38.row_of, s32[32,16]{1,0:T(8,128)S(1)} %get-tuple-element.39.rank_of, ...), custom_call_target="tpu_custom_call" | custom-call | flops 1000000000 | bytes 12582912 | tf_op jit(solution)/shard_map/pallas_call | solution.py:588
  65.6 1.3 %collective-permute-start.16 = (f32[8,4,2,64]{3,2,1,0:T(2,128)}, f32[8,4,2,64]{3,2,1,0:T(2,128)}, u32[]{:S(2)}, u32[]{:S(2)}) collective-permute-start(f32[8,4,2,64]{3,2,1,0:T(2,128)} %get-tuple-element.63), channel_id=1, source_target_pairs={{4,8},{5,9},{6,10},{7,11},{8,4},{9,5},{10,6},{11,7},{20,24},{21,25... | collective-permute-start | bytes 49160 | tf_op jit(solution)/shard_map/ppermute | solution.py:735
  66.8 2.4 %reshape.20 = bf16[8,4,4,16,128]{4,3,2,1,0:T(8,128)(2,1)} reshape(bf16[8,4,8192]{2,1,0:T(4,128)(2,1)} %param.23) | data formatting | bytes 1048576 | tf_op jit(solution)/shard_map/reshape | solution.py:715
  69.2 1.1 copy.20
  70.4 0.8 collective-permute-done.14.refs_10_
  71.3 2.8 %collective-permute-start.2 = (bf16[2,16,8,512]{3,2,1,0:T(8,128)(2,1)}, bf16[2,16,8,512]{3,2,1,0:T(8,128)(2,1)S(1)}, u32[]{:S(2)}, u32[]{:S(2)}) collective-permute-start(bf16[2,16,8,512]{3,2,1,0:T(8,128)(2,1)} %get-tuple-element.44), channel_id=1, source_target_pairs={{0,5},{1,6},{2,7},{3,4},{4,1},{5,2},{6,3},{7,0},{8,13},{9,14},{10,... | collective-permute-start | bytes 786440 | tf_op jit(solution)/shard_map/ppermute | solution.py:708
  74.0 5.0 %collective-permute-done.15.refs_11_ = bf16[2,16,8,512]{3,2,1,0:T(8,128)(2,1)} collective-permute-done((bf16[2,16,8,512]{3,2,1,0:T(8,128)(2,1)}, bf16[2,16,8,512]{3,2,1,0:T(8,128)(2,1)}, u32[]{:S(2)}, u32[]{:S(2)}) %collective-permute-start.15) | collective-permute-done | bytes 262176 | tf_op jit(solution)/shard_map/ppermute | solution.py:708
  79.0 11.4 %collective-permute-start.4 = (bf16[2,16,8,512]{3,2,1,0:T(8,128)(2,1)}, bf16[2,16,8,512]{3,2,1,0:T(8,128)(2,1)S(1)}, u32[]{:S(2)}, u32[]{:S(2)}) collective-permute-start(bf16[2,16,8,512]{3,2,1,0:T(8,128)(2,1)} %get-tuple-element.46), channel_id=1, source_target_pairs={{0,7},{1,4},{2,5},{3,6},{4,3},{5,0},{6,1},{7,2},{8,15},{9,12},{10,... | collective-permute-start | bytes 786440 | tf_op jit(solution)/shard_map/ppermute | solution.py:708
  92.6 7.4 %resident.1 = (f32[8,4,64,128]{3,2,1,0:T(8,128)S(1)}, f32[8,4,64,128]{3,2,1,0:T(8,128)}, f32[8,4,64,128]{3,2,1,0:T(8,128)}) custom-call(s32[8]{0:T(128)S(1)} %copy-done.16, bf16[8,4,64,128]{3,2,1,0:T(8,128)(2,1)S(1)} %bitcast.15, bf16[8,4,512]{2,1,0:T(4,128)(2,1)S(1)} %copy-done.6, bf16[8,4,512]{2,1,0:T(4,128)(2,1)S(1)} %copy-done.7, ...), custom_call_target="tpu_custom_call" | custom-call | flops 2000000000 | bytes 16777216 | tf_op jit(solution)/shard_map/resident/pallas_call | solution.py:379
  100.0 1.2 copy-done
  101.2 1.2 %copy-done.1 = f32[8,4,64,128]{3,2,1,0:T(8,128)S(1)} copy-done((f32[8,4,64,128]{3,2,1,0:T(8,128)S(1)}, f32[8,4,64,128]{3,2,1,0:T(8,128)}, u32[]{:S(2)}) %copy-start.1) | copy-done | bytes 1048600
  102.4 12.2 %shard_map.155 = (f32[8,4,64,128]{3,2,1,0:T(8,128)S(1)}, f32[8,4,64,128]{3,2,1,0:T(8,128)S(1)}, f32[8,4,64,128]{3,2,1,0:T(8,128)S(1)}, f32[8,4,64,128]{3,2,1,0:T(8,128)S(1)}) custom-call(s32[4,16]{1,0:T(4,128)S(1)} %copy-done.14, s32[32,16]{1,0:T(8,128)S(1)} %get-tuple-element.37.place_of, s32[32,16]{1,0:T(8,128)S(1)} %get-tuple-element.38.row_of, ...), custom_call_target="tpu_custom_call" | custom-call | flops 1000000000 | bytes 12582912 | tf_op jit(solution)/shard_map/pallas_call | solution.py:588
  114.7 7.1 %shard_map.156 = bf16[8,4,8192]{2,1,0:T(4,128)(2,1)} custom-call(s32[4,16]{1,0:T(4,128)S(1)} %copy-done.14, s32[32,16]{1,0:T(8,128)S(1)} %get-tuple-element.37.place_of, s32[32,16]{1,0:T(8,128)S(1)} %get-tuple-element.38.row_of, s32[32,16]{1,0:T(8,128)S(1)} %get-tuple-element.39.rank_of, s32[32,16]{1,0:T(8,128)S(1)} %get-tuple-element.40.used, ...), custom_call_target="tpu_custom_call" | custom-call | flops 1000000000 | bytes 12582912 | tf_op jit(solution)/shard_map/pallas_call | solution.py:588
  (54 shorter events, 4.6 us)
Async XLA Ops:
  0.0 58.0 %copy-start.2 = (f32[321,128]{1,0:T(8,128)S(1)}, f32[321,128]{1,0:T(8,128)}, u32[]{:S(2)}) copy-start(f32[321,128]{1,0:T(8,128)} %constant.27.clone.sb) | copy-start | bytes 493060
  0.0 58.0 %copy-start.3 = (f32[321,128]{1,0:T(8,128)S(1)}, f32[321,128]{1,0:T(8,128)}, u32[]{:S(2)}) copy-start(f32[321,128]{1,0:T(8,128)} %constant.26.clone.cb) | copy-start | bytes 493060
  0.0 58.0 %copy-start.8 = (f32[16,128]{1,0:T(8,128)S(1)}, f32[16,128]{1,0:T(8,128)}, u32[]{:S(2)}) copy-start(f32[16,128]{1,0:T(8,128)} %constant.25.clone.sa) | copy-start | bytes 24580
  0.0 58.0 %copy-start.9 = (f32[16,128]{1,0:T(8,128)S(1)}, f32[16,128]{1,0:T(8,128)}, u32[]{:S(2)}) copy-start(f32[16,128]{1,0:T(8,128)} %constant.24.clone.ca) | copy-start | bytes 24580
  0.0 58.0 %copy-start.15 = (s32[8]{0:T(128)S(1)}, s32[8]{0:T(128)}, u32[]{:S(2)}) copy-start(s32[8]{0:T(128)} %lens.9) | copy-start | bytes 100
  0.0 29.7 %collective-permute-start = (bf16[8,4,8192]{2,1,0:T(4,128)(2,1)}, bf16[8,4,8192]{2,1,0:T(4,128)(2,1)}, u32[]{:S(2)}, u32[]{:S(2)}) collective-permute-start(bf16[8,4,8192]{2,1,0:T(4,128)(2,1)} %param.23), channel_id=1, source_target_pairs={{4,8},{5,9},{6,10},{7,11},{8,4},{9,5},{10,6},{11,7},{20,24},{21,25... | collective-permute-start | bytes 1572872 | tf_op jit(solution)/shard_map/ppermute | solution.py:691
  6.1 14.5 %collective-permute-start.5 = (bf16[2,16,8,512]{3,2,1,0:T(8,128)(2,1)}, bf16[2,16,8,512]{3,2,1,0:T(8,128)(2,1)S(1)}, u32[]{:S(2)}, u32[]{:S(2)}) collective-permute-start(bf16[2,16,8,512]{3,2,1,0:T(8,128)(2,1)} %get-tuple-element.47), channel_id=1, source_target_pairs={{0,4},{1,5},{2,6},{3,7},{4,12},{5,13},{6,14},{7,15},{8,0},{9,1},{1... | collective-permute-start | bytes 786440 | tf_op jit(solution)/shard_map/ppermute | solution.py:708
  7.0 21.2 %collective-permute-start.6 = (bf16[2,16,8,512]{3,2,1,0:T(8,128)(2,1)}, bf16[2,16,8,512]{3,2,1,0:T(8,128)(2,1)S(1)}, u32[]{:S(2)}, u32[]{:S(2)}) collective-permute-start(bf16[2,16,8,512]{3,2,1,0:T(8,128)(2,1)} %get-tuple-element.48), channel_id=1, source_target_pairs={{0,5},{1,6},{2,7},{3,4},{4,13},{5,14},{6,15},{7,12},{8,1},{9,2},{1... | collective-permute-start | bytes 786440 | tf_op jit(solution)/shard_map/ppermute | solution.py:708
  8.8 39.9 %collective-permute-start.7 = (bf16[2,16,8,512]{3,2,1,0:T(8,128)(2,1)}, bf16[2,16,8,512]{3,2,1,0:T(8,128)(2,1)S(1)}, u32[]{:S(2)}, u32[]{:S(2)}) collective-permute-start(bf16[2,16,8,512]{3,2,1,0:T(8,128)(2,1)} %get-tuple-element.49), channel_id=1, source_target_pairs={{0,6},{1,7},{2,4},{3,5},{4,14},{5,15},{6,12},{7,13},{8,2},{9,3},{1... | collective-permute-start | bytes 786440 | tf_op jit(solution)/shard_map/ppermute | solution.py:708
  11.5 40.2 %collective-permute-start.8 = (bf16[2,16,8,512]{3,2,1,0:T(8,128)(2,1)}, bf16[2,16,8,512]{3,2,1,0:T(8,128)(2,1)S(1)}, u32[]{:S(2)}, u32[]{:S(2)}) collective-permute-start(bf16[2,16,8,512]{3,2,1,0:T(8,128)(2,1)} %get-tuple-element.50), channel_id=1, source_target_pairs={{0,7},{1,4},{2,5},{3,6},{4,15},{5,12},{6,13},{7,14},{8,3},{9,0},{1... | collective-permute-start | bytes 786440 | tf_op jit(solution)/shard_map/ppermute | solution.py:708
  20.6 34.4 %collective-permute-start.9 = (bf16[2,16,8,512]{3,2,1,0:T(8,128)(2,1)}, bf16[2,16,8,512]{3,2,1,0:T(8,128)(2,1)S(1)}, u32[]{:S(2)}, u32[]{:S(2)}) collective-permute-start(bf16[2,16,8,512]{3,2,1,0:T(8,128)(2,1)} %get-tuple-element.52), channel_id=1, source_target_pairs={{0,1},{1,2},{2,3},{3,0},{4,5},{5,6},{6,7},{7,4},{8,9},{9,10},{10,1... | collective-permute-start | bytes 786440 | tf_op jit(solution)/shard_map/ppermute | solution.py:708
  28.2 28.3 %collective-permute-start.10 = (bf16[2,16,8,512]{3,2,1,0:T(8,128)(2,1)}, bf16[2,16,8,512]{3,2,1,0:T(8,128)(2,1)S(1)}, u32[]{:S(2)}, u32[]{:S(2)}) collective-permute-start(bf16[2,16,8,512]{3,2,1,0:T(8,128)(2,1)} %get-tuple-element.53), channel_id=1, source_target_pairs={{0,2},{1,3},{2,0},{3,1},{4,6},{5,7},{6,4},{7,5},{8,10},{9,11},{10,... | collective-permute-start | bytes 786440 | tf_op jit(solution)/shard_map/ppermute | solution.py:708
  29.7 28.3 %collective-permute-start.11 = (bf16[2,16,8,512]{3,2,1,0:T(8,128)(2,1)}, bf16[2,16,8,512]{3,2,1,0:T(8,128)(2,1)S(1)}, u32[]{:S(2)}, u32[]{:S(2)}) collective-permute-start(bf16[2,16,8,512]{3,2,1,0:T(8,128)(2,1)} %get-tuple-element.54), channel_id=1, source_target_pairs={{0,3},{1,0},{2,1},{3,2},{4,7},{5,4},{6,5},{7,6},{8,11},{9,8},{10,9... | collective-permute-start | bytes 786440 | tf_op jit(solution)/shard_map/ppermute | solution.py:708
  34.1 12.4 %all-to-all-start = ((s32[16,1,384]{2,1,0:T(1,128)}), s32[16,1,384]{2,1,0:T(1,128)S(1)}, u32[]{:S(2)}, u32[]{:S(2)}) async-start(s32[16,1,384]{2,1,0:T(1,128)} %copy.19), calls=%async_computation | async-start | bytes 49152 | tf_op jit(solution)/shard_map/all_to_all | solution.py:723
  41.1 23.8 %copy-start.13 = (s32[4,16]{1,0:T(4,128)}, s32[4,16]{1,0:T(4,128)S(1)}, u32[]{:S(2)}) copy-start(s32[4,16]{1,0:T(4,128)S(1)} %dynamic-slice_bitcast_fusion.stages.mine) | copy-start | bytes 772
  47.0 17.8 %copy-start.11 = (s32[16,128]{1,0:T(8,128)}, s32[16,128]{1,0:T(8,128)S(1)}, u32[]{:S(2)}) copy-start(s32[16,128]{1,0:T(8,128)S(1)} %get-tuple-element.41.tally) | copy-start | bytes 24580
  48.7 16.9 %collective-permute-start.12 = (bf16[2,16,8,512]{3,2,1,0:T(8,128)(2,1)}, bf16[2,16,8,512]{3,2,1,0:T(8,128)(2,1)S(1)}, u32[]{:S(2)}, u32[]{:S(2)}) collective-permute-start(bf16[2,16,8,512]{3,2,1,0:T(8,128)(2,1)} %get-tuple-element.55), channel_id=1, source_target_pairs={{0,12},{1,13},{2,14},{3,15},{4,4},{5,5},{6,6},{7,7},{8,8},{9,9},{1... | collective-permute-start | bytes 786440 | tf_op jit(solution)/shard_map/ppermute | solution.py:708
  51.7 18.6 %collective-permute-start.13 = (bf16[2,16,8,512]{3,2,1,0:T(8,128)(2,1)}, bf16[2,16,8,512]{3,2,1,0:T(8,128)(2,1)S(1)}, u32[]{:S(2)}, u32[]{:S(2)}) collective-permute-start(bf16[2,16,8,512]{3,2,1,0:T(8,128)(2,1)} %get-tuple-element.56), channel_id=1, source_target_pairs={{0,13},{1,14},{2,15},{3,12},{4,5},{5,6},{6,7},{7,4},{8,9},{9,10},{... | collective-permute-start | bytes 786440 | tf_op jit(solution)/shard_map/ppermute | solution.py:708
  55.0 16.3 %collective-permute-start.14 = (bf16[2,16,8,512]{3,2,1,0:T(8,128)(2,1)}, bf16[2,16,8,512]{3,2,1,0:T(8,128)(2,1)S(1)}, u32[]{:S(2)}, u32[]{:S(2)}) collective-permute-start(bf16[2,16,8,512]{3,2,1,0:T(8,128)(2,1)} %get-tuple-element.57), channel_id=1, source_target_pairs={{0,14},{1,15},{2,12},{3,13},{4,6},{5,7},{6,4},{7,5},{8,10},{9,11},... | collective-permute-start | bytes 786440 | tf_op jit(solution)/shard_map/ppermute | solution.py:708
  56.5 22.5 %collective-permute-start.15 = (bf16[2,16,8,512]{3,2,1,0:T(8,128)(2,1)}, bf16[2,16,8,512]{3,2,1,0:T(8,128)(2,1)}, u32[]{:S(2)}, u32[]{:S(2)}) collective-permute-start(bf16[2,16,8,512]{3,2,1,0:T(8,128)(2,1)} %get-tuple-element.58), channel_id=1, source_target_pairs={{0,15},{1,12},{2,13},{3,14},{4,7},{5,4},{6,5},{7,6},{8,11},{9,8},{... | collective-permute-start | bytes 786440 | tf_op jit(solution)/shard_map/ppermute | solution.py:708
  64.9 49.9 %collective-permute-start.17 = (bf16[8,4,64,128]{3,2,1,0:T(8,128)(2,1)}, bf16[8,4,64,128]{3,2,1,0:T(8,128)(2,1)S(1)}, u32[]{:S(2)}, u32[]{:S(2)}) collective-permute-start(bf16[8,4,64,128]{3,2,1,0:T(8,128)(2,1)} %get-tuple-element.68), channel_id=1, source_target_pairs={{4,8},{5,9},{6,10},{7,11},{8,4},{9,5},{10,6},{11,7},{20,24},{21,25... | collective-permute-start | bytes 1572872 | tf_op jit(solution)/shard_map/ppermute | solution.py:734
  65.6 13.4 %collective-permute-start.16 = (f32[8,4,2,64]{3,2,1,0:T(2,128)}, f32[8,4,2,64]{3,2,1,0:T(2,128)}, u32[]{:S(2)}, u32[]{:S(2)}) collective-permute-start(f32[8,4,2,64]{3,2,1,0:T(2,128)} %get-tuple-element.63), channel_id=1, source_target_pairs={{4,8},{5,9},{6,10},{7,11},{8,4},{9,5},{10,6},{11,7},{20,24},{21,25... | collective-permute-start | bytes 49160 | tf_op jit(solution)/shard_map/ppermute | solution.py:735
  70.3 44.4 %collective-permute-start.1 = (bf16[2,16,8,512]{3,2,1,0:T(8,128)(2,1)}, bf16[2,16,8,512]{3,2,1,0:T(8,128)(2,1)S(1)}, u32[]{:S(2)}, u32[]{:S(2)}) collective-permute-start(bf16[2,16,8,512]{3,2,1,0:T(8,128)(2,1)} %get-tuple-element.43), channel_id=1, source_target_pairs={{0,4},{1,5},{2,6},{3,7},{4,0},{5,1},{6,2},{7,3},{8,12},{9,13},{10,... | collective-permute-start | bytes 786440 | tf_op jit(solution)/shard_map/ppermute | solution.py:708
  71.3 43.5 %collective-permute-start.2 = (bf16[2,16,8,512]{3,2,1,0:T(8,128)(2,1)}, bf16[2,16,8,512]{3,2,1,0:T(8,128)(2,1)S(1)}, u32[]{:S(2)}, u32[]{:S(2)}) collective-permute-start(bf16[2,16,8,512]{3,2,1,0:T(8,128)(2,1)} %get-tuple-element.44), channel_id=1, source_target_pairs={{0,5},{1,6},{2,7},{3,4},{4,1},{5,2},{6,3},{7,0},{8,13},{9,14},{10,... | collective-permute-start | bytes 786440 | tf_op jit(solution)/shard_map/ppermute | solution.py:708
  79.0 35.7 %collective-permute-start.3 = (bf16[2,16,8,512]{3,2,1,0:T(8,128)(2,1)}, bf16[2,16,8,512]{3,2,1,0:T(8,128)(2,1)S(1)}, u32[]{:S(2)}, u32[]{:S(2)}) collective-permute-start(bf16[2,16,8,512]{3,2,1,0:T(8,128)(2,1)} %get-tuple-element.45), channel_id=1, source_target_pairs={{0,6},{1,7},{2,4},{3,5},{4,2},{5,3},{6,0},{7,1},{8,14},{9,15},{10,... | collective-permute-start | bytes 786440 | tf_op jit(solution)/shard_map/ppermute | solution.py:708
  79.0 35.7 %collective-permute-start.4 = (bf16[2,16,8,512]{3,2,1,0:T(8,128)(2,1)}, bf16[2,16,8,512]{3,2,1,0:T(8,128)(2,1)S(1)}, u32[]{:S(2)}, u32[]{:S(2)}) collective-permute-start(bf16[2,16,8,512]{3,2,1,0:T(8,128)(2,1)} %get-tuple-element.46), channel_id=1, source_target_pairs={{0,7},{1,4},{2,5},{3,6},{4,3},{5,0},{6,1},{7,2},{8,15},{9,12},{10,... | collective-permute-start | bytes 786440 | tf_op jit(solution)/shard_map/ppermute | solution.py:708
  92.6 7.4 %copy-start.5 = (bf16[2,16,8,512]{3,2,1,0:T(8,128)(2,1)S(1)}, bf16[2,16,8,512]{3,2,1,0:T(8,128)(2,1)}, u32[]{:S(2)}) copy-start(bf16[2,16,8,512]{3,2,1,0:T(8,128)(2,1)} %get-tuple-element.51.refs_4_) | copy-start | bytes 786436
  92.6 7.4 %copy-start.10 = (f32[16,128]{1,0:T(8,128)S(1)}, f32[16,128]{1,0:T(8,128)}, u32[]{:S(2)}) copy-start(f32[16,128]{1,0:T(8,128)} %constant.24.clone.ca) | copy-start | bytes 24580
  92.6 7.4 %copy-start.12 = (s32[16,128]{1,0:T(8,128)S(1)}, s32[16,128]{1,0:T(8,128)}, u32[]{:S(2)}) copy-start(s32[16,128]{1,0:T(8,128)} %copy-done.11) | copy-start | bytes 24580
  92.6 7.4 %copy-start.14 = (s32[4,16]{1,0:T(4,128)S(1)}, s32[4,16]{1,0:T(4,128)}, u32[]{:S(2)}) copy-start(s32[4,16]{1,0:T(4,128)} %copy-done.13) | copy-start | bytes 772
  100.0 1.2 %copy-start = (f32[8,4,64,128]{3,2,1,0:T(8,128)S(1)}, f32[8,4,64,128]{3,2,1,0:T(8,128)}, u32[]{:S(2)}) copy-start(f32[8,4,64,128]{3,2,1,0:T(8,128)} %get-tuple-element.60.refs_13_) | copy-start | bytes 3145732
  101.2 1.2 %copy-start.1 = (f32[8,4,64,128]{3,2,1,0:T(8,128)S(1)}, f32[8,4,64,128]{3,2,1,0:T(8,128)}, u32[]{:S(2)}) copy-start(f32[8,4,64,128]{3,2,1,0:T(8,128)} %get-tuple-element.61.refs_14_) | copy-start | bytes 3145732
  (4 other events, 3.1 us)

commit v11 on v8

--- a/solution.py
+++ b/solution.py
@@ -117,7 +117,7 @@
     lax.fori_loop(0, n, clear, 0, unroll=min(n, 16))
     my_twin = twins[lax.axis_index("seq")]
     for k in range(lens.shape[0]):
-        notes[my_twin, 2 * LANES + k] = lens[k]
+        notes[my_twin, 0, 2 * LANES + k] = lens[k]
 
     def put(step, _):
         ready = []
@@ -128,15 +128,15 @@
             fill[dest] = slot + 1
             ready.append((dest, twins[dest], slot, rows[b]))
         for dest, twin, slot, row in ready:
-            notes[dest, slot] = row
-            notes[twin, LANES + slot] = row
+            notes[dest, 0, slot] = row
+            notes[twin, 0, LANES + slot] = row
         return 0
 
     lax.fori_loop(0, rows.shape[0] // PACKED, put, 0)
 
     def close(i, _):
-        notes[i, LANES - 1] = fill[i]
-        notes[twins[i], 2 * LANES - 1] = fill[i]
+        notes[i, 0, LANES - 1] = fill[i]
+        notes[twins[i], 0, 2 * LANES - 1] = fill[i]
         return 0
 
     lax.fori_loop(0, n, close, 0, unroll=min(n, 4))
@@ -146,7 +146,7 @@
     smem = pl.BlockSpec(memory_space=pltpu.SMEM)
     return pl.pallas_call(
         functools.partial(note_kernel, n),
-        out_shape=jax.ShapeDtypeStruct((n, 3 * LANES), jnp.int32),
+        out_shape=jax.ShapeDtypeStruct((n, 1, 3 * LANES), jnp.int32),
         in_specs=[smem] * 3,
         out_specs=smem,
         scratch_shapes=[pltpu.SMEM((n,), jnp.int32), pltpu.SMEM((n,), jnp.int32)],
@@ -171,8 +171,9 @@
     mates = [jnp.where(line == post, sooner, 0.0) for line, post in zip(lines, posts)]
     kernel, lane = iotas((8, LANES))
     counts = jnp.zeros((8, LANES), f32)
+    locals_ = []
     for side in range(2):
-        there = notes[:, side * LANES : (side + 1) * LANES]
+        there = notes[:, 0, side * LANES : (side + 1) * LANES]
         valid = lax.broadcasted_iota(jnp.int32, (n, cap), 1) < there[:, LANES - 1 :]
         rows_here = jnp.where(valid, there[:, :cap], -1)
         rank = jnp.zeros((n, cap), f32)
@@ -192,17 +193,30 @@
                     )
                     counts += jnp.where((kernel == stage) & (lane == r), number, 0.0)
         span = slice(side * n, side * n + n)
-        place[span, :] = jnp.where(valid, local, -1.0).astype(jnp.int32)
+        locals_.append((span, valid, rows_here, local))
         row_of[span, :] = jnp.maximum(rows_here, 0)
         rank_of[span, :] = rank.astype(jnp.int32)
         filled = jnp.sum(valid.astype(f32), axis=1, keepdims=True)
         used[span, :] = jnp.broadcast_to(filled, (n, cap)).astype(jnp.int32)
     a, b = iotas((LANES, LANES))
     begin = jnp.dot(counts, (a < b).astype(f32), preferred_element_type=f32)
-    twin = twin_index(n // PLANES, lax.axis_index("seq"))
+    in_plane = n // PLANES
+    messages = {0: 2 * in_plane, 1: 3 * in_plane, 2: in_plane}
+    for side, (span, valid, rows_here, local) in enumerate(locals_):
+        unfilled = jnp.zeros((n, 1), f32)
+        for stage in range(3):
+            if (stage == 0) != (side == 1):
+                continue
+            mine = posts[side] == stage
+            unfilled += jnp.where(mine, float(messages[stage] * cap + SPAN // BLK), 0.0)
+            for r in range(rows):
+                here = jnp.where(mine, begin[stage : stage + 1, r : r + 1], 0.0)
+                local += jnp.where(rows_here == r, here, 0.0)
+        place[span, :] = (jnp.where(valid, local, unfilled) * BLK).astype(jnp.int32)
+    twin = twin_index(in_plane, lax.axis_index("seq"))
     source = lax.broadcasted_iota(jnp.int32, (n, LANES), 0)
     lens = jnp.sum(
-        jnp.where(source == twin, notes[:, 2 * LANES :], 0), axis=0, keepdims=True
+        jnp.where(source == twin, notes[:, 0, 2 * LANES :], 0), axis=0, keepdims=True
     )
     tally[0:8, :] = jnp.where(kernel == 3, lens, begin.astype(jnp.int32))
     tally[8:16, :] = (counts * BLK).astype(jnp.int32)
@@ -392,7 +406,7 @@
     elif kind == "state":
         acc, top, total, kbuf, vbuf = refs[3:]
     else:
-        part, stats, out, acc, top, total, scr, kbuf, vbuf = refs[3:]
+        part, stats, out_all, acc, top, total, scr, out, sems, kbuf, vbuf = refs[3:]
     state = (acc, top, total)
     rows = q_ref.shape[0]
     width = q_ref.shape[2]
@@ -401,7 +415,6 @@
     tail = pl.ds(pl.multiple_of(last, BLK), SPAN)
     vbuf[tail, :] = jnp.zeros((SPAN, feature), jnp.float32)
     unroll = min(UNROLL, cap)
-    trash = count * cap + SPAN // BLK
     for j in range(count):
 
         @pl.when(mine[1, first + j] == kernel)
@@ -415,15 +428,14 @@
                     k = step * unroll + u
                     r = row_of[source, k]
                     rank = rank_of[source, k]
-                    local = place_of[source, k]
-                    slot = jnp.where(local < 0, trash, tally[kernel, r] + local)
                     length = tally[3, r] if kind == "partial" else lens[r]
-                    fine, coarse = pl.ds(length % BLK, BLK), pl.ds(length // BLK + rank, 1)
+                    fine = pl.ds(length & (BLK - 1), BLK)
+                    coarse = pl.ds(lax.shift_right_logical(length, BLK.bit_length() - 1) + rank, 1)
                     c_a, s_a = ca[fine, :], sa[fine, :]
                     c_b, s_b = cb[coarse, :], sb[coarse, :]
                     cosine = c_a * c_b - s_a * s_b
                     sine = s_a * c_b + c_a * s_b
-                    where = pl.ds(pl.multiple_of(slot * BLK, BLK), BLK)
+                    where = pl.ds(pl.multiple_of(place_of[source, k], BLK), BLK)
                     value = message[1, k].astype(jnp.float32)
                     key = message[0, k].astype(jnp.float32)
                     turned = []
@@ -537,6 +549,12 @@
                 beyond(r)
             put_out(pair, [held(r, state) for r in pair])
 
+        for r in pair:
+            write(r).start()
+
+    def write(r):
+        return pltpu.make_async_copy(out.at[r], out_all.at[r], sems.at[r])
+
     run = {"partial": partial_rows, "state": state_rows, "final": final_rows}[kind]
     together = 2 if rows % 2 == 0 else 1
 
@@ -545,6 +563,9 @@
         return 0
 
     lax.fori_loop(0, rows // together, some_rows, 0)
+    if kind == "final":
+        for r in range(rows):
+            write(r).wait()
 
 
 def span(kind, kernel, first, cap, scalars, grouped, tables, messages, state, extra, steps):
@@ -566,13 +587,19 @@
         out_shape = state_shapes(rows, width)
     else:
         out_shape = jax.ShapeDtypeStruct((rows, steps, QH * HD), jnp.bfloat16)
-        scratch += running + [pltpu.VMEM((2 * KVH, width, HD), jnp.float32)]
+        scratch += running + [
+            pltpu.VMEM((2 * KVH, width, HD), jnp.float32),
+            pltpu.VMEM((rows, steps, QH * HD), jnp.bfloat16),
+            pltpu.SemaphoreType.DMA((rows,)),
+        ]
     scratch += [pltpu.VMEM((room, feature), jnp.float32)] * 2
     return pl.pallas_call(
         functools.partial(span_kernel, kind, kernel, first, count, cap),
         out_shape=out_shape,
         in_specs=[smem] * 7 + [vmem] * (5 + count + len(state) + len(extra)),
-        out_specs=jax.tree.map(lambda _: vmem, out_shape),
+        out_specs=pl.BlockSpec(memory_space=pltpu.HBM)
+        if kind == "final"
+        else jax.tree.map(lambda _: vmem, out_shape),
         scratch_shapes=scratch,
         compiler_params=pltpu.CompilerParams(vmem_limit_bytes=GRANT),
         cost_estimate=pl.CostEstimate(

time: 116 us -> 116 us (level)
  waiting for transfers between devices: 18 us -> 19.7 us
  local copies, waits for them, and re-layouts: 13.3 us -> 12 us
    all_to_all x1, waiting for transfers between devices: 5.46 us -> 7.14 us  [body(): lax.all_to_all(notes, 'seq', split_axis=0, concat_axis=0, tiled=True)]
    all_to_all x1 -> x0, local copies, waits for them, and re-layouts: 1.36 us -> none  [body(): lax.all_to_all(notes, 'seq', split_axis=0, concat_axis=0, tiled=True)]
    unnamed x39 -> x38, local copies, waits for them, and re-layouts: 6.2 us -> 6.2 us
  transfers between devices with their start and end apart: 19 -> 19, of which waited for: 3 -> 3; matrix products, arithmetic and copies ran while one was open for 6% -> 5% of each run, Pallas kernels for 29% -> 29%
where the time goes in v11:
time: 116 us; the launch traced here: 115 us
  starting transfers between devices  43 us (37%)
  Pallas kernels  40.1 us (35%)
  waiting for transfers between devices  19.7 us (17%)
  local copies, waits for them, and re-layouts  12 us (10%)
    ppermute x15, starting transfers between devices, send(): value = lax.ppermute(value, 'seq', pairs)  33.8 us
    pallas_call x3, Pallas kernels, span(): pl.pallas_call(functools.partial(span_kernel, kind, kernel, first, count,...  25 us
    ppermute x15, waiting for transfers between devices, send(): value = lax.ppermute(value, 'seq', pairs)  12.6 us
    pallas_call x1, Pallas kernels, resident(): pl.pallas_call(resident_kernel, out_shape=state_shapes(rows, grouped.shap...  7.37 us
    all_to_all x1, waiting for transfers between devices, body(): lax.all_to_all(notes, 'seq', split_axis=0, concat_axis=0, tiled=True)  7.14 us
    all_to_all x1, starting transfers between devices, body(): lax.all_to_all(notes, 'seq', split_axis=0, concat_axis=0, tiled=True)  6.31 us
    unnamed x38, local copies, waits for them, and re-layouts  6.2 us
    reshape x4, local copies, waits for them, and re-layouts, regroup(): value = value.reshape(rows, steps, KVH, group, HD).transpose(0, 2, 1, 3, 4)  5.1 us
  transfers between devices with their start and end apart: 19, of which 3 were waited for; matrix products, arithmetic and copies ran while one was open for 5% of the time, Pallas kernels for 29%

profile of v11, /device:TPU:27, one launch (start us, length us, event | category | flops | bytes accessed | tf_op | source)
XLA Modules:
  0.0 115.2 jit_solution(9210121075282357551)
XLA Ops:
  0.0 1.6 %collective-permute-start = (bf16[8,4,8192]{2,1,0:T(4,128)(2,1)}, bf16[8,4,8192]{2,1,0:T(4,128)(2,1)}, u32[]{:S(2)}, u32[]{:S(2)}) collective-permute-start(bf16[8,4,8192]{2,1,0:T(4,128)(2,1)} %param.23), channel_id=1, source_target_pairs={{4,8},{5,9},{6,10},{7,11},{8,4},{9,5},{10,6},{11,7},{20,24},{21,25... | collective-permute-start | bytes 1572872 | tf_op jit(solution)/shard_map/ppermute | solution.py:701
  1.6 4.5 %pack.1 = (bf16[2,16,8,512]{3,2,1,0:T(8,128)(2,1)}, bf16[2,16,8,512]{3,2,1,0:T(8,128)(2,1)}, bf16[2,16,8,512]{3,2,1,0:T(8,128)(2,1)}, bf16[2,16,8,512]{3,2,1,0:T...) custom-call(s32[4,4]{1,0:T(4,128)} %constant.22.clone.phase_table, ...), custom_call_target="tpu_custom_call" | custom-call | tf_op jit(solution)/shard_map/pack/pallas_call | solution.py:88
  6.1 0.9 collective-permute-start.5
  7.0 1.9 %collective-permute-start.6 = (bf16[2,16,8,512]{3,2,1,0:T(8,128)(2,1)}, bf16[2,16,8,512]{3,2,1,0:T(8,128)(2,1)S(1)}, u32[]{:S(2)}, u32[]{:S(2)}) collective-permute-start(bf16[2,16,8,512]{3,2,1,0:T(8,128)(2,1)} %get-tuple-element.47), channel_id=1, source_target_pairs={{0,5},{1,6},{2,7},{3,4},{4,13},{5,14},{6,15},{7,12},{8,1},{9,2},{1... | collective-permute-start | bytes 786440 | tf_op jit(solution)/shard_map/ppermute | solution.py:718
  8.9 2.6 %collective-permute-start.7 = (bf16[2,16,8,512]{3,2,1,0:T(8,128)(2,1)}, bf16[2,16,8,512]{3,2,1,0:T(8,128)(2,1)S(1)}, u32[]{:S(2)}, u32[]{:S(2)}) collective-permute-start(bf16[2,16,8,512]{3,2,1,0:T(8,128)(2,1)} %get-tuple-element.48), channel_id=1, source_target_pairs={{0,6},{1,7},{2,4},{3,5},{4,14},{5,15},{6,12},{7,13},{8,2},{9,3},{1... | collective-permute-start | bytes 786440 | tf_op jit(solution)/shard_map/ppermute | solution.py:718
  11.8 8.7 %collective-permute-done.5.refs_0_ = bf16[2,16,8,512]{3,2,1,0:T(8,128)(2,1)S(1)} collective-permute-done((bf16[2,16,8,512]{3,2,1,0:T(8,128)(2,1)}, bf16[2,16,8,512]{3,2,1,0:T(8,128)(2,1)S(1)}, u32[]{:S(2)}, u32[]{:S(2)}) %collective-permute-start.5) | collective-permute-done | bytes 262176 | tf_op jit(solution)/shard_map/ppermute | solution.py:718
  20.6 3.8 %collective-permute-start.9 = (bf16[2,16,8,512]{3,2,1,0:T(8,128)(2,1)}, bf16[2,16,8,512]{3,2,1,0:T(8,128)(2,1)S(1)}, u32[]{:S(2)}, u32[]{:S(2)}) collective-permute-start(bf16[2,16,8,512]{3,2,1,0:T(8,128)(2,1)} %get-tuple-element.51), channel_id=1, source_target_pairs={{0,1},{1,2},{2,3},{3,0},{4,5},{5,6},{6,7},{7,4},{8,9},{9,10},{10,1... | collective-permute-start | bytes 786440 | tf_op jit(solution)/shard_map/ppermute | solution.py:718
  24.4 3.8 %collective-permute-done.6.refs_1_ = bf16[2,16,8,512]{3,2,1,0:T(8,128)(2,1)S(1)} collective-permute-done((bf16[2,16,8,512]{3,2,1,0:T(8,128)(2,1)}, bf16[2,16,8,512]{3,2,1,0:T(8,128)(2,1)S(1)}, u32[]{:S(2)}, u32[]{:S(2)}) %collective-permute-start.6) | collective-permute-done | bytes 262176 | tf_op jit(solution)/shard_map/ppermute | solution.py:718
  28.2 1.5 %collective-permute-start.10 = (bf16[2,16,8,512]{3,2,1,0:T(8,128)(2,1)}, bf16[2,16,8,512]{3,2,1,0:T(8,128)(2,1)S(1)}, u32[]{:S(2)}, u32[]{:S(2)}) collective-permute-start(bf16[2,16,8,512]{3,2,1,0:T(8,128)(2,1)} %get-tuple-element.52), channel_id=1, source_target_pairs={{0,2},{1,3},{2,0},{3,1},{4,6},{5,7},{6,4},{7,5},{8,10},{9,11},{10,... | collective-permute-start | bytes 786440 | tf_op jit(solution)/shard_map/ppermute | solution.py:718
  29.7 2.7 %note.1 = s32[16,1,384]{2,1,0:T(1,128)} custom-call(s32[128]{0:T(128)} %bitcast.18, s32[128]{0:T(128)} %rows.1, s32[8]{0:T(128)} %lens.9), custom_call_target="tpu_custom_call" | custom-call | tf_op jit(solution)/shard_map/note/pallas_call | solution.py:147
  32.4 6.3 %all-to-all-start = ((s32[16,1,384]{2,1,0:T(1,128)}), s32[16,1,384]{2,1,0:T(1,128)S(1)}, u32[]{:S(2)}, u32[]{:S(2)}) async-start(s32[16,1,384]{2,1,0:T(1,128)} %note.1), calls=%async_computation | async-start | bytes 49152 | tf_op jit(solution)/shard_map/all_to_all | solution.py:733
  38.7 0.7 dynamic-slice_bitcast_fusion.stages.mine
  39.4 7.1 %all-to-all-done.notes = s32[16,1,384]{2,1,0:T(1,128)S(1)} async-done(((s32[16,1,384]{2,1,0:T(1,128)}), s32[16,1,384]{2,1,0:T(1,128)S(1)}, u32[]{:S(2)}, u32[]{:S(2)}) %all-to-all-start) | async-done | bytes 24608 | tf_op jit(solution)/shard_map/all_to_all | solution.py:733
  47.1 1.6 %reshape.22 = bf16[8,4,4,16,128]{4,3,2,1,0:T(8,128)(2,1)S(1)} reshape(bf16[8,4,8192]{2,1,0:T(4,128)(2,1)} %collective-permute-done) | data formatting | bytes 1048576 | tf_op jit(solution)/shard_map/reshape | solution.py:725
  48.8 3.0 %collective-permute-start.12 = (bf16[2,16,8,512]{3,2,1,0:T(8,128)(2,1)}, bf16[2,16,8,512]{3,2,1,0:T(8,128)(2,1)S(1)}, u32[]{:S(2)}, u32[]{:S(2)}) collective-permute-start(bf16[2,16,8,512]{3,2,1,0:T(8,128)(2,1)} %get-tuple-element.54), channel_id=1, source_target_pairs={{0,12},{1,13},{2,14},{3,15},{4,4},{5,5},{6,6},{7,7},{8,8},{9,9},{1... | collective-permute-start | bytes 786440 | tf_op jit(solution)/shard_map/ppermute | solution.py:718
  51.8 3.3 %collective-permute-start.13 = (bf16[2,16,8,512]{3,2,1,0:T(8,128)(2,1)}, bf16[2,16,8,512]{3,2,1,0:T(8,128)(2,1)S(1)}, u32[]{:S(2)}, u32[]{:S(2)}) collective-permute-start(bf16[2,16,8,512]{3,2,1,0:T(8,128)(2,1)} %get-tuple-element.55), channel_id=1, source_target_pairs={{0,13},{1,14},{2,15},{3,12},{4,5},{5,6},{6,7},{7,4},{8,9},{9,10},{... | collective-permute-start | bytes 786440 | tf_op jit(solution)/shard_map/ppermute | solution.py:718
  55.1 1.5 %collective-permute-start.14 = (bf16[2,16,8,512]{3,2,1,0:T(8,128)(2,1)}, bf16[2,16,8,512]{3,2,1,0:T(8,128)(2,1)}, u32[]{:S(2)}, u32[]{:S(2)}) collective-permute-start(bf16[2,16,8,512]{3,2,1,0:T(8,128)(2,1)} %get-tuple-element.56), channel_id=1, source_target_pairs={{0,14},{1,15},{2,12},{3,13},{4,6},{5,7},{6,4},{7,5},{8,10},{9,11},... | collective-permute-start | bytes 786440 | tf_op jit(solution)/shard_map/ppermute | solution.py:718
  56.7 0.9 copy-done.4
  57.6 5.9 %shard_map.155 = (bf16[8,4,64,128]{3,2,1,0:T(8,128)(2,1)}, f32[8,4,2,64]{3,2,1,0:T(2,128)S(1)}) custom-call(s32[4,16]{1,0:T(4,128)S(1)} %dynamic-slice_bitcast_fusion.stages.mine, s32[32,16]{1,0:T(8,128)S(1)} %get-tuple-element.36.place_of, s32[32,16]{1,0:T(8,128)S(1)} %get-tuple-element.37.row_of, s32[32,16]{1,0:T(8,128)S(1)} %get-tuple-element.38.rank_of, ...), custom_call_target="tpu_custom_call" | custom-call | flops 1000000000 | bytes 12582912 | tf_op jit(solution)/shard_map/pallas_call | solution.py:596
  64.1 0.7 collective-permute-start.16
  64.8 1.5 %collective-permute-start.15 = (bf16[2,16,8,512]{3,2,1,0:T(8,128)(2,1)}, bf16[2,16,8,512]{3,2,1,0:T(8,128)(2,1)}, u32[]{:S(2)}, u32[]{:S(2)}) collective-permute-start(bf16[2,16,8,512]{3,2,1,0:T(8,128)(2,1)} %get-tuple-element.57), channel_id=1, source_target_pairs={{0,15},{1,12},{2,13},{3,14},{4,7},{5,4},{6,5},{7,6},{8,11},{9,8},{... | collective-permute-start | bytes 786440 | tf_op jit(solution)/shard_map/ppermute | solution.py:718
  66.4 2.4 %reshape.18 = bf16[8,4,4,16,128]{4,3,2,1,0:T(8,128)(2,1)} reshape(bf16[8,4,8192]{2,1,0:T(4,128)(2,1)} %param.23) | data formatting | bytes 1048576 | tf_op jit(solution)/shard_map/reshape | solution.py:725
  68.7 1.1 copy.17
  69.8 10.6 %collective-permute-start.2 = (bf16[2,16,8,512]{3,2,1,0:T(8,128)(2,1)}, bf16[2,16,8,512]{3,2,1,0:T(8,128)(2,1)S(1)}, u32[]{:S(2)}, u32[]{:S(2)}) collective-permute-start(bf16[2,16,8,512]{3,2,1,0:T(8,128)(2,1)} %get-tuple-element.43), channel_id=1, source_target_pairs={{0,5},{1,6},{2,7},{3,4},{4,1},{5,2},{6,3},{7,0},{8,13},{9,14},{10,... | collective-permute-start | bytes 786440 | tf_op jit(solution)/shard_map/ppermute | solution.py:718
  80.4 2.8 %collective-permute-start.3 = (bf16[2,16,8,512]{3,2,1,0:T(8,128)(2,1)}, bf16[2,16,8,512]{3,2,1,0:T(8,128)(2,1)S(1)}, u32[]{:S(2)}, u32[]{:S(2)}) collective-permute-start(bf16[2,16,8,512]{3,2,1,0:T(8,128)(2,1)} %get-tuple-element.44), channel_id=1, source_target_pairs={{0,6},{1,7},{2,4},{3,5},{4,2},{5,3},{6,0},{7,1},{8,14},{9,15},{10,... | collective-permute-start | bytes 786440 | tf_op jit(solution)/shard_map/ppermute | solution.py:718
  83.2 0.8 copy-done.6
  84.0 0.8 copy-done.7
  85.4 7.4 %resident.1 = (f32[8,4,64,128]{3,2,1,0:T(8,128)S(1)}, f32[8,4,64,128]{3,2,1,0:T(8,128)}, f32[8,4,64,128]{3,2,1,0:T(8,128)}) custom-call(s32[8]{0:T(128)S(1)} %copy-done.16, bf16[8,4,64,128]{3,2,1,0:T(8,128)(2,1)S(1)} %bitcast.11, bf16[8,4,512]{2,1,0:T(4,128)(2,1)S(1)} %copy-done.6, bf16[8,4,512]{2,1,0:T(4,128)(2,1)S(1)} %copy-done.7, ...), custom_call_target="tpu_custom_call" | custom-call | flops 2000000000 | bytes 16777216 | tf_op jit(solution)/shard_map/resident/pallas_call | solution.py:379
  93.5 1.2 %copy-done = f32[8,4,64,128]{3,2,1,0:T(8,128)S(1)} copy-done((f32[8,4,64,128]{3,2,1,0:T(8,128)S(1)}, f32[8,4,64,128]{3,2,1,0:T(8,128)}, u32[]{:S(2)}) %copy-start) | copy-done | bytes 1048600
  94.7 1.2 %copy-done.1 = f32[8,4,64,128]{3,2,1,0:T(8,128)S(1)} copy-done((f32[8,4,64,128]{3,2,1,0:T(8,128)S(1)}, f32[8,4,64,128]{3,2,1,0:T(8,128)}, u32[]{:S(2)}) %copy-start.1) | copy-done | bytes 1048600
  96.0 12.0 %shard_map.154 = (f32[8,4,64,128]{3,2,1,0:T(8,128)S(1)}, f32[8,4,64,128]{3,2,1,0:T(8,128)S(1)}, f32[8,4,64,128]{3,2,1,0:T(8,128)S(1)}) custom-call(s32[4,16]{1,0:T(4,128)S(1)} %copy-done.14, s32[32,16]{1,0:T(8,128)S(1)} %get-tuple-element.36.place_of, s32[32,16]{1,0:T(8,128)S(1)} %get-tuple-element.37.row_of, s32[32,16]{1,0:T(8,128)S(1)} %get-tuple-element.38.rank_of, ...), custom_call_target="tpu_custom_call" | custom-call | flops 1000000000 | bytes 12582912 | tf_op jit(solution)/shard_map/pallas_call | solution.py:596
  108.0 7.2 %shard_map.156 = bf16[8,4,8192]{2,1,0:T(4,128)(2,1)} custom-call(s32[4,16]{1,0:T(4,128)S(1)} %copy-done.14, s32[32,16]{1,0:T(8,128)S(1)} %get-tuple-element.36.place_of, s32[32,16]{1,0:T(8,128)S(1)} %get-tuple-element.37.row_of, s32[32,16]{1,0:T(8,128)S(1)} %get-tuple-element.38.rank_of, s32[32,16]{1,0:T(8,128)S(1)} %get-tuple-element.39.used, ...), custom_call_target="tpu_custom_call" | custom-call | flops 1000000000 | bytes 12582912 | tf_op jit(solution)/shard_map/pallas_call | solution.py:596
  (56 shorter events, 3.0 us)
Async XLA Ops:
  0.0 56.6 %copy-start.8 = (f32[16,128]{1,0:T(8,128)S(1)}, f32[16,128]{1,0:T(8,128)}, u32[]{:S(2)}) copy-start(f32[16,128]{1,0:T(8,128)} %constant.24.clone.ca) | copy-start | bytes 24580
  0.0 56.6 %copy-start.9 = (f32[16,128]{1,0:T(8,128)S(1)}, f32[16,128]{1,0:T(8,128)}, u32[]{:S(2)}) copy-start(f32[16,128]{1,0:T(8,128)} %constant.25.clone.sa) | copy-start | bytes 24580
  0.0 56.6 %copy-start.2 = (f32[321,128]{1,0:T(8,128)S(1)}, f32[321,128]{1,0:T(8,128)}, u32[]{:S(2)}) copy-start(f32[321,128]{1,0:T(8,128)} %constant.26.clone.cb) | copy-start | bytes 493060
  0.0 56.6 %copy-start.3 = (f32[321,128]{1,0:T(8,128)S(1)}, f32[321,128]{1,0:T(8,128)}, u32[]{:S(2)}) copy-start(f32[321,128]{1,0:T(8,128)} %constant.27.clone.sb) | copy-start | bytes 493060
  0.0 56.6 %copy-start.15 = (s32[8]{0:T(128)S(1)}, s32[8]{0:T(128)}, u32[]{:S(2)}) copy-start(s32[8]{0:T(128)} %lens.9) | copy-start | bytes 100
  0.0 29.7 %collective-permute-start = (bf16[8,4,8192]{2,1,0:T(4,128)(2,1)}, bf16[8,4,8192]{2,1,0:T(4,128)(2,1)}, u32[]{:S(2)}, u32[]{:S(2)}) collective-permute-start(bf16[8,4,8192]{2,1,0:T(4,128)(2,1)} %param.23), channel_id=1, source_target_pairs={{4,8},{5,9},{6,10},{7,11},{8,4},{9,5},{10,6},{11,7},{20,24},{21,25... | collective-permute-start | bytes 1572872 | tf_op jit(solution)/shard_map/ppermute | solution.py:701
  6.1 14.5 %collective-permute-start.5 = (bf16[2,16,8,512]{3,2,1,0:T(8,128)(2,1)}, bf16[2,16,8,512]{3,2,1,0:T(8,128)(2,1)S(1)}, u32[]{:S(2)}, u32[]{:S(2)}) collective-permute-start(bf16[2,16,8,512]{3,2,1,0:T(8,128)(2,1)} %get-tuple-element.46), channel_id=1, source_target_pairs={{0,4},{1,5},{2,6},{3,7},{4,12},{5,13},{6,14},{7,15},{8,0},{9,1},{1... | collective-permute-start | bytes 786440 | tf_op jit(solution)/shard_map/ppermute | solution.py:718
  7.0 21.2 %collective-permute-start.6 = (bf16[2,16,8,512]{3,2,1,0:T(8,128)(2,1)}, bf16[2,16,8,512]{3,2,1,0:T(8,128)(2,1)S(1)}, u32[]{:S(2)}, u32[]{:S(2)}) collective-permute-start(bf16[2,16,8,512]{3,2,1,0:T(8,128)(2,1)} %get-tuple-element.47), channel_id=1, source_target_pairs={{0,5},{1,6},{2,7},{3,4},{4,13},{5,14},{6,15},{7,12},{8,1},{9,2},{1... | collective-permute-start | bytes 786440 | tf_op jit(solution)/shard_map/ppermute | solution.py:718
  8.9 39.9 %collective-permute-start.7 = (bf16[2,16,8,512]{3,2,1,0:T(8,128)(2,1)}, bf16[2,16,8,512]{3,2,1,0:T(8,128)(2,1)S(1)}, u32[]{:S(2)}, u32[]{:S(2)}) collective-permute-start(bf16[2,16,8,512]{3,2,1,0:T(8,128)(2,1)} %get-tuple-element.48), channel_id=1, source_target_pairs={{0,6},{1,7},{2,4},{3,5},{4,14},{5,15},{6,12},{7,13},{8,2},{9,3},{1... | collective-permute-start | bytes 786440 | tf_op jit(solution)/shard_map/ppermute | solution.py:718
  11.5 37.3 %collective-permute-start.8 = (bf16[2,16,8,512]{3,2,1,0:T(8,128)(2,1)}, bf16[2,16,8,512]{3,2,1,0:T(8,128)(2,1)S(1)}, u32[]{:S(2)}, u32[]{:S(2)}) collective-permute-start(bf16[2,16,8,512]{3,2,1,0:T(8,128)(2,1)} %get-tuple-element.49), channel_id=1, source_target_pairs={{0,7},{1,4},{2,5},{3,6},{4,15},{5,12},{6,13},{7,14},{8,3},{9,0},{1... | collective-permute-start | bytes 786440 | tf_op jit(solution)/shard_map/ppermute | solution.py:718
  20.6 31.2 %collective-permute-start.9 = (bf16[2,16,8,512]{3,2,1,0:T(8,128)(2,1)}, bf16[2,16,8,512]{3,2,1,0:T(8,128)(2,1)S(1)}, u32[]{:S(2)}, u32[]{:S(2)}) collective-permute-start(bf16[2,16,8,512]{3,2,1,0:T(8,128)(2,1)} %get-tuple-element.51), channel_id=1, source_target_pairs={{0,1},{1,2},{2,3},{3,0},{4,5},{5,6},{6,7},{7,4},{8,9},{9,10},{10,1... | collective-permute-start | bytes 786440 | tf_op jit(solution)/shard_map/ppermute | solution.py:718
  28.2 26.9 %collective-permute-start.10 = (bf16[2,16,8,512]{3,2,1,0:T(8,128)(2,1)}, bf16[2,16,8,512]{3,2,1,0:T(8,128)(2,1)S(1)}, u32[]{:S(2)}, u32[]{:S(2)}) collective-permute-start(bf16[2,16,8,512]{3,2,1,0:T(8,128)(2,1)} %get-tuple-element.52), channel_id=1, source_target_pairs={{0,2},{1,3},{2,0},{3,1},{4,6},{5,7},{6,4},{7,5},{8,10},{9,11},{10,... | collective-permute-start | bytes 786440 | tf_op jit(solution)/shard_map/ppermute | solution.py:718
  29.7 26.9 %collective-permute-start.11 = (bf16[2,16,8,512]{3,2,1,0:T(8,128)(2,1)}, bf16[2,16,8,512]{3,2,1,0:T(8,128)(2,1)S(1)}, u32[]{:S(2)}, u32[]{:S(2)}) collective-permute-start(bf16[2,16,8,512]{3,2,1,0:T(8,128)(2,1)} %get-tuple-element.53), channel_id=1, source_target_pairs={{0,3},{1,0},{2,1},{3,2},{4,7},{5,4},{6,5},{7,6},{8,11},{9,8},{10,9... | collective-permute-start | bytes 786440 | tf_op jit(solution)/shard_map/ppermute | solution.py:718
  32.4 14.1 %all-to-all-start = ((s32[16,1,384]{2,1,0:T(1,128)}), s32[16,1,384]{2,1,0:T(1,128)S(1)}, u32[]{:S(2)}, u32[]{:S(2)}) async-start(s32[16,1,384]{2,1,0:T(1,128)} %note.1), calls=%async_computation | async-start | bytes 49152 | tf_op jit(solution)/shard_map/all_to_all | solution.py:733
  39.4 24.1 %copy-start.13 = (s32[4,16]{1,0:T(4,128)}, s32[4,16]{1,0:T(4,128)S(1)}, u32[]{:S(2)}) copy-start(s32[4,16]{1,0:T(4,128)S(1)} %dynamic-slice_bitcast_fusion.stages.mine) | copy-start | bytes 772
  47.1 16.4 %copy-start.11 = (s32[16,128]{1,0:T(8,128)}, s32[16,128]{1,0:T(8,128)S(1)}, u32[]{:S(2)}) copy-start(s32[16,128]{1,0:T(8,128)S(1)} %get-tuple-element.40.tally) | copy-start | bytes 24580
  48.7 16.1 %collective-permute-start.1 = (bf16[2,16,8,512]{3,2,1,0:T(8,128)(2,1)}, bf16[2,16,8,512]{3,2,1,0:T(8,128)(2,1)S(1)}, u32[]{:S(2)}, u32[]{:S(2)}) collective-permute-start(bf16[2,16,8,512]{3,2,1,0:T(8,128)(2,1)} %get-tuple-element.42), channel_id=1, source_target_pairs={{0,4},{1,5},{2,6},{3,7},{4,0},{5,1},{6,2},{7,3},{8,12},{9,13},{10,... | collective-permute-start | bytes 786440 | tf_op jit(solution)/shard_map/ppermute | solution.py:718
  48.8 21.0 %collective-permute-start.12 = (bf16[2,16,8,512]{3,2,1,0:T(8,128)(2,1)}, bf16[2,16,8,512]{3,2,1,0:T(8,128)(2,1)S(1)}, u32[]{:S(2)}, u32[]{:S(2)}) collective-permute-start(bf16[2,16,8,512]{3,2,1,0:T(8,128)(2,1)} %get-tuple-element.54), channel_id=1, source_target_pairs={{0,12},{1,13},{2,14},{3,15},{4,4},{5,5},{6,6},{7,7},{8,8},{9,9},{1... | collective-permute-start | bytes 786440 | tf_op jit(solution)/shard_map/ppermute | solution.py:718
  51.8 28.6 %collective-permute-start.13 = (bf16[2,16,8,512]{3,2,1,0:T(8,128)(2,1)}, bf16[2,16,8,512]{3,2,1,0:T(8,128)(2,1)S(1)}, u32[]{:S(2)}, u32[]{:S(2)}) collective-permute-start(bf16[2,16,8,512]{3,2,1,0:T(8,128)(2,1)} %get-tuple-element.55), channel_id=1, source_target_pairs={{0,13},{1,14},{2,15},{3,12},{4,5},{5,6},{6,7},{7,4},{8,9},{9,10},{... | collective-permute-start | bytes 786440 | tf_op jit(solution)/shard_map/ppermute | solution.py:718
  55.1 28.1 %collective-permute-start.14 = (bf16[2,16,8,512]{3,2,1,0:T(8,128)(2,1)}, bf16[2,16,8,512]{3,2,1,0:T(8,128)(2,1)}, u32[]{:S(2)}, u32[]{:S(2)}) collective-permute-start(bf16[2,16,8,512]{3,2,1,0:T(8,128)(2,1)} %get-tuple-element.56), channel_id=1, source_target_pairs={{0,14},{1,15},{2,12},{3,13},{4,6},{5,7},{6,4},{7,5},{8,10},{9,11},... | collective-permute-start | bytes 786440 | tf_op jit(solution)/shard_map/ppermute | solution.py:718
  64.1 43.9 %collective-permute-start.16 = (bf16[8,4,64,128]{3,2,1,0:T(8,128)(2,1)}, bf16[8,4,64,128]{3,2,1,0:T(8,128)(2,1)S(1)}, u32[]{:S(2)}, u32[]{:S(2)}) collective-permute-start(bf16[8,4,64,128]{3,2,1,0:T(8,128)(2,1)} %get-tuple-element.65), channel_id=1, source_target_pairs={{4,8},{5,9},{6,10},{7,11},{8,4},{9,5},{10,6},{11,7},{20,24},{21,25... | collective-permute-start | bytes 1572872 | tf_op jit(solution)/shard_map/ppermute | solution.py:744
  64.8 28.0 %collective-permute-start.15 = (bf16[2,16,8,512]{3,2,1,0:T(8,128)(2,1)}, bf16[2,16,8,512]{3,2,1,0:T(8,128)(2,1)}, u32[]{:S(2)}, u32[]{:S(2)}) collective-permute-start(bf16[2,16,8,512]{3,2,1,0:T(8,128)(2,1)} %get-tuple-element.57), channel_id=1, source_target_pairs={{0,15},{1,12},{2,13},{3,14},{4,7},{5,4},{6,5},{7,6},{8,11},{9,8},{... | collective-permute-start | bytes 786440 | tf_op jit(solution)/shard_map/ppermute | solution.py:718
  69.8 38.1 %collective-permute-start.2 = (bf16[2,16,8,512]{3,2,1,0:T(8,128)(2,1)}, bf16[2,16,8,512]{3,2,1,0:T(8,128)(2,1)S(1)}, u32[]{:S(2)}, u32[]{:S(2)}) collective-permute-start(bf16[2,16,8,512]{3,2,1,0:T(8,128)(2,1)} %get-tuple-element.43), channel_id=1, source_target_pairs={{0,5},{1,6},{2,7},{3,4},{4,1},{5,2},{6,3},{7,0},{8,13},{9,14},{10,... | collective-permute-start | bytes 786440 | tf_op jit(solution)/shard_map/ppermute | solution.py:718
  80.4 27.5 %collective-permute-start.3 = (bf16[2,16,8,512]{3,2,1,0:T(8,128)(2,1)}, bf16[2,16,8,512]{3,2,1,0:T(8,128)(2,1)S(1)}, u32[]{:S(2)}, u32[]{:S(2)}) collective-permute-start(bf16[2,16,8,512]{3,2,1,0:T(8,128)(2,1)} %get-tuple-element.44), channel_id=1, source_target_pairs={{0,6},{1,7},{2,4},{3,5},{4,2},{5,3},{6,0},{7,1},{8,14},{9,15},{10,... | collective-permute-start | bytes 786440 | tf_op jit(solution)/shard_map/ppermute | solution.py:718
  83.2 24.8 %collective-permute-start.4 = (bf16[2,16,8,512]{3,2,1,0:T(8,128)(2,1)}, bf16[2,16,8,512]{3,2,1,0:T(8,128)(2,1)S(1)}, u32[]{:S(2)}, u32[]{:S(2)}) collective-permute-start(bf16[2,16,8,512]{3,2,1,0:T(8,128)(2,1)} %get-tuple-element.45), channel_id=1, source_target_pairs={{0,7},{1,4},{2,5},{3,6},{4,3},{5,0},{6,1},{7,2},{8,15},{9,12},{10,... | collective-permute-start | bytes 786440 | tf_op jit(solution)/shard_map/ppermute | solution.py:718
  85.4 7.4 %copy-start.18 = (f32[8,4,2,64]{3,2,1,0:T(2,128)S(1)}, f32[8,4,2,64]{3,2,1,0:T(2,128)}, u32[]{:S(2)}) copy-start(f32[8,4,2,64]{3,2,1,0:T(2,128)} %copy-done.17) | copy-start | bytes 49156
  85.4 8.1 %copy-start.5 = (bf16[2,16,8,512]{3,2,1,0:T(8,128)(2,1)S(1)}, bf16[2,16,8,512]{3,2,1,0:T(8,128)(2,1)}, u32[]{:S(2)}) copy-start(bf16[2,16,8,512]{3,2,1,0:T(8,128)(2,1)} %get-tuple-element.50.refs_4_) | copy-start | bytes 786436
  85.4 8.1 %copy-start.10 = (f32[16,128]{1,0:T(8,128)S(1)}, f32[16,128]{1,0:T(8,128)}, u32[]{:S(2)}) copy-start(f32[16,128]{1,0:T(8,128)} %constant.25.clone.sa) | copy-start | bytes 24580
  85.4 8.1 %copy-start.12 = (s32[16,128]{1,0:T(8,128)S(1)}, s32[16,128]{1,0:T(8,128)}, u32[]{:S(2)}) copy-start(s32[16,128]{1,0:T(8,128)} %copy-done.11) | copy-start | bytes 24580
  85.4 8.1 %copy-start.14 = (s32[4,16]{1,0:T(4,128)S(1)}, s32[4,16]{1,0:T(4,128)}, u32[]{:S(2)}) copy-start(s32[4,16]{1,0:T(4,128)} %copy-done.13) | copy-start | bytes 772
  92.8 15.2 %collective-permute-start.17 = (f32[8,4,2,64]{3,2,1,0:T(2,128)S(1)}, f32[8,4,2,64]{3,2,1,0:T(2,128)S(1)}, u32[]{:S(2)}, u32[]{:S(2)}) collective-permute-start(f32[8,4,2,64]{3,2,1,0:T(2,128)S(1)} %copy-done.18), channel_id=1, source_target_pairs={{4,8},{5,9},{6,10},{7,11},{8,4},{9,5},{10,6},{11,7},{20,24},{21,25... | collective-permute-start | bytes 49160 | tf_op jit(solution)/shard_map/ppermute | solution.py:745
  93.5 1.2 %copy-start = (f32[8,4,64,128]{3,2,1,0:T(8,128)S(1)}, f32[8,4,64,128]{3,2,1,0:T(8,128)}, u32[]{:S(2)}) copy-start(f32[8,4,64,128]{3,2,1,0:T(8,128)} %get-tuple-element.59.refs_13_) | copy-start | bytes 3145732
  (6 other events, 4.9 us)

commit v12 on v11

--- a/solution.py
+++ b/solution.py
@@ -309,7 +309,6 @@
     pieces = slot_count // piece
     steps = step_k.shape[1]
     width = q_ref.shape[2]
-    group = width // steps
 
     def copies(r, i):
         part = pl.ds(i * piece, piece)
@@ -332,7 +331,7 @@
     lane = lax.broadcasted_iota(jnp.int32, (width, piece), 1)
     causal = (
         lax.broadcasted_iota(jnp.int32, (width, steps), 1)
-        <= lax.broadcasted_iota(jnp.int32, (width, steps), 0) // group
+        <= lax.rem(lax.broadcasted_iota(jnp.int32, (width, steps), 0), steps)
     )
 
     def one_row(r, _):
@@ -406,7 +405,7 @@
     elif kind == "state":
         acc, top, total, kbuf, vbuf = refs[3:]
     else:
-        part, stats, out_all, acc, top, total, scr, out, sems, kbuf, vbuf = refs[3:]
+        part, stats, out_all, acc, top, total, _, out, sems, kbuf, vbuf = refs[3:]
     state = (acc, top, total)
     rows = q_ref.shape[0]
     width = q_ref.shape[2]
@@ -522,17 +521,15 @@
             beyond(r)
 
     def put_out(pair, new):
-        done = [value / amount for one in new for value, _, amount in one]
-        for i, value in enumerate(done):
-            scr[i] = value
         steps = out.shape[1]
         group = width // steps
-        for i, r in enumerate(pair):
-            for head in range(KVH):
+        for r, one in zip(pair, new):
+            for head, (value, _, amount) in enumerate(one):
+                done = value / amount
                 for g in range(group):
                     column = (head * group + g) * HD
-                    out[r, :, column : column + HD] = scr[
-                        i * KVH + head, pl.ds(g, steps, stride=group), :
+                    out[r, :, column : column + HD] = done[
+                        g * steps : (g + 1) * steps, :
                     ].astype(jnp.bfloat16)
 
     def final_rows(pair):
@@ -722,7 +719,7 @@
     got = {phase: send(phase) for phase in names}
 
     def regroup(value):
-        value = value.reshape(rows, steps, KVH, group, HD).transpose(0, 2, 1, 3, 4)
+        value = value.reshape(rows, steps, KVH, group, HD).transpose(0, 2, 3, 1, 4)
         return value.reshape(rows, KVH, steps * group, HD)
 
     queries, mirrored = lax.optimization_barrier((queries, mirrored))

time: 116 us -> 108 us (0.931)
  local copies, waits for them, and re-layouts: 12 us -> 8 us
  starting transfers between devices: 43 us -> 40.5 us
    reshape x4 -> x0, local copies, waits for them, and re-layouts: 5.1 us -> none  [regroup(): value = value.reshape(rows, steps, KVH, group, HD).transpose(0, 2, 1, 3, 4)]
    ppermute x15, starting transfers between devices: 33.8 us -> 32 us  [send(): value = lax.ppermute(value, 'seq', pairs)]
    unnamed x38 -> x34, local copies, waits for them, and re-layouts: 6.2 us -> 7.32 us
  transfers between devices with their start and end apart: 19 -> 19, of which waited for: 3 -> 3; matrix products, arithmetic and copies ran while one was open for 5% -> 1% of each run, Pallas kernels for 29% -> 30%
where the time goes in v12:
time: 108 us
  starting transfers between devices  40.5 us (38%)
  Pallas kernels  39.1 us (36%)
  waiting for transfers between devices  19.7 us (18%)
  local copies, waits for them, and re-layouts  8 us (7%)
    ppermute x15, starting transfers between devices, send(): value = lax.ppermute(value, 'seq', pairs)  32 us
    pallas_call x3, Pallas kernels, span(): pl.pallas_call(functools.partial(span_kernel, kind, kernel, first, count,...  24 us
    ppermute x15, waiting for transfers between devices, send(): value = lax.ppermute(value, 'seq', pairs)  12.6 us
    pallas_call x1, Pallas kernels, resident(): pl.pallas_call(resident_kernel, out_shape=state_shapes(rows, grouped.shap...  7.35 us
    unnamed x34, local copies, waits for them, and re-layouts  7.32 us
    all_to_all x1, waiting for transfers between devices, body(): lax.all_to_all(notes, 'seq', split_axis=0, concat_axis=0, tiled=True)  7.14 us
    all_to_all x1, starting transfers between devices, body(): lax.all_to_all(notes, 'seq', split_axis=0, concat_axis=0, tiled=True)  6.31 us
    pallas_call x1, Pallas kernels, pack(): pl.pallas_call(functools.partial(pack_kernel, n), out_shape=(message,) *...  4.51 us
  transfers between devices with their start and end apart: 19, of which 3 were waited for; matrix products, arithmetic and copies ran while one was open for 1% of the time, Pallas kernels for 30%

profile of v12, /device:TPU:27, one launch (start us, length us, event | category | flops | bytes accessed | tf_op | source)
XLA Modules:
  0.0 107.6 jit_solution(17127451194625018284)
XLA Ops:
  0.0 0.8 collective-permute-start
  0.9 4.5 %pack.1 = (bf16[2,16,8,512]{3,2,1,0:T(8,128)(2,1)}, bf16[2,16,8,512]{3,2,1,0:T(8,128)(2,1)}, bf16[2,16,8,512]{3,2,1,0:T(8,128)(2,1)}, bf16[2,16,8,512]{3,2,1,0:T...) custom-call(s32[4,4]{1,0:T(4,128)} %constant.22.clone.phase_table, ...), custom_call_target="tpu_custom_call" | custom-call | tf_op jit(solution)/shard_map/pack/pallas_call | solution.py:88
  5.4 1.6 %collective-permute-start.5 = (bf16[2,16,8,512]{3,2,1,0:T(8,128)(2,1)}, bf16[2,16,8,512]{3,2,1,0:T(8,128)(2,1)S(1)}, u32[]{:S(2)}, u32[]{:S(2)}) collective-permute-start(bf16[2,16,8,512]{3,2,1,0:T(8,128)(2,1)} %get-tuple-element.46), channel_id=1, source_target_pairs={{0,4},{1,5},{2,6},{3,7},{4,12},{5,13},{6,14},{7,15},{8,0},{9,1},{1... | collective-permute-start | bytes 786440 | tf_op jit(solution)/shard_map/ppermute | solution.py:715
  7.0 1.9 %collective-permute-start.6 = (bf16[2,16,8,512]{3,2,1,0:T(8,128)(2,1)}, bf16[2,16,8,512]{3,2,1,0:T(8,128)(2,1)S(1)}, u32[]{:S(2)}, u32[]{:S(2)}) collective-permute-start(bf16[2,16,8,512]{3,2,1,0:T(8,128)(2,1)} %get-tuple-element.47), channel_id=1, source_target_pairs={{0,5},{1,6},{2,7},{3,4},{4,13},{5,14},{6,15},{7,12},{8,1},{9,2},{1... | collective-permute-start | bytes 786440 | tf_op jit(solution)/shard_map/ppermute | solution.py:715
  8.8 2.6 %collective-permute-start.7 = (bf16[2,16,8,512]{3,2,1,0:T(8,128)(2,1)}, bf16[2,16,8,512]{3,2,1,0:T(8,128)(2,1)S(1)}, u32[]{:S(2)}, u32[]{:S(2)}) collective-permute-start(bf16[2,16,8,512]{3,2,1,0:T(8,128)(2,1)} %get-tuple-element.48), channel_id=1, source_target_pairs={{0,6},{1,7},{2,4},{3,5},{4,14},{5,15},{6,12},{7,13},{8,2},{9,3},{1... | collective-permute-start | bytes 786440 | tf_op jit(solution)/shard_map/ppermute | solution.py:715
  11.8 8.8 %collective-permute-done.5.refs_0_ = bf16[2,16,8,512]{3,2,1,0:T(8,128)(2,1)S(1)} collective-permute-done((bf16[2,16,8,512]{3,2,1,0:T(8,128)(2,1)}, bf16[2,16,8,512]{3,2,1,0:T(8,128)(2,1)S(1)}, u32[]{:S(2)}, u32[]{:S(2)}) %collective-permute-start.5) | collective-permute-done | bytes 262176 | tf_op jit(solution)/shard_map/ppermute | solution.py:715
  20.6 3.8 %collective-permute-start.9 = (bf16[2,16,8,512]{3,2,1,0:T(8,128)(2,1)}, bf16[2,16,8,512]{3,2,1,0:T(8,128)(2,1)S(1)}, u32[]{:S(2)}, u32[]{:S(2)}) collective-permute-start(bf16[2,16,8,512]{3,2,1,0:T(8,128)(2,1)} %get-tuple-element.51), channel_id=1, source_target_pairs={{0,1},{1,2},{2,3},{3,0},{4,5},{5,6},{6,7},{7,4},{8,9},{9,10},{10,1... | collective-permute-start | bytes 786440 | tf_op jit(solution)/shard_map/ppermute | solution.py:715
  24.4 3.8 %collective-permute-done.6.refs_1_ = bf16[2,16,8,512]{3,2,1,0:T(8,128)(2,1)S(1)} collective-permute-done((bf16[2,16,8,512]{3,2,1,0:T(8,128)(2,1)}, bf16[2,16,8,512]{3,2,1,0:T(8,128)(2,1)S(1)}, u32[]{:S(2)}, u32[]{:S(2)}) %collective-permute-start.6) | collective-permute-done | bytes 262176 | tf_op jit(solution)/shard_map/ppermute | solution.py:715
  28.2 1.5 %collective-permute-start.10 = (bf16[2,16,8,512]{3,2,1,0:T(8,128)(2,1)}, bf16[2,16,8,512]{3,2,1,0:T(8,128)(2,1)S(1)}, u32[]{:S(2)}, u32[]{:S(2)}) collective-permute-start(bf16[2,16,8,512]{3,2,1,0:T(8,128)(2,1)} %get-tuple-element.52), channel_id=1, source_target_pairs={{0,2},{1,3},{2,0},{3,1},{4,6},{5,7},{6,4},{7,5},{8,10},{9,11},{10,... | collective-permute-start | bytes 786440 | tf_op jit(solution)/shard_map/ppermute | solution.py:715
  29.7 2.7 %note.1 = s32[16,1,384]{2,1,0:T(1,128)} custom-call(s32[128]{0:T(128)} %bitcast.22, s32[128]{0:T(128)} %rows.1, s32[8]{0:T(128)} %lens.9), custom_call_target="tpu_custom_call" | custom-call | tf_op jit(solution)/shard_map/note/pallas_call | solution.py:147
  32.4 6.3 %all-to-all-start = ((s32[16,1,384]{2,1,0:T(1,128)}), s32[16,1,384]{2,1,0:T(1,128)S(1)}, u32[]{:S(2)}, u32[]{:S(2)}) async-start(s32[16,1,384]{2,1,0:T(1,128)} %note.1), calls=%async_computation | async-start | bytes 49152 | tf_op jit(solution)/shard_map/all_to_all | solution.py:730
  38.7 0.7 dynamic-slice_bitcast_fusion.stages.mine
  39.4 7.1 %all-to-all-done.notes = s32[16,1,384]{2,1,0:T(1,128)S(1)} async-done(((s32[16,1,384]{2,1,0:T(1,128)}), s32[16,1,384]{2,1,0:T(1,128)S(1)}, u32[]{:S(2)}, u32[]{:S(2)}) %all-to-all-start) | async-done | bytes 24608 | tf_op jit(solution)/shard_map/all_to_all | solution.py:730
  47.2 3.0 %collective-permute-start.12 = (bf16[2,16,8,512]{3,2,1,0:T(8,128)(2,1)}, bf16[2,16,8,512]{3,2,1,0:T(8,128)(2,1)S(1)}, u32[]{:S(2)}, u32[]{:S(2)}) collective-permute-start(bf16[2,16,8,512]{3,2,1,0:T(8,128)(2,1)} %get-tuple-element.54), channel_id=1, source_target_pairs={{0,12},{1,13},{2,14},{3,15},{4,4},{5,5},{6,6},{7,7},{8,8},{9,9},{1... | collective-permute-start | bytes 786440 | tf_op jit(solution)/shard_map/ppermute | solution.py:715
  50.2 3.3 %collective-permute-start.13 = (bf16[2,16,8,512]{3,2,1,0:T(8,128)(2,1)}, bf16[2,16,8,512]{3,2,1,0:T(8,128)(2,1)S(1)}, u32[]{:S(2)}, u32[]{:S(2)}) collective-permute-start(bf16[2,16,8,512]{3,2,1,0:T(8,128)(2,1)} %get-tuple-element.55), channel_id=1, source_target_pairs={{0,13},{1,14},{2,15},{3,12},{4,5},{5,6},{6,7},{7,4},{8,9},{9,10},{... | collective-permute-start | bytes 786440 | tf_op jit(solution)/shard_map/ppermute | solution.py:715
  53.4 1.5 %collective-permute-start.14 = (bf16[2,16,8,512]{3,2,1,0:T(8,128)(2,1)}, bf16[2,16,8,512]{3,2,1,0:T(8,128)(2,1)S(1)}, u32[]{:S(2)}, u32[]{:S(2)}) collective-permute-start(bf16[2,16,8,512]{3,2,1,0:T(8,128)(2,1)} %get-tuple-element.56), channel_id=1, source_target_pairs={{0,14},{1,15},{2,12},{3,13},{4,6},{5,7},{6,4},{7,5},{8,10},{9,11},... | collective-permute-start | bytes 786440 | tf_op jit(solution)/shard_map/ppermute | solution.py:715
  54.9 0.9 copy-done.3
  55.9 0.9 copy-done.5
  56.8 0.9 copy-done.7
  57.7 0.7 copy-done.11
  58.4 0.7 copy-done.13
  59.8 5.1 %shard_map.155 = (bf16[8,4,64,128]{3,2,1,0:T(8,128)(2,1)S(1)}, f32[8,4,2,64]{3,2,1,0:T(2,128)S(1)}) custom-call(s32[4,16]{1,0:T(4,128)S(1)} %dynamic-slice_bitcast_fusion.stages.mine, s32[32,16]{1,0:T(8,128)S(1)} %get-tuple-element.36.place_of, s32[32,16]{1,0:T(8,128)S(1)} %get-tuple-element.37.row_of, s32[32,16]{1,0:T(8,128)S(1)} %get-tuple-element.38.rank_of, ...), custom_call_target="tpu_custom_call" | custom-call | flops 1000000000 | bytes 12582912 | tf_op jit(solution)/shard_map/pallas_call | solution.py:593
  64.9 0.7 collective-permute-start.16
  65.6 1.5 %collective-permute-start.15 = (bf16[2,16,8,512]{3,2,1,0:T(8,128)(2,1)}, bf16[2,16,8,512]{3,2,1,0:T(8,128)(2,1)S(1)}, u32[]{:S(2)}, u32[]{:S(2)}) collective-permute-start(bf16[2,16,8,512]{3,2,1,0:T(8,128)(2,1)} %get-tuple-element.57), channel_id=1, source_target_pairs={{0,15},{1,12},{2,13},{3,14},{4,7},{5,4},{6,5},{7,6},{8,11},{9,8},{... | collective-permute-start | bytes 786440 | tf_op jit(solution)/shard_map/ppermute | solution.py:715
  67.1 8.1 %collective-permute-start.2 = (bf16[2,16,8,512]{3,2,1,0:T(8,128)(2,1)}, bf16[2,16,8,512]{3,2,1,0:T(8,128)(2,1)S(1)}, u32[]{:S(2)}, u32[]{:S(2)}) collective-permute-start(bf16[2,16,8,512]{3,2,1,0:T(8,128)(2,1)} %get-tuple-element.43), channel_id=1, source_target_pairs={{0,5},{1,6},{2,7},{3,4},{4,1},{5,2},{6,3},{7,0},{8,13},{9,14},{10,... | collective-permute-start | bytes 786440 | tf_op jit(solution)/shard_map/ppermute | solution.py:715
  75.2 2.8 %collective-permute-start.3 = (bf16[2,16,8,512]{3,2,1,0:T(8,128)(2,1)}, bf16[2,16,8,512]{3,2,1,0:T(8,128)(2,1)S(1)}, u32[]{:S(2)}, u32[]{:S(2)}) collective-permute-start(bf16[2,16,8,512]{3,2,1,0:T(8,128)(2,1)} %get-tuple-element.44), channel_id=1, source_target_pairs={{0,6},{1,7},{2,4},{3,5},{4,2},{5,3},{6,0},{7,1},{8,14},{9,15},{10,... | collective-permute-start | bytes 786440 | tf_op jit(solution)/shard_map/ppermute | solution.py:715
  78.1 7.3 %resident.1 = (f32[8,4,64,128]{3,2,1,0:T(8,128)S(1)}, f32[8,4,64,128]{3,2,1,0:T(8,128)}, f32[8,4,64,128]{3,2,1,0:T(8,128)}) custom-call(s32[8]{0:T(128)S(1)} %copy-done.16, bf16[8,4,64,128]{3,2,1,0:T(8,128)(2,1)S(1)} %bitcast.15, bf16[8,4,512]{2,1,0:T(4,128)(2,1)S(1)} %copy-done.9, bf16[8,4,512]{2,1,0:T(4,128)(2,1)S(1)} %copy-done.10, ...), custom_call_target="tpu_custom_call" | custom-call | flops 2000000000 | bytes 16777216 | tf_op jit(solution)/shard_map/resident/pallas_call | solution.py:378
  85.5 0.7 collective-permute-start.17
  86.2 1.2 %copy-done.1 = f32[8,4,64,128]{3,2,1,0:T(8,128)S(1)} copy-done((f32[8,4,64,128]{3,2,1,0:T(8,128)S(1)}, f32[8,4,64,128]{3,2,1,0:T(8,128)}, u32[]{:S(2)}) %copy-start.1) | copy-done | bytes 1048600
  87.4 1.2 %copy-done.2 = f32[8,4,64,128]{3,2,1,0:T(8,128)S(1)} copy-done((f32[8,4,64,128]{3,2,1,0:T(8,128)S(1)}, f32[8,4,64,128]{3,2,1,0:T(8,128)}, u32[]{:S(2)}) %copy-start.2) | copy-done | bytes 1048600
  88.6 12.0 %shard_map.154 = (f32[8,4,64,128]{3,2,1,0:T(8,128)S(1)}, f32[8,4,64,128]{3,2,1,0:T(8,128)S(1)}, f32[8,4,64,128]{3,2,1,0:T(8,128)S(1)}) custom-call(s32[4,16]{1,0:T(4,128)S(1)} %dynamic-slice_bitcast_fusion.stages.mine, s32[32,16]{1,0:T(8,128)S(1)} %get-tuple-element.36.place_of, s32[32,16]{1,0:T(8,128)S(1)} %get-tuple-element.37.row_of, ...), custom_call_target="tpu_custom_call" | custom-call | flops 1000000000 | bytes 12582912 | tf_op jit(solution)/shard_map/pallas_call | solution.py:593
  100.7 6.9 %shard_map.156 = bf16[8,4,8192]{2,1,0:T(4,128)(2,1)} custom-call(s32[4,16]{1,0:T(4,128)S(1)} %dynamic-slice_bitcast_fusion.stages.mine, s32[32,16]{1,0:T(8,128)S(1)} %get-tuple-element.36.place_of, s32[32,16]{1,0:T(8,128)S(1)} %get-tuple-element.37.row_of, s32[32,16]{1,0:T(8,128)S(1)} %get-tuple-element.38.rank_of, s32[32,16]{1,0:T(8,128)S(1)} %get-tuple-element.39.used, ...), custom_call_target="tpu_custom_call" | custom-call | flops 1000000000 | bytes 12582912 | tf_op jit(solution)/shard_map/pallas_call | solution.py:593
  (48 shorter events, 1.7 us)
Async XLA Ops:
  0.0 78.0 %copy-start = (bf16[8,4,8192]{2,1,0:T(4,128)(2,1)S(1)}, bf16[8,4,8192]{2,1,0:T(4,128)(2,1)}, u32[]{:S(2)}) copy-start(bf16[8,4,8192]{2,1,0:T(4,128)(2,1)} %param.23) | copy-start | bytes 1572868
  0.0 78.0 %copy-start.16 = (s32[8]{0:T(128)S(1)}, s32[8]{0:T(128)}, u32[]{:S(2)}) copy-start(s32[8]{0:T(128)} %lens.9) | copy-start | bytes 100
  0.0 78.0 %copy-start.9 = (bf16[8,4,512]{2,1,0:T(4,128)(2,1)S(1)}, bf16[8,4,512]{2,1,0:T(4,128)(2,1)}, u32[]{:S(2)}) copy-start(bf16[8,4,512]{2,1,0:T(4,128)(2,1)} %step_k.1) | copy-start | bytes 98308
  0.0 78.0 %copy-start.10 = (bf16[8,4,512]{2,1,0:T(4,128)(2,1)S(1)}, bf16[8,4,512]{2,1,0:T(4,128)(2,1)}, u32[]{:S(2)}) copy-start(bf16[8,4,512]{2,1,0:T(4,128)(2,1)} %step_v.1) | copy-start | bytes 98308
  0.0 29.7 %collective-permute-start = (bf16[8,4,8192]{2,1,0:T(4,128)(2,1)}, bf16[8,4,8192]{2,1,0:T(4,128)(2,1)S(1)}, u32[]{:S(2)}, u32[]{:S(2)}) collective-permute-start(bf16[8,4,8192]{2,1,0:T(4,128)(2,1)} %param.23), channel_id=1, source_target_pairs={{4,8},{5,9},{6,10},{7,11},{8,4},{9,5},{10,6},{11,7},{20,24},{21,25... | collective-permute-start | bytes 1572872 | tf_op jit(solution)/shard_map/ppermute | solution.py:698
  5.4 15.2 %collective-permute-start.5 = (bf16[2,16,8,512]{3,2,1,0:T(8,128)(2,1)}, bf16[2,16,8,512]{3,2,1,0:T(8,128)(2,1)S(1)}, u32[]{:S(2)}, u32[]{:S(2)}) collective-permute-start(bf16[2,16,8,512]{3,2,1,0:T(8,128)(2,1)} %get-tuple-element.46), channel_id=1, source_target_pairs={{0,4},{1,5},{2,6},{3,7},{4,12},{5,13},{6,14},{7,15},{8,0},{9,1},{1... | collective-permute-start | bytes 786440 | tf_op jit(solution)/shard_map/ppermute | solution.py:715
  7.0 21.2 %collective-permute-start.6 = (bf16[2,16,8,512]{3,2,1,0:T(8,128)(2,1)}, bf16[2,16,8,512]{3,2,1,0:T(8,128)(2,1)S(1)}, u32[]{:S(2)}, u32[]{:S(2)}) collective-permute-start(bf16[2,16,8,512]{3,2,1,0:T(8,128)(2,1)} %get-tuple-element.47), channel_id=1, source_target_pairs={{0,5},{1,6},{2,7},{3,4},{4,13},{5,14},{6,15},{7,12},{8,1},{9,2},{1... | collective-permute-start | bytes 786440 | tf_op jit(solution)/shard_map/ppermute | solution.py:715
  8.8 38.2 %collective-permute-start.7 = (bf16[2,16,8,512]{3,2,1,0:T(8,128)(2,1)}, bf16[2,16,8,512]{3,2,1,0:T(8,128)(2,1)S(1)}, u32[]{:S(2)}, u32[]{:S(2)}) collective-permute-start(bf16[2,16,8,512]{3,2,1,0:T(8,128)(2,1)} %get-tuple-element.48), channel_id=1, source_target_pairs={{0,6},{1,7},{2,4},{3,5},{4,14},{5,15},{6,12},{7,13},{8,2},{9,3},{1... | collective-permute-start | bytes 786440 | tf_op jit(solution)/shard_map/ppermute | solution.py:715
  11.5 35.7 %collective-permute-start.8 = (bf16[2,16,8,512]{3,2,1,0:T(8,128)(2,1)}, bf16[2,16,8,512]{3,2,1,0:T(8,128)(2,1)S(1)}, u32[]{:S(2)}, u32[]{:S(2)}) collective-permute-start(bf16[2,16,8,512]{3,2,1,0:T(8,128)(2,1)} %get-tuple-element.49), channel_id=1, source_target_pairs={{0,7},{1,4},{2,5},{3,6},{4,15},{5,12},{6,13},{7,14},{8,3},{9,0},{1... | collective-permute-start | bytes 786440 | tf_op jit(solution)/shard_map/ppermute | solution.py:715
  20.6 29.6 %collective-permute-start.9 = (bf16[2,16,8,512]{3,2,1,0:T(8,128)(2,1)}, bf16[2,16,8,512]{3,2,1,0:T(8,128)(2,1)S(1)}, u32[]{:S(2)}, u32[]{:S(2)}) collective-permute-start(bf16[2,16,8,512]{3,2,1,0:T(8,128)(2,1)} %get-tuple-element.51), channel_id=1, source_target_pairs={{0,1},{1,2},{2,3},{3,0},{4,5},{5,6},{6,7},{7,4},{8,9},{9,10},{10,1... | collective-permute-start | bytes 786440 | tf_op jit(solution)/shard_map/ppermute | solution.py:715
  28.2 25.3 %collective-permute-start.10 = (bf16[2,16,8,512]{3,2,1,0:T(8,128)(2,1)}, bf16[2,16,8,512]{3,2,1,0:T(8,128)(2,1)S(1)}, u32[]{:S(2)}, u32[]{:S(2)}) collective-permute-start(bf16[2,16,8,512]{3,2,1,0:T(8,128)(2,1)} %get-tuple-element.52), channel_id=1, source_target_pairs={{0,2},{1,3},{2,0},{3,1},{4,6},{5,7},{6,4},{7,5},{8,10},{9,11},{10,... | collective-permute-start | bytes 786440 | tf_op jit(solution)/shard_map/ppermute | solution.py:715
  29.7 25.2 %collective-permute-start.11 = (bf16[2,16,8,512]{3,2,1,0:T(8,128)(2,1)}, bf16[2,16,8,512]{3,2,1,0:T(8,128)(2,1)S(1)}, u32[]{:S(2)}, u32[]{:S(2)}) collective-permute-start(bf16[2,16,8,512]{3,2,1,0:T(8,128)(2,1)} %get-tuple-element.53), channel_id=1, source_target_pairs={{0,3},{1,0},{2,1},{3,2},{4,7},{5,4},{6,5},{7,6},{8,11},{9,8},{10,9... | collective-permute-start | bytes 786440 | tf_op jit(solution)/shard_map/ppermute | solution.py:715
  32.4 14.1 %all-to-all-start = ((s32[16,1,384]{2,1,0:T(1,128)}), s32[16,1,384]{2,1,0:T(1,128)S(1)}, u32[]{:S(2)}, u32[]{:S(2)}) async-start(s32[16,1,384]{2,1,0:T(1,128)} %note.1), calls=%async_computation | async-start | bytes 49152 | tf_op jit(solution)/shard_map/all_to_all | solution.py:730
  47.1 18.5 %collective-permute-start.1 = (bf16[2,16,8,512]{3,2,1,0:T(8,128)(2,1)}, bf16[2,16,8,512]{3,2,1,0:T(8,128)(2,1)S(1)}, u32[]{:S(2)}, u32[]{:S(2)}) collective-permute-start(bf16[2,16,8,512]{3,2,1,0:T(8,128)(2,1)} %get-tuple-element.42), channel_id=1, source_target_pairs={{0,4},{1,5},{2,6},{3,7},{4,0},{5,1},{6,2},{7,3},{8,12},{9,13},{10,... | collective-permute-start | bytes 786440 | tf_op jit(solution)/shard_map/ppermute | solution.py:715
  47.2 20.0 %collective-permute-start.12 = (bf16[2,16,8,512]{3,2,1,0:T(8,128)(2,1)}, bf16[2,16,8,512]{3,2,1,0:T(8,128)(2,1)S(1)}, u32[]{:S(2)}, u32[]{:S(2)}) collective-permute-start(bf16[2,16,8,512]{3,2,1,0:T(8,128)(2,1)} %get-tuple-element.54), channel_id=1, source_target_pairs={{0,12},{1,13},{2,14},{3,15},{4,4},{5,5},{6,6},{7,7},{8,8},{9,9},{1... | collective-permute-start | bytes 786440 | tf_op jit(solution)/shard_map/ppermute | solution.py:715
  50.2 25.1 %collective-permute-start.13 = (bf16[2,16,8,512]{3,2,1,0:T(8,128)(2,1)}, bf16[2,16,8,512]{3,2,1,0:T(8,128)(2,1)S(1)}, u32[]{:S(2)}, u32[]{:S(2)}) collective-permute-start(bf16[2,16,8,512]{3,2,1,0:T(8,128)(2,1)} %get-tuple-element.55), channel_id=1, source_target_pairs={{0,13},{1,14},{2,15},{3,12},{4,5},{5,6},{6,7},{7,4},{8,9},{9,10},{... | collective-permute-start | bytes 786440 | tf_op jit(solution)/shard_map/ppermute | solution.py:715
  53.4 24.6 %collective-permute-start.14 = (bf16[2,16,8,512]{3,2,1,0:T(8,128)(2,1)}, bf16[2,16,8,512]{3,2,1,0:T(8,128)(2,1)S(1)}, u32[]{:S(2)}, u32[]{:S(2)}) collective-permute-start(bf16[2,16,8,512]{3,2,1,0:T(8,128)(2,1)} %get-tuple-element.56), channel_id=1, source_target_pairs={{0,14},{1,15},{2,12},{3,13},{4,6},{5,7},{6,4},{7,5},{8,10},{9,11},... | collective-permute-start | bytes 786440 | tf_op jit(solution)/shard_map/ppermute | solution.py:715
  54.9 0.9 copy-start.3
  56.8 0.9 copy-start.7
  64.9 35.8 %collective-permute-start.16 = (bf16[8,4,64,128]{3,2,1,0:T(8,128)(2,1)S(1)}, bf16[8,4,64,128]{3,2,1,0:T(8,128)(2,1)S(1)}, u32[]{:S(2)}, u32[]{:S(2)}) collective-permute-start(bf16[8,4,64,128]{3,2,1,0:T(8,128)(2,1)S(1)} %get-tuple-element.65), channel_id=1, source_target_pairs={{4,8},{5,9},{6,10},{7,11},{8,4},{9,5},{10,6},{11,7},{20,24},{21,25... | collective-permute-start | bytes 1572872 | tf_op jit(solution)/shard_map/ppermute | solution.py:741
  65.6 19.9 %collective-permute-start.15 = (bf16[2,16,8,512]{3,2,1,0:T(8,128)(2,1)}, bf16[2,16,8,512]{3,2,1,0:T(8,128)(2,1)S(1)}, u32[]{:S(2)}, u32[]{:S(2)}) collective-permute-start(bf16[2,16,8,512]{3,2,1,0:T(8,128)(2,1)} %get-tuple-element.57), channel_id=1, source_target_pairs={{0,15},{1,12},{2,13},{3,14},{4,7},{5,4},{6,5},{7,6},{8,11},{9,8},{... | collective-permute-start | bytes 786440 | tf_op jit(solution)/shard_map/ppermute | solution.py:715
  67.1 33.5 %collective-permute-start.2 = (bf16[2,16,8,512]{3,2,1,0:T(8,128)(2,1)}, bf16[2,16,8,512]{3,2,1,0:T(8,128)(2,1)S(1)}, u32[]{:S(2)}, u32[]{:S(2)}) collective-permute-start(bf16[2,16,8,512]{3,2,1,0:T(8,128)(2,1)} %get-tuple-element.43), channel_id=1, source_target_pairs={{0,5},{1,6},{2,7},{3,4},{4,1},{5,2},{6,3},{7,0},{8,13},{9,14},{10,... | collective-permute-start | bytes 786440 | tf_op jit(solution)/shard_map/ppermute | solution.py:715
  75.2 25.4 %collective-permute-start.3 = (bf16[2,16,8,512]{3,2,1,0:T(8,128)(2,1)}, bf16[2,16,8,512]{3,2,1,0:T(8,128)(2,1)S(1)}, u32[]{:S(2)}, u32[]{:S(2)}) collective-permute-start(bf16[2,16,8,512]{3,2,1,0:T(8,128)(2,1)} %get-tuple-element.44), channel_id=1, source_target_pairs={{0,6},{1,7},{2,4},{3,5},{4,2},{5,3},{6,0},{7,1},{8,14},{9,15},{10,... | collective-permute-start | bytes 786440 | tf_op jit(solution)/shard_map/ppermute | solution.py:715
  78.0 22.6 %collective-permute-start.4 = (bf16[2,16,8,512]{3,2,1,0:T(8,128)(2,1)}, bf16[2,16,8,512]{3,2,1,0:T(8,128)(2,1)S(1)}, u32[]{:S(2)}, u32[]{:S(2)}) collective-permute-start(bf16[2,16,8,512]{3,2,1,0:T(8,128)(2,1)} %get-tuple-element.45), channel_id=1, source_target_pairs={{0,7},{1,4},{2,5},{3,6},{4,3},{5,0},{6,1},{7,2},{8,15},{9,12},{10,... | collective-permute-start | bytes 786440 | tf_op jit(solution)/shard_map/ppermute | solution.py:715
  78.0 8.1 %copy-start.4 = (f32[321,128]{1,0:T(8,128)S(1)}, f32[321,128]{1,0:T(8,128)}, u32[]{:S(2)}) copy-start(f32[321,128]{1,0:T(8,128)} %constant.26.clone.cb) | copy-start | bytes 493060
  78.0 8.1 %copy-start.6 = (f32[321,128]{1,0:T(8,128)S(1)}, f32[321,128]{1,0:T(8,128)}, u32[]{:S(2)}) copy-start(f32[321,128]{1,0:T(8,128)} %constant.27.clone.sb) | copy-start | bytes 493060
  78.1 8.1 %copy-start.8 = (bf16[2,16,8,512]{3,2,1,0:T(8,128)(2,1)S(1)}, bf16[2,16,8,512]{3,2,1,0:T(8,128)(2,1)}, u32[]{:S(2)}) copy-start(bf16[2,16,8,512]{3,2,1,0:T(8,128)(2,1)} %get-tuple-element.50.refs_4_) | copy-start | bytes 786436
  78.1 8.1 %copy-start.12 = (f32[16,128]{1,0:T(8,128)S(1)}, f32[16,128]{1,0:T(8,128)}, u32[]{:S(2)}) copy-start(f32[16,128]{1,0:T(8,128)} %constant.24.clone.ca) | copy-start | bytes 24580
  78.1 8.1 %copy-start.14 = (f32[16,128]{1,0:T(8,128)S(1)}, f32[16,128]{1,0:T(8,128)}, u32[]{:S(2)}) copy-start(f32[16,128]{1,0:T(8,128)} %constant.25.clone.sa) | copy-start | bytes 24580
  85.5 15.2 %collective-permute-start.17 = (f32[8,4,2,64]{3,2,1,0:T(2,128)S(1)}, f32[8,4,2,64]{3,2,1,0:T(2,128)S(1)}, u32[]{:S(2)}, u32[]{:S(2)}) collective-permute-start(f32[8,4,2,64]{3,2,1,0:T(2,128)S(1)} %get-tuple-element.66), channel_id=1, source_target_pairs={{4,8},{5,9},{6,10},{7,11},{8,4},{9,5},{10,6},{11,7},{20,24},{21,25... | collective-permute-start | bytes 49160 | tf_op jit(solution)/shard_map/ppermute | solution.py:742
  86.2 1.2 %copy-start.1 = (f32[8,4,64,128]{3,2,1,0:T(8,128)S(1)}, f32[8,4,64,128]{3,2,1,0:T(8,128)}, u32[]{:S(2)}) copy-start(f32[8,4,64,128]{3,2,1,0:T(8,128)} %get-tuple-element.59.refs_13_) | copy-start | bytes 3145732
  87.4 1.2 %copy-start.2 = (f32[8,4,64,128]{3,2,1,0:T(8,128)S(1)}, f32[8,4,64,128]{3,2,1,0:T(8,128)}, u32[]{:S(2)}) copy-start(f32[8,4,64,128]{3,2,1,0:T(8,128)} %get-tuple-element.60.refs_14_) | copy-start | bytes 3145732
  (4 other events, 3.0 us)
